TPU v7x, 512 devices: a whole 4x4x16 slice. The times are simulated.
512 devices in a mesh: row: 8 (over x, core), col: 16 (over z), layer: 4 (over y).
Axes of the slice: x: 4, y: 4, z: 16, core: 2. Of those that a mesh axis runs over, the one named last changes fastest.
Arguments:
- occurrences: bfloat16 [8192, 10240], P(('row', 'col', 'layer')), may hold values from -6 to 6
- idf_weight: float32 [8192], P(('row', 'col', 'layer')), may hold values from 0.25 to 2
- pattern: int32 [64, 80], replicated, may hold values 0 or 1
Outputs:
- margin: bfloat16 [10240, 10240], P('row', 'col')
All inputs are finite; a program needn't handle non-finite values.
Results may differ from a plain program's by a relative error of at most 0.0058.
Values may be sent and summed in bfloat16 or wider, within the bound.
No kernel may reach another device: no remote copies, remote signals or barrier semaphores. Data moves between devices by JAX's collectives and lax.ppermute only.
A program may use at most 64 MiB of HBM per device.

v0:
```python
import math

import jax
import jax.numpy as jnp
from jax import lax
from jax.sharding import PartitionSpec as P


def finish(partial_rows, row_start, col_start, factor):
    row_ids = row_start + lax.broadcasted_iota(jnp.int32, partial_rows.shape, 0)
    col_ids = col_start + lax.broadcasted_iota(jnp.int32, partial_rows.shape, 1)
    result = jnp.where(row_ids == col_ids, jnp.float32(0.0), partial_rows * factor)
    return result.astype(jnp.bfloat16)


def body(occurrences, idf_weight, pattern):
    owned, reads = occurrences.shape
    n_rows = lax.axis_size("row")
    n_cols = lax.axis_size("col")
    n_layers = lax.axis_size("layer")
    factor = 1.0 / math.sqrt(owned * n_rows * n_cols * n_layers)
    owner = lax.axis_index(("row", "col", "layer"))
    block_row = owner * owned // 128
    flags = lax.dynamic_slice_in_dim(pattern, block_row, 1, 0)[0]
    read_mask = jnp.repeat(flags.astype(jnp.float32), 128)
    weighted = (occurrences.astype(jnp.float32) * idf_weight[:, None] * read_mask[None, :]).astype(
        jnp.bfloat16
    )
    piece_len = reads // (n_rows * n_cols)
    reordered = (
        weighted.reshape(owned, n_cols, n_rows, piece_len)
        .transpose(0, 2, 1, 3)
        .reshape(owned, reads)
    )
    row_part, col_part = (
        lax.all_to_all(weighted, ("row", "col"), split_axis=1, concat_axis=0, tiled=True),
        lax.all_to_all(reordered, ("row", "col"), split_axis=1, concat_axis=0, tiled=True),
    )
    column_reads = lax.all_gather(col_part, "row", axis=1, tiled=True)
    partial_tile = lax.dot_general(
        lax.all_gather(row_part, "col", axis=1, tiled=True),
        column_reads,
        (((0,), (0,)), ((), ())),
        preferred_element_type=jnp.float32,
    )
    row_count = partial_tile.shape[0]
    row_start = lax.axis_index("row") * row_count
    col_start = lax.axis_index("col") * partial_tile.shape[1]
    total = lax.psum(partial_tile, "layer")
    return finish(total, row_start, col_start, factor)


def solution(mesh):
    placed = (P(("row", "col", "layer"), None), P(("row", "col", "layer")), P())
    return jax.shard_map(
        body, mesh=mesh, in_specs=placed, out_specs=P("row", "col"), check_vma=False
    )
```

profile of v0, /device:TPU:1, one launch (start us, length us, event | category | flops | bytes accessed | tf_op | source)
XLA Modules:
  0.0 287.5 jit_solution(10885676402827663510)
XLA Ops:
  6.5 0.0 all-gather.5.cloned.1.call-start
  6.5 0.7 convert_bitcast_fusion
  7.2 0.1 broadcast_bitcast_fusion
  7.3 1.1 multiply_convert_fusion
  8.4 0.6 reshape.14
  9.1 0.1 copy.9
  9.2 0.3 copy.10
  9.6 52.5 %all_to_all.38 = bf16[16,128,80]{2,0,1:T(8,128)(2,1)S(1)} all-to-all(bf16[16,128,80]{2,0,1:T(8,128)(2,1)S(1)} %copy.10), channel_id=1, replica_groups=mesh['row'=8,'col'=16,'layer'=4] {'row','col'}, dimensions={1} | all-to-all | bytes 655360 | tf_op jit(solution)/shard_map/all_to_all | solution.py:37
  62.0 0.9 copy.11
  63.0 0.0 all-gather.5.cloned.1.call-update
  63.0 0.0 all-gather.3.cloned.1.call-start
  63.0 0.6 all_to_all.28
  63.7 0.3 copy.7
  64.0 39.7 %all_to_all.39 = bf16[16,128,80]{2,0,1:T(8,128)(2,1)S(1)} all-to-all(bf16[16,128,80]{2,0,1:T(8,128)(2,1)S(1)} %copy.7), channel_id=1, replica_groups=mesh['row'=8,'col'=16,'layer'=4] {'row','col'}, dimensions={1} | all-to-all | bytes 655360 | tf_op jit(solution)/shard_map/all_to_all | solution.py:36
  103.8 0.9 copy.8
  104.7 0.0 all-gather.3.cloned.1.call-update
  104.7 0.0 all-reduce.2.cloned.1.call-start
  104.8 0.0 all-gather.5.cloned.1.call-done
  104.8 67.3 %all-gather.3.cloned.1.call-done = bf16[2048,1280]{0,1:T(8,128)(2,1)} async-done(((bf16[2048,80]{0,1:T(8,128)(2,1)}), bf16[2048,1280]{0,1:T(8,128)(2,1)}) %all-gather.3.cloned.1.call-update) | async-done | bytes 5242896 | tf_op jit(solution)/shard_map/all_gather | solution.py:41
  172.1 9.3 %fusion = f32[1280,640]{1,0:T(8,128)} fusion(bf16[2048,1280]{0,1:T(8,128)(2,1)} %all-gather.3.cloned.1.call-done, bf16[2048,640]{0,1:T(8,128)(2,1)} %all-gather.5.cloned.1.call-done), kind=kOutput, calls=%fused_computation.6 | convolution fusion | flops 3355443200 | bytes 11141120 | tf_op jit(solution)/shard_map/dot_general | solution.py:40
  181.3 0.0 all-reduce.2.cloned.1.call-update
  181.4 96.0 %all-reduce.2.cloned.1.call-done = f32[1280,640]{1,0:T(8,128)} async-done(((f32[1280,640]{1,0:T(8,128)}), f32[1280,640]{1,0:T(8,128)}) %all-reduce.2.cloned.1.call-update) | async-done | bytes 3276816 | tf_op jit(solution)/shard_map/psum | solution.py:49
  277.4 3.5 %select_convert_fusion = bf16[1280,640]{1,0:T(8,128)(2,1)} fusion(f32[1280,640]{1,0:T(8,128)} %all-reduce.2.cloned.1.call-done, s32[640]{0:T(1024)S(1)} %iota_add_fusion.1, s32[1280]{0:T(1024)S(1)} %iota_add_fusion), kind=kLoop, calls=%fused_computation | loop fusion | flops 3276800 | bytes 4922880 | tf_op jit(solution)/shard_map/convert_element_type | solution.py:13
  (2 shorter events, 0.0 us)
Async XLA Ops:
  6.5 98.3 %all-gather.5.cloned.1.call-start = ((), (), s32[]{:S(2)}) async-start(), calls=%async_computation.3 | async-start | bytes 2949120 | tf_op jit(solution)/shard_map/all_gather | solution.py:39
  63.0 109.1 %all-gather.3.cloned.1.call-start = ((), (), s32[]{:S(2)}) async-start(), calls=%async_computation.2 | async-start | bytes 5570560 | tf_op jit(solution)/shard_map/all_gather | solution.py:41
  104.7 172.7 %all-reduce.2.cloned.1.call-start = ((), (), s32[]{:S(2)}) async-start(), calls=%async_computation.4 | async-start | bytes 6553600 | tf_op jit(solution)/shard_map/psum | solution.py:49
Sparse Core Ops, SparseCore 0:
  63.1 29.0 all-gather.4
  104.9 67.1 all-gather.2
  181.5 95.8 all-reduce.1
where the time goes:
time: 288 us; the launch traced here: 287 us
  waiting for transfers between devices  163 us (57%)
  blocking collectives  92.2 us (32%)
  between operations  13.2 us (5%)
  matrix products  9.28 us (3%)
  other arithmetic  5.36 us (2%)
  local copies, waits for them, and re-layouts  4.02 us (1%)
    psum x1, waiting for transfers between devices, body(): total = lax.psum(partial_tile, 'layer')  96 us
    all_gather x1, waiting for transfers between devices, body(): lax.all_gather(row_part, 'col', axis=1, tiled=True)  67.3 us
    all_to_all x1, blocking collectives, body(): lax.all_to_all(reordered, ('row', 'col'), split_axis=1, concat_axis=0, ti...  52.5 us
    all_to_all x1, blocking collectives, body(): lax.all_to_all(weighted, ('row', 'col'), split_axis=1, concat_axis=0, til...  39.7 us
    dot_general x1, matrix products, body(): lax.dot_general(lax.all_gather(row_part, 'col', axis=1, tiled=True), colu...  9.28 us
  transfers between devices with their start and end apart: 3, of which 2 were waited for; matrix products, arithmetic and copies ran while one was open for 0% of the time, Pallas kernels for 0%

commit v1 on v0

v1 whole, which is shorter than its diff:
```python
import math

import jax
import jax.numpy as jnp
from jax import lax
from jax.experimental import pallas as pl
from jax.experimental.pallas import tpu as pltpu
from jax.sharding import Mesh
from jax.sharding import PartitionSpec as P

PLANE = ("x", "layer")
VMEM = pl.BlockSpec(memory_space=pltpu.VMEM)
SMEM = pl.BlockSpec(memory_space=pltpu.SMEM)


def order_kernel(first, step, n, near, place_ref, held_ref, near_ref, far_ref):
    start = place_ref[0]
    way = place_ref[1]
    for k in range(n):
        block = held_ref[lax.rem(start + way * k + n, n)]
        if k < near:
            near_ref[k] = block
        else:
            far_ref[n - 1 - k] = block


def gram_kernel(slots, half, place_ref, cols_ref, *refs):
    rows, (keep_ref, send_ref, acc_ref) = refs[:slots], refs[slots:]
    width = cols_ref.shape[-1]
    for s in range(slots):
        part = lax.dot_general(
            rows[s][...],
            cols_ref[:, s].reshape(-1, width),
            (((0,), (0,)), ((), ())),
            preferred_element_type=jnp.float32,
        )
        if s == 0:
            acc_ref[...] = part
        else:
            acc_ref[...] += part
    first = place_ref[0] == 0

    @pl.when(first)
    def _():
        keep_ref[...] = acc_ref[:half]
        send_ref[...] = acc_ref[half:]

    @pl.when(jnp.logical_not(first))
    def _():
        keep_ref[...] = acc_ref[half:]
        send_ref[...] = acc_ref[:half]


def body(occurrences, idf_weight, pattern):
    owned, reads = occurrences.shape
    nx, nc = lax.axis_size("x"), lax.axis_size("core")
    nz, ny = lax.axis_size("col"), lax.axis_size("layer")
    x, c = lax.axis_index("x"), lax.axis_index("core")
    z, y = lax.axis_index("col"), lax.axis_index("layer")
    factor = 1.0 / math.sqrt(owned * nx * nc * nz * ny)
    owner = lax.axis_index(("x", "core", "col", "layer"))
    flags = lax.dynamic_slice_in_dim(pattern, owner * owned // 128, 1, 0)[0]
    read_mask = jnp.repeat(flags.astype(jnp.float32), 128)
    weighted = (
        occurrences.astype(jnp.float32) * idf_weight[:, None] * read_mask[None, :]
    ).astype(jnp.bfloat16)

    width = reads // nz
    half = reads // (nx * nc * ny)
    tile = nc * half
    by_col = weighted.reshape(owned, nz, width).transpose(1, 0, 2)
    col_part = lax.all_to_all(by_col, "col", split_axis=0, concat_axis=0, tiled=True)
    by_chip = (
        weighted.reshape(owned, nx, nc, ny, half)
        .transpose(1, 3, 0, 2, 4)
        .reshape(nx * ny, owned, tile)
    )
    own = lax.all_to_all(by_chip, PLANE, split_axis=0, concat_axis=0, tiled=True)
    own = own.reshape(nx * ny * owned, tile)
    swap = [(0, 1), (1, 0)]
    other = lax.ppermute(own, "core", swap)
    ring = [(i, (i + 1) % nz) for i in range(nz)]
    ring += [(nz + i, nz + (i - 1) % nz) for i in range(nz)]
    chain_a, chain_b = [own], [other]
    for k in range(1, nz // 2):
        chain_a.append(lax.ppermute(chain_a[-1], ("core", "col"), ring))
        chain_b.append(lax.ppermute(chain_b[-1], ("core", "col"), ring))
    chain_a.append(lax.ppermute(chain_a[-1], ("core", "col"), ring))
    rows = chain_a + chain_b[1:]
    slots = len(rows)

    near = len(chain_a)
    way = 2 * c - 1
    place = jnp.stack([z, way]).astype(jnp.int32)
    near_part, far_part = pl.pallas_call(
        lambda *refs: order_kernel(0, 0, nz, near, *refs),
        out_shape=(
            jax.ShapeDtypeStruct((near, owned, width), jnp.bfloat16),
            jax.ShapeDtypeStruct((nz - near, owned, width), jnp.bfloat16),
        ),
        in_specs=[SMEM, VMEM],
        out_specs=(VMEM, VMEM),
        name="order",
    )(place, col_part)
    far_part = lax.ppermute(far_part, "core", swap)
    cols = jnp.concatenate([near_part, far_part], 0)
    chips = nx * ny
    cols = lax.all_to_all(
        jnp.broadcast_to(cols[None], (chips,) + cols.shape),
        PLANE,
        split_axis=0,
        concat_axis=0,
        tiled=True,
    )
    side = jnp.reshape(c, (1,)).astype(jnp.int32)
    keep, send = pl.pallas_call(
        lambda *refs: gram_kernel(slots, half, *refs),
        out_shape=(jax.ShapeDtypeStruct((half, width), jnp.float32),) * 2,
        in_specs=[SMEM] + [VMEM] * (1 + slots),
        out_specs=(VMEM, VMEM),
        scratch_shapes=[pltpu.VMEM((tile, width), jnp.float32)],
        compiler_params=pltpu.CompilerParams(vmem_limit_bytes=40 << 20),
        cost_estimate=pl.CostEstimate(
            flops=2 * tile * width * slots * chips * owned,
            bytes_accessed=2 * (tile + width) * slots * chips * owned,
            transcendentals=0,
        ),
        name="gram",
    )(side, cols, *rows)
    total = (keep + lax.ppermute(send, "core", swap)) * factor
    row_ids = ((x * nc + c) * ny + y) * half + lax.broadcasted_iota(jnp.int32, total.shape, 0)
    col_ids = z * width + lax.broadcasted_iota(jnp.int32, total.shape, 1)
    piece = jnp.where(row_ids == col_ids, jnp.float32(0.0), total).astype(jnp.bfloat16)
    copies = jnp.broadcast_to(piece[None], (ny,) + piece.shape)
    out = lax.all_to_all(copies, "layer", split_axis=0, concat_axis=0, tiled=True)
    return out.reshape(ny * half, width)


def solution(mesh):
    rows, cols, layers = mesh.devices.shape
    fine = Mesh(mesh.devices.reshape(rows // 2, 2, cols, layers), ("x", "core", "col", "layer"))
    owners = ("x", "core", "col", "layer")
    return jax.shard_map(
        body,
        mesh=fine,
        in_specs=(P(owners, None), P(owners), P()),
        out_specs=P(("x", "core"), "col"),
        check_vma=False,
    )
```

time: 288 us -> 199 us (0.69)
  the two profiles are of different devices: /device:TPU:1 before, /device:TPU:4 now
where the time goes in v1:
time: 199 us; the launch traced here: 198 us
  starting transfers between devices  67.6 us (34%)
  waiting for transfers between devices  65.9 us (33%)
  blocking collectives  26.5 us (13%)
  local copies, waits for them, and re-layouts  25.7 us (13%)
  Pallas kernels  8.63 us (4%)
  other arithmetic  3.56 us (2%)
    ppermute x8, waiting for transfers between devices, body(): chain_a.append(lax.ppermute(chain_a[-1], ('core', 'col'), ring))  35.7 us
    all_to_all x1, blocking collectives, body(): lax.all_to_all(copies, 'layer', split_axis=0, concat_axis=0, tiled=True)  26.5 us
    unnamed x47, local copies, waits for them, and re-layouts  19.9 us
    all_to_all x1, waiting for transfers between devices, body(): lax.all_to_all(by_col, 'col', split_axis=0, concat_axis=0, tiled=True)  18.9 us
    ppermute x8, starting transfers between devices, body(): chain_a.append(lax.ppermute(chain_a[-1], ('core', 'col'), ring))  16.4 us
    ppermute x7, starting transfers between devices, body(): chain_b.append(lax.ppermute(chain_b[-1], ('core', 'col'), ring))  15.6 us
    all_to_all x1, starting transfers between devices, body(): lax.all_to_all(by_col, 'col', split_axis=0, concat_axis=0, tiled=True)  15.2 us
    ppermute x7, waiting for transfers between devices, body(): chain_b.append(lax.ppermute(chain_b[-1], ('core', 'col'), ring))  7.49 us
  transfers between devices with their start and end apart: 21, of which 18 were waited for; matrix products, arithmetic and copies ran while one was open for 2% of the time, Pallas kernels for 1%

profile of v1, /device:TPU:4, one launch (start us, length us, event | category | flops | bytes accessed | tf_op | source)
XLA Modules:
  0.0 198.1 jit_solution(17293111871786396847)
XLA Ops:
  0.8 1.1 multiply_convert_fusion
  1.9 0.8 copy.9
  2.6 15.2 %all-to-all-start = ((bf16[16,16,640]{2,1,0:T(8,128)(2,1)}), bf16[16,16,640]{2,1,0:T(8,128)(2,1)S(1)}, u32[]{:S(2)}, u32[]{:S(2)}) async-start(bf16[16,16,640]{2,1,0:T(8,128)(2,1)} %bitcast.16), calls=%async_computation | async-start | bytes 655360 | tf_op jit(solution)/shard_map/all_to_all | solution.py:72
  18.7 1.0 reshape.26
  19.7 18.9 %all-to-all-done.refs_1_ = bf16[16,16,640]{2,1,0:T(8,128)(2,1)S(1)} async-done(((bf16[16,16,640]{2,1,0:T(8,128)(2,1)}), bf16[16,16,640]{2,1,0:T(8,128)(2,1)S(1)}, u32[]{:S(2)}, u32[]{:S(2)}) %all-to-all-start) | async-done | bytes 327712 | tf_op jit(solution)/shard_map/all_to_all | solution.py:72
  38.6 7.5 %all-to-all-start.2 = ((bf16[16,16,640]{2,1,0:T(8,128)(2,1)}), bf16[16,16,640]{2,1,0:T(8,128)(2,1)S(1)}, u32[]{:S(2)}, u32[]{:S(2)}) async-start(bf16[16,16,640]{2,1,0:T(8,128)(2,1)} %reshape.26), calls=%async_computation.2 | async-start | bytes 655360 | tf_op jit(solution)/shard_map/all_to_all | solution.py:78
  46.7 1.8 order.1
  48.5 1.9 collective-permute-start
  50.4 1.5 collective-permute-done
  51.9 1.0 pad_maximum_fusion
  52.9 3.0 %broadcast_in_dim.22 = bf16[16,16,16,640]{3,2,1,0:T(8,128)(2,1)} broadcast(bf16[16,16,640]{2,1,0:T(8,128)(2,1)S(1)} %pad_maximum_fusion), dimensions={1,2,3} | broadcast | bytes 5570560 | tf_op jit(solution)/shard_map/broadcast_in_dim | solution.py:109
  55.9 7.2 %all-to-all-start.1 = ((bf16[16,16,16,640]{3,2,1,0:T(8,128)(2,1)}), bf16[16,16,16,640]{3,2,1,0:T(8,128)(2,1)}, u32[]{:S(2)}, u32[]{:S(2)}) async-start(bf16[16,16,16,640]{3,2,1,0:T(8,128)(2,1)} %broadcast_in_dim.22), calls=%async_computation.1 | async-start | bytes 10485760 | tf_op jit(solution)/shard_map/all_to_all | solution.py:108
  63.1 1.9 collective-permute-start.9
  65.0 3.0 %collective-permute-start.1 = (bf16[256,640]{1,0:T(8,128)(2,1)S(1)}, bf16[256,640]{1,0:T(8,128)(2,1)S(1)}, u32[]{:S(2)}, u32[]{:S(2)}) collective-permute-start(bf16[256,640]{1,0:T(8,128)(2,1)S(1)} %bitcast.18), channel_id=1, source_target_pairs={{0,4},{4,8},{8,12},{12,16},{16,20},{20,24},{24,28},{28,32},{32,36}... | collective-permute-start | bytes 983048 | tf_op jit(solution)/shard_map/ppermute | solution.py:86
  68.1 4.1 %collective-permute-start.10 = (bf16[256,640]{1,0:T(8,128)(2,1)S(1)}, bf16[256,640]{1,0:T(8,128)(2,1)S(1)}, u32[]{:S(2)}, u32[]{:S(2)}) collective-permute-start(bf16[256,640]{1,0:T(8,128)(2,1)S(1)} %collective-permute-done.9), channel_id=1, source_target_pairs={{0,4},{4,8},{8,12},{12,16},{16,20},{20,24},{24,28},{28,32},{32,36}... | collective-permute-start | bytes 983048 | tf_op jit(solution)/shard_map/ppermute | solution.py:87
  72.2 4.2 %collective-permute-done.1.refs_3_ = bf16[256,640]{1,0:T(8,128)(2,1)S(1)} collective-permute-done((bf16[256,640]{1,0:T(8,128)(2,1)S(1)}, bf16[256,640]{1,0:T(8,128)(2,1)S(1)}, u32[]{:S(2)}, u32[]{:S(2)}) %collective-permute-start.1) | collective-permute-done | bytes 327712 | tf_op jit(solution)/shard_map/ppermute | solution.py:86
  76.4 1.9 collective-permute-start.2
  78.3 1.6 collective-permute-done.10.refs_11_
  79.9 1.9 collective-permute-start.11
  81.8 4.7 %collective-permute-done.2.refs_4_ = bf16[256,640]{1,0:T(8,128)(2,1)S(1)} collective-permute-done((bf16[256,640]{1,0:T(8,128)(2,1)S(1)}, bf16[256,640]{1,0:T(8,128)(2,1)S(1)}, u32[]{:S(2)}, u32[]{:S(2)}) %collective-permute-start.2) | collective-permute-done | bytes 327712 | tf_op jit(solution)/shard_map/ppermute | solution.py:86
  86.6 1.9 collective-permute-start.3
  88.5 1.6 collective-permute-done.11.refs_12_
  90.1 1.9 collective-permute-start.12
  92.0 4.7 %collective-permute-done.3.refs_5_ = bf16[256,640]{1,0:T(8,128)(2,1)S(1)} collective-permute-done((bf16[256,640]{1,0:T(8,128)(2,1)S(1)}, bf16[256,640]{1,0:T(8,128)(2,1)S(1)}, u32[]{:S(2)}, u32[]{:S(2)}) %collective-permute-start.3) | collective-permute-done | bytes 327712 | tf_op jit(solution)/shard_map/ppermute | solution.py:86
  96.8 1.9 collective-permute-start.4
  99.4 0.9 collective-permute-done.12.refs_13_
  100.3 1.9 collective-permute-start.13
  102.2 0.8 copy-done.2
  102.9 4.0 %collective-permute-done.4.refs_6_ = bf16[256,640]{1,0:T(8,128)(2,1)S(1)} collective-permute-done((bf16[256,640]{1,0:T(8,128)(2,1)S(1)}, bf16[256,640]{1,0:T(8,128)(2,1)S(1)}, u32[]{:S(2)}, u32[]{:S(2)}) %collective-permute-start.4) | collective-permute-done | bytes 327712 | tf_op jit(solution)/shard_map/ppermute | solution.py:86
  106.9 1.9 collective-permute-start.5
  109.6 0.9 collective-permute-done.13.refs_14_
  110.4 1.9 collective-permute-start.14
  112.4 0.7 copy-done.6
  113.1 4.0 %collective-permute-done.5.refs_7_ = bf16[256,640]{1,0:T(8,128)(2,1)S(1)} collective-permute-done((bf16[256,640]{1,0:T(8,128)(2,1)S(1)}, bf16[256,640]{1,0:T(8,128)(2,1)S(1)}, u32[]{:S(2)}, u32[]{:S(2)}) %collective-permute-start.5) | collective-permute-done | bytes 327712 | tf_op jit(solution)/shard_map/ppermute | solution.py:86
  117.1 1.9 collective-permute-start.6
  119.0 0.7 copy-done.8
  119.7 0.9 collective-permute-done.14.refs_15_
  120.6 1.9 collective-permute-start.15
  123.2 4.0 %collective-permute-done.6.refs_8_ = bf16[256,640]{1,0:T(8,128)(2,1)S(1)} collective-permute-done((bf16[256,640]{1,0:T(8,128)(2,1)S(1)}, bf16[256,640]{1,0:T(8,128)(2,1)S(1)}, u32[]{:S(2)}, u32[]{:S(2)}) %collective-permute-start.6) | collective-permute-done | bytes 327712 | tf_op jit(solution)/shard_map/ppermute | solution.py:86
  127.3 1.9 collective-permute-start.7
  129.9 0.9 collective-permute-done.15.refs_16_
  130.8 1.9 collective-permute-start.16
  133.4 4.0 %collective-permute-done.7.refs_9_ = bf16[256,640]{1,0:T(8,128)(2,1)S(1)} collective-permute-done((bf16[256,640]{1,0:T(8,128)(2,1)S(1)}, bf16[256,640]{1,0:T(8,128)(2,1)S(1)}, u32[]{:S(2)}, u32[]{:S(2)}) %collective-permute-start.7) | collective-permute-done | bytes 327712 | tf_op jit(solution)/shard_map/ppermute | solution.py:86
  137.4 1.9 collective-permute-start.8
  139.3 0.7 copy-done.16
  140.1 0.8 collective-permute-done.16.refs_17_
  141.7 5.9 %collective-permute-done.8.refs_10_ = bf16[256,640]{1,0:T(8,128)(2,1)S(1)} collective-permute-done((bf16[256,640]{1,0:T(8,128)(2,1)S(1)}, bf16[256,640]{1,0:T(8,128)(2,1)S(1)}, u32[]{:S(2)}, u32[]{:S(2)}) %collective-permute-start.8) | collective-permute-done | bytes 327712 | tf_op jit(solution)/shard_map/ppermute | solution.py:88
  147.6 0.7 copy-done.20
  148.3 1.0 copy-done.1
  149.3 1.0 copy-done.3
  150.3 1.0 copy-done.5
  151.3 1.0 copy-done.7
  152.2 1.0 copy-done.9
  153.2 1.0 copy-done.11
  154.2 1.0 copy-done.13
  155.2 1.0 copy-done.15
  156.1 1.0 copy-done.17
  157.1 1.0 copy-done.19
  158.1 1.0 copy-done.21
  159.0 6.9 %gram.1 = (f32[320,640]{1,0:T(8,128)S(1)}, f32[320,640]{1,0:T(8,128)S(1)}) custom-call(s32[1]{0:T(128)} %bitcast.refs_0_, bf16[16,16,16,640]{3,2,1,0:T(8,128)(2,1)} %all-to-all-done.1.refs_1_, bf16[256,640]{1,0:T(8,128)(2,1)S(1)} %bitcast.19, bf16[256,640]{1,0:T(8,128)(2,1)S(1)} %collective-permute-done.1.refs_3_, ...), custom_call_target="tpu_custom_call" | custom-call | flops 3355443200 | bytes 10485760 | tf_op jit(solution)/shard_map/gram/pallas_call | solution.py:116
  165.9 1.9 collective-permute-start.17
  167.9 2.3 %collective-permute-done.17 = f32[320,640]{1,0:T(8,128)S(1)} collective-permute-done((f32[320,640]{1,0:T(8,128)S(1)}, f32[320,640]{1,0:T(8,128)S(1)}, u32[]{:S(2)}, u32[]{:S(2)}) %collective-permute-start.17) | collective-permute-done | bytes 819232 | tf_op jit(solution)/shard_map/ppermute | solution.py:130
  170.5 26.5 %all_to_all.20 = bf16[4,320,640]{2,1,0:T(8,128)(2,1)S(1)} all-to-all(bf16[4,320,640]{2,1,0:T(8,128)(2,1)S(1)} %broadcast_in_dim.23), channel_id=1, replica_groups=mesh['x'=4,'core'=2,'col'=16,'layer'=4] {'layer'}, dimensions={0} | all-to-all | bytes 3276800 | tf_op jit(solution)/shard_map/all_to_all | solution.py:135
  196.9 1.2 copy.11
  (42 shorter events, 6.8 us)
Async XLA Ops:
  2.6 36.0 %all-to-all-start = ((bf16[16,16,640]{2,1,0:T(8,128)(2,1)}), bf16[16,16,640]{2,1,0:T(8,128)(2,1)S(1)}, u32[]{:S(2)}, u32[]{:S(2)}) async-start(bf16[16,16,640]{2,1,0:T(8,128)(2,1)} %bitcast.16), calls=%async_computation | async-start | bytes 655360 | tf_op jit(solution)/shard_map/all_to_all | solution.py:72
  38.6 8.1 %copy-start.22 = (bf16[16,16,640]{2,1,0:T(8,128)(2,1)}, bf16[16,16,640]{2,1,0:T(8,128)(2,1)S(1)}, u32[]{:S(2)}) copy-start(bf16[16,16,640]{2,1,0:T(8,128)(2,1)S(1)} %all-to-all-done.refs_1_) | copy-start | bytes 983044
  38.6 14.2 %all-to-all-start.2 = ((bf16[16,16,640]{2,1,0:T(8,128)(2,1)}), bf16[16,16,640]{2,1,0:T(8,128)(2,1)S(1)}, u32[]{:S(2)}, u32[]{:S(2)}) async-start(bf16[16,16,640]{2,1,0:T(8,128)(2,1)} %reshape.26), calls=%async_computation.2 | async-start | bytes 655360 | tf_op jit(solution)/shard_map/all_to_all | solution.py:78
  48.5 3.5 %collective-permute-start = (bf16[7,16,640]{2,1,0:T(8,128)(2,1)}, bf16[7,16,640]{2,1,0:T(8,128)(2,1)S(1)}, u32[]{:S(2)}, u32[]{:S(2)}) collective-permute-start(bf16[7,16,640]{2,1,0:T(8,128)(2,1)} %get-tuple-element.10), channel_id=1, source_target_pairs={{0,64},{64,0},{1,65},{65,1},{2,66},{66,2},{3,67},{67,3},{4,68},{68... | collective-permute-start | bytes 430088 | tf_op jit(solution)/shard_map/ppermute | solution.py:105
  55.9 92.5 %all-to-all-start.1 = ((bf16[16,16,16,640]{3,2,1,0:T(8,128)(2,1)}), bf16[16,16,16,640]{3,2,1,0:T(8,128)(2,1)}, u32[]{:S(2)}, u32[]{:S(2)}) async-start(bf16[16,16,16,640]{3,2,1,0:T(8,128)(2,1)} %broadcast_in_dim.22), calls=%async_computation.1 | async-start | bytes 10485760 | tf_op jit(solution)/shard_map/all_to_all | solution.py:108
  63.1 5.0 %collective-permute-start.9 = (bf16[256,640]{1,0:T(8,128)(2,1)S(1)}, bf16[256,640]{1,0:T(8,128)(2,1)S(1)}, u32[]{:S(2)}, u32[]{:S(2)}) collective-permute-start(bf16[256,640]{1,0:T(8,128)(2,1)S(1)} %bitcast.17), channel_id=1, source_target_pairs={{0,64},{64,0},{1,65},{65,1},{2,66},{66,2},{3,67},{67,3},{4,68},{68... | collective-permute-start | bytes 983048 | tf_op jit(solution)/shard_map/ppermute | solution.py:81
  65.0 11.4 %collective-permute-start.1 = (bf16[256,640]{1,0:T(8,128)(2,1)S(1)}, bf16[256,640]{1,0:T(8,128)(2,1)S(1)}, u32[]{:S(2)}, u32[]{:S(2)}) collective-permute-start(bf16[256,640]{1,0:T(8,128)(2,1)S(1)} %bitcast.18), channel_id=1, source_target_pairs={{0,4},{4,8},{8,12},{12,16},{16,20},{20,24},{24,28},{28,32},{32,36}... | collective-permute-start | bytes 983048 | tf_op jit(solution)/shard_map/ppermute | solution.py:86
  68.1 11.9 %collective-permute-start.10 = (bf16[256,640]{1,0:T(8,128)(2,1)S(1)}, bf16[256,640]{1,0:T(8,128)(2,1)S(1)}, u32[]{:S(2)}, u32[]{:S(2)}) collective-permute-start(bf16[256,640]{1,0:T(8,128)(2,1)S(1)} %collective-permute-done.9), channel_id=1, source_target_pairs={{0,4},{4,8},{8,12},{12,16},{16,20},{20,24},{24,28},{28,32},{32,36}... | collective-permute-start | bytes 983048 | tf_op jit(solution)/shard_map/ppermute | solution.py:87
  76.4 10.2 %collective-permute-start.2 = (bf16[256,640]{1,0:T(8,128)(2,1)S(1)}, bf16[256,640]{1,0:T(8,128)(2,1)S(1)}, u32[]{:S(2)}, u32[]{:S(2)}) collective-permute-start(bf16[256,640]{1,0:T(8,128)(2,1)S(1)} %collective-permute-done.1.refs_3_), channel_id=1, source_target_pairs={{0,4},{4,8},{8,12},{12,16},{16,20},{20,24},{24,28},{28,32},{32,36}... | collective-permute-start | bytes 983048 | tf_op jit(solution)/shard_map/ppermute | solution.py:86
  79.9 10.2 %collective-permute-start.11 = (bf16[256,640]{1,0:T(8,128)(2,1)S(1)}, bf16[256,640]{1,0:T(8,128)(2,1)S(1)}, u32[]{:S(2)}, u32[]{:S(2)}) collective-permute-start(bf16[256,640]{1,0:T(8,128)(2,1)S(1)} %collective-permute-done.10.refs_11_), channel_id=1, source_target_pairs={{0,4},{4,8},{8,12},{12,16},{16,20},{20,24},{24,28},{28,32},{32,36}... | collective-permute-start | bytes 983048 | tf_op jit(solution)/shard_map/ppermute | solution.py:87
  86.6 10.2 %collective-permute-start.3 = (bf16[256,640]{1,0:T(8,128)(2,1)S(1)}, bf16[256,640]{1,0:T(8,128)(2,1)S(1)}, u32[]{:S(2)}, u32[]{:S(2)}) collective-permute-start(bf16[256,640]{1,0:T(8,128)(2,1)S(1)} %collective-permute-done.2.refs_4_), channel_id=1, source_target_pairs={{0,4},{4,8},{8,12},{12,16},{16,20},{20,24},{24,28},{28,32},{32,36}... | collective-permute-start | bytes 983048 | tf_op jit(solution)/shard_map/ppermute | solution.py:86
  90.1 10.2 %collective-permute-start.12 = (bf16[256,640]{1,0:T(8,128)(2,1)S(1)}, bf16[256,640]{1,0:T(8,128)(2,1)S(1)}, u32[]{:S(2)}, u32[]{:S(2)}) collective-permute-start(bf16[256,640]{1,0:T(8,128)(2,1)S(1)} %collective-permute-done.11.refs_12_), channel_id=1, source_target_pairs={{0,4},{4,8},{8,12},{12,16},{16,20},{20,24},{24,28},{28,32},{32,36}... | collective-permute-start | bytes 983048 | tf_op jit(solution)/shard_map/ppermute | solution.py:87
  96.8 10.2 %collective-permute-start.4 = (bf16[256,640]{1,0:T(8,128)(2,1)S(1)}, bf16[256,640]{1,0:T(8,128)(2,1)S(1)}, u32[]{:S(2)}, u32[]{:S(2)}) collective-permute-start(bf16[256,640]{1,0:T(8,128)(2,1)S(1)} %collective-permute-done.3.refs_5_), channel_id=1, source_target_pairs={{0,4},{4,8},{8,12},{12,16},{16,20},{20,24},{24,28},{28,32},{32,36}... | collective-permute-start | bytes 983048 | tf_op jit(solution)/shard_map/ppermute | solution.py:86
  98.7 0.7 copy-start
  100.3 10.2 %collective-permute-start.13 = (bf16[256,640]{1,0:T(8,128)(2,1)S(1)}, bf16[256,640]{1,0:T(8,128)(2,1)S(1)}, u32[]{:S(2)}, u32[]{:S(2)}) collective-permute-start(bf16[256,640]{1,0:T(8,128)(2,1)S(1)} %collective-permute-done.12.refs_13_), channel_id=1, source_target_pairs={{0,4},{4,8},{8,12},{12,16},{16,20},{20,24},{24,28},{28,32},{32,36}... | collective-permute-start | bytes 983048 | tf_op jit(solution)/shard_map/ppermute | solution.py:87
  102.2 0.8 copy-start.2
  106.9 10.2 %collective-permute-start.5 = (bf16[256,640]{1,0:T(8,128)(2,1)S(1)}, bf16[256,640]{1,0:T(8,128)(2,1)S(1)}, u32[]{:S(2)}, u32[]{:S(2)}) collective-permute-start(bf16[256,640]{1,0:T(8,128)(2,1)S(1)} %collective-permute-done.4.refs_6_), channel_id=1, source_target_pairs={{0,4},{4,8},{8,12},{12,16},{16,20},{20,24},{24,28},{28,32},{32,36}... | collective-permute-start | bytes 983048 | tf_op jit(solution)/shard_map/ppermute | solution.py:86
  108.8 0.7 copy-start.4
  110.4 10.2 %collective-permute-start.14 = (bf16[256,640]{1,0:T(8,128)(2,1)S(1)}, bf16[256,640]{1,0:T(8,128)(2,1)S(1)}, u32[]{:S(2)}, u32[]{:S(2)}) collective-permute-start(bf16[256,640]{1,0:T(8,128)(2,1)S(1)} %collective-permute-done.13.refs_14_), channel_id=1, source_target_pairs={{0,4},{4,8},{8,12},{12,16},{16,20},{20,24},{24,28},{28,32},{32,36}... | collective-permute-start | bytes 983048 | tf_op jit(solution)/shard_map/ppermute | solution.py:87
  112.3 0.7 copy-start.6
  117.1 10.2 %collective-permute-start.6 = (bf16[256,640]{1,0:T(8,128)(2,1)S(1)}, bf16[256,640]{1,0:T(8,128)(2,1)S(1)}, u32[]{:S(2)}, u32[]{:S(2)}) collective-permute-start(bf16[256,640]{1,0:T(8,128)(2,1)S(1)} %collective-permute-done.5.refs_7_), channel_id=1, source_target_pairs={{0,4},{4,8},{8,12},{12,16},{16,20},{20,24},{24,28},{28,32},{32,36}... | collective-permute-start | bytes 983048 | tf_op jit(solution)/shard_map/ppermute | solution.py:86
  119.0 0.7 copy-start.8
  120.6 10.2 %collective-permute-start.15 = (bf16[256,640]{1,0:T(8,128)(2,1)S(1)}, bf16[256,640]{1,0:T(8,128)(2,1)S(1)}, u32[]{:S(2)}, u32[]{:S(2)}) collective-permute-start(bf16[256,640]{1,0:T(8,128)(2,1)S(1)} %collective-permute-done.14.refs_15_), channel_id=1, source_target_pairs={{0,4},{4,8},{8,12},{12,16},{16,20},{20,24},{24,28},{28,32},{32,36}... | collective-permute-start | bytes 983048 | tf_op jit(solution)/shard_map/ppermute | solution.py:87
  122.5 0.7 copy-start.10
  127.3 10.2 %collective-permute-start.7 = (bf16[256,640]{1,0:T(8,128)(2,1)S(1)}, bf16[256,640]{1,0:T(8,128)(2,1)S(1)}, u32[]{:S(2)}, u32[]{:S(2)}) collective-permute-start(bf16[256,640]{1,0:T(8,128)(2,1)S(1)} %collective-permute-done.6.refs_8_), channel_id=1, source_target_pairs={{0,4},{4,8},{8,12},{12,16},{16,20},{20,24},{24,28},{28,32},{32,36}... | collective-permute-start | bytes 983048 | tf_op jit(solution)/shard_map/ppermute | solution.py:86
  129.2 0.7 copy-start.12
  130.8 10.2 %collective-permute-start.16 = (bf16[256,640]{1,0:T(8,128)(2,1)S(1)}, bf16[256,640]{1,0:T(8,128)(2,1)S(1)}, u32[]{:S(2)}, u32[]{:S(2)}) collective-permute-start(bf16[256,640]{1,0:T(8,128)(2,1)S(1)} %collective-permute-done.15.refs_16_), channel_id=1, source_target_pairs={{0,4},{4,8},{8,12},{12,16},{16,20},{20,24},{24,28},{28,32},{32,36}... | collective-permute-start | bytes 983048 | tf_op jit(solution)/shard_map/ppermute | solution.py:87
  132.7 0.7 copy-start.14
  137.4 10.2 %collective-permute-start.8 = (bf16[256,640]{1,0:T(8,128)(2,1)S(1)}, bf16[256,640]{1,0:T(8,128)(2,1)S(1)}, u32[]{:S(2)}, u32[]{:S(2)}) collective-permute-start(bf16[256,640]{1,0:T(8,128)(2,1)S(1)} %collective-permute-done.7.refs_9_), channel_id=1, source_target_pairs={{0,4},{4,8},{8,12},{12,16},{16,20},{20,24},{24,28},{28,32},{32,36}... | collective-permute-start | bytes 983048 | tf_op jit(solution)/shard_map/ppermute | solution.py:88
  139.3 0.7 copy-start.16
  140.9 0.7 copy-start.18
  147.6 0.7 copy-start.20
  148.3 1.0 copy-start.1
  149.3 1.0 copy-start.3
  150.3 1.0 copy-start.5
  151.3 1.0 copy-start.7
  152.2 1.0 copy-start.9
  153.2 1.0 copy-start.11
  154.2 1.0 copy-start.13
  155.2 1.0 copy-start.15
  156.1 1.0 copy-start.17
  157.1 1.0 copy-start.19
  158.1 1.0 copy-start.21
  165.9 4.2 %collective-permute-start.17 = (f32[320,640]{1,0:T(8,128)S(1)}, f32[320,640]{1,0:T(8,128)S(1)}, u32[]{:S(2)}, u32[]{:S(2)}) collective-permute-start(f32[320,640]{1,0:T(8,128)S(1)} %get-tuple-element.12), channel_id=1, source_target_pairs={{0,64},{64,0},{1,65},{65,1},{2,66},{66,2},{3,67},{67,3},{4,68},{68... | collective-permute-start | bytes 2457608 | tf_op jit(solution)/shard_map/ppermute | solution.py:130

commit v2 on v1

v2 whole, which is shorter than its diff:
```python
import math

import jax
import jax.numpy as jnp
from jax import lax
from jax.experimental import pallas as pl
from jax.experimental.pallas import tpu as pltpu
from jax.sharding import Mesh
from jax.sharding import PartitionSpec as P

SMEM = pl.BlockSpec(memory_space=pltpu.SMEM)


def around(n, shift):
    return [(i, (i + shift) % n) for i in range(n)]


def spread(value, axis, n):
    return [value] + [lax.ppermute(value, axis, around(n, s)) for s in (1, 3, 2)]


SHIFTS = (0, 1, 3, 2)


def gram_kernel(half, planes, place_ref, rows_ref, *refs):
    x, y, c = place_ref[0], place_ref[1], place_ref[2]
    by_y, by_x = refs[:4], refs[4:8]
    keep_ref, send_ref, acc_ref = refs[8:]
    k = pl.program_id(0)

    @pl.when(k == 0)
    def _():
        acc_ref[...] = jnp.zeros_like(acc_ref)

    def add(right):
        left = []
        for s in SHIFTS:
            for t in SHIFTS:
                slot = lax.rem(x - s + 4, 4) * 4 + lax.rem(y - t + 4, 4)
                left.append(rows_ref[0, slot])
        acc_ref[...] += lax.dot_general(
            jnp.concatenate(left, 0),
            jnp.concatenate(right, 0),
            (((0,), (0,)), ((), ())),
            preferred_element_type=jnp.float32,
        )

    @pl.when(k < planes // 2)
    def _():
        add([by_y[j][i, 0] for i in range(4) for j in range(4)])

    @pl.when(k >= planes // 2)
    def _():
        add([by_x[i][j, 0] for i in range(4) for j in range(4)])

    last = k == planes - 1

    @pl.when(jnp.logical_and(last, c == 0))
    def _():
        keep_ref[...] = acc_ref[:half]
        send_ref[...] = acc_ref[half:]

    @pl.when(jnp.logical_and(last, c != 0))
    def _():
        keep_ref[...] = acc_ref[half:]
        send_ref[...] = acc_ref[:half]


def body(occurrences, idf_weight, pattern):
    owned, reads = occurrences.shape
    nx, nc = lax.axis_size("x"), lax.axis_size("core")
    nz, ny = lax.axis_size("col"), lax.axis_size("layer")
    x, c = lax.axis_index("x"), lax.axis_index("core")
    z, y = lax.axis_index("col"), lax.axis_index("layer")
    factor = 1.0 / math.sqrt(owned * nx * nc * nz * ny)
    owner = lax.axis_index(("x", "core", "col", "layer"))
    flags = lax.dynamic_slice_in_dim(pattern, owner * owned // 128, 1, 0)[0]
    read_mask = jnp.repeat(flags.astype(jnp.float32), 128)
    weighted = (
        occurrences.astype(jnp.float32) * idf_weight[:, None] * read_mask[None, :]
    ).astype(jnp.bfloat16)

    width = reads // nz
    half = reads // (nx * nc * ny)
    tile = nc * half
    chips = nx * ny
    by_chip = (
        weighted.reshape(owned, nx, nc, ny, half)
        .transpose(1, 3, 0, 2, 4)
        .reshape(chips, owned, tile)
    )
    own = lax.all_to_all(by_chip, ("x", "layer"), split_axis=0, concat_axis=0, tiled=True)
    own = own.reshape(chips * owned, tile)
    rows = lax.all_gather(own, "col", axis=0, tiled=True).reshape(nz, chips, owned, tile)
    by_col = weighted.reshape(owned, nz, width).transpose(1, 0, 2)
    by_col, own = lax.optimization_barrier((by_col, own))
    part = lax.all_to_all(by_col, "col", split_axis=0, concat_axis=0, tiled=True)
    upper, lower = part[: nz // 2], part[nz // 2 :]
    along_x = jnp.stack(spread(upper, "x", nx))
    along_y = jnp.stack(spread(lower, "layer", ny))
    by_y = spread(along_x, "layer", ny)
    by_x = spread(along_y, "x", nx)

    place = jnp.stack([x, y, c]).astype(jnp.int32)
    n = nz // 2
    block = (nx, 1, owned, width)
    keep, send = pl.pallas_call(
        lambda *refs: gram_kernel(half, nz, *refs),
        out_shape=(jax.ShapeDtypeStruct((half, width), jnp.float32),) * 2,
        grid=(nz,),
        in_specs=[SMEM, pl.BlockSpec((1, chips, owned, tile), lambda k: (k, 0, 0, 0))]
        + [pl.BlockSpec(block, lambda k: (0, jnp.minimum(k, n - 1), 0, 0))] * ny
        + [pl.BlockSpec(block, lambda k: (0, jnp.maximum(k - n, 0), 0, 0))] * nx,
        out_specs=(pl.BlockSpec((half, width), lambda k: (0, 0)),) * 2,
        scratch_shapes=[pltpu.VMEM((tile, width), jnp.float32)],
        compiler_params=pltpu.CompilerParams(vmem_limit_bytes=60 << 20),
        cost_estimate=pl.CostEstimate(
            flops=2 * tile * width * nz * chips * owned,
            bytes_accessed=2 * (tile + width) * nz * chips * owned,
            transcendentals=0,
        ),
        name="gram",
    )(place, rows, *by_y, *by_x)
    total = (keep + lax.ppermute(send, "core", [(0, 1), (1, 0)])) * factor
    row_ids = ((x * nc + c) * ny + y) * half + lax.broadcasted_iota(jnp.int32, total.shape, 0)
    col_ids = z * width + lax.broadcasted_iota(jnp.int32, total.shape, 1)
    piece = jnp.where(row_ids == col_ids, jnp.float32(0.0), total).astype(jnp.bfloat16)
    copies = jnp.broadcast_to(piece[None], (ny,) + piece.shape)
    out = lax.all_to_all(copies, "layer", split_axis=0, concat_axis=0, tiled=True)
    return out.reshape(ny * half, width)


def solution(mesh):
    rows, cols, layers = mesh.devices.shape
    fine = Mesh(mesh.devices.reshape(rows // 2, 2, cols, layers), ("x", "core", "col", "layer"))
    owners = ("x", "core", "col", "layer")
    return jax.shard_map(
        body,
        mesh=fine,
        in_specs=(P(owners, None), P(owners), P()),
        out_specs=P(("x", "core"), "col"),
        check_vma=False,
    )
```

time: 199 us -> 189 us (0.950)
  the two profiles are of different devices: /device:TPU:4 before, /device:TPU:166 now
where the time goes in v2:
time: 189 us; the launch traced here: 188 us
  blocking collectives  73.5 us (39%)
  starting transfers between devices  42.3 us (22%)
  waiting for transfers between devices  35.3 us (19%)
  Pallas kernels  15.5 us (8%)
  between operations  13.7 us (7%)
  other arithmetic  3.98 us (2%)
  local copies, waits for them, and re-layouts  3.47 us (2%)
    ppermute x12, starting transfers between devices, spread(): lax.ppermute(value, axis, around(n, s))  40.4 us
    ppermute x12, waiting for transfers between devices, spread(): lax.ppermute(value, axis, around(n, s))  32.8 us
    all_to_all x1, blocking collectives, body(): lax.all_to_all(by_col, 'col', split_axis=0, concat_axis=0, tiled=True)  32.5 us
    all_to_all x1, blocking collectives, body(): lax.all_to_all(copies, 'layer', split_axis=0, concat_axis=0, tiled=True)  26.5 us
    pallas_call x1, Pallas kernels, body(): pl.pallas_call(lambda *refs: gram_kernel(half, nz, *refs), out_shape=(jax...  15.5 us
    all_to_all x1, blocking collectives, body(): lax.all_to_all(by_chip, ('x', 'layer'), split_axis=0, concat_axis=0, tile...  14.5 us
  transfers between devices with their start and end apart: 14, of which 7 were waited for; matrix products, arithmetic and copies ran while one was open for 0% of the time, Pallas kernels for 0%

profile of v2, /device:TPU:166, one launch (start us, length us, event | category | flops | bytes accessed | tf_op | source)
XLA Modules:
  0.0 187.6 jit_solution(16238848375301005236)
XLA Ops:
  6.5 0.0 all-gather.2.cloned.1.call-start
  6.5 0.7 convert_bitcast_fusion
  7.2 0.1 broadcast_bitcast_fusion
  7.3 1.1 multiply_convert_fusion
  8.4 0.5 reshape.22
  9.0 0.3 copy.9
  9.3 0.3 reshape.23
  9.6 14.5 %all_to_all.15 = bf16[16,16,640]{2,1,0:T(8,128)(2,1)} all-to-all(bf16[16,16,640]{2,1,0:T(8,128)(2,1)S(1)} %reshape.23), channel_id=1, replica_groups=mesh['x'=4,'core'=2,'col'=16,'layer'=4] {'x','layer'}, dimensions={0} | all-to-all | bytes 655360 | tf_op jit(solution)/shard_map/all_to_all | solution.py:92
  24.1 0.0 all-gather.2.cloned.1.call-update
  24.1 32.5 %all_to_all.16 = bf16[16,16,640]{2,1,0:T(8,128)(2,1)S(1)} all-to-all(bf16[16,16,640]{2,1,0:T(8,128)(2,1)S(1)} %bitcast.34), channel_id=1, replica_groups=mesh['x'=4,'core'=2,'col'=16,'layer'=4] {'col'}, dimensions={0} | all-to-all | bytes 655360 | tf_op jit(solution)/shard_map/all_to_all | solution.py:97
  56.6 0.1 slice_bitcast_fusion
  56.7 2.4 %collective-permute-start.6 = (bf16[8,16,640]{2,1,0:T(8,128)(2,1)S(1)}, bf16[8,16,640]{2,1,0:T(8,128)(2,1)S(1)}, u32[]{:S(2)}, u32[]{:S(2)}) collective-permute-start(bf16[8,16,640]{2,1,0:T(8,128)(2,1)S(1)} %get-tuple-element.13), channel_id=1, source_target_pairs={{0,1},{1,2},{2,3},{3,0},{4,5},{5,6},{6,7},{7,4},{8,9},{9,10},{10,1... | collective-permute-start | bytes 491528 | tf_op jit(solution)/shard_map/ppermute | solution.py:19
  59.1 4.6 %collective-permute-start.7 = (bf16[8,16,640]{2,1,0:T(8,128)(2,1)S(1)}, bf16[8,16,640]{2,1,0:T(8,128)(2,1)S(1)}, u32[]{:S(2)}, u32[]{:S(2)}) collective-permute-start(bf16[8,16,640]{2,1,0:T(8,128)(2,1)S(1)} %get-tuple-element.13), channel_id=1, source_target_pairs={{0,3},{1,0},{2,1},{3,2},{4,7},{5,4},{6,5},{7,6},{8,11},{9,8},{10,9... | collective-permute-start | bytes 491528 | tf_op jit(solution)/shard_map/ppermute | solution.py:19
  63.8 1.9 %collective-permute-start.8 = (bf16[8,16,640]{2,1,0:T(8,128)(2,1)S(1)}, bf16[8,16,640]{2,1,0:T(8,128)(2,1)S(1)}, u32[]{:S(2)}, u32[]{:S(2)}) collective-permute-start(bf16[8,16,640]{2,1,0:T(8,128)(2,1)S(1)} %get-tuple-element.13), channel_id=1, source_target_pairs={{0,2},{1,3},{2,0},{3,1},{4,6},{5,7},{6,4},{7,5},{8,10},{9,11},{10,... | collective-permute-start | bytes 491528 | tf_op jit(solution)/shard_map/ppermute | solution.py:19
  65.7 0.0 collective-permute-done.6
  65.7 1.5 collective-permute-done.7
  67.2 5.3 %collective-permute-done.8 = bf16[8,16,640]{2,1,0:T(8,128)(2,1)S(1)} collective-permute-done((bf16[8,16,640]{2,1,0:T(8,128)(2,1)S(1)}, bf16[8,16,640]{2,1,0:T(8,128)(2,1)S(1)}, u32[]{:S(2)}, u32[]{:S(2)}) %collective-permute-start.8) | collective-permute-done | bytes 163872 | tf_op jit(solution)/shard_map/ppermute | solution.py:19
  72.5 0.1 pad_maximum_fusion.1.refs_6_
  72.6 0.0 copy-start
  72.6 2.3 %collective-permute-start.10 = (bf16[4,8,16,640]{3,2,1,0:T(8,128)(2,1)S(1)}, bf16[4,8,16,640]{3,2,1,0:T(8,128)(2,1)S(1)}, u32[]{:S(2)}, u32[]{:S(2)}) collective-permute-start(bf16[4,8,16,640]{3,2,1,0:T(8,128)(2,1)S(1)} %pad_maximum_fusion.1.refs_6_), channel_id=1, source_target_pairs={{0,384},{128,0},{256,128},{384,256},{1,385},{129,1},{257,129},{385... | collective-permute-start | bytes 1966088 | tf_op jit(solution)/shard_map/ppermute | solution.py:19
  74.9 4.8 %collective-permute-start = (bf16[8,16,640]{2,1,0:T(8,128)(2,1)S(1)}, bf16[8,16,640]{2,1,0:T(8,128)(2,1)S(1)}, u32[]{:S(2)}, u32[]{:S(2)}) collective-permute-start(bf16[8,16,640]{2,1,0:T(8,128)(2,1)S(1)} %get-tuple-element.14), channel_id=1, source_target_pairs={{0,128},{128,256},{256,384},{384,0},{1,129},{129,257},{257,385},{3... | collective-permute-start | bytes 491528 | tf_op jit(solution)/shard_map/ppermute | solution.py:19
  79.7 1.9 %collective-permute-start.1 = (bf16[8,16,640]{2,1,0:T(8,128)(2,1)S(1)}, bf16[8,16,640]{2,1,0:T(8,128)(2,1)S(1)}, u32[]{:S(2)}, u32[]{:S(2)}) collective-permute-start(bf16[8,16,640]{2,1,0:T(8,128)(2,1)S(1)} %get-tuple-element.14), channel_id=1, source_target_pairs={{0,384},{128,0},{256,128},{384,256},{1,385},{129,1},{257,129},{385... | collective-permute-start | bytes 491528 | tf_op jit(solution)/shard_map/ppermute | solution.py:19
  81.6 4.2 %collective-permute-start.2 = (bf16[8,16,640]{2,1,0:T(8,128)(2,1)S(1)}, bf16[8,16,640]{2,1,0:T(8,128)(2,1)S(1)}, u32[]{:S(2)}, u32[]{:S(2)}) collective-permute-start(bf16[8,16,640]{2,1,0:T(8,128)(2,1)S(1)} %get-tuple-element.14), channel_id=1, source_target_pairs={{0,256},{128,384},{256,0},{384,128},{1,257},{129,385},{257,1},{385... | collective-permute-start | bytes 491528 | tf_op jit(solution)/shard_map/ppermute | solution.py:19
  85.8 3.2 %collective-permute-start.11 = (bf16[4,8,16,640]{3,2,1,0:T(8,128)(2,1)S(1)}, bf16[4,8,16,640]{3,2,1,0:T(8,128)(2,1)S(1)}, u32[]{:S(2)}, u32[]{:S(2)}) collective-permute-start(bf16[4,8,16,640]{3,2,1,0:T(8,128)(2,1)S(1)} %pad_maximum_fusion.1.refs_6_), channel_id=1, source_target_pairs={{0,256},{128,384},{256,0},{384,128},{1,257},{129,385},{257,1},{385... | collective-permute-start | bytes 1966088 | tf_op jit(solution)/shard_map/ppermute | solution.py:19
  89.0 6.4 %collective-permute-done = bf16[8,16,640]{2,1,0:T(8,128)(2,1)S(1)} collective-permute-done((bf16[8,16,640]{2,1,0:T(8,128)(2,1)S(1)}, bf16[8,16,640]{2,1,0:T(8,128)(2,1)S(1)}, u32[]{:S(2)}, u32[]{:S(2)}) %collective-permute-start) | collective-permute-done | bytes 163872 | tf_op jit(solution)/shard_map/ppermute | solution.py:19
  95.4 6.1 %collective-permute-start.9 = (bf16[4,8,16,640]{3,2,1,0:T(8,128)(2,1)S(1)}, bf16[4,8,16,640]{3,2,1,0:T(8,128)(2,1)S(1)}, u32[]{:S(2)}, u32[]{:S(2)}) collective-permute-start(bf16[4,8,16,640]{3,2,1,0:T(8,128)(2,1)S(1)} %pad_maximum_fusion.1.refs_6_), channel_id=1, source_target_pairs={{0,128},{128,256},{256,384},{384,0},{1,129},{129,257},{257,385},{3... | collective-permute-start | bytes 1966088 | tf_op jit(solution)/shard_map/ppermute | solution.py:19
  101.5 7.1 %collective-permute-done.1 = bf16[8,16,640]{2,1,0:T(8,128)(2,1)S(1)} collective-permute-done((bf16[8,16,640]{2,1,0:T(8,128)(2,1)S(1)}, bf16[8,16,640]{2,1,0:T(8,128)(2,1)S(1)}, u32[]{:S(2)}, u32[]{:S(2)}) %collective-permute-start.1) | collective-permute-done | bytes 163872 | tf_op jit(solution)/shard_map/ppermute | solution.py:19
  108.6 0.0 collective-permute-done.2
  108.6 0.1 pad_maximum_fusion.refs_2_
  108.7 0.0 copy-start.1
  108.7 2.3 %collective-permute-start.3 = (bf16[4,8,16,640]{3,2,1,0:T(8,128)(2,1)S(1)}, bf16[4,8,16,640]{3,2,1,0:T(8,128)(2,1)S(1)}, u32[]{:S(2)}, u32[]{:S(2)}) collective-permute-start(bf16[4,8,16,640]{3,2,1,0:T(8,128)(2,1)S(1)} %pad_maximum_fusion.refs_2_), channel_id=1, source_target_pairs={{0,1},{1,2},{2,3},{3,0},{4,5},{5,6},{6,7},{7,4},{8,9},{9,10},{10,1... | collective-permute-start | bytes 1966088 | tf_op jit(solution)/shard_map/ppermute | solution.py:19
  111.0 4.7 %collective-permute-start.4 = (bf16[4,8,16,640]{3,2,1,0:T(8,128)(2,1)S(1)}, bf16[4,8,16,640]{3,2,1,0:T(8,128)(2,1)S(1)}, u32[]{:S(2)}, u32[]{:S(2)}) collective-permute-start(bf16[4,8,16,640]{3,2,1,0:T(8,128)(2,1)S(1)} %pad_maximum_fusion.refs_2_), channel_id=1, source_target_pairs={{0,3},{1,0},{2,1},{3,2},{4,7},{5,4},{6,5},{7,6},{8,11},{9,8},{10,9... | collective-permute-start | bytes 1966088 | tf_op jit(solution)/shard_map/ppermute | solution.py:19
  115.7 0.0 collective-permute-done.10.refs_8_
  115.8 0.0 copy-start.2
  115.8 1.9 %collective-permute-start.5 = (bf16[4,8,16,640]{3,2,1,0:T(8,128)(2,1)S(1)}, bf16[4,8,16,640]{3,2,1,0:T(8,128)(2,1)}, u32[]{:S(2)}, u32[]{:S(2)}) collective-permute-start(bf16[4,8,16,640]{3,2,1,0:T(8,128)(2,1)S(1)} %pad_maximum_fusion.refs_2_), channel_id=1, source_target_pairs={{0,2},{1,3},{2,0},{3,1},{4,6},{5,7},{6,4},{7,5},{8,10},{9,11},{10,... | collective-permute-start | bytes 1966088 | tf_op jit(solution)/shard_map/ppermute | solution.py:19
  117.7 0.6 pad_add_fusion.refs_0_
  118.3 0.0 collective-permute-done.11.refs_9_
  118.3 0.0 copy-start.3
  118.3 0.0 collective-permute-done.9.refs_7_
  118.3 0.0 copy-start.4
  118.4 4.0 %collective-permute-done.3.refs_3_ = bf16[4,8,16,640]{3,2,1,0:T(8,128)(2,1)S(1)} collective-permute-done((bf16[4,8,16,640]{3,2,1,0:T(8,128)(2,1)S(1)}, bf16[4,8,16,640]{3,2,1,0:T(8,128)(2,1)S(1)}, u32[]{:S(2)}, u32[]{:S(2)}) %collective-permute-start.3) | collective-permute-done | bytes 655392 | tf_op jit(solution)/shard_map/ppermute | solution.py:19
  122.4 0.0 copy-start.5
  122.4 8.5 %collective-permute-done.4.refs_4_ = bf16[4,8,16,640]{3,2,1,0:T(8,128)(2,1)S(1)} collective-permute-done((bf16[4,8,16,640]{3,2,1,0:T(8,128)(2,1)S(1)}, bf16[4,8,16,640]{3,2,1,0:T(8,128)(2,1)S(1)}, u32[]{:S(2)}, u32[]{:S(2)}) %collective-permute-start.4) | collective-permute-done | bytes 655392 | tf_op jit(solution)/shard_map/ppermute | solution.py:19
  130.9 0.0 copy-done.5
  130.9 0.0 copy-start.6
  130.9 0.9 copy-done.6
  131.7 0.0 collective-permute-done.5.refs_5_
  131.7 0.0 all-gather.2.cloned.1.call-done
  131.7 0.0 copy-done
  131.7 0.0 copy-done.1
  131.7 0.0 copy-done.2
  131.8 0.0 copy-done.3
  131.8 0.0 copy-done.4
  131.8 15.5 %gram.1 = (f32[320,640]{1,0:T(8,128)}, f32[320,640]{1,0:T(8,128)}) custom-call(s32[3]{0:T(128)} %pad_add_fusion.refs_0_, bf16[16,16,16,640]{3,2,1,0:T(8,128)(2,1)} %bitcast.41, bf16[4,8,16,640]{3,2,1,0:T(8,128)(2,1)} %copy-done.1, bf16[4,8,16,640]{3,2,1,0:T(8,128)(2,1)} %copy-done.5, bf16[4,8,16,640]{3,2,1,0:T(8,128)(2,1)} %copy-done.6, ...), custom_call_target="tpu_custom_call" | custom-call | flops 3355443200 | bytes 10485760 | tf_op jit(solution)/shard_map/gram/pallas_call | solution.py:107
  147.3 1.9 %collective-permute-start.12 = (f32[320,640]{1,0:T(8,128)}, f32[320,640]{1,0:T(8,128)S(1)}, u32[]{:S(2)}, u32[]{:S(2)}) collective-permute-start(f32[320,640]{1,0:T(8,128)} %get-tuple-element.10), channel_id=1, source_target_pairs={{0,64},{64,0},{1,65},{65,1},{2,66},{66,2},{3,67},{67,3},{4,68},{68... | collective-permute-start | bytes 2457608 | tf_op jit(solution)/shard_map/ppermute | solution.py:124
  149.2 2.5 %collective-permute-done.12 = f32[320,640]{1,0:T(8,128)S(1)} collective-permute-done((f32[320,640]{1,0:T(8,128)}, f32[320,640]{1,0:T(8,128)S(1)}, u32[]{:S(2)}, u32[]{:S(2)}) %collective-permute-start.12) | collective-permute-done | bytes 819232 | tf_op jit(solution)/shard_map/ppermute | solution.py:124
  151.7 1.3 select_convert_fusion
  153.0 0.1 broadcast_in_dim.16
  153.1 26.5 %all_to_all.17 = bf16[4,320,640]{2,1,0:T(8,128)(2,1)S(1)} all-to-all(bf16[4,320,640]{2,1,0:T(8,128)(2,1)S(1)} %broadcast_in_dim.16), channel_id=1, replica_groups=mesh['x'=4,'core'=2,'col'=16,'layer'=4] {'layer'}, dimensions={0} | all-to-all | bytes 3276800 | tf_op jit(solution)/shard_map/all_to_all | solution.py:129
  179.6 1.2 copy.12
  (3 shorter events, 0.0 us)
Async XLA Ops:
  6.5 125.2 %all-gather.2.cloned.1.call-start = ((), (), s32[]{:S(2)}) async-start(), calls=%async_computation.3 | async-start | bytes 5570560 | tf_op jit(solution)/shard_map/all_gather | solution.py:94
  56.7 9.0 %collective-permute-start.6 = (bf16[8,16,640]{2,1,0:T(8,128)(2,1)S(1)}, bf16[8,16,640]{2,1,0:T(8,128)(2,1)S(1)}, u32[]{:S(2)}, u32[]{:S(2)}) collective-permute-start(bf16[8,16,640]{2,1,0:T(8,128)(2,1)S(1)} %get-tuple-element.13), channel_id=1, source_target_pairs={{0,1},{1,2},{2,3},{3,0},{4,5},{5,6},{6,7},{7,4},{8,9},{9,10},{10,1... | collective-permute-start | bytes 491528 | tf_op jit(solution)/shard_map/ppermute | solution.py:19
  59.1 8.1 %collective-permute-start.7 = (bf16[8,16,640]{2,1,0:T(8,128)(2,1)S(1)}, bf16[8,16,640]{2,1,0:T(8,128)(2,1)S(1)}, u32[]{:S(2)}, u32[]{:S(2)}) collective-permute-start(bf16[8,16,640]{2,1,0:T(8,128)(2,1)S(1)} %get-tuple-element.13), channel_id=1, source_target_pairs={{0,3},{1,0},{2,1},{3,2},{4,7},{5,4},{6,5},{7,6},{8,11},{9,8},{10,9... | collective-permute-start | bytes 491528 | tf_op jit(solution)/shard_map/ppermute | solution.py:19
  63.8 8.7 %collective-permute-start.8 = (bf16[8,16,640]{2,1,0:T(8,128)(2,1)S(1)}, bf16[8,16,640]{2,1,0:T(8,128)(2,1)S(1)}, u32[]{:S(2)}, u32[]{:S(2)}) collective-permute-start(bf16[8,16,640]{2,1,0:T(8,128)(2,1)S(1)} %get-tuple-element.13), channel_id=1, source_target_pairs={{0,2},{1,3},{2,0},{3,1},{4,6},{5,7},{6,4},{7,5},{8,10},{9,11},{10,... | collective-permute-start | bytes 491528 | tf_op jit(solution)/shard_map/ppermute | solution.py:19
  72.6 59.1 %copy-start = (bf16[4,8,16,640]{3,2,1,0:T(8,128)(2,1)}, bf16[4,8,16,640]{3,2,1,0:T(8,128)(2,1)S(1)}, u32[]{:S(2)}) copy-start(bf16[4,8,16,640]{3,2,1,0:T(8,128)(2,1)S(1)} %pad_maximum_fusion.1.refs_6_) | copy-start | bytes 1966084
  72.6 43.2 %collective-permute-start.10 = (bf16[4,8,16,640]{3,2,1,0:T(8,128)(2,1)S(1)}, bf16[4,8,16,640]{3,2,1,0:T(8,128)(2,1)S(1)}, u32[]{:S(2)}, u32[]{:S(2)}) collective-permute-start(bf16[4,8,16,640]{3,2,1,0:T(8,128)(2,1)S(1)} %pad_maximum_fusion.1.refs_6_), channel_id=1, source_target_pairs={{0,384},{128,0},{256,128},{384,256},{1,385},{129,1},{257,129},{385... | collective-permute-start | bytes 1966088 | tf_op jit(solution)/shard_map/ppermute | solution.py:19
  74.9 20.5 %collective-permute-start = (bf16[8,16,640]{2,1,0:T(8,128)(2,1)S(1)}, bf16[8,16,640]{2,1,0:T(8,128)(2,1)S(1)}, u32[]{:S(2)}, u32[]{:S(2)}) collective-permute-start(bf16[8,16,640]{2,1,0:T(8,128)(2,1)S(1)} %get-tuple-element.14), channel_id=1, source_target_pairs={{0,128},{128,256},{256,384},{384,0},{1,129},{129,257},{257,385},{3... | collective-permute-start | bytes 491528 | tf_op jit(solution)/shard_map/ppermute | solution.py:19
  79.7 28.9 %collective-permute-start.1 = (bf16[8,16,640]{2,1,0:T(8,128)(2,1)S(1)}, bf16[8,16,640]{2,1,0:T(8,128)(2,1)S(1)}, u32[]{:S(2)}, u32[]{:S(2)}) collective-permute-start(bf16[8,16,640]{2,1,0:T(8,128)(2,1)S(1)} %get-tuple-element.14), channel_id=1, source_target_pairs={{0,384},{128,0},{256,128},{384,256},{1,385},{129,1},{257,129},{385... | collective-permute-start | bytes 491528 | tf_op jit(solution)/shard_map/ppermute | solution.py:19
  81.6 27.0 %collective-permute-start.2 = (bf16[8,16,640]{2,1,0:T(8,128)(2,1)S(1)}, bf16[8,16,640]{2,1,0:T(8,128)(2,1)S(1)}, u32[]{:S(2)}, u32[]{:S(2)}) collective-permute-start(bf16[8,16,640]{2,1,0:T(8,128)(2,1)S(1)} %get-tuple-element.14), channel_id=1, source_target_pairs={{0,256},{128,384},{256,0},{384,128},{1,257},{129,385},{257,1},{385... | collective-permute-start | bytes 491528 | tf_op jit(solution)/shard_map/ppermute | solution.py:19
  85.8 32.6 %collective-permute-start.11 = (bf16[4,8,16,640]{3,2,1,0:T(8,128)(2,1)S(1)}, bf16[4,8,16,640]{3,2,1,0:T(8,128)(2,1)S(1)}, u32[]{:S(2)}, u32[]{:S(2)}) collective-permute-start(bf16[4,8,16,640]{3,2,1,0:T(8,128)(2,1)S(1)} %pad_maximum_fusion.1.refs_6_), channel_id=1, source_target_pairs={{0,256},{128,384},{256,0},{384,128},{1,257},{129,385},{257,1},{385... | collective-permute-start | bytes 1966088 | tf_op jit(solution)/shard_map/ppermute | solution.py:19
  95.4 23.0 %collective-permute-start.9 = (bf16[4,8,16,640]{3,2,1,0:T(8,128)(2,1)S(1)}, bf16[4,8,16,640]{3,2,1,0:T(8,128)(2,1)S(1)}, u32[]{:S(2)}, u32[]{:S(2)}) collective-permute-start(bf16[4,8,16,640]{3,2,1,0:T(8,128)(2,1)S(1)} %pad_maximum_fusion.1.refs_6_), channel_id=1, source_target_pairs={{0,128},{128,256},{256,384},{384,0},{1,129},{129,257},{257,385},{3... | collective-permute-start | bytes 1966088 | tf_op jit(solution)/shard_map/ppermute | solution.py:19
  108.7 23.1 %copy-start.1 = (bf16[4,8,16,640]{3,2,1,0:T(8,128)(2,1)}, bf16[4,8,16,640]{3,2,1,0:T(8,128)(2,1)S(1)}, u32[]{:S(2)}) copy-start(bf16[4,8,16,640]{3,2,1,0:T(8,128)(2,1)S(1)} %pad_maximum_fusion.refs_2_) | copy-start | bytes 1966084
  108.7 13.7 %collective-permute-start.3 = (bf16[4,8,16,640]{3,2,1,0:T(8,128)(2,1)S(1)}, bf16[4,8,16,640]{3,2,1,0:T(8,128)(2,1)S(1)}, u32[]{:S(2)}, u32[]{:S(2)}) collective-permute-start(bf16[4,8,16,640]{3,2,1,0:T(8,128)(2,1)S(1)} %pad_maximum_fusion.refs_2_), channel_id=1, source_target_pairs={{0,1},{1,2},{2,3},{3,0},{4,5},{5,6},{6,7},{7,4},{8,9},{9,10},{10,1... | collective-permute-start | bytes 1966088 | tf_op jit(solution)/shard_map/ppermute | solution.py:19
  111.0 19.8 %collective-permute-start.4 = (bf16[4,8,16,640]{3,2,1,0:T(8,128)(2,1)S(1)}, bf16[4,8,16,640]{3,2,1,0:T(8,128)(2,1)S(1)}, u32[]{:S(2)}, u32[]{:S(2)}) collective-permute-start(bf16[4,8,16,640]{3,2,1,0:T(8,128)(2,1)S(1)} %pad_maximum_fusion.refs_2_), channel_id=1, source_target_pairs={{0,3},{1,0},{2,1},{3,2},{4,7},{5,4},{6,5},{7,6},{8,11},{9,8},{10,9... | collective-permute-start | bytes 1966088 | tf_op jit(solution)/shard_map/ppermute | solution.py:19
  115.8 16.0 %copy-start.2 = (bf16[4,8,16,640]{3,2,1,0:T(8,128)(2,1)}, bf16[4,8,16,640]{3,2,1,0:T(8,128)(2,1)S(1)}, u32[]{:S(2)}) copy-start(bf16[4,8,16,640]{3,2,1,0:T(8,128)(2,1)S(1)} %collective-permute-done.10.refs_8_) | copy-start | bytes 1966084
  115.8 16.0 %collective-permute-start.5 = (bf16[4,8,16,640]{3,2,1,0:T(8,128)(2,1)S(1)}, bf16[4,8,16,640]{3,2,1,0:T(8,128)(2,1)}, u32[]{:S(2)}, u32[]{:S(2)}) collective-permute-start(bf16[4,8,16,640]{3,2,1,0:T(8,128)(2,1)S(1)} %pad_maximum_fusion.refs_2_), channel_id=1, source_target_pairs={{0,2},{1,3},{2,0},{3,1},{4,6},{5,7},{6,4},{7,5},{8,10},{9,11},{10,... | collective-permute-start | bytes 1966088 | tf_op jit(solution)/shard_map/ppermute | solution.py:19
  118.3 13.4 %copy-start.3 = (bf16[4,8,16,640]{3,2,1,0:T(8,128)(2,1)}, bf16[4,8,16,640]{3,2,1,0:T(8,128)(2,1)S(1)}, u32[]{:S(2)}) copy-start(bf16[4,8,16,640]{3,2,1,0:T(8,128)(2,1)S(1)} %collective-permute-done.11.refs_9_) | copy-start | bytes 1966084
  118.3 13.4 %copy-start.4 = (bf16[4,8,16,640]{3,2,1,0:T(8,128)(2,1)}, bf16[4,8,16,640]{3,2,1,0:T(8,128)(2,1)S(1)}, u32[]{:S(2)}) copy-start(bf16[4,8,16,640]{3,2,1,0:T(8,128)(2,1)S(1)} %collective-permute-done.9.refs_7_) | copy-start | bytes 1966084
  122.4 8.5 %copy-start.5 = (bf16[4,8,16,640]{3,2,1,0:T(8,128)(2,1)}, bf16[4,8,16,640]{3,2,1,0:T(8,128)(2,1)S(1)}, u32[]{:S(2)}) copy-start(bf16[4,8,16,640]{3,2,1,0:T(8,128)(2,1)S(1)} %collective-permute-done.3.refs_3_) | copy-start | bytes 1966084
  130.9 0.9 copy-start.6
  147.3 4.4 %collective-permute-start.12 = (f32[320,640]{1,0:T(8,128)}, f32[320,640]{1,0:T(8,128)S(1)}, u32[]{:S(2)}, u32[]{:S(2)}) collective-permute-start(f32[320,640]{1,0:T(8,128)} %get-tuple-element.10), channel_id=1, source_target_pairs={{0,64},{64,0},{1,65},{65,1},{2,66},{66,2},{3,67},{67,3},{4,68},{68... | collective-permute-start | bytes 2457608 | tf_op jit(solution)/shard_map/ppermute | solution.py:124
Sparse Core Ops, SparseCore 0:
  24.2 86.7 all-gather.1

commit v3 on v2

--- a/solution.py
+++ b/solution.py
@@ -8,6 +8,7 @@
 from jax.sharding import Mesh
 from jax.sharding import PartitionSpec as P
 
+VMEM = pl.BlockSpec(memory_space=pltpu.VMEM)
 SMEM = pl.BlockSpec(memory_space=pltpu.SMEM)
 
 
@@ -16,44 +17,62 @@
 
 
 def spread(value, axis, n):
-    return [value] + [lax.ppermute(value, axis, around(n, s)) for s in (1, 3, 2)]
+    return [value] + [lax.ppermute(value, axis, around(n, s)) for s in SHIFTS[1:]]
+
+
+def collect(value, axis, n):
+    copies = jnp.broadcast_to(value[None], (n,) + value.shape)
+    return lax.all_to_all(copies, axis, split_axis=0, concat_axis=0, tiled=True)
 
 
 SHIFTS = (0, 1, 3, 2)
+GROUP = 4
 
 
-def gram_kernel(half, planes, place_ref, rows_ref, *refs):
+def gram_kernel(half, steps, place_ref, rows_ref, by_y_ref, *refs):
     x, y, c = place_ref[0], place_ref[1], place_ref[2]
-    by_y, by_x = refs[:4], refs[4:8]
-    keep_ref, send_ref, acc_ref = refs[8:]
+    by_x, (keep_ref, send_ref, acc_ref) = refs[:4], refs[4:]
     k = pl.program_id(0)
 
-    @pl.when(k == 0)
-    def _():
-        acc_ref[...] = jnp.zeros_like(acc_ref)
-
-    def add(right):
-        left = []
-        for s in SHIFTS:
-            for t in SHIFTS:
-                slot = lax.rem(x - s + 4, 4) * 4 + lax.rem(y - t + 4, 4)
-                left.append(rows_ref[0, slot])
-        acc_ref[...] += lax.dot_general(
+    def product(left, right):
+        return lax.dot_general(
             jnp.concatenate(left, 0),
             jnp.concatenate(right, 0),
             (((0,), (0,)), ((), ())),
             preferred_element_type=jnp.float32,
         )
 
-    @pl.when(k < planes // 2)
+    def first():
+        left, right = [], []
+        for p in range(GROUP):
+            for i in range(4):
+                for j in range(4):
+                    left.append(rows_ref[p, i * 4 + j])
+                    right.append(by_y_ref[j, i, p])
+        return product(left, right)
+
+    def second():
+        left, right = [], []
+        for p in range(GROUP):
+            for i, s in enumerate(SHIFTS):
+                for j, t in enumerate(SHIFTS):
+                    left.append(rows_ref[p, lax.rem(x - s + 4, 4) * 4 + lax.rem(y - t + 4, 4)])
+                    right.append(by_x[i][j, p])
+        return product(left, right)
+
+    @pl.when(k == 0)
     def _():
-        add([by_y[j][i, 0] for i in range(4) for j in range(4)])
+        acc_ref[...] = first()
 
-    @pl.when(k >= planes // 2)
+    @pl.when(jnp.logical_and(k > 0, k < steps // 2))
     def _():
-        add([by_x[i][j, 0] for i in range(4) for j in range(4)])
+        acc_ref[...] += first()
 
-    last = k == planes - 1
+    @pl.when(k >= steps // 2)
+    def _():
+        acc_ref[...] += second()
+
+    last = k == steps - 1
 
     @pl.when(jnp.logical_and(last, c == 0))
     def _():
@@ -64,6 +83,16 @@
     def _():
         keep_ref[...] = acc_ref[half:]
         send_ref[...] = acc_ref[:half]
+
+
+def finish_kernel(factor, place_ref, keep_ref, add_ref, out_ref):
+    shape = keep_ref.shape
+    row_ids = place_ref[0] + lax.broadcasted_iota(jnp.int32, shape, 0)
+    col_ids = place_ref[1] + lax.broadcasted_iota(jnp.int32, shape, 1)
+    total = (keep_ref[...] + add_ref[...]) * factor
+    piece = jnp.where(row_ids == col_ids, jnp.float32(0.0), total).astype(jnp.bfloat16)
+    for i in range(out_ref.shape[0]):
+        out_ref[i] = piece
 
 
 def body(occurrences, idf_weight, pattern):
@@ -96,21 +125,32 @@
     by_col, own = lax.optimization_barrier((by_col, own))
     part = lax.all_to_all(by_col, "col", split_axis=0, concat_axis=0, tiled=True)
     upper, lower = part[: nz // 2], part[nz // 2 :]
-    along_x = jnp.stack(spread(upper, "x", nx))
+    along_x = collect(upper, "x", nx)
     along_y = jnp.stack(spread(lower, "layer", ny))
-    by_y = spread(along_x, "layer", ny)
+    along_x, along_y = lax.optimization_barrier((along_x, along_y))
+    by_y = collect(along_x, "layer", ny)
     by_x = spread(along_y, "x", nx)
 
     place = jnp.stack([x, y, c]).astype(jnp.int32)
-    n = nz // 2
-    block = (nx, 1, owned, width)
+    steps = nz // GROUP
+    n = steps // 2
     keep, send = pl.pallas_call(
-        lambda *refs: gram_kernel(half, nz, *refs),
+        lambda *refs: gram_kernel(half, steps, *refs),
         out_shape=(jax.ShapeDtypeStruct((half, width), jnp.float32),) * 2,
-        grid=(nz,),
-        in_specs=[SMEM, pl.BlockSpec((1, chips, owned, tile), lambda k: (k, 0, 0, 0))]
-        + [pl.BlockSpec(block, lambda k: (0, jnp.minimum(k, n - 1), 0, 0))] * ny
-        + [pl.BlockSpec(block, lambda k: (0, jnp.maximum(k - n, 0), 0, 0))] * nx,
+        grid=(steps,),
+        in_specs=[
+            SMEM,
+            pl.BlockSpec((GROUP, chips, owned, tile), lambda k: (k, 0, 0, 0)),
+            pl.BlockSpec(
+                (ny, nx, GROUP, owned, width), lambda k: (0, 0, jnp.minimum(k, n - 1), 0, 0)
+            ),
+        ]
+        + [
+            pl.BlockSpec(
+                (ny, GROUP, owned, width), lambda k: (0, jnp.maximum(k - n, 0), 0, 0)
+            )
+        ]
+        * nx,
         out_specs=(pl.BlockSpec((half, width), lambda k: (0, 0)),) * 2,
         scratch_shapes=[pltpu.VMEM((tile, width), jnp.float32)],
         compiler_params=pltpu.CompilerParams(vmem_limit_bytes=60 << 20),
@@ -120,12 +160,17 @@
             transcendentals=0,
         ),
         name="gram",
-    )(place, rows, *by_y, *by_x)
-    total = (keep + lax.ppermute(send, "core", [(0, 1), (1, 0)])) * factor
-    row_ids = ((x * nc + c) * ny + y) * half + lax.broadcasted_iota(jnp.int32, total.shape, 0)
-    col_ids = z * width + lax.broadcasted_iota(jnp.int32, total.shape, 1)
-    piece = jnp.where(row_ids == col_ids, jnp.float32(0.0), total).astype(jnp.bfloat16)
-    copies = jnp.broadcast_to(piece[None], (ny,) + piece.shape)
+    )(place, rows, by_y, *by_x)
+    add = lax.ppermute(send, "core", [(0, 1), (1, 0)])
+    corner = jnp.stack([((x * nc + c) * ny + y) * half, z * width]).astype(jnp.int32)
+    copies = pl.pallas_call(
+        lambda *refs: finish_kernel(factor, *refs),
+        out_shape=jax.ShapeDtypeStruct((ny, half, width), jnp.bfloat16),
+        in_specs=[SMEM, VMEM, VMEM],
+        out_specs=VMEM,
+        compiler_params=pltpu.CompilerParams(vmem_limit_bytes=8 << 20),
+        name="finish",
+    )(corner, keep, add)
     out = lax.all_to_all(copies, "layer", split_axis=0, concat_axis=0, tiled=True)
     return out.reshape(ny * half, width)
 

time: 189 us -> 171 us (0.905)
  the two profiles are of different devices: /device:TPU:166 before, /device:TPU:34 now
where the time goes in v3:
time: 171 us; the launch traced here: 170 us
  blocking collectives  76.9 us (45%)
  starting transfers between devices  29.9 us (17%)
  waiting for transfers between devices  28.9 us (17%)
  between operations  13.6 us (8%)
  Pallas kernels  9.61 us (6%)
  local copies, waits for them, and re-layouts  8.58 us (5%)
  other arithmetic  2.57 us (2%)
    all_to_all x1, blocking collectives, body(): lax.all_to_all(by_col, 'col', split_axis=0, concat_axis=0, tiled=True)  36.2 us
    ppermute x6, waiting for transfers between devices, spread(): lax.ppermute(value, axis, around(n, s))  26.4 us
    all_to_all x1, blocking collectives, body(): lax.all_to_all(copies, 'layer', split_axis=0, concat_axis=0, tiled=True)  26 us
    ppermute x6, starting transfers between devices, spread(): lax.ppermute(value, axis, around(n, s))  18.3 us
    all_to_all x1, blocking collectives, body(): lax.all_to_all(by_chip, ('x', 'layer'), split_axis=0, concat_axis=0, tile...  14.7 us
    all_to_all x2, starting transfers between devices, collect(): return lax.all_to_all(copies, axis, split_axis=0, concat_axis=0, tiled=True)  9.76 us
    pallas_call x1, Pallas kernels, body(): pl.pallas_call(lambda *refs: gram_kernel(half, steps, *refs), out_shape=(...  8.92 us
    unnamed x11, local copies, waits for them, and re-layouts  4.65 us
  transfers between devices with their start and end apart: 10, of which 7 were waited for; matrix products, arithmetic and copies ran while one was open for 2% of the time, Pallas kernels for 0%

profile of v3, /device:TPU:34, one launch (start us, length us, event | category | flops | bytes accessed | tf_op | source)
XLA Modules:
  0.0 170.1 jit_solution(2788827246934523315)
XLA Ops:
  6.5 0.0 all-gather.2.cloned.1.call-start
  6.5 0.7 convert_bitcast_fusion
  7.2 0.1 broadcast_bitcast_fusion
  7.3 1.1 multiply_convert_fusion
  8.4 0.5 reshape.23
  9.0 0.3 copy.9
  9.3 0.3 reshape.24
  9.6 14.7 %all_to_all.25 = bf16[16,16,640]{2,1,0:T(8,128)(2,1)} all-to-all(bf16[16,16,640]{2,1,0:T(8,128)(2,1)S(1)} %reshape.24), channel_id=1, replica_groups=mesh['x'=4,'core'=2,'col'=16,'layer'=4] {'x','layer'}, dimensions={0} | all-to-all | bytes 655360 | tf_op jit(solution)/shard_map/all_to_all | solution.py:121
  24.3 0.0 all-gather.2.cloned.1.call-update
  24.4 36.2 %all_to_all.26 = bf16[16,16,640]{2,1,0:T(8,128)(2,1)S(1)} all-to-all(bf16[16,16,640]{2,1,0:T(8,128)(2,1)S(1)} %bitcast.31), channel_id=1, replica_groups=mesh['x'=4,'core'=2,'col'=16,'layer'=4] {'col'}, dimensions={0} | all-to-all | bytes 655360 | tf_op jit(solution)/shard_map/all_to_all | solution.py:126
  60.6 0.9 broadcast_in_dim.7
  61.5 6.1 %all-to-all-start.2 = ((bf16[4,8,16,640]{3,2,1,0:T(8,128)(2,1)}), bf16[4,8,16,640]{3,2,1,0:T(8,128)(2,1)S(1)}, u32[]{:S(2)}, u32[]{:S(2)}) async-start(bf16[4,8,16,640]{3,2,1,0:T(8,128)(2,1)} %broadcast_in_dim.7), calls=%async_computation.2 | async-start | bytes 1310720 | tf_op jit(solution)/shard_map/all_to_all | solution.py:25
  67.6 2.6 %collective-permute-start.2 = (bf16[8,16,640]{2,1,0:T(8,128)(2,1)S(1)}, bf16[8,16,640]{2,1,0:T(8,128)(2,1)S(1)}, u32[]{:S(2)}, u32[]{:S(2)}) collective-permute-start(bf16[8,16,640]{2,1,0:T(8,128)(2,1)S(1)} %get-tuple-element.16), channel_id=1, source_target_pairs={{0,2},{1,3},{2,0},{3,1},{4,6},{5,7},{6,4},{7,5},{8,10},{9,11},{10,... | collective-permute-start | bytes 491528 | tf_op jit(solution)/shard_map/ppermute | solution.py:20
  70.2 3.9 %collective-permute-start.1 = (bf16[8,16,640]{2,1,0:T(8,128)(2,1)S(1)}, bf16[8,16,640]{2,1,0:T(8,128)(2,1)S(1)}, u32[]{:S(2)}, u32[]{:S(2)}) collective-permute-start(bf16[8,16,640]{2,1,0:T(8,128)(2,1)S(1)} %get-tuple-element.16), channel_id=1, source_target_pairs={{0,3},{1,0},{2,1},{3,2},{4,7},{5,4},{6,5},{7,6},{8,11},{9,8},{10,9... | collective-permute-start | bytes 491528 | tf_op jit(solution)/shard_map/ppermute | solution.py:20
  74.2 1.9 %collective-permute-start = (bf16[8,16,640]{2,1,0:T(8,128)(2,1)S(1)}, bf16[8,16,640]{2,1,0:T(8,128)(2,1)S(1)}, u32[]{:S(2)}, u32[]{:S(2)}) collective-permute-start(bf16[8,16,640]{2,1,0:T(8,128)(2,1)S(1)} %get-tuple-element.16), channel_id=1, source_target_pairs={{0,1},{1,2},{2,3},{3,0},{4,5},{5,6},{6,7},{7,4},{8,9},{9,10},{10,1... | collective-permute-start | bytes 491528 | tf_op jit(solution)/shard_map/ppermute | solution.py:20
  76.1 0.9 collective-permute-done.2
  77.0 0.5 collective-permute-done.1
  77.5 5.1 %collective-permute-done = bf16[8,16,640]{2,1,0:T(8,128)(2,1)S(1)} collective-permute-done((bf16[8,16,640]{2,1,0:T(8,128)(2,1)S(1)}, bf16[8,16,640]{2,1,0:T(8,128)(2,1)S(1)}, u32[]{:S(2)}, u32[]{:S(2)}) %collective-permute-start) | collective-permute-done | bytes 163872 | tf_op jit(solution)/shard_map/ppermute | solution.py:20
  82.6 0.1 pad_maximum_fusion.refs_3_
  82.7 0.0 copy-start.2
  82.7 0.0 all-to-all-done.2
  82.7 1.8 %broadcast_in_dim.8 = bf16[4,4,8,16,640]{4,3,2,1,0:T(8,128)(2,1)} broadcast(bf16[4,8,16,640]{3,2,1,0:T(8,128)(2,1)S(1)} %all-to-all-done.2), dimensions={1,2,3,4} | broadcast | bytes 3276800 | tf_op jit(solution)/shard_map/broadcast_in_dim | solution.py:24
  84.5 3.7 %all-to-all-start.3 = ((bf16[4,4,8,16,640]{4,3,2,1,0:T(8,128)(2,1)}), bf16[4,4,8,16,640]{4,3,2,1,0:T(8,128)(2,1)S(1)}, u32[]{:S(2)}, u32[]{:S(2)}) async-start(bf16[4,4,8,16,640]{4,3,2,1,0:T(8,128)(2,1)} %broadcast_in_dim.8), calls=%async_computation.3 | async-start | bytes 5242880 | tf_op jit(solution)/shard_map/all_to_all | solution.py:25
  88.2 3.4 %collective-permute-start.3 = (bf16[4,8,16,640]{3,2,1,0:T(8,128)(2,1)S(1)}, bf16[4,8,16,640]{3,2,1,0:T(8,128)(2,1)S(1)}, u32[]{:S(2)}, u32[]{:S(2)}) collective-permute-start(bf16[4,8,16,640]{3,2,1,0:T(8,128)(2,1)S(1)} %pad_maximum_fusion.refs_3_), channel_id=1, source_target_pairs={{0,128},{128,256},{256,384},{384,0},{1,129},{129,257},{257,385},{3... | collective-permute-start | bytes 1966088 | tf_op jit(solution)/shard_map/ppermute | solution.py:20
  91.5 2.5 %collective-permute-start.4 = (bf16[4,8,16,640]{3,2,1,0:T(8,128)(2,1)S(1)}, bf16[4,8,16,640]{3,2,1,0:T(8,128)(2,1)S(1)}, u32[]{:S(2)}, u32[]{:S(2)}) collective-permute-start(bf16[4,8,16,640]{3,2,1,0:T(8,128)(2,1)S(1)} %pad_maximum_fusion.refs_3_), channel_id=1, source_target_pairs={{0,384},{128,0},{256,128},{384,256},{1,385},{129,1},{257,129},{385... | collective-permute-start | bytes 1966088 | tf_op jit(solution)/shard_map/ppermute | solution.py:20
  94.0 0.0 copy-done.2
  94.0 4.0 %collective-permute-start.5 = (bf16[4,8,16,640]{3,2,1,0:T(8,128)(2,1)S(1)}, bf16[4,8,16,640]{3,2,1,0:T(8,128)(2,1)}, u32[]{:S(2)}, u32[]{:S(2)}) collective-permute-start(bf16[4,8,16,640]{3,2,1,0:T(8,128)(2,1)S(1)} %pad_maximum_fusion.refs_3_), channel_id=1, source_target_pairs={{0,256},{128,384},{256,0},{384,128},{1,257},{129,385},{257,1},{385... | collective-permute-start | bytes 1966088 | tf_op jit(solution)/shard_map/ppermute | solution.py:20
  98.0 0.6 pad_add_fusion.1.refs_0_
  98.6 9.1 %collective-permute-done.3.refs_4_ = bf16[4,8,16,640]{3,2,1,0:T(8,128)(2,1)S(1)} collective-permute-done((bf16[4,8,16,640]{3,2,1,0:T(8,128)(2,1)S(1)}, bf16[4,8,16,640]{3,2,1,0:T(8,128)(2,1)S(1)}, u32[]{:S(2)}, u32[]{:S(2)}) %collective-permute-start.3) | collective-permute-done | bytes 655392 | tf_op jit(solution)/shard_map/ppermute | solution.py:20
  107.7 0.0 copy-start.3
  107.7 2.8 %collective-permute-done.4.refs_5_ = bf16[4,8,16,640]{3,2,1,0:T(8,128)(2,1)S(1)} collective-permute-done((bf16[4,8,16,640]{3,2,1,0:T(8,128)(2,1)S(1)}, bf16[4,8,16,640]{3,2,1,0:T(8,128)(2,1)S(1)}, u32[]{:S(2)}, u32[]{:S(2)}) %collective-permute-start.4) | collective-permute-done | bytes 655392 | tf_op jit(solution)/shard_map/ppermute | solution.py:20
  110.5 0.0 copy-done.3
  110.5 0.0 copy-start.4
  110.5 0.9 copy-done.4
  111.4 8.0 %collective-permute-done.5.refs_6_ = bf16[4,8,16,640]{3,2,1,0:T(8,128)(2,1)} collective-permute-done((bf16[4,8,16,640]{3,2,1,0:T(8,128)(2,1)S(1)}, bf16[4,8,16,640]{3,2,1,0:T(8,128)(2,1)}, u32[]{:S(2)}, u32[]{:S(2)}) %collective-permute-start.5) | collective-permute-done | bytes 655392 | tf_op jit(solution)/shard_map/ppermute | solution.py:20
  119.4 0.0 all-to-all-done.3.refs_2_
  119.4 0.0 copy-start.1
  119.4 0.0 all-gather.2.cloned.1.call-done
  119.4 1.5 copy-done.1
  120.9 8.9 %gram.1 = (f32[320,640]{1,0:T(8,128)}, f32[320,640]{1,0:T(8,128)}) custom-call(s32[3]{0:T(128)} %pad_add_fusion.1.refs_0_, bf16[16,16,16,640]{3,2,1,0:T(8,128)(2,1)} %bitcast.35, bf16[4,4,8,16,640]{4,3,2,1,0:T(8,128)(2,1)} %copy-done.1, bf16[4,8,16,640]{3,2,1,0:T(8,128)(2,1)} %copy-done.2, bf16[4,8,16,640]{3,2,1,0:T(8,128)(2,1)} %copy-done.3, ...), custom_call_target="tpu_custom_call" | custom-call | flops 3355443200 | bytes 10485760 | tf_op jit(solution)/shard_map/gram/pallas_call | solution.py:137
  129.8 1.9 %collective-permute-start.6 = (f32[320,640]{1,0:T(8,128)}, f32[320,640]{1,0:T(8,128)S(1)}, u32[]{:S(2)}, u32[]{:S(2)}) collective-permute-start(f32[320,640]{1,0:T(8,128)} %get-tuple-element.14), channel_id=1, source_target_pairs={{0,64},{64,0},{1,65},{65,1},{2,66},{66,2},{3,67},{67,3},{4,68},{68... | collective-permute-start | bytes 2457608 | tf_op jit(solution)/shard_map/ppermute | solution.py:164
  131.7 0.1 pad_add_fusion.refs_0_
  131.8 2.4 %collective-permute-done.6.refs_2_ = f32[320,640]{1,0:T(8,128)S(1)} collective-permute-done((f32[320,640]{1,0:T(8,128)}, f32[320,640]{1,0:T(8,128)S(1)}, u32[]{:S(2)}, u32[]{:S(2)}) %collective-permute-start.6) | collective-permute-done | bytes 819232 | tf_op jit(solution)/shard_map/ppermute | solution.py:164
  134.2 0.0 copy-start
  134.2 1.1 copy-done
  135.4 0.7 finish.1
  136.1 26.0 %all_to_all.27 = bf16[4,320,640]{2,1,0:T(8,128)(2,1)S(1)} all-to-all(bf16[4,320,640]{2,1,0:T(8,128)(2,1)S(1)} %finish.1), channel_id=1, replica_groups=mesh['x'=4,'core'=2,'col'=16,'layer'=4] {'layer'}, dimensions={0} | all-to-all | bytes 3276800 | tf_op jit(solution)/shard_map/all_to_all | solution.py:174
  162.1 1.2 copy.12
  (2 shorter events, 0.1 us)
Async XLA Ops:
  6.5 112.9 %all-gather.2.cloned.1.call-start = ((), (), s32[]{:S(2)}) async-start(), calls=%async_computation.5 | async-start | bytes 5570560 | tf_op jit(solution)/shard_map/all_gather | solution.py:123
  61.5 21.2 %all-to-all-start.2 = ((bf16[4,8,16,640]{3,2,1,0:T(8,128)(2,1)}), bf16[4,8,16,640]{3,2,1,0:T(8,128)(2,1)S(1)}, u32[]{:S(2)}, u32[]{:S(2)}) async-start(bf16[4,8,16,640]{3,2,1,0:T(8,128)(2,1)} %broadcast_in_dim.7), calls=%async_computation.2 | async-start | bytes 1310720 | tf_op jit(solution)/shard_map/all_to_all | solution.py:25
  67.6 9.3 %collective-permute-start.2 = (bf16[8,16,640]{2,1,0:T(8,128)(2,1)S(1)}, bf16[8,16,640]{2,1,0:T(8,128)(2,1)S(1)}, u32[]{:S(2)}, u32[]{:S(2)}) collective-permute-start(bf16[8,16,640]{2,1,0:T(8,128)(2,1)S(1)} %get-tuple-element.16), channel_id=1, source_target_pairs={{0,2},{1,3},{2,0},{3,1},{4,6},{5,7},{6,4},{7,5},{8,10},{9,11},{10,... | collective-permute-start | bytes 491528 | tf_op jit(solution)/shard_map/ppermute | solution.py:20
  70.2 7.2 %collective-permute-start.1 = (bf16[8,16,640]{2,1,0:T(8,128)(2,1)S(1)}, bf16[8,16,640]{2,1,0:T(8,128)(2,1)S(1)}, u32[]{:S(2)}, u32[]{:S(2)}) collective-permute-start(bf16[8,16,640]{2,1,0:T(8,128)(2,1)S(1)} %get-tuple-element.16), channel_id=1, source_target_pairs={{0,3},{1,0},{2,1},{3,2},{4,7},{5,4},{6,5},{7,6},{8,11},{9,8},{10,9... | collective-permute-start | bytes 491528 | tf_op jit(solution)/shard_map/ppermute | solution.py:20
  74.2 8.4 %collective-permute-start = (bf16[8,16,640]{2,1,0:T(8,128)(2,1)S(1)}, bf16[8,16,640]{2,1,0:T(8,128)(2,1)S(1)}, u32[]{:S(2)}, u32[]{:S(2)}) collective-permute-start(bf16[8,16,640]{2,1,0:T(8,128)(2,1)S(1)} %get-tuple-element.16), channel_id=1, source_target_pairs={{0,1},{1,2},{2,3},{3,0},{4,5},{5,6},{6,7},{7,4},{8,9},{9,10},{10,1... | collective-permute-start | bytes 491528 | tf_op jit(solution)/shard_map/ppermute | solution.py:20
  82.7 11.3 %copy-start.2 = (bf16[4,8,16,640]{3,2,1,0:T(8,128)(2,1)}, bf16[4,8,16,640]{3,2,1,0:T(8,128)(2,1)S(1)}, u32[]{:S(2)}) copy-start(bf16[4,8,16,640]{3,2,1,0:T(8,128)(2,1)S(1)} %pad_maximum_fusion.refs_3_) | copy-start | bytes 1966084
  84.5 34.9 %all-to-all-start.3 = ((bf16[4,4,8,16,640]{4,3,2,1,0:T(8,128)(2,1)}), bf16[4,4,8,16,640]{4,3,2,1,0:T(8,128)(2,1)S(1)}, u32[]{:S(2)}, u32[]{:S(2)}) async-start(bf16[4,4,8,16,640]{4,3,2,1,0:T(8,128)(2,1)} %broadcast_in_dim.8), calls=%async_computation.3 | async-start | bytes 5242880 | tf_op jit(solution)/shard_map/all_to_all | solution.py:25
  88.2 19.6 %collective-permute-start.3 = (bf16[4,8,16,640]{3,2,1,0:T(8,128)(2,1)S(1)}, bf16[4,8,16,640]{3,2,1,0:T(8,128)(2,1)S(1)}, u32[]{:S(2)}, u32[]{:S(2)}) collective-permute-start(bf16[4,8,16,640]{3,2,1,0:T(8,128)(2,1)S(1)} %pad_maximum_fusion.refs_3_), channel_id=1, source_target_pairs={{0,128},{128,256},{256,384},{384,0},{1,129},{129,257},{257,385},{3... | collective-permute-start | bytes 1966088 | tf_op jit(solution)/shard_map/ppermute | solution.py:20
  91.5 19.0 %collective-permute-start.4 = (bf16[4,8,16,640]{3,2,1,0:T(8,128)(2,1)S(1)}, bf16[4,8,16,640]{3,2,1,0:T(8,128)(2,1)S(1)}, u32[]{:S(2)}, u32[]{:S(2)}) collective-permute-start(bf16[4,8,16,640]{3,2,1,0:T(8,128)(2,1)S(1)} %pad_maximum_fusion.refs_3_), channel_id=1, source_target_pairs={{0,384},{128,0},{256,128},{384,256},{1,385},{129,1},{257,129},{385... | collective-permute-start | bytes 1966088 | tf_op jit(solution)/shard_map/ppermute | solution.py:20
  94.0 25.4 %collective-permute-start.5 = (bf16[4,8,16,640]{3,2,1,0:T(8,128)(2,1)S(1)}, bf16[4,8,16,640]{3,2,1,0:T(8,128)(2,1)}, u32[]{:S(2)}, u32[]{:S(2)}) collective-permute-start(bf16[4,8,16,640]{3,2,1,0:T(8,128)(2,1)S(1)} %pad_maximum_fusion.refs_3_), channel_id=1, source_target_pairs={{0,256},{128,384},{256,0},{384,128},{1,257},{129,385},{257,1},{385... | collective-permute-start | bytes 1966088 | tf_op jit(solution)/shard_map/ppermute | solution.py:20
  107.7 2.8 %copy-start.3 = (bf16[4,8,16,640]{3,2,1,0:T(8,128)(2,1)}, bf16[4,8,16,640]{3,2,1,0:T(8,128)(2,1)S(1)}, u32[]{:S(2)}) copy-start(bf16[4,8,16,640]{3,2,1,0:T(8,128)(2,1)S(1)} %collective-permute-done.3.refs_4_) | copy-start | bytes 1966084
  110.5 0.9 copy-start.4
  119.4 1.5 copy-start.1
  129.8 4.4 %collective-permute-start.6 = (f32[320,640]{1,0:T(8,128)}, f32[320,640]{1,0:T(8,128)S(1)}, u32[]{:S(2)}, u32[]{:S(2)}) collective-permute-start(f32[320,640]{1,0:T(8,128)} %get-tuple-element.14), channel_id=1, source_target_pairs={{0,64},{64,0},{1,65},{65,1},{2,66},{66,2},{3,67},{67,3},{4,68},{68... | collective-permute-start | bytes 2457608 | tf_op jit(solution)/shard_map/ppermute | solution.py:164
  134.2 1.1 copy-start
Sparse Core Ops, SparseCore 0:
  24.5 90.7 all-gather.1

commit v4 on v3

v4 whole, which is shorter than its diff:
```python
import math

import jax
import jax.numpy as jnp
from jax import lax
from jax.experimental import pallas as pl
from jax.experimental.pallas import tpu as pltpu
from jax.sharding import Mesh
from jax.sharding import PartitionSpec as P

VMEM = pl.BlockSpec(memory_space=pltpu.VMEM)
SMEM = pl.BlockSpec(memory_space=pltpu.SMEM)


def around(n, shift):
    return [(i, (i + shift) % n) for i in range(n)]


def spread(value, axis, n):
    return [value] + [lax.ppermute(value, axis, around(n, s)) for s in SHIFTS[1:]]


def collect(value, axis, n):
    copies = jnp.broadcast_to(value[None], (n,) + value.shape)
    return lax.all_to_all(copies, axis, split_axis=0, concat_axis=0, tiled=True)


SHIFTS = (0, 1, 3, 2)
GROUP = 4


def turn_kernel(block_ref, turned_ref):
    turned_ref[...] = block_ref[...].T


def gram_kernel(steps, place_ref, rows_ref, by_y_ref, *refs):
    by_x, (out_ref, right_ref) = refs[:4], refs[4:]
    x, y = place_ref[1], place_ref[2]
    k = pl.program_id(0)
    owned = by_y_ref.shape[3]
    width = by_y_ref.shape[4]
    chips = 16

    def product(right):
        left = jnp.concatenate([rows_ref[p] for p in range(GROUP)], 1)
        return jnp.dot(left, right, preferred_element_type=jnp.float32)

    def first():
        blocks = [
            by_y_ref[j, i, p] for p in range(GROUP) for i in range(4) for j in range(4)
        ]
        return product(jnp.concatenate(blocks, 0))

    @pl.when(k == 0)
    def _():
        out_ref[...] = first()

    @pl.when(jnp.logical_and(k > 0, k < steps // 2))
    def _():
        out_ref[...] += first()

    @pl.when(k >= steps // 2)
    def _():
        for i, s in enumerate(SHIFTS):
            for j, t in enumerate(SHIFTS):
                slot = lax.rem(x - s + 4, 4) * 4 + lax.rem(y - t + 4, 4)
                for p in range(GROUP):
                    start = pl.multiple_of(p * chips * owned + slot * owned, owned)
                    right_ref[pl.ds(start, owned), :] = by_x[i][j, p]
        out_ref[...] += product(right_ref[...])


def gram_half(place, rows, by_y, by_x, pick):
    planes, tile, depth = rows.shape
    ny, nx, _, owned, width = by_y.shape
    half = tile // 2
    steps = planes // GROUP
    n = steps // 2

    def half_of(place_ref):
        return place_ref[0] if pick == 0 else 1 - place_ref[0]

    grid_spec = pltpu.PrefetchScalarGridSpec(
        num_scalar_prefetch=1,
        grid=(steps,),
        in_specs=[
            pl.BlockSpec((GROUP, half, depth), lambda k, place_ref: (k, half_of(place_ref), 0)),
            pl.BlockSpec(
                (ny, nx, GROUP, owned, width),
                lambda k, place_ref: (0, 0, jnp.minimum(k, n - 1), 0, 0),
            ),
        ]
        + [
            pl.BlockSpec(
                (ny, GROUP, owned, width),
                lambda k, place_ref: (0, jnp.maximum(k - n, 0), 0, 0),
            )
        ]
        * nx,
        out_specs=pl.BlockSpec((half, width), lambda k, place_ref: (0, 0)),
        scratch_shapes=[pltpu.VMEM((GROUP * depth, width), jnp.bfloat16)],
    )
    return pl.pallas_call(
        lambda *refs: gram_kernel(steps, *refs),
        out_shape=jax.ShapeDtypeStruct((half, width), jnp.float32),
        grid_spec=grid_spec,
        compiler_params=pltpu.CompilerParams(vmem_limit_bytes=60 << 20),
        cost_estimate=pl.CostEstimate(
            flops=2 * half * width * planes * depth,
            bytes_accessed=2 * (half + width) * planes * depth,
            transcendentals=0,
        ),
        name="gram",
    )(place, rows, by_y, *by_x)


def finish_kernel(factor, place_ref, keep_ref, add_ref, out_ref):
    shape = keep_ref.shape
    row_ids = place_ref[0] + lax.broadcasted_iota(jnp.int32, shape, 0)
    col_ids = place_ref[1] + lax.broadcasted_iota(jnp.int32, shape, 1)
    total = (keep_ref[...] + add_ref[...]) * factor
    piece = jnp.where(row_ids == col_ids, jnp.float32(0.0), total).astype(jnp.bfloat16)
    for i in range(out_ref.shape[0]):
        out_ref[i] = piece


def body(occurrences, idf_weight, pattern):
    owned, reads = occurrences.shape
    nx, nc = lax.axis_size("x"), lax.axis_size("core")
    nz, ny = lax.axis_size("col"), lax.axis_size("layer")
    x, c = lax.axis_index("x"), lax.axis_index("core")
    z, y = lax.axis_index("col"), lax.axis_index("layer")
    factor = 1.0 / math.sqrt(owned * nx * nc * nz * ny)
    owner = lax.axis_index(("x", "core", "col", "layer"))
    flags = lax.dynamic_slice_in_dim(pattern, owner * owned // 128, 1, 0)[0]
    read_mask = jnp.repeat(flags.astype(jnp.float32), 128)
    weighted = (
        occurrences.astype(jnp.float32) * idf_weight[:, None] * read_mask[None, :]
    ).astype(jnp.bfloat16)

    width = reads // nz
    half = reads // (nx * nc * ny)
    tile = nc * half
    chips = nx * ny
    by_chip = (
        weighted.reshape(owned, nx, nc, ny, half)
        .transpose(1, 3, 0, 2, 4)
        .reshape(chips, owned, tile)
    )
    own = lax.all_to_all(by_chip, ("x", "layer"), split_axis=0, concat_axis=0, tiled=True)
    turned = pl.pallas_call(
        turn_kernel,
        out_shape=jax.ShapeDtypeStruct((tile, chips * owned), jnp.bfloat16),
        in_specs=[VMEM],
        out_specs=VMEM,
        compiler_params=pltpu.CompilerParams(vmem_limit_bytes=8 << 20),
        name="turn",
    )(own.reshape(chips * owned, tile))
    rows = lax.all_gather(turned, "col", axis=0, tiled=False)
    by_col = weighted.reshape(owned, nz, width).transpose(1, 0, 2)
    by_col, _ = lax.optimization_barrier((by_col, turned))
    part = lax.all_to_all(by_col, "col", split_axis=0, concat_axis=0, tiled=True)
    upper, lower = part[: nz // 2], part[nz // 2 :]
    along_x = collect(upper, "x", nx)
    along_y = jnp.stack(spread(lower, "layer", ny))
    along_x, along_y = lax.optimization_barrier((along_x, along_y))
    by_y = collect(along_x, "layer", ny)
    by_x = spread(along_y, "x", nx)

    place = jnp.stack([c, x, y]).astype(jnp.int32)
    send = gram_half(place, rows, by_y, by_x, 1)
    keep = gram_half(place, rows, by_y, by_x, 0)
    add = lax.ppermute(send, "core", [(0, 1), (1, 0)])
    corner = jnp.stack([((x * nc + c) * ny + y) * half, z * width]).astype(jnp.int32)
    copies = pl.pallas_call(
        lambda *refs: finish_kernel(factor, *refs),
        out_shape=jax.ShapeDtypeStruct((ny, half, width), jnp.bfloat16),
        in_specs=[SMEM, VMEM, VMEM],
        out_specs=VMEM,
        compiler_params=pltpu.CompilerParams(vmem_limit_bytes=8 << 20),
        name="finish",
    )(corner, keep, add)
    out = lax.all_to_all(copies, "layer", split_axis=0, concat_axis=0, tiled=True)
    return out.reshape(ny * half, width)


def solution(mesh):
    rows, cols, layers = mesh.devices.shape
    fine = Mesh(mesh.devices.reshape(rows // 2, 2, cols, layers), ("x", "core", "col", "layer"))
    owners = ("x", "core", "col", "layer")
    return jax.shard_map(
        body,
        mesh=fine,
        in_specs=(P(owners, None), P(owners), P()),
        out_specs=P(("x", "core"), "col"),
        check_vma=False,
    )
```

time: 171 us -> 175 us (1.023)
  Pallas kernels: 9.61 us -> 16.2 us
  waiting for transfers between devices: 28.9 us -> 26.4 us
    pallas_call x1 -> x3, Pallas kernels: 8.92 us -> 15.5 us  [the longest x2 14.6 us: gram_half(): pl.pallas_call(lambda *refs: gram_kernel(steps, *refs), out_shape=jax.Sha...]
    ppermute x1, waiting for transfers between devices: 2.42 us -> 0.01 us  [body(): add = lax.ppermute(send, 'core', [(0, 1), (1, 0)])]
  transfers between devices with their start and end apart: 10 -> 10, of which waited for: 7 -> 6; matrix products, arithmetic and copies ran while one was open for 2% -> 2% of each run, Pallas kernels for 0% -> 4%
where the time goes in v4:
time: 175 us; the launch traced here: 174 us
  blocking collectives  77.2 us (44%)
  starting transfers between devices  29.9 us (17%)
  waiting for transfers between devices  26.4 us (15%)
  Pallas kernels  16.2 us (9%)
  between operations  13.6 us (8%)
  local copies, waits for them, and re-layouts  8.59 us (5%)
  other arithmetic  2.66 us (2%)
    all_to_all x1, blocking collectives, body(): lax.all_to_all(by_col, 'col', split_axis=0, concat_axis=0, tiled=True)  36.2 us
    all_to_all x1, blocking collectives, body(): lax.all_to_all(copies, 'layer', split_axis=0, concat_axis=0, tiled=True)  26.3 us
    ppermute x6, waiting for transfers between devices, spread(): lax.ppermute(value, axis, around(n, s))  26.3 us
    ppermute x6, starting transfers between devices, spread(): lax.ppermute(value, axis, around(n, s))  18.3 us
    all_to_all x1, blocking collectives, body(): lax.all_to_all(by_chip, ('x', 'layer'), split_axis=0, concat_axis=0, tile...  14.6 us
    pallas_call x2, Pallas kernels, gram_half(): pl.pallas_call(lambda *refs: gram_kernel(steps, *refs), out_shape=jax.Sha...  14.6 us
    all_to_all x2, starting transfers between devices, collect(): return lax.all_to_all(copies, axis, split_axis=0, concat_axis=0, tiled=True)  9.76 us
    unnamed x11, local copies, waits for them, and re-layouts  4.65 us
  transfers between devices with their start and end apart: 10, of which 6 were waited for; matrix products, arithmetic and copies ran while one was open for 2% of the time, Pallas kernels for 4%

profile of v4, /device:TPU:34, one launch (start us, length us, event | category | flops | bytes accessed | tf_op | source)
XLA Modules:
  0.0 174.5 jit_solution(2487110559460261371)
XLA Ops:
  6.5 0.0 all-gather.3.cloned.1.call-start
  6.5 0.7 convert_bitcast_fusion
  7.2 0.1 broadcast_bitcast_fusion
  7.3 1.1 multiply_convert_fusion
  8.4 0.5 reshape.20
  9.0 0.3 copy.5
  9.3 0.3 reshape.21
  9.6 14.6 %all_to_all.25 = bf16[16,16,640]{2,1,0:T(8,128)(2,1)S(1)} all-to-all(bf16[16,16,640]{2,1,0:T(8,128)(2,1)S(1)} %reshape.21), channel_id=1, replica_groups=mesh['x'=4,'core'=2,'col'=16,'layer'=4] {'x','layer'}, dimensions={0} | all-to-all | bytes 655360 | tf_op jit(solution)/shard_map/all_to_all | solution.py:150
  24.2 0.9 turn.1
  25.1 0.0 all-gather.3.cloned.1.call-update
  25.2 36.2 %all_to_all.26 = bf16[16,16,640]{2,1,0:T(8,128)(2,1)S(1)} all-to-all(bf16[16,16,640]{2,1,0:T(8,128)(2,1)S(1)} %bitcast.31), channel_id=1, replica_groups=mesh['x'=4,'core'=2,'col'=16,'layer'=4] {'col'}, dimensions={0} | all-to-all | bytes 655360 | tf_op jit(solution)/shard_map/all_to_all | solution.py:162
  61.4 0.9 broadcast_in_dim.7
  62.3 6.1 %all-to-all-start.2 = ((bf16[4,8,16,640]{3,2,1,0:T(8,128)(2,1)}), bf16[4,8,16,640]{3,2,1,0:T(8,128)(2,1)S(1)}, u32[]{:S(2)}, u32[]{:S(2)}) async-start(bf16[4,8,16,640]{3,2,1,0:T(8,128)(2,1)} %broadcast_in_dim.7), calls=%async_computation.2 | async-start | bytes 1310720 | tf_op jit(solution)/shard_map/all_to_all | solution.py:25
  68.4 2.6 %collective-permute-start.2 = (bf16[8,16,640]{2,1,0:T(8,128)(2,1)S(1)}, bf16[8,16,640]{2,1,0:T(8,128)(2,1)S(1)}, u32[]{:S(2)}, u32[]{:S(2)}) collective-permute-start(bf16[8,16,640]{2,1,0:T(8,128)(2,1)S(1)} %get-tuple-element.12), channel_id=1, source_target_pairs={{0,2},{1,3},{2,0},{3,1},{4,6},{5,7},{6,4},{7,5},{8,10},{9,11},{10,... | collective-permute-start | bytes 491528 | tf_op jit(solution)/shard_map/ppermute | solution.py:20
  71.0 3.9 %collective-permute-start.1 = (bf16[8,16,640]{2,1,0:T(8,128)(2,1)S(1)}, bf16[8,16,640]{2,1,0:T(8,128)(2,1)S(1)}, u32[]{:S(2)}, u32[]{:S(2)}) collective-permute-start(bf16[8,16,640]{2,1,0:T(8,128)(2,1)S(1)} %get-tuple-element.12), channel_id=1, source_target_pairs={{0,3},{1,0},{2,1},{3,2},{4,7},{5,4},{6,5},{7,6},{8,11},{9,8},{10,9... | collective-permute-start | bytes 491528 | tf_op jit(solution)/shard_map/ppermute | solution.py:20
  75.0 1.9 %collective-permute-start = (bf16[8,16,640]{2,1,0:T(8,128)(2,1)S(1)}, bf16[8,16,640]{2,1,0:T(8,128)(2,1)S(1)}, u32[]{:S(2)}, u32[]{:S(2)}) collective-permute-start(bf16[8,16,640]{2,1,0:T(8,128)(2,1)S(1)} %get-tuple-element.12), channel_id=1, source_target_pairs={{0,1},{1,2},{2,3},{3,0},{4,5},{5,6},{6,7},{7,4},{8,9},{9,10},{10,1... | collective-permute-start | bytes 491528 | tf_op jit(solution)/shard_map/ppermute | solution.py:20
  76.9 0.9 collective-permute-done.2
  77.8 0.5 collective-permute-done.1
  78.3 5.1 %collective-permute-done = bf16[8,16,640]{2,1,0:T(8,128)(2,1)S(1)} collective-permute-done((bf16[8,16,640]{2,1,0:T(8,128)(2,1)S(1)}, bf16[8,16,640]{2,1,0:T(8,128)(2,1)S(1)}, u32[]{:S(2)}, u32[]{:S(2)}) %collective-permute-start) | collective-permute-done | bytes 163872 | tf_op jit(solution)/shard_map/ppermute | solution.py:20
  83.4 0.1 pad_maximum_fusion.refs_3_
  83.5 0.0 copy-start.2
  83.5 0.0 all-to-all-done.2
  83.5 1.8 %broadcast_in_dim.8 = bf16[4,4,8,16,640]{4,3,2,1,0:T(8,128)(2,1)} broadcast(bf16[4,8,16,640]{3,2,1,0:T(8,128)(2,1)S(1)} %all-to-all-done.2), dimensions={1,2,3,4} | broadcast | bytes 3276800 | tf_op jit(solution)/shard_map/broadcast_in_dim | solution.py:24
  85.3 3.7 %all-to-all-start.3 = ((bf16[4,4,8,16,640]{4,3,2,1,0:T(8,128)(2,1)}), bf16[4,4,8,16,640]{4,3,2,1,0:T(8,128)(2,1)S(1)}, u32[]{:S(2)}, u32[]{:S(2)}) async-start(bf16[4,4,8,16,640]{4,3,2,1,0:T(8,128)(2,1)} %broadcast_in_dim.8), calls=%async_computation.3 | async-start | bytes 5242880 | tf_op jit(solution)/shard_map/all_to_all | solution.py:25
  89.0 3.4 %collective-permute-start.3 = (bf16[4,8,16,640]{3,2,1,0:T(8,128)(2,1)S(1)}, bf16[4,8,16,640]{3,2,1,0:T(8,128)(2,1)S(1)}, u32[]{:S(2)}, u32[]{:S(2)}) collective-permute-start(bf16[4,8,16,640]{3,2,1,0:T(8,128)(2,1)S(1)} %pad_maximum_fusion.refs_3_), channel_id=1, source_target_pairs={{0,128},{128,256},{256,384},{384,0},{1,129},{129,257},{257,385},{3... | collective-permute-start | bytes 1966088 | tf_op jit(solution)/shard_map/ppermute | solution.py:20
  92.3 2.5 %collective-permute-start.4 = (bf16[4,8,16,640]{3,2,1,0:T(8,128)(2,1)S(1)}, bf16[4,8,16,640]{3,2,1,0:T(8,128)(2,1)S(1)}, u32[]{:S(2)}, u32[]{:S(2)}) collective-permute-start(bf16[4,8,16,640]{3,2,1,0:T(8,128)(2,1)S(1)} %pad_maximum_fusion.refs_3_), channel_id=1, source_target_pairs={{0,384},{128,0},{256,128},{384,256},{1,385},{129,1},{257,129},{385... | collective-permute-start | bytes 1966088 | tf_op jit(solution)/shard_map/ppermute | solution.py:20
  94.8 0.0 copy-done.2
  94.8 4.0 %collective-permute-start.5 = (bf16[4,8,16,640]{3,2,1,0:T(8,128)(2,1)S(1)}, bf16[4,8,16,640]{3,2,1,0:T(8,128)(2,1)}, u32[]{:S(2)}, u32[]{:S(2)}) collective-permute-start(bf16[4,8,16,640]{3,2,1,0:T(8,128)(2,1)S(1)} %pad_maximum_fusion.refs_3_), channel_id=1, source_target_pairs={{0,256},{128,384},{256,0},{384,128},{1,257},{129,385},{257,1},{385... | collective-permute-start | bytes 1966088 | tf_op jit(solution)/shard_map/ppermute | solution.py:20
  98.8 0.7 pad_add_fusion.1.refs_0_
  99.5 9.0 %collective-permute-done.3.refs_4_ = bf16[4,8,16,640]{3,2,1,0:T(8,128)(2,1)S(1)} collective-permute-done((bf16[4,8,16,640]{3,2,1,0:T(8,128)(2,1)S(1)}, bf16[4,8,16,640]{3,2,1,0:T(8,128)(2,1)S(1)}, u32[]{:S(2)}, u32[]{:S(2)}) %collective-permute-start.3) | collective-permute-done | bytes 655392 | tf_op jit(solution)/shard_map/ppermute | solution.py:20
  108.5 0.0 copy-start.3
  108.5 2.8 %collective-permute-done.4.refs_5_ = bf16[4,8,16,640]{3,2,1,0:T(8,128)(2,1)S(1)} collective-permute-done((bf16[4,8,16,640]{3,2,1,0:T(8,128)(2,1)S(1)}, bf16[4,8,16,640]{3,2,1,0:T(8,128)(2,1)S(1)}, u32[]{:S(2)}, u32[]{:S(2)}) %collective-permute-start.4) | collective-permute-done | bytes 655392 | tf_op jit(solution)/shard_map/ppermute | solution.py:20
  111.3 0.0 copy-done.3
  111.3 0.0 copy-start.4
  111.3 0.9 copy-done.4
  112.2 8.0 %collective-permute-done.5.refs_6_ = bf16[4,8,16,640]{3,2,1,0:T(8,128)(2,1)} collective-permute-done((bf16[4,8,16,640]{3,2,1,0:T(8,128)(2,1)S(1)}, bf16[4,8,16,640]{3,2,1,0:T(8,128)(2,1)}, u32[]{:S(2)}, u32[]{:S(2)}) %collective-permute-start.5) | collective-permute-done | bytes 655392 | tf_op jit(solution)/shard_map/ppermute | solution.py:20
  120.2 0.0 all-to-all-done.3.refs_2_
  120.2 0.0 copy-start.1
  120.2 0.0 all-gather.3.cloned.1.call-done
  120.2 1.5 copy-done.1
  121.7 7.3 %gram.3 = f32[320,640]{1,0:T(8,128)} custom-call(s32[3]{0:T(128)} %pad_add_fusion.1.refs_0_, bf16[16,640,256]{2,1,0:T(8,128)(2,1)} %bitcast.26, bf16[4,4,8,16,640]{4,3,2,1,0:T(8,128)(2,1)} %copy-done.1, bf16[4,8,16,640]{3,2,1,0:T(8,128)(2,1)} %copy-done.2, bf16[4,8,16,640]{3,2,1,0:T(8,128)(2,1)} %copy-done.3, bf16[4,8,16,640]{3,2,1,0:T(8,128)(2,1)} %copy-done.4, ...), custom_call_target="tpu_custom_call" | custom-call | flops 1677721600 | bytes 7864320 | tf_op jit(solution)/shard_map/gram/pallas_call | solution.py:103
  129.0 1.9 %collective-permute-start.6 = (f32[320,640]{1,0:T(8,128)}, f32[320,640]{1,0:T(8,128)S(1)}, u32[]{:S(2)}, u32[]{:S(2)}) collective-permute-start(f32[320,640]{1,0:T(8,128)} %gram.3), channel_id=1, source_target_pairs={{0,64},{64,0},{1,65},{65,1},{2,66},{66,2},{3,67},{67,3},{4,68},{68... | collective-permute-start | bytes 2457608 | tf_op jit(solution)/shard_map/ppermute | solution.py:173
  130.9 0.1 pad_add_fusion.refs_0_
  131.0 7.2 %gram.2.refs_1_ = f32[320,640]{1,0:T(8,128)} custom-call(s32[3]{0:T(128)} %pad_add_fusion.1.refs_0_, bf16[16,640,256]{2,1,0:T(8,128)(2,1)} %bitcast.27, bf16[4,4,8,16,640]{4,3,2,1,0:T(8,128)(2,1)} %copy-done.1, bf16[4,8,16,640]{3,2,1,0:T(8,128)(2,1)} %copy-done.2, bf16[4,8,16,640]{3,2,1,0:T(8,128)(2,1)} %copy-done.3, bf16[4,8,16,640]{3,2,1,0:T(8,128)(2,1)} %copy-done.4, ...), custom_call_target="tpu_custom_call" | custom-call | flops 1677721600 | bytes 7864320 | tf_op jit(solution)/shard_map/gram/pallas_call | solution.py:103
  138.3 0.0 collective-permute-done.6.refs_2_
  138.3 0.0 copy-start
  138.3 1.1 copy-done
  139.4 0.7 finish.1
  140.1 26.3 %all_to_all.27 = bf16[4,320,640]{2,1,0:T(8,128)(2,1)S(1)} all-to-all(bf16[4,320,640]{2,1,0:T(8,128)(2,1)S(1)} %finish.1), channel_id=1, replica_groups=mesh['x'=4,'core'=2,'col'=16,'layer'=4] {'layer'}, dimensions={0} | all-to-all | bytes 3276800 | tf_op jit(solution)/shard_map/all_to_all | solution.py:183
  166.5 1.2 copy.11
  (2 shorter events, 0.1 us)
Async XLA Ops:
  6.5 113.7 %all-gather.3.cloned.1.call-start = ((), (), s32[]{:S(2)}) async-start(), calls=%async_computation.5 | async-start | bytes 5570560 | tf_op jit(solution)/shard_map/all_gather | solution.py:159
  62.3 21.2 %all-to-all-start.2 = ((bf16[4,8,16,640]{3,2,1,0:T(8,128)(2,1)}), bf16[4,8,16,640]{3,2,1,0:T(8,128)(2,1)S(1)}, u32[]{:S(2)}, u32[]{:S(2)}) async-start(bf16[4,8,16,640]{3,2,1,0:T(8,128)(2,1)} %broadcast_in_dim.7), calls=%async_computation.2 | async-start | bytes 1310720 | tf_op jit(solution)/shard_map/all_to_all | solution.py:25
  68.4 9.3 %collective-permute-start.2 = (bf16[8,16,640]{2,1,0:T(8,128)(2,1)S(1)}, bf16[8,16,640]{2,1,0:T(8,128)(2,1)S(1)}, u32[]{:S(2)}, u32[]{:S(2)}) collective-permute-start(bf16[8,16,640]{2,1,0:T(8,128)(2,1)S(1)} %get-tuple-element.12), channel_id=1, source_target_pairs={{0,2},{1,3},{2,0},{3,1},{4,6},{5,7},{6,4},{7,5},{8,10},{9,11},{10,... | collective-permute-start | bytes 491528 | tf_op jit(solution)/shard_map/ppermute | solution.py:20
  71.0 7.2 %collective-permute-start.1 = (bf16[8,16,640]{2,1,0:T(8,128)(2,1)S(1)}, bf16[8,16,640]{2,1,0:T(8,128)(2,1)S(1)}, u32[]{:S(2)}, u32[]{:S(2)}) collective-permute-start(bf16[8,16,640]{2,1,0:T(8,128)(2,1)S(1)} %get-tuple-element.12), channel_id=1, source_target_pairs={{0,3},{1,0},{2,1},{3,2},{4,7},{5,4},{6,5},{7,6},{8,11},{9,8},{10,9... | collective-permute-start | bytes 491528 | tf_op jit(solution)/shard_map/ppermute | solution.py:20
  75.0 8.4 %collective-permute-start = (bf16[8,16,640]{2,1,0:T(8,128)(2,1)S(1)}, bf16[8,16,640]{2,1,0:T(8,128)(2,1)S(1)}, u32[]{:S(2)}, u32[]{:S(2)}) collective-permute-start(bf16[8,16,640]{2,1,0:T(8,128)(2,1)S(1)} %get-tuple-element.12), channel_id=1, source_target_pairs={{0,1},{1,2},{2,3},{3,0},{4,5},{5,6},{6,7},{7,4},{8,9},{9,10},{10,1... | collective-permute-start | bytes 491528 | tf_op jit(solution)/shard_map/ppermute | solution.py:20
  83.5 11.3 %copy-start.2 = (bf16[4,8,16,640]{3,2,1,0:T(8,128)(2,1)}, bf16[4,8,16,640]{3,2,1,0:T(8,128)(2,1)S(1)}, u32[]{:S(2)}) copy-start(bf16[4,8,16,640]{3,2,1,0:T(8,128)(2,1)S(1)} %pad_maximum_fusion.refs_3_) | copy-start | bytes 1966084
  85.3 34.9 %all-to-all-start.3 = ((bf16[4,4,8,16,640]{4,3,2,1,0:T(8,128)(2,1)}), bf16[4,4,8,16,640]{4,3,2,1,0:T(8,128)(2,1)S(1)}, u32[]{:S(2)}, u32[]{:S(2)}) async-start(bf16[4,4,8,16,640]{4,3,2,1,0:T(8,128)(2,1)} %broadcast_in_dim.8), calls=%async_computation.3 | async-start | bytes 5242880 | tf_op jit(solution)/shard_map/all_to_all | solution.py:25
  89.0 19.6 %collective-permute-start.3 = (bf16[4,8,16,640]{3,2,1,0:T(8,128)(2,1)S(1)}, bf16[4,8,16,640]{3,2,1,0:T(8,128)(2,1)S(1)}, u32[]{:S(2)}, u32[]{:S(2)}) collective-permute-start(bf16[4,8,16,640]{3,2,1,0:T(8,128)(2,1)S(1)} %pad_maximum_fusion.refs_3_), channel_id=1, source_target_pairs={{0,128},{128,256},{256,384},{384,0},{1,129},{129,257},{257,385},{3... | collective-permute-start | bytes 1966088 | tf_op jit(solution)/shard_map/ppermute | solution.py:20
  92.3 19.0 %collective-permute-start.4 = (bf16[4,8,16,640]{3,2,1,0:T(8,128)(2,1)S(1)}, bf16[4,8,16,640]{3,2,1,0:T(8,128)(2,1)S(1)}, u32[]{:S(2)}, u32[]{:S(2)}) collective-permute-start(bf16[4,8,16,640]{3,2,1,0:T(8,128)(2,1)S(1)} %pad_maximum_fusion.refs_3_), channel_id=1, source_target_pairs={{0,384},{128,0},{256,128},{384,256},{1,385},{129,1},{257,129},{385... | collective-permute-start | bytes 1966088 | tf_op jit(solution)/shard_map/ppermute | solution.py:20
  94.8 25.4 %collective-permute-start.5 = (bf16[4,8,16,640]{3,2,1,0:T(8,128)(2,1)S(1)}, bf16[4,8,16,640]{3,2,1,0:T(8,128)(2,1)}, u32[]{:S(2)}, u32[]{:S(2)}) collective-permute-start(bf16[4,8,16,640]{3,2,1,0:T(8,128)(2,1)S(1)} %pad_maximum_fusion.refs_3_), channel_id=1, source_target_pairs={{0,256},{128,384},{256,0},{384,128},{1,257},{129,385},{257,1},{385... | collective-permute-start | bytes 1966088 | tf_op jit(solution)/shard_map/ppermute | solution.py:20
  108.5 2.8 %copy-start.3 = (bf16[4,8,16,640]{3,2,1,0:T(8,128)(2,1)}, bf16[4,8,16,640]{3,2,1,0:T(8,128)(2,1)S(1)}, u32[]{:S(2)}) copy-start(bf16[4,8,16,640]{3,2,1,0:T(8,128)(2,1)S(1)} %collective-permute-done.3.refs_4_) | copy-start | bytes 1966084
  111.3 0.9 copy-start.4
  120.2 1.5 copy-start.1
  129.0 9.3 %collective-permute-start.6 = (f32[320,640]{1,0:T(8,128)}, f32[320,640]{1,0:T(8,128)S(1)}, u32[]{:S(2)}, u32[]{:S(2)}) collective-permute-start(f32[320,640]{1,0:T(8,128)} %gram.3), channel_id=1, source_target_pairs={{0,64},{64,0},{1,65},{65,1},{2,66},{66,2},{3,67},{67,3},{4,68},{68... | collective-permute-start | bytes 2457608 | tf_op jit(solution)/shard_map/ppermute | solution.py:173
  138.3 1.1 copy-start
Sparse Core Ops, SparseCore 0:
  25.3 90.7 all-gather.2

commit v5 on v3

--- a/solution.py
+++ b/solution.py
@@ -27,6 +27,34 @@
 
 SHIFTS = (0, 1, 3, 2)
 GROUP = 4
+
+
+def weigh_kernel(owned, nz, place_ref, pattern_ref, weight_ref, block_ref, by_col_ref, by_chip_ref):
+    lanes = 128
+    row = place_ref[0]
+    weight = weight_ref[...]
+    width = by_col_ref.shape[2]
+    count = width // lanes
+    chips, _, tile = by_chip_ref.shape
+    half = tile // 2
+    strips = []
+    for z in range(nz):
+        parts = []
+        for i in range(count):
+            j = z * count + i
+            flag = pattern_ref[row, j].astype(jnp.float32)
+            block = block_ref[:, j * lanes : (j + 1) * lanes].astype(jnp.float32)
+            parts.append((block * weight * flag).astype(jnp.bfloat16))
+        strip = jnp.concatenate(parts, 1)
+        by_col_ref[z] = strip
+        strips.append(strip)
+    for x in range(4):
+        for core in range(2):
+            pair = jnp.concatenate(strips[x * 4 + core * 2 : x * 4 + core * 2 + 2], 1)
+            for y in range(4):
+                by_chip_ref[x * 4 + y, :, core * half : (core + 1) * half] = pair[
+                    :, y * half : (y + 1) * half
+                ]
 
 
 def gram_kernel(half, steps, place_ref, rows_ref, by_y_ref, *refs):
@@ -87,7 +115,7 @@
 
 def finish_kernel(factor, place_ref, keep_ref, add_ref, out_ref):
     shape = keep_ref.shape
-    row_ids = place_ref[0] + lax.broadcasted_iota(jnp.int32, shape, 0)
+    row_ids = place_ref[0] + pl.program_id(0) * shape[0] + lax.broadcasted_iota(jnp.int32, shape, 0)
     col_ids = place_ref[1] + lax.broadcasted_iota(jnp.int32, shape, 1)
     total = (keep_ref[...] + add_ref[...]) * factor
     piece = jnp.where(row_ids == col_ids, jnp.float32(0.0), total).astype(jnp.bfloat16)
@@ -103,25 +131,25 @@
     z, y = lax.axis_index("col"), lax.axis_index("layer")
     factor = 1.0 / math.sqrt(owned * nx * nc * nz * ny)
     owner = lax.axis_index(("x", "core", "col", "layer"))
-    flags = lax.dynamic_slice_in_dim(pattern, owner * owned // 128, 1, 0)[0]
-    read_mask = jnp.repeat(flags.astype(jnp.float32), 128)
-    weighted = (
-        occurrences.astype(jnp.float32) * idf_weight[:, None] * read_mask[None, :]
-    ).astype(jnp.bfloat16)
-
     width = reads // nz
     half = reads // (nx * nc * ny)
     tile = nc * half
     chips = nx * ny
-    by_chip = (
-        weighted.reshape(owned, nx, nc, ny, half)
-        .transpose(1, 3, 0, 2, 4)
-        .reshape(chips, owned, tile)
-    )
+    block_row = jnp.reshape(owner * owned // 128, (1,)).astype(jnp.int32)
+    by_col, by_chip = pl.pallas_call(
+        lambda *refs: weigh_kernel(owned, nz, *refs),
+        out_shape=(
+            jax.ShapeDtypeStruct((nz, owned, width), jnp.bfloat16),
+            jax.ShapeDtypeStruct((chips, owned, tile), jnp.bfloat16),
+        ),
+        in_specs=[SMEM, SMEM, VMEM, VMEM],
+        out_specs=(VMEM, VMEM),
+        compiler_params=pltpu.CompilerParams(vmem_limit_bytes=8 << 20),
+        name="weigh",
+    )(block_row, pattern, idf_weight.reshape(owned, 1), occurrences)
     own = lax.all_to_all(by_chip, ("x", "layer"), split_axis=0, concat_axis=0, tiled=True)
     own = own.reshape(chips * owned, tile)
     rows = lax.all_gather(own, "col", axis=0, tiled=True).reshape(nz, chips, owned, tile)
-    by_col = weighted.reshape(owned, nz, width).transpose(1, 0, 2)
     by_col, own = lax.optimization_barrier((by_col, own))
     part = lax.all_to_all(by_col, "col", split_axis=0, concat_axis=0, tiled=True)
     upper, lower = part[: nz // 2], part[nz // 2 :]
@@ -151,9 +179,9 @@
             )
         ]
         * nx,
-        out_specs=(pl.BlockSpec((half, width), lambda k: (0, 0)),) * 2,
+        out_specs=(VMEM, VMEM),
         scratch_shapes=[pltpu.VMEM((tile, width), jnp.float32)],
-        compiler_params=pltpu.CompilerParams(vmem_limit_bytes=60 << 20),
+        compiler_params=pltpu.CompilerParams(vmem_limit_bytes=50 << 20),
         cost_estimate=pl.CostEstimate(
             flops=2 * tile * width * nz * chips * owned,
             bytes_accessed=2 * (tile + width) * nz * chips * owned,
@@ -163,12 +191,15 @@
     )(place, rows, by_y, *by_x)
     add = lax.ppermute(send, "core", [(0, 1), (1, 0)])
     corner = jnp.stack([((x * nc + c) * ny + y) * half, z * width]).astype(jnp.int32)
+    bands = 2
+    band = pl.BlockSpec((half // bands, width), lambda k: (k, 0))
     copies = pl.pallas_call(
         lambda *refs: finish_kernel(factor, *refs),
         out_shape=jax.ShapeDtypeStruct((ny, half, width), jnp.bfloat16),
-        in_specs=[SMEM, VMEM, VMEM],
-        out_specs=VMEM,
-        compiler_params=pltpu.CompilerParams(vmem_limit_bytes=8 << 20),
+        grid=(bands,),
+        in_specs=[SMEM, band, band],
+        out_specs=pl.BlockSpec((ny, half // bands, width), lambda k: (0, k, 0)),
+        compiler_params=pltpu.CompilerParams(vmem_limit_bytes=16 << 20),
         name="finish",
     )(corner, keep, add)
     out = lax.all_to_all(copies, "layer", split_axis=0, concat_axis=0, tiled=True)

time: 171 us -> 169 us (0.988)
  other arithmetic: 2.57 us -> 0.25 us
  local copies, waits for them, and re-layouts: 8.58 us -> 6.46 us
    convert_element_type x2 -> x0, other arithmetic: 1.82 us -> none  [the longest x1 1.12 us: body(): weighted = (occurrences.astype(jnp.float32) * idf_weight[:, None] * read_...]
    unnamed x11 -> x5, local copies, waits for them, and re-layouts: 4.65 us -> 2.89 us
where the time goes in v5:
time: 169 us; the launch traced here: 168 us
  blocking collectives  76.9 us (46%)
  starting transfers between devices  30.9 us (18%)
  waiting for transfers between devices  30.1 us (18%)
  between operations  13.5 us (8%)
  Pallas kernels  10.2 us (6%)
  local copies, waits for them, and re-layouts  6.46 us (4%)
    all_to_all x1, blocking collectives, body(): lax.all_to_all(by_col, 'col', split_axis=0, concat_axis=0, tiled=True)  36.2 us
    ppermute x6, waiting for transfers between devices, spread(): lax.ppermute(value, axis, around(n, s))  27.7 us
    all_to_all x1, blocking collectives, body(): lax.all_to_all(copies, 'layer', split_axis=0, concat_axis=0, tiled=True)  26 us
    ppermute x6, starting transfers between devices, spread(): lax.ppermute(value, axis, around(n, s))  18.4 us
    all_to_all x1, blocking collectives, body(): lax.all_to_all(by_chip, ('x', 'layer'), split_axis=0, concat_axis=0, tile...  14.7 us
    all_to_all x2, starting transfers between devices, collect(): return lax.all_to_all(copies, axis, split_axis=0, concat_axis=0, tiled=True)  10.6 us
    pallas_call x1, Pallas kernels, body(): pl.pallas_call(lambda *refs: gram_kernel(half, steps, *refs), out_shape=(...  8.03 us
  transfers between devices with their start and end apart: 10, of which 7 were waited for; matrix products, arithmetic and copies ran while one was open for 2% of the time, Pallas kernels for 0%

profile of v5, /device:TPU:34, one launch (start us, length us, event | category | flops | bytes accessed | tf_op | source)
XLA Modules:
  0.0 168.4 jit_solution(5274248938056897270)
XLA Ops:
  6.5 0.0 all-gather.2.cloned.1.call-start
  6.5 0.7 copy.4.refs_2_
  7.3 0.0 copy-start
  7.3 1.0 copy-done
  8.2 0.0 copy-start.1
  8.2 0.8 copy-done.1
  9.0 1.3 weigh.1
  10.3 14.7 %all_to_all.25 = bf16[16,16,640]{2,1,0:T(8,128)(2,1)} all-to-all(bf16[16,16,640]{2,1,0:T(8,128)(2,1)S(1)} %get-tuple-element.12), channel_id=1, replica_groups=mesh['x'=4,'core'=2,'col'=16,'layer'=4] {'x','layer'}, dimensions={0} | all-to-all | bytes 655360 | tf_op jit(solution)/shard_map/all_to_all | solution.py:150
  25.1 0.0 all-gather.2.cloned.1.call-update
  25.1 36.2 %all_to_all.26 = bf16[16,16,640]{2,1,0:T(8,128)(2,1)S(1)} all-to-all(bf16[16,16,640]{2,1,0:T(8,128)(2,1)S(1)} %get-tuple-element.14), channel_id=1, replica_groups=mesh['x'=4,'core'=2,'col'=16,'layer'=4] {'col'}, dimensions={0} | all-to-all | bytes 655360 | tf_op jit(solution)/shard_map/all_to_all | solution.py:154
  61.3 0.9 broadcast_in_dim.4
  62.2 6.0 %all-to-all-start.2 = ((bf16[4,8,16,640]{3,2,1,0:T(8,128)(2,1)}), bf16[4,8,16,640]{3,2,1,0:T(8,128)(2,1)S(1)}, u32[]{:S(2)}, u32[]{:S(2)}) async-start(bf16[4,8,16,640]{3,2,1,0:T(8,128)(2,1)} %broadcast_in_dim.4), calls=%async_computation.2 | async-start | bytes 1310720 | tf_op jit(solution)/shard_map/all_to_all | solution.py:25
  68.2 2.7 %collective-permute-start.2 = (bf16[8,16,640]{2,1,0:T(8,128)(2,1)S(1)}, bf16[8,16,640]{2,1,0:T(8,128)(2,1)S(1)}, u32[]{:S(2)}, u32[]{:S(2)}) collective-permute-start(bf16[8,16,640]{2,1,0:T(8,128)(2,1)S(1)} %get-tuple-element.20), channel_id=1, source_target_pairs={{0,2},{1,3},{2,0},{3,1},{4,6},{5,7},{6,4},{7,5},{8,10},{9,11},{10,... | collective-permute-start | bytes 491528 | tf_op jit(solution)/shard_map/ppermute | solution.py:20
  70.9 3.9 %collective-permute-start.1 = (bf16[8,16,640]{2,1,0:T(8,128)(2,1)S(1)}, bf16[8,16,640]{2,1,0:T(8,128)(2,1)S(1)}, u32[]{:S(2)}, u32[]{:S(2)}) collective-permute-start(bf16[8,16,640]{2,1,0:T(8,128)(2,1)S(1)} %get-tuple-element.20), channel_id=1, source_target_pairs={{0,3},{1,0},{2,1},{3,2},{4,7},{5,4},{6,5},{7,6},{8,11},{9,8},{10,9... | collective-permute-start | bytes 491528 | tf_op jit(solution)/shard_map/ppermute | solution.py:20
  74.8 2.0 %collective-permute-start = (bf16[8,16,640]{2,1,0:T(8,128)(2,1)S(1)}, bf16[8,16,640]{2,1,0:T(8,128)(2,1)S(1)}, u32[]{:S(2)}, u32[]{:S(2)}) collective-permute-start(bf16[8,16,640]{2,1,0:T(8,128)(2,1)S(1)} %get-tuple-element.20), channel_id=1, source_target_pairs={{0,1},{1,2},{2,3},{3,0},{4,5},{5,6},{6,7},{7,4},{8,9},{9,10},{10,1... | collective-permute-start | bytes 491528 | tf_op jit(solution)/shard_map/ppermute | solution.py:20
  76.8 0.9 collective-permute-done.2
  77.7 0.5 collective-permute-done.1
  78.2 5.1 %collective-permute-done = bf16[8,16,640]{2,1,0:T(8,128)(2,1)S(1)} collective-permute-done((bf16[8,16,640]{2,1,0:T(8,128)(2,1)S(1)}, bf16[8,16,640]{2,1,0:T(8,128)(2,1)S(1)}, u32[]{:S(2)}, u32[]{:S(2)}) %collective-permute-start) | collective-permute-done | bytes 163872 | tf_op jit(solution)/shard_map/ppermute | solution.py:20
  83.3 0.1 pad_maximum_fusion.refs_3_
  83.4 0.0 all-to-all-done.2
  83.4 1.9 %broadcast_in_dim.5 = bf16[4,4,8,16,640]{4,3,2,1,0:T(8,128)(2,1)} broadcast(bf16[4,8,16,640]{3,2,1,0:T(8,128)(2,1)S(1)} %all-to-all-done.2), dimensions={1,2,3,4} | broadcast | bytes 3276800 | tf_op jit(solution)/shard_map/broadcast_in_dim | solution.py:24
  85.3 4.6 %all-to-all-start.3 = ((bf16[4,4,8,16,640]{4,3,2,1,0:T(8,128)(2,1)}), bf16[4,4,8,16,640]{4,3,2,1,0:T(8,128)(2,1)}, u32[]{:S(2)}, u32[]{:S(2)}) async-start(bf16[4,4,8,16,640]{4,3,2,1,0:T(8,128)(2,1)} %broadcast_in_dim.5), calls=%async_computation.3 | async-start | bytes 5242880 | tf_op jit(solution)/shard_map/all_to_all | solution.py:25
  89.9 3.4 %collective-permute-start.3 = (bf16[4,8,16,640]{3,2,1,0:T(8,128)(2,1)S(1)}, bf16[4,8,16,640]{3,2,1,0:T(8,128)(2,1)S(1)}, u32[]{:S(2)}, u32[]{:S(2)}) collective-permute-start(bf16[4,8,16,640]{3,2,1,0:T(8,128)(2,1)S(1)} %pad_maximum_fusion.refs_3_), channel_id=1, source_target_pairs={{0,128},{128,256},{256,384},{384,0},{1,129},{129,257},{257,385},{3... | collective-permute-start | bytes 1966088 | tf_op jit(solution)/shard_map/ppermute | solution.py:20
  93.2 2.5 %collective-permute-start.4 = (bf16[4,8,16,640]{3,2,1,0:T(8,128)(2,1)S(1)}, bf16[4,8,16,640]{3,2,1,0:T(8,128)(2,1)S(1)}, u32[]{:S(2)}, u32[]{:S(2)}) collective-permute-start(bf16[4,8,16,640]{3,2,1,0:T(8,128)(2,1)S(1)} %pad_maximum_fusion.refs_3_), channel_id=1, source_target_pairs={{0,384},{128,0},{256,128},{384,256},{1,385},{129,1},{257,129},{385... | collective-permute-start | bytes 1966088 | tf_op jit(solution)/shard_map/ppermute | solution.py:20
  95.7 4.0 %collective-permute-start.5 = (bf16[4,8,16,640]{3,2,1,0:T(8,128)(2,1)S(1)}, bf16[4,8,16,640]{3,2,1,0:T(8,128)(2,1)S(1)}, u32[]{:S(2)}, u32[]{:S(2)}) collective-permute-start(bf16[4,8,16,640]{3,2,1,0:T(8,128)(2,1)S(1)} %pad_maximum_fusion.refs_3_), channel_id=1, source_target_pairs={{0,256},{128,384},{256,0},{384,128},{1,257},{129,385},{257,1},{385... | collective-permute-start | bytes 1966088 | tf_op jit(solution)/shard_map/ppermute | solution.py:20
  99.7 0.1 pad_add_fusion.1.refs_0_
  99.8 9.6 %collective-permute-done.3.refs_4_ = bf16[4,8,16,640]{3,2,1,0:T(8,128)(2,1)S(1)} collective-permute-done((bf16[4,8,16,640]{3,2,1,0:T(8,128)(2,1)S(1)}, bf16[4,8,16,640]{3,2,1,0:T(8,128)(2,1)S(1)}, u32[]{:S(2)}, u32[]{:S(2)}) %collective-permute-start.3) | collective-permute-done | bytes 655392 | tf_op jit(solution)/shard_map/ppermute | solution.py:20
  109.4 2.8 %collective-permute-done.4.refs_5_ = bf16[4,8,16,640]{3,2,1,0:T(8,128)(2,1)S(1)} collective-permute-done((bf16[4,8,16,640]{3,2,1,0:T(8,128)(2,1)S(1)}, bf16[4,8,16,640]{3,2,1,0:T(8,128)(2,1)S(1)}, u32[]{:S(2)}, u32[]{:S(2)}) %collective-permute-start.4) | collective-permute-done | bytes 655392 | tf_op jit(solution)/shard_map/ppermute | solution.py:20
  112.2 8.8 %collective-permute-done.5.refs_6_ = bf16[4,8,16,640]{3,2,1,0:T(8,128)(2,1)S(1)} collective-permute-done((bf16[4,8,16,640]{3,2,1,0:T(8,128)(2,1)S(1)}, bf16[4,8,16,640]{3,2,1,0:T(8,128)(2,1)S(1)}, u32[]{:S(2)}, u32[]{:S(2)}) %collective-permute-start.5) | collective-permute-done | bytes 655392 | tf_op jit(solution)/shard_map/ppermute | solution.py:20
  121.0 0.0 all-to-all-done.3.refs_2_
  121.0 0.0 all-gather.2.cloned.1.call-done
  121.0 8.0 %gram.1 = (f32[320,640]{1,0:T(8,128)S(1)}, f32[320,640]{1,0:T(8,128)}) custom-call(s32[3]{0:T(128)S(1)} %pad_add_fusion.1.refs_0_, bf16[16,16,16,640]{3,2,1,0:T(8,128)(2,1)} %bitcast.21, bf16[4,4,8,16,640]{4,3,2,1,0:T(8,128)(2,1)} %all-to-all-done.3.refs_2_, bf16[4,8,16,640]{3,2,1,0:T(8,128)(2,1)S(1)} %pad_maximum_fusion.refs_3_, ...), custom_call_target="tpu_custom_call" | custom-call | flops 3355443200 | bytes 10485760 | tf_op jit(solution)/shard_map/gram/pallas_call | solution.py:165
  129.1 1.9 %collective-permute-start.6 = (f32[320,640]{1,0:T(8,128)}, f32[320,640]{1,0:T(8,128)S(1)}, u32[]{:S(2)}, u32[]{:S(2)}) collective-permute-start(f32[320,640]{1,0:T(8,128)} %get-tuple-element.18), channel_id=1, source_target_pairs={{0,64},{64,0},{1,65},{65,1},{2,66},{66,2},{3,67},{67,3},{4,68},{68... | collective-permute-start | bytes 2457608 | tf_op jit(solution)/shard_map/ppermute | solution.py:192
  131.0 0.1 pad_add_fusion.refs_0_
  131.1 2.4 %collective-permute-done.6.refs_2_ = f32[320,640]{1,0:T(8,128)S(1)} collective-permute-done((f32[320,640]{1,0:T(8,128)}, f32[320,640]{1,0:T(8,128)S(1)}, u32[]{:S(2)}, u32[]{:S(2)}) %collective-permute-start.6) | collective-permute-done | bytes 819232 | tf_op jit(solution)/shard_map/ppermute | solution.py:192
  133.5 0.9 finish.1
  134.4 26.0 %all_to_all.27 = bf16[4,320,640]{2,1,0:T(8,128)(2,1)S(1)} all-to-all(bf16[4,320,640]{2,1,0:T(8,128)(2,1)S(1)} %finish.1), channel_id=1, replica_groups=mesh['x'=4,'core'=2,'col'=16,'layer'=4] {'layer'}, dimensions={0} | all-to-all | bytes 3276800 | tf_op jit(solution)/shard_map/all_to_all | solution.py:205
  160.4 1.2 copy.6
  (1 shorter events, 0.0 us)
Async XLA Ops:
  6.5 114.5 %all-gather.2.cloned.1.call-start = ((), (), s32[]{:S(2)}) async-start(), calls=%async_computation.5 | async-start | bytes 5570560 | tf_op jit(solution)/shard_map/all_gather | solution.py:152
  7.3 1.0 copy-start
  8.2 0.8 copy-start.1
  62.2 21.2 %all-to-all-start.2 = ((bf16[4,8,16,640]{3,2,1,0:T(8,128)(2,1)}), bf16[4,8,16,640]{3,2,1,0:T(8,128)(2,1)S(1)}, u32[]{:S(2)}, u32[]{:S(2)}) async-start(bf16[4,8,16,640]{3,2,1,0:T(8,128)(2,1)} %broadcast_in_dim.4), calls=%async_computation.2 | async-start | bytes 1310720 | tf_op jit(solution)/shard_map/all_to_all | solution.py:25
  68.2 9.4 %collective-permute-start.2 = (bf16[8,16,640]{2,1,0:T(8,128)(2,1)S(1)}, bf16[8,16,640]{2,1,0:T(8,128)(2,1)S(1)}, u32[]{:S(2)}, u32[]{:S(2)}) collective-permute-start(bf16[8,16,640]{2,1,0:T(8,128)(2,1)S(1)} %get-tuple-element.20), channel_id=1, source_target_pairs={{0,2},{1,3},{2,0},{3,1},{4,6},{5,7},{6,4},{7,5},{8,10},{9,11},{10,... | collective-permute-start | bytes 491528 | tf_op jit(solution)/shard_map/ppermute | solution.py:20
  70.9 7.2 %collective-permute-start.1 = (bf16[8,16,640]{2,1,0:T(8,128)(2,1)S(1)}, bf16[8,16,640]{2,1,0:T(8,128)(2,1)S(1)}, u32[]{:S(2)}, u32[]{:S(2)}) collective-permute-start(bf16[8,16,640]{2,1,0:T(8,128)(2,1)S(1)} %get-tuple-element.20), channel_id=1, source_target_pairs={{0,3},{1,0},{2,1},{3,2},{4,7},{5,4},{6,5},{7,6},{8,11},{9,8},{10,9... | collective-permute-start | bytes 491528 | tf_op jit(solution)/shard_map/ppermute | solution.py:20
  74.8 8.4 %collective-permute-start = (bf16[8,16,640]{2,1,0:T(8,128)(2,1)S(1)}, bf16[8,16,640]{2,1,0:T(8,128)(2,1)S(1)}, u32[]{:S(2)}, u32[]{:S(2)}) collective-permute-start(bf16[8,16,640]{2,1,0:T(8,128)(2,1)S(1)} %get-tuple-element.20), channel_id=1, source_target_pairs={{0,1},{1,2},{2,3},{3,0},{4,5},{5,6},{6,7},{7,4},{8,9},{9,10},{10,1... | collective-permute-start | bytes 491528 | tf_op jit(solution)/shard_map/ppermute | solution.py:20
  85.3 35.8 %all-to-all-start.3 = ((bf16[4,4,8,16,640]{4,3,2,1,0:T(8,128)(2,1)}), bf16[4,4,8,16,640]{4,3,2,1,0:T(8,128)(2,1)}, u32[]{:S(2)}, u32[]{:S(2)}) async-start(bf16[4,4,8,16,640]{4,3,2,1,0:T(8,128)(2,1)} %broadcast_in_dim.5), calls=%async_computation.3 | async-start | bytes 5242880 | tf_op jit(solution)/shard_map/all_to_all | solution.py:25
  89.9 19.6 %collective-permute-start.3 = (bf16[4,8,16,640]{3,2,1,0:T(8,128)(2,1)S(1)}, bf16[4,8,16,640]{3,2,1,0:T(8,128)(2,1)S(1)}, u32[]{:S(2)}, u32[]{:S(2)}) collective-permute-start(bf16[4,8,16,640]{3,2,1,0:T(8,128)(2,1)S(1)} %pad_maximum_fusion.refs_3_), channel_id=1, source_target_pairs={{0,128},{128,256},{256,384},{384,0},{1,129},{129,257},{257,385},{3... | collective-permute-start | bytes 1966088 | tf_op jit(solution)/shard_map/ppermute | solution.py:20
  93.2 19.0 %collective-permute-start.4 = (bf16[4,8,16,640]{3,2,1,0:T(8,128)(2,1)S(1)}, bf16[4,8,16,640]{3,2,1,0:T(8,128)(2,1)S(1)}, u32[]{:S(2)}, u32[]{:S(2)}) collective-permute-start(bf16[4,8,16,640]{3,2,1,0:T(8,128)(2,1)S(1)} %pad_maximum_fusion.refs_3_), channel_id=1, source_target_pairs={{0,384},{128,0},{256,128},{384,256},{1,385},{129,1},{257,129},{385... | collective-permute-start | bytes 1966088 | tf_op jit(solution)/shard_map/ppermute | solution.py:20
  95.7 25.3 %collective-permute-start.5 = (bf16[4,8,16,640]{3,2,1,0:T(8,128)(2,1)S(1)}, bf16[4,8,16,640]{3,2,1,0:T(8,128)(2,1)S(1)}, u32[]{:S(2)}, u32[]{:S(2)}) collective-permute-start(bf16[4,8,16,640]{3,2,1,0:T(8,128)(2,1)S(1)} %pad_maximum_fusion.refs_3_), channel_id=1, source_target_pairs={{0,256},{128,384},{256,0},{384,128},{1,257},{129,385},{257,1},{385... | collective-permute-start | bytes 1966088 | tf_op jit(solution)/shard_map/ppermute | solution.py:20
  129.1 4.4 %collective-permute-start.6 = (f32[320,640]{1,0:T(8,128)}, f32[320,640]{1,0:T(8,128)S(1)}, u32[]{:S(2)}, u32[]{:S(2)}) collective-permute-start(f32[320,640]{1,0:T(8,128)} %get-tuple-element.18), channel_id=1, source_target_pairs={{0,64},{64,0},{1,65},{65,1},{2,66},{66,2},{3,67},{67,3},{4,68},{68... | collective-permute-start | bytes 2457608 | tf_op jit(solution)/shard_map/ppermute | solution.py:192
Sparse Core Ops, SparseCore 0:
  25.2 90.7 all-gather.1

commit v6 on v5

--- a/solution.py
+++ b/solution.py
@@ -32,7 +32,11 @@
 def weigh_kernel(owned, nz, place_ref, pattern_ref, weight_ref, block_ref, by_col_ref, by_chip_ref):
     lanes = 128
     row = place_ref[0]
-    weight = weight_ref[...]
+    diagonal = lax.broadcasted_iota(jnp.int32, (owned, owned), 0) == lax.broadcasted_iota(
+        jnp.int32, (owned, owned), 1
+    )
+    spread_weight = jnp.broadcast_to(weight_ref[...], (owned, owned))
+    weight = jnp.sum(jnp.where(diagonal, spread_weight, 0.0), axis=1, keepdims=True)
     width = by_col_ref.shape[2]
     count = width // lanes
     chips, _, tile = by_chip_ref.shape
@@ -118,9 +122,58 @@
     row_ids = place_ref[0] + pl.program_id(0) * shape[0] + lax.broadcasted_iota(jnp.int32, shape, 0)
     col_ids = place_ref[1] + lax.broadcasted_iota(jnp.int32, shape, 1)
     total = (keep_ref[...] + add_ref[...]) * factor
-    piece = jnp.where(row_ids == col_ids, jnp.float32(0.0), total).astype(jnp.bfloat16)
-    for i in range(out_ref.shape[0]):
-        out_ref[i] = piece
+    out_ref[...] = jnp.where(row_ids == col_ids, jnp.float32(0.0), total).astype(jnp.bfloat16)
+
+
+def place_kernel(order_ref, *refs):
+    *piece_refs, out_ref = refs
+    k = pl.program_id(0)
+    for i, piece_ref in enumerate(piece_refs):
+
+        @pl.when(k == i)
+        def _():
+            out_ref[0] = piece_ref[...]
+
+
+def last_kernel(order_ref, held_ref, piece_ref, out_ref):
+    out_ref[0] = piece_ref[...]
+
+
+def assemble(order, pieces, last):
+    rows, width = last.shape
+    shape = jax.ShapeDtypeStruct((len(pieces) + 1, rows, width), last.dtype)
+
+    def block(shift):
+        return pl.BlockSpec((1, rows, width), lambda k, order_ref: (order_ref[k + shift], 0, 0))
+
+    held = pl.pallas_call(
+        place_kernel,
+        out_shape=shape,
+        grid_spec=pltpu.PrefetchScalarGridSpec(
+            num_scalar_prefetch=1,
+            grid=(len(pieces),),
+            in_specs=[pl.BlockSpec((rows, width), lambda k, order_ref: (0, 0))] * len(pieces),
+            out_specs=block(0),
+        ),
+        compiler_params=pltpu.CompilerParams(vmem_limit_bytes=16 << 20),
+        name="place",
+    )(order, *pieces)
+    return pl.pallas_call(
+        last_kernel,
+        out_shape=shape,
+        grid_spec=pltpu.PrefetchScalarGridSpec(
+            num_scalar_prefetch=1,
+            grid=(1,),
+            in_specs=[
+                pl.BlockSpec(memory_space=pl.ANY),
+                pl.BlockSpec((rows, width), lambda k, order_ref: (0, 0)),
+            ],
+            out_specs=block(len(pieces)),
+        ),
+        input_output_aliases={1: 0},
+        compiler_params=pltpu.CompilerParams(vmem_limit_bytes=16 << 20),
+        name="last",
+    )(order, held, last)
 
 
 def body(occurrences, idf_weight, pattern):
@@ -144,9 +197,9 @@
         ),
         in_specs=[SMEM, SMEM, VMEM, VMEM],
         out_specs=(VMEM, VMEM),
-        compiler_params=pltpu.CompilerParams(vmem_limit_bytes=8 << 20),
+        compiler_params=pltpu.CompilerParams(vmem_limit_bytes=58 << 20),
         name="weigh",
-    )(block_row, pattern, idf_weight.reshape(owned, 1), occurrences)
+    )(block_row, pattern, idf_weight.reshape(1, owned), occurrences)
     own = lax.all_to_all(by_chip, ("x", "layer"), split_axis=0, concat_axis=0, tiled=True)
     own = own.reshape(chips * owned, tile)
     rows = lax.all_gather(own, "col", axis=0, tiled=True).reshape(nz, chips, owned, tile)
@@ -193,16 +246,24 @@
     corner = jnp.stack([((x * nc + c) * ny + y) * half, z * width]).astype(jnp.int32)
     bands = 2
     band = pl.BlockSpec((half // bands, width), lambda k: (k, 0))
-    copies = pl.pallas_call(
+    piece = pl.pallas_call(
         lambda *refs: finish_kernel(factor, *refs),
-        out_shape=jax.ShapeDtypeStruct((ny, half, width), jnp.bfloat16),
+        out_shape=jax.ShapeDtypeStruct((half, width), jnp.bfloat16),
         grid=(bands,),
         in_specs=[SMEM, band, band],
-        out_specs=pl.BlockSpec((ny, half // bands, width), lambda k: (0, k, 0)),
+        out_specs=band,
         compiler_params=pltpu.CompilerParams(vmem_limit_bytes=16 << 20),
         name="finish",
     )(corner, keep, add)
-    out = lax.all_to_all(copies, "layer", split_axis=0, concat_axis=0, tiled=True)
+    up = around(ny, 1)
+    down = around(ny, ny - 1)
+    ways = [up + [(ny + i, ny + j) for i, j in down], down + [(ny + i, ny + j) for i, j in up]]
+    ahead = lax.ppermute(piece, ("core", "layer"), ways[0])
+    behind = lax.ppermute(piece, ("core", "layer"), ways[1])
+    across = lax.ppermute(ahead, ("core", "layer"), ways[0])
+    way = 1 - 2 * c
+    order = jnp.stack([y, (y - way + ny) % ny, (y + way + ny) % ny, (y + 2) % ny])
+    out = assemble(order.astype(jnp.int32), [piece, ahead, behind], across)
     return out.reshape(ny * half, width)
 
 

time: 169 us -> 167 us (0.988)
  blocking collectives: 76.9 us -> 51.6 us
  starting transfers between devices: 30.9 us -> 41.5 us
  waiting for transfers between devices: 30.1 us -> 40.1 us
  Pallas kernels: 10.2 us -> 14.4 us
  local copies, waits for them, and re-layouts: 6.46 us -> 4.75 us
    all_to_all x1 -> x0, blocking collectives: 26 us -> none  [body(): lax.all_to_all(copies, 'layer', split_axis=0, concat_axis=0, tiled=True)]
    ppermute x0 -> x3, starting transfers between devices: none -> 10.8 us  [the longest x1 3.77 us: body(): across = lax.ppermute(ahead, ('core', 'layer'), ways[0])]
    ppermute x0 -> x3, waiting for transfers between devices: none -> 10.1 us  [the longest x1 5.48 us: body(): across = lax.ppermute(ahead, ('core', 'layer'), ways[0])]
    pallas_call x0 -> x2, Pallas kernels: none -> 3.47 us  [the longest x1 2.15 us: assemble(): pl.pallas_call(place_kernel, out_shape=shape, grid_spec=pltpu.PrefetchSca...]
  transfers between devices with their start and end apart: 10 -> 13, of which waited for: 7 -> 9; matrix products, arithmetic and copies ran while one was open for 2% -> 2% of each run, Pallas kernels for 0% -> 1%
where the time goes in v6:
time: 167 us; the launch traced here: 166 us
  blocking collectives  51.6 us (31%)
  starting transfers between devices  41.5 us (25%)
  waiting for transfers between devices  40.1 us (24%)
  Pallas kernels  14.4 us (9%)
  between operations  13.6 us (8%)
  local copies, waits for them, and re-layouts  4.75 us (3%)
    all_to_all x1, blocking collectives, body(): lax.all_to_all(by_col, 'col', split_axis=0, concat_axis=0, tiled=True)  36.6 us
    ppermute x6, waiting for transfers between devices, spread(): lax.ppermute(value, axis, around(n, s))  27.6 us
    ppermute x6, starting transfers between devices, spread(): lax.ppermute(value, axis, around(n, s))  17.9 us
    all_to_all x1, blocking collectives, body(): lax.all_to_all(by_chip, ('x', 'layer'), split_axis=0, concat_axis=0, tile...  14.9 us
    all_to_all x2, starting transfers between devices, collect(): return lax.all_to_all(copies, axis, split_axis=0, concat_axis=0, tiled=True)  10.9 us
    pallas_call x1, Pallas kernels, body(): pl.pallas_call(lambda *refs: gram_kernel(half, steps, *refs), out_shape=(...  8.01 us
    ppermute x1, waiting for transfers between devices, body(): across = lax.ppermute(ahead, ('core', 'layer'), ways[0])  5.48 us
    ppermute x1, waiting for transfers between devices, body(): ahead = lax.ppermute(piece, ('core', 'layer'), ways[0])  4.62 us
  transfers between devices with their start and end apart: 13, of which 9 were waited for; matrix products, arithmetic and copies ran while one was open for 2% of the time, Pallas kernels for 1%

profile of v6, /device:TPU:34, one launch (start us, length us, event | category | flops | bytes accessed | tf_op | source)
XLA Modules:
  0.0 166.2 jit_solution(10840294984406695820)
XLA Ops:
  6.5 0.0 all-gather.2.cloned.1.call-start
  6.5 2.2 %weigh.1 = (bf16[16,16,640]{2,1,0:T(8,128)(2,1)}, bf16[16,16,640]{2,1,0:T(8,128)(2,1)}) custom-call(s32[1]{0:T(128)} %bitcast.8.refs_0_, s32[64,80]{1,0:T(8,128)} %refs_1_.1, f32[1,16]{1,0:T(1,128)} %bitcast.22, bf16[16,10240]{1,0:T(8,128)(2,1)} %refs_3_.1), custom_call_target="tpu_custom_call" | custom-call | tf_op jit(solution)/shard_map/weigh/pallas_call | solution.py:192
  8.8 14.9 %all_to_all.20 = bf16[16,16,640]{2,1,0:T(8,128)(2,1)} all-to-all(bf16[16,16,640]{2,1,0:T(8,128)(2,1)} %get-tuple-element.12), channel_id=1, replica_groups=mesh['x'=4,'core'=2,'col'=16,'layer'=4] {'x','layer'}, dimensions={0} | all-to-all | bytes 655360 | tf_op jit(solution)/shard_map/all_to_all | solution.py:203
  23.7 0.0 all-gather.2.cloned.1.call-update
  23.7 36.6 %all_to_all.21 = bf16[16,16,640]{2,1,0:T(8,128)(2,1)S(1)} all-to-all(bf16[16,16,640]{2,1,0:T(8,128)(2,1)} %get-tuple-element.14), channel_id=1, replica_groups=mesh['x'=4,'core'=2,'col'=16,'layer'=4] {'col'}, dimensions={0} | all-to-all | bytes 655360 | tf_op jit(solution)/shard_map/all_to_all | solution.py:207
  60.4 0.9 broadcast_in_dim.4
  61.3 6.3 %all-to-all-start.2 = ((bf16[4,8,16,640]{3,2,1,0:T(8,128)(2,1)}), bf16[4,8,16,640]{3,2,1,0:T(8,128)(2,1)S(1)}, u32[]{:S(2)}, u32[]{:S(2)}) async-start(bf16[4,8,16,640]{3,2,1,0:T(8,128)(2,1)} %broadcast_in_dim.4), calls=%async_computation.2 | async-start | bytes 1310720 | tf_op jit(solution)/shard_map/all_to_all | solution.py:25
  67.6 2.2 %collective-permute-start.2 = (bf16[8,16,640]{2,1,0:T(8,128)(2,1)S(1)}, bf16[8,16,640]{2,1,0:T(8,128)(2,1)S(1)}, u32[]{:S(2)}, u32[]{:S(2)}) collective-permute-start(bf16[8,16,640]{2,1,0:T(8,128)(2,1)S(1)} %get-tuple-element.20), channel_id=1, source_target_pairs={{0,2},{1,3},{2,0},{3,1},{4,6},{5,7},{6,4},{7,5},{8,10},{9,11},{10,... | collective-permute-start | bytes 491528 | tf_op jit(solution)/shard_map/ppermute | solution.py:20
  69.8 3.9 %collective-permute-start.1 = (bf16[8,16,640]{2,1,0:T(8,128)(2,1)S(1)}, bf16[8,16,640]{2,1,0:T(8,128)(2,1)S(1)}, u32[]{:S(2)}, u32[]{:S(2)}) collective-permute-start(bf16[8,16,640]{2,1,0:T(8,128)(2,1)S(1)} %get-tuple-element.20), channel_id=1, source_target_pairs={{0,3},{1,0},{2,1},{3,2},{4,7},{5,4},{6,5},{7,6},{8,11},{9,8},{10,9... | collective-permute-start | bytes 491528 | tf_op jit(solution)/shard_map/ppermute | solution.py:20
  73.7 1.9 %collective-permute-start = (bf16[8,16,640]{2,1,0:T(8,128)(2,1)S(1)}, bf16[8,16,640]{2,1,0:T(8,128)(2,1)S(1)}, u32[]{:S(2)}, u32[]{:S(2)}) collective-permute-start(bf16[8,16,640]{2,1,0:T(8,128)(2,1)S(1)} %get-tuple-element.20), channel_id=1, source_target_pairs={{0,1},{1,2},{2,3},{3,0},{4,5},{5,6},{6,7},{7,4},{8,9},{9,10},{10,1... | collective-permute-start | bytes 491528 | tf_op jit(solution)/shard_map/ppermute | solution.py:20
  75.6 0.8 collective-permute-done.2
  76.5 0.5 collective-permute-done.1
  77.0 5.1 %collective-permute-done = bf16[8,16,640]{2,1,0:T(8,128)(2,1)S(1)} collective-permute-done((bf16[8,16,640]{2,1,0:T(8,128)(2,1)S(1)}, bf16[8,16,640]{2,1,0:T(8,128)(2,1)S(1)}, u32[]{:S(2)}, u32[]{:S(2)}) %collective-permute-start) | collective-permute-done | bytes 163872 | tf_op jit(solution)/shard_map/ppermute | solution.py:20
  82.1 0.1 pad_maximum_fusion.refs_3_
  82.2 0.0 all-to-all-done.2
  82.2 1.9 %broadcast_in_dim.5 = bf16[4,4,8,16,640]{4,3,2,1,0:T(8,128)(2,1)} broadcast(bf16[4,8,16,640]{3,2,1,0:T(8,128)(2,1)S(1)} %all-to-all-done.2), dimensions={1,2,3,4} | broadcast | bytes 3276800 | tf_op jit(solution)/shard_map/broadcast_in_dim | solution.py:24
  84.2 4.6 %all-to-all-start.3 = ((bf16[4,4,8,16,640]{4,3,2,1,0:T(8,128)(2,1)}), bf16[4,4,8,16,640]{4,3,2,1,0:T(8,128)(2,1)}, u32[]{:S(2)}, u32[]{:S(2)}) async-start(bf16[4,4,8,16,640]{4,3,2,1,0:T(8,128)(2,1)} %broadcast_in_dim.5), calls=%async_computation.3 | async-start | bytes 5242880 | tf_op jit(solution)/shard_map/all_to_all | solution.py:25
  88.7 3.4 %collective-permute-start.3 = (bf16[4,8,16,640]{3,2,1,0:T(8,128)(2,1)S(1)}, bf16[4,8,16,640]{3,2,1,0:T(8,128)(2,1)S(1)}, u32[]{:S(2)}, u32[]{:S(2)}) collective-permute-start(bf16[4,8,16,640]{3,2,1,0:T(8,128)(2,1)S(1)} %pad_maximum_fusion.refs_3_), channel_id=1, source_target_pairs={{0,128},{128,256},{256,384},{384,0},{1,129},{129,257},{257,385},{3... | collective-permute-start | bytes 1966088 | tf_op jit(solution)/shard_map/ppermute | solution.py:20
  92.1 2.5 %collective-permute-start.4 = (bf16[4,8,16,640]{3,2,1,0:T(8,128)(2,1)S(1)}, bf16[4,8,16,640]{3,2,1,0:T(8,128)(2,1)S(1)}, u32[]{:S(2)}, u32[]{:S(2)}) collective-permute-start(bf16[4,8,16,640]{3,2,1,0:T(8,128)(2,1)S(1)} %pad_maximum_fusion.refs_3_), channel_id=1, source_target_pairs={{0,384},{128,0},{256,128},{384,256},{1,385},{129,1},{257,129},{385... | collective-permute-start | bytes 1966088 | tf_op jit(solution)/shard_map/ppermute | solution.py:20
  94.6 4.0 %collective-permute-start.5 = (bf16[4,8,16,640]{3,2,1,0:T(8,128)(2,1)S(1)}, bf16[4,8,16,640]{3,2,1,0:T(8,128)(2,1)S(1)}, u32[]{:S(2)}, u32[]{:S(2)}) collective-permute-start(bf16[4,8,16,640]{3,2,1,0:T(8,128)(2,1)S(1)} %pad_maximum_fusion.refs_3_), channel_id=1, source_target_pairs={{0,256},{128,384},{256,0},{384,128},{1,257},{129,385},{257,1},{385... | collective-permute-start | bytes 1966088 | tf_op jit(solution)/shard_map/ppermute | solution.py:20
  98.6 0.1 pad_add_fusion.2.refs_0_
  98.7 9.6 %collective-permute-done.3.refs_4_ = bf16[4,8,16,640]{3,2,1,0:T(8,128)(2,1)S(1)} collective-permute-done((bf16[4,8,16,640]{3,2,1,0:T(8,128)(2,1)S(1)}, bf16[4,8,16,640]{3,2,1,0:T(8,128)(2,1)S(1)}, u32[]{:S(2)}, u32[]{:S(2)}) %collective-permute-start.3) | collective-permute-done | bytes 655392 | tf_op jit(solution)/shard_map/ppermute | solution.py:20
  108.3 2.8 %collective-permute-done.4.refs_5_ = bf16[4,8,16,640]{3,2,1,0:T(8,128)(2,1)S(1)} collective-permute-done((bf16[4,8,16,640]{3,2,1,0:T(8,128)(2,1)S(1)}, bf16[4,8,16,640]{3,2,1,0:T(8,128)(2,1)S(1)}, u32[]{:S(2)}, u32[]{:S(2)}) %collective-permute-start.4) | collective-permute-done | bytes 655392 | tf_op jit(solution)/shard_map/ppermute | solution.py:20
  111.1 8.7 %collective-permute-done.5.refs_6_ = bf16[4,8,16,640]{3,2,1,0:T(8,128)(2,1)S(1)} collective-permute-done((bf16[4,8,16,640]{3,2,1,0:T(8,128)(2,1)S(1)}, bf16[4,8,16,640]{3,2,1,0:T(8,128)(2,1)S(1)}, u32[]{:S(2)}, u32[]{:S(2)}) %collective-permute-start.5) | collective-permute-done | bytes 655392 | tf_op jit(solution)/shard_map/ppermute | solution.py:20
  119.8 0.0 copy-start
  119.8 0.8 copy-done
  120.6 0.0 all-to-all-done.3.refs_2_
  120.6 0.0 all-gather.2.cloned.1.call-done
  120.6 0.0 copy-start.1
  120.6 1.1 copy-done.1
  121.7 8.0 %gram.1 = (f32[320,640]{1,0:T(8,128)S(1)}, f32[320,640]{1,0:T(8,128)}) custom-call(s32[3]{0:T(128)S(1)} %pad_add_fusion.2.refs_0_, bf16[16,16,16,640]{3,2,1,0:T(8,128)(2,1)} %bitcast.23, bf16[4,4,8,16,640]{4,3,2,1,0:T(8,128)(2,1)} %all-to-all-done.3.refs_2_, bf16[4,8,16,640]{3,2,1,0:T(8,128)(2,1)S(1)} %pad_maximum_fusion.refs_3_, ...), custom_call_target="tpu_custom_call" | custom-call | flops 3355443200 | bytes 10485760 | tf_op jit(solution)/shard_map/gram/pallas_call | solution.py:218
  129.7 1.9 %collective-permute-start.6 = (f32[320,640]{1,0:T(8,128)}, f32[320,640]{1,0:T(8,128)S(1)}, u32[]{:S(2)}, u32[]{:S(2)}) collective-permute-start(f32[320,640]{1,0:T(8,128)} %get-tuple-element.18), channel_id=1, source_target_pairs={{0,64},{64,0},{1,65},{65,1},{2,66},{66,2},{3,67},{67,3},{4,68},{68... | collective-permute-start | bytes 2457608 | tf_op jit(solution)/shard_map/ppermute | solution.py:245
  131.6 0.1 pad_add_fusion.1.refs_0_
  131.7 2.4 %collective-permute-done.6.refs_2_ = f32[320,640]{1,0:T(8,128)S(1)} collective-permute-done((f32[320,640]{1,0:T(8,128)}, f32[320,640]{1,0:T(8,128)S(1)}, u32[]{:S(2)}, u32[]{:S(2)}) %collective-permute-start.6) | collective-permute-done | bytes 819232 | tf_op jit(solution)/shard_map/ppermute | solution.py:245
  134.1 0.7 finish.1.refs_0_
  134.9 3.6 %collective-permute-start.7 = (bf16[320,640]{1,0:T(8,128)(2,1)S(1)}, bf16[320,640]{1,0:T(8,128)(2,1)S(1)}, u32[]{:S(2)}, u32[]{:S(2)}) collective-permute-start(bf16[320,640]{1,0:T(8,128)(2,1)S(1)} %finish.1.refs_0_), channel_id=1, source_target_pairs={{0,1},{1,2},{2,3},{3,0},{64,67},{65,64},{66,65},{67,66},{4,5},{5,6... | collective-permute-start | bytes 1228808 | tf_op jit(solution)/shard_map/ppermute | solution.py:261
  138.5 3.5 %collective-permute-start.8 = (bf16[320,640]{1,0:T(8,128)(2,1)S(1)}, bf16[320,640]{1,0:T(8,128)(2,1)S(1)}, u32[]{:S(2)}, u32[]{:S(2)}) collective-permute-start(bf16[320,640]{1,0:T(8,128)(2,1)S(1)} %finish.1.refs_0_), channel_id=1, source_target_pairs={{0,3},{1,0},{2,1},{3,2},{64,65},{65,66},{66,67},{67,64},{4,7},{5,4... | collective-permute-start | bytes 1228808 | tf_op jit(solution)/shard_map/ppermute | solution.py:262
  141.9 4.6 %collective-permute-done.7.refs_1_ = bf16[320,640]{1,0:T(8,128)(2,1)S(1)} collective-permute-done((bf16[320,640]{1,0:T(8,128)(2,1)S(1)}, bf16[320,640]{1,0:T(8,128)(2,1)S(1)}, u32[]{:S(2)}, u32[]{:S(2)}) %collective-permute-start.7) | collective-permute-done | bytes 409632 | tf_op jit(solution)/shard_map/ppermute | solution.py:261
  146.5 3.8 %collective-permute-start.9 = (bf16[320,640]{1,0:T(8,128)(2,1)S(1)}, bf16[320,640]{1,0:T(8,128)(2,1)S(1)}, u32[]{:S(2)}, u32[]{:S(2)}) collective-permute-start(bf16[320,640]{1,0:T(8,128)(2,1)S(1)} %collective-permute-done.7.refs_1_), channel_id=1, source_target_pairs={{0,1},{1,2},{2,3},{3,0},{64,67},{65,64},{66,65},{67,66},{4,5},{5,6... | collective-permute-start | bytes 1228808 | tf_op jit(solution)/shard_map/ppermute | solution.py:263
  150.4 0.1 pad_add_fusion.order_ref
  150.4 0.0 collective-permute-done.8.refs_2_
  150.4 2.1 %place.1.held_ref = bf16[4,320,640]{2,1,0:T(8,128)(2,1)} custom-call(s32[4]{0:T(128)S(1)} %pad_add_fusion.order_ref, bf16[320,640]{1,0:T(8,128)(2,1)S(1)} %finish.1.refs_0_, bf16[320,640]{1,0:T(8,128)(2,1)S(1)} %collective-permute-done.7.refs_1_, bf16[320,640]{1,0:T(8,128)(2,1)S(1)} %collective-permute-done.8.refs_2_), custom_call_target="tpu_custom_call" | custom-call | tf_op jit(solution)/shard_map/place/pallas_call | solution.py:149
  152.6 5.5 %collective-permute-done.9.piece_ref = bf16[320,640]{1,0:T(8,128)(2,1)S(1)} collective-permute-done((bf16[320,640]{1,0:T(8,128)(2,1)S(1)}, bf16[320,640]{1,0:T(8,128)(2,1)S(1)}, u32[]{:S(2)}, u32[]{:S(2)}) %collective-permute-start.9) | collective-permute-done | bytes 409632 | tf_op jit(solution)/shard_map/ppermute | solution.py:263
  158.1 1.3 last.1
  (1 shorter events, 0.0 us)
Async XLA Ops:
  6.5 114.1 %all-gather.2.cloned.1.call-start = ((), (), s32[]{:S(2)}) async-start(), calls=%async_computation.4 | async-start | bytes 5570560 | tf_op jit(solution)/shard_map/all_gather | solution.py:205
  61.3 21.0 %all-to-all-start.2 = ((bf16[4,8,16,640]{3,2,1,0:T(8,128)(2,1)}), bf16[4,8,16,640]{3,2,1,0:T(8,128)(2,1)S(1)}, u32[]{:S(2)}, u32[]{:S(2)}) async-start(bf16[4,8,16,640]{3,2,1,0:T(8,128)(2,1)} %broadcast_in_dim.4), calls=%async_computation.2 | async-start | bytes 1310720 | tf_op jit(solution)/shard_map/all_to_all | solution.py:25
  67.6 8.9 %collective-permute-start.2 = (bf16[8,16,640]{2,1,0:T(8,128)(2,1)S(1)}, bf16[8,16,640]{2,1,0:T(8,128)(2,1)S(1)}, u32[]{:S(2)}, u32[]{:S(2)}) collective-permute-start(bf16[8,16,640]{2,1,0:T(8,128)(2,1)S(1)} %get-tuple-element.20), channel_id=1, source_target_pairs={{0,2},{1,3},{2,0},{3,1},{4,6},{5,7},{6,4},{7,5},{8,10},{9,11},{10,... | collective-permute-start | bytes 491528 | tf_op jit(solution)/shard_map/ppermute | solution.py:20
  69.8 7.2 %collective-permute-start.1 = (bf16[8,16,640]{2,1,0:T(8,128)(2,1)S(1)}, bf16[8,16,640]{2,1,0:T(8,128)(2,1)S(1)}, u32[]{:S(2)}, u32[]{:S(2)}) collective-permute-start(bf16[8,16,640]{2,1,0:T(8,128)(2,1)S(1)} %get-tuple-element.20), channel_id=1, source_target_pairs={{0,3},{1,0},{2,1},{3,2},{4,7},{5,4},{6,5},{7,6},{8,11},{9,8},{10,9... | collective-permute-start | bytes 491528 | tf_op jit(solution)/shard_map/ppermute | solution.py:20
  73.7 8.4 %collective-permute-start = (bf16[8,16,640]{2,1,0:T(8,128)(2,1)S(1)}, bf16[8,16,640]{2,1,0:T(8,128)(2,1)S(1)}, u32[]{:S(2)}, u32[]{:S(2)}) collective-permute-start(bf16[8,16,640]{2,1,0:T(8,128)(2,1)S(1)} %get-tuple-element.20), channel_id=1, source_target_pairs={{0,1},{1,2},{2,3},{3,0},{4,5},{5,6},{6,7},{7,4},{8,9},{9,10},{10,1... | collective-permute-start | bytes 491528 | tf_op jit(solution)/shard_map/ppermute | solution.py:20
  84.2 36.5 %all-to-all-start.3 = ((bf16[4,4,8,16,640]{4,3,2,1,0:T(8,128)(2,1)}), bf16[4,4,8,16,640]{4,3,2,1,0:T(8,128)(2,1)}, u32[]{:S(2)}, u32[]{:S(2)}) async-start(bf16[4,4,8,16,640]{4,3,2,1,0:T(8,128)(2,1)} %broadcast_in_dim.5), calls=%async_computation.3 | async-start | bytes 5242880 | tf_op jit(solution)/shard_map/all_to_all | solution.py:25
  88.7 19.6 %collective-permute-start.3 = (bf16[4,8,16,640]{3,2,1,0:T(8,128)(2,1)S(1)}, bf16[4,8,16,640]{3,2,1,0:T(8,128)(2,1)S(1)}, u32[]{:S(2)}, u32[]{:S(2)}) collective-permute-start(bf16[4,8,16,640]{3,2,1,0:T(8,128)(2,1)S(1)} %pad_maximum_fusion.refs_3_), channel_id=1, source_target_pairs={{0,128},{128,256},{256,384},{384,0},{1,129},{129,257},{257,385},{3... | collective-permute-start | bytes 1966088 | tf_op jit(solution)/shard_map/ppermute | solution.py:20
  92.1 19.0 %collective-permute-start.4 = (bf16[4,8,16,640]{3,2,1,0:T(8,128)(2,1)S(1)}, bf16[4,8,16,640]{3,2,1,0:T(8,128)(2,1)S(1)}, u32[]{:S(2)}, u32[]{:S(2)}) collective-permute-start(bf16[4,8,16,640]{3,2,1,0:T(8,128)(2,1)S(1)} %pad_maximum_fusion.refs_3_), channel_id=1, source_target_pairs={{0,384},{128,0},{256,128},{384,256},{1,385},{129,1},{257,129},{385... | collective-permute-start | bytes 1966088 | tf_op jit(solution)/shard_map/ppermute | solution.py:20
  94.6 25.2 %collective-permute-start.5 = (bf16[4,8,16,640]{3,2,1,0:T(8,128)(2,1)S(1)}, bf16[4,8,16,640]{3,2,1,0:T(8,128)(2,1)S(1)}, u32[]{:S(2)}, u32[]{:S(2)}) collective-permute-start(bf16[4,8,16,640]{3,2,1,0:T(8,128)(2,1)S(1)} %pad_maximum_fusion.refs_3_), channel_id=1, source_target_pairs={{0,256},{128,384},{256,0},{384,128},{1,257},{129,385},{257,1},{385... | collective-permute-start | bytes 1966088 | tf_op jit(solution)/shard_map/ppermute | solution.py:20
  119.8 0.8 copy-start
  120.6 1.1 copy-start.1
  129.7 4.4 %collective-permute-start.6 = (f32[320,640]{1,0:T(8,128)}, f32[320,640]{1,0:T(8,128)S(1)}, u32[]{:S(2)}, u32[]{:S(2)}) collective-permute-start(f32[320,640]{1,0:T(8,128)} %get-tuple-element.18), channel_id=1, source_target_pairs={{0,64},{64,0},{1,65},{65,1},{2,66},{66,2},{3,67},{67,3},{4,68},{68... | collective-permute-start | bytes 2457608 | tf_op jit(solution)/shard_map/ppermute | solution.py:245
  134.9 11.7 %collective-permute-start.7 = (bf16[320,640]{1,0:T(8,128)(2,1)S(1)}, bf16[320,640]{1,0:T(8,128)(2,1)S(1)}, u32[]{:S(2)}, u32[]{:S(2)}) collective-permute-start(bf16[320,640]{1,0:T(8,128)(2,1)S(1)} %finish.1.refs_0_), channel_id=1, source_target_pairs={{0,1},{1,2},{2,3},{3,0},{64,67},{65,64},{66,65},{67,66},{4,5},{5,6... | collective-permute-start | bytes 1228808 | tf_op jit(solution)/shard_map/ppermute | solution.py:261
  138.5 12.0 %collective-permute-start.8 = (bf16[320,640]{1,0:T(8,128)(2,1)S(1)}, bf16[320,640]{1,0:T(8,128)(2,1)S(1)}, u32[]{:S(2)}, u32[]{:S(2)}) collective-permute-start(bf16[320,640]{1,0:T(8,128)(2,1)S(1)} %finish.1.refs_0_), channel_id=1, source_target_pairs={{0,3},{1,0},{2,1},{3,2},{64,65},{65,66},{66,67},{67,64},{4,7},{5,4... | collective-permute-start | bytes 1228808 | tf_op jit(solution)/shard_map/ppermute | solution.py:262
  146.5 11.5 %collective-permute-start.9 = (bf16[320,640]{1,0:T(8,128)(2,1)S(1)}, bf16[320,640]{1,0:T(8,128)(2,1)S(1)}, u32[]{:S(2)}, u32[]{:S(2)}) collective-permute-start(bf16[320,640]{1,0:T(8,128)(2,1)S(1)} %collective-permute-done.7.refs_1_), channel_id=1, source_target_pairs={{0,1},{1,2},{2,3},{3,0},{64,67},{65,64},{66,65},{67,66},{4,5},{5,6... | collective-permute-start | bytes 1228808 | tf_op jit(solution)/shard_map/ppermute | solution.py:263
Sparse Core Ops, SparseCore 0:
  23.8 90.7 all-gather.1

commit v7 on v5

--- a/solution.py
+++ b/solution.py
@@ -20,6 +20,27 @@
     return [value] + [lax.ppermute(value, axis, around(n, s)) for s in SHIFTS[1:]]
 
 
+def relay(values, axes, sizes):
+    groups, ways = [], []
+    for axis, n in zip(axes, sizes):
+        if axis == "x":
+            groups.append(("x", "core"))
+            spot = lambda core, i: 2 * i + core
+        else:
+            groups.append(("core", axis))
+            spot = lambda core, i, n=n: core * n + i
+        ways.append(
+            [
+                [(spot(core, i), spot(core, j)) for core in (0, 1) for i, j in around(n, way * (1 - 2 * core))]
+                for way in (1, -1)
+            ]
+        )
+    ahead = [lax.ppermute(v, g, w[0]) for v, g, w in zip(values, groups, ways)]
+    behind = [lax.ppermute(v, g, w[1]) for v, g, w in zip(values, groups, ways)]
+    across = [lax.ppermute(v, g, w[0]) for v, g, w in zip(ahead, groups, ways)]
+    return [list(blocks) for blocks in zip(values, ahead, behind, across)]
+
+
 def collect(value, axis, n):
     copies = jnp.broadcast_to(value[None], (n,) + value.shape)
     return lax.all_to_all(copies, axis, split_axis=0, concat_axis=0, tiled=True)
@@ -32,7 +53,11 @@
 def weigh_kernel(owned, nz, place_ref, pattern_ref, weight_ref, block_ref, by_col_ref, by_chip_ref):
     lanes = 128
     row = place_ref[0]
-    weight = weight_ref[...]
+    diagonal = lax.broadcasted_iota(jnp.int32, (owned, owned), 0) == lax.broadcasted_iota(
+        jnp.int32, (owned, owned), 1
+    )
+    spread_weight = jnp.broadcast_to(weight_ref[...], (owned, owned))
+    weight = jnp.sum(jnp.where(diagonal, spread_weight, 0.0), axis=1, keepdims=True)
     width = by_col_ref.shape[2]
     count = width // lanes
     chips, _, tile = by_chip_ref.shape
@@ -57,10 +82,15 @@
                 ]
 
 
-def gram_kernel(half, steps, place_ref, rows_ref, by_y_ref, *refs):
+def gram_kernel(half, steps, place_ref, rows_ref, *refs):
     x, y, c = place_ref[0], place_ref[1], place_ref[2]
-    by_x, (keep_ref, send_ref, acc_ref) = refs[:4], refs[4:]
+    by_y, by_x, (keep_ref, send_ref, acc_ref) = refs[:4], refs[4:8], refs[8:]
     k = pl.program_id(0)
+    way = 1 - 2 * c
+    offsets = (0, way, -way, 2)
+
+    def before(position, offset):
+        return lax.rem(position - offset + 4, 4)
 
     def product(left, right):
         return lax.dot_general(
@@ -75,16 +105,18 @@
         for p in range(GROUP):
             for i in range(4):
                 for j in range(4):
-                    left.append(rows_ref[p, i * 4 + j])
-                    right.append(by_y_ref[j, i, p])
+                    left.append(rows_ref[p, i * 4 + before(y, offsets[j])])
+                    right.append(by_y[j][i, p])
         return product(left, right)
 
     def second():
         left, right = [], []
         for p in range(GROUP):
-            for i, s in enumerate(SHIFTS):
-                for j, t in enumerate(SHIFTS):
-                    left.append(rows_ref[p, lax.rem(x - s + 4, 4) * 4 + lax.rem(y - t + 4, 4)])
+            for i in range(4):
+                for j in range(4):
+                    left.append(
+                        rows_ref[p, before(x, offsets[i]) * 4 + before(y, SHIFTS[j])]
+                    )
                     right.append(by_x[i][j, p])
         return product(left, right)
 
@@ -113,14 +145,68 @@
         send_ref[...] = acc_ref[:half]
 
 
-def finish_kernel(factor, place_ref, keep_ref, add_ref, out_ref):
-    shape = keep_ref.shape
-    row_ids = place_ref[0] + pl.program_id(0) * shape[0] + lax.broadcasted_iota(jnp.int32, shape, 0)
-    col_ids = place_ref[1] + lax.broadcasted_iota(jnp.int32, shape, 1)
-    total = (keep_ref[...] + add_ref[...]) * factor
-    piece = jnp.where(row_ids == col_ids, jnp.float32(0.0), total).astype(jnp.bfloat16)
-    for i in range(out_ref.shape[0]):
-        out_ref[i] = piece
+def finish_kernel(factor, corner_ref, keep_ref, add_ref, out_ref, held_ref, sems):
+    bands = held_ref.shape[0]
+    rows, width = held_ref.shape[1:]
+    copies = [
+        pltpu.make_async_copy(keep_ref.at[pl.ds(i * rows, rows)], held_ref.at[i], sems.at[i])
+        for i in range(bands)
+    ]
+    for copy in copies:
+        copy.start()
+    for i, copy in enumerate(copies):
+        row_ids = corner_ref[0] + i * rows + lax.broadcasted_iota(jnp.int32, (rows, width), 0)
+        col_ids = corner_ref[1] + lax.broadcasted_iota(jnp.int32, (rows, width), 1)
+        copy.wait()
+        total = (held_ref[i] + add_ref[i * rows : (i + 1) * rows]) * factor
+        out_ref[i * rows : (i + 1) * rows] = jnp.where(
+            row_ids == col_ids, jnp.float32(0.0), total
+        ).astype(jnp.bfloat16)
+
+
+def place_kernel(own_ref, ahead_ref, behind_ref, out_ref, sems):
+    y = lax.axis_index("layer")
+    way = 1 - 2 * lax.axis_index("core")
+    copies = []
+    for i, (ref, offset) in enumerate(((own_ref, 0), (ahead_ref, way), (behind_ref, -way))):
+        slot = lax.rem(y - offset + 4, 4)
+        copies.append(pltpu.make_async_copy(ref, out_ref.at[slot], sems.at[i]))
+    for copy in copies:
+        copy.start()
+    for copy in copies:
+        copy.wait()
+
+
+def last_kernel(held_ref, across_ref, out_ref, sem):
+    slot = lax.rem(lax.axis_index("layer") + 2, 4)
+    copy = pltpu.make_async_copy(across_ref, out_ref.at[slot], sem)
+    copy.start()
+    copy.wait()
+
+
+def assemble(own, ahead, behind, across):
+    shape = jax.ShapeDtypeStruct((4,) + own.shape, own.dtype)
+    params = pltpu.CompilerParams(vmem_limit_bytes=8 << 20)
+    anywhere = pl.BlockSpec(memory_space=pl.ANY)
+    held = pl.pallas_call(
+        place_kernel,
+        out_shape=shape,
+        in_specs=[VMEM] * 3,
+        out_specs=anywhere,
+        scratch_shapes=[pltpu.SemaphoreType.DMA((3,))],
+        compiler_params=params,
+        name="place",
+    )(own, ahead, behind)
+    return pl.pallas_call(
+        last_kernel,
+        out_shape=shape,
+        in_specs=[anywhere, VMEM],
+        out_specs=anywhere,
+        scratch_shapes=[pltpu.SemaphoreType.DMA],
+        input_output_aliases={0: 0},
+        compiler_params=params,
+        name="last",
+    )(held, across)
 
 
 def body(occurrences, idf_weight, pattern):
@@ -144,9 +230,9 @@
         ),
         in_specs=[SMEM, SMEM, VMEM, VMEM],
         out_specs=(VMEM, VMEM),
-        compiler_params=pltpu.CompilerParams(vmem_limit_bytes=8 << 20),
+        compiler_params=pltpu.CompilerParams(vmem_limit_bytes=58 << 20),
         name="weigh",
-    )(block_row, pattern, idf_weight.reshape(owned, 1), occurrences)
+    )(block_row, pattern, idf_weight.reshape(1, owned), occurrences)
     own = lax.all_to_all(by_chip, ("x", "layer"), split_axis=0, concat_axis=0, tiled=True)
     own = own.reshape(chips * owned, tile)
     rows = lax.all_gather(own, "col", axis=0, tiled=True).reshape(nz, chips, owned, tile)
@@ -156,8 +242,7 @@
     along_x = collect(upper, "x", nx)
     along_y = jnp.stack(spread(lower, "layer", ny))
     along_x, along_y = lax.optimization_barrier((along_x, along_y))
-    by_y = collect(along_x, "layer", ny)
-    by_x = spread(along_y, "x", nx)
+    by_x, by_y = relay([along_y, along_x], ["x", "layer"], [nx, ny])
 
     place = jnp.stack([x, y, c]).astype(jnp.int32)
     steps = nz // GROUP
@@ -169,41 +254,42 @@
         in_specs=[
             SMEM,
             pl.BlockSpec((GROUP, chips, owned, tile), lambda k: (k, 0, 0, 0)),
-            pl.BlockSpec(
-                (ny, nx, GROUP, owned, width), lambda k: (0, 0, jnp.minimum(k, n - 1), 0, 0)
-            ),
         ]
         + [
-            pl.BlockSpec(
-                (ny, GROUP, owned, width), lambda k: (0, jnp.maximum(k - n, 0), 0, 0)
-            )
+            pl.BlockSpec((nx, GROUP, owned, width), lambda k: (0, jnp.minimum(k, n - 1), 0, 0))
+        ]
+        * ny
+        + [
+            pl.BlockSpec((ny, GROUP, owned, width), lambda k: (0, jnp.maximum(k - n, 0), 0, 0))
         ]
         * nx,
         out_specs=(VMEM, VMEM),
         scratch_shapes=[pltpu.VMEM((tile, width), jnp.float32)],
-        compiler_params=pltpu.CompilerParams(vmem_limit_bytes=50 << 20),
+        compiler_params=pltpu.CompilerParams(vmem_limit_bytes=52846592),
         cost_estimate=pl.CostEstimate(
             flops=2 * tile * width * nz * chips * owned,
             bytes_accessed=2 * (tile + width) * nz * chips * owned,
             transcendentals=0,
         ),
         name="gram",
-    )(place, rows, by_y, *by_x)
+    )(place, rows, *by_y, *by_x)
     add = lax.ppermute(send, "core", [(0, 1), (1, 0)])
     corner = jnp.stack([((x * nc + c) * ny + y) * half, z * width]).astype(jnp.int32)
     bands = 2
-    band = pl.BlockSpec((half // bands, width), lambda k: (k, 0))
-    copies = pl.pallas_call(
+    piece = pl.pallas_call(
         lambda *refs: finish_kernel(factor, *refs),
-        out_shape=jax.ShapeDtypeStruct((ny, half, width), jnp.bfloat16),
-        grid=(bands,),
-        in_specs=[SMEM, band, band],
-        out_specs=pl.BlockSpec((ny, half // bands, width), lambda k: (0, k, 0)),
+        out_shape=jax.ShapeDtypeStruct((half, width), jnp.bfloat16),
+        in_specs=[SMEM, pl.BlockSpec(memory_space=pl.ANY), VMEM],
+        out_specs=VMEM,
+        scratch_shapes=[
+            pltpu.VMEM((bands, half // bands, width), jnp.float32),
+            pltpu.SemaphoreType.DMA((bands,)),
+        ],
         compiler_params=pltpu.CompilerParams(vmem_limit_bytes=16 << 20),
         name="finish",
     )(corner, keep, add)
-    out = lax.all_to_all(copies, "layer", split_axis=0, concat_axis=0, tiled=True)
-    return out.reshape(ny * half, width)
+    (pieces,) = relay([piece], ["layer"], [ny])
+    return assemble(*pieces).reshape(ny * half, width)
 
 
 def solution(mesh):

time: 169 us -> 166 us (0.982)
  the two profiles are of different devices: /device:TPU:34 before, /device:TPU:32 now
where the time goes in v7:
time: 166 us; the launch traced here: 165 us
  blocking collectives  53.9 us (32%)
  waiting for transfers between devices  41.3 us (25%)
  starting transfers between devices  40.4 us (24%)
  between operations  13.6 us (8%)
  Pallas kernels  13.5 us (8%)
  local copies, waits for them, and re-layouts  2.08 us (1%)
    all_to_all x1, blocking collectives, body(): lax.all_to_all(by_col, 'col', split_axis=0, concat_axis=0, tiled=True)  37.6 us
    all_to_all x1, blocking collectives, body(): lax.all_to_all(by_chip, ('x', 'layer'), split_axis=0, concat_axis=0, tile...  16.3 us
    ppermute x3, waiting for transfers between devices, relay(): across = [lax.ppermute(v, g, w[0]) for v, g, w in zip(ahead, groups, ways)]  15.7 us
    ppermute x3, starting transfers between devices, relay(): behind = [lax.ppermute(v, g, w[1]) for v, g, w in zip(values, groups, ways)]  12.7 us
    ppermute x3, waiting for transfers between devices, relay(): ahead = [lax.ppermute(v, g, w[0]) for v, g, w in zip(values, groups, ways)]  12.6 us
    ppermute x3, starting transfers between devices, relay(): ahead = [lax.ppermute(v, g, w[0]) for v, g, w in zip(values, groups, ways)]  8.51 us
    pallas_call x1, Pallas kernels, body(): pl.pallas_call(lambda *refs: gram_kernel(half, steps, *refs), out_shape=(...  8.37 us
    ppermute x3, starting transfers between devices, spread(): lax.ppermute(value, axis, around(n, s))  8.07 us
  transfers between devices with their start and end apart: 15, of which 11 were waited for; matrix products, arithmetic and copies ran while one was open for 1% of the time, Pallas kernels for 1%

profile of v7, /device:TPU:32, one launch (start us, length us, event | category | flops | bytes accessed | tf_op | source)
XLA Modules:
  0.0 164.9 jit_solution(6525154568656861656)
XLA Ops:
  6.5 0.0 all-gather.2.cloned.1.call-start
  6.5 2.2 %weigh.1 = (bf16[16,16,640]{2,1,0:T(8,128)(2,1)}, bf16[16,16,640]{2,1,0:T(8,128)(2,1)}) custom-call(s32[1]{0:T(128)} %bitcast.5.refs_0_, s32[64,80]{1,0:T(8,128)} %refs_1_.1, f32[1,16]{1,0:T(1,128)} %bitcast.19, bf16[16,10240]{1,0:T(8,128)(2,1)} %refs_3_.1), custom_call_target="tpu_custom_call" | custom-call | tf_op jit(solution)/shard_map/weigh/pallas_call | solution.py:225
  8.7 16.3 %all_to_all.15 = bf16[16,16,640]{2,1,0:T(8,128)(2,1)} all-to-all(bf16[16,16,640]{2,1,0:T(8,128)(2,1)} %get-tuple-element.12), channel_id=1, replica_groups=mesh['x'=4,'core'=2,'col'=16,'layer'=4] {'x','layer'}, dimensions={0} | all-to-all | bytes 655360 | tf_op jit(solution)/shard_map/all_to_all | solution.py:236
  25.0 0.0 all-gather.2.cloned.1.call-update
  25.1 37.6 %all_to_all.16 = bf16[16,16,640]{2,1,0:T(8,128)(2,1)S(1)} all-to-all(bf16[16,16,640]{2,1,0:T(8,128)(2,1)} %get-tuple-element.14), channel_id=1, replica_groups=mesh['x'=4,'core'=2,'col'=16,'layer'=4] {'col'}, dimensions={0} | all-to-all | bytes 655360 | tf_op jit(solution)/shard_map/all_to_all | solution.py:240
  62.7 0.9 broadcast_in_dim.2
  63.5 3.5 %all-to-all-start.2 = ((bf16[4,8,16,640]{3,2,1,0:T(8,128)(2,1)}), bf16[4,8,16,640]{3,2,1,0:T(8,128)(2,1)S(1)}, u32[]{:S(2)}, u32[]{:S(2)}) async-start(bf16[4,8,16,640]{3,2,1,0:T(8,128)(2,1)} %broadcast_in_dim.2), calls=%async_computation.2 | async-start | bytes 1310720 | tf_op jit(solution)/shard_map/all_to_all | solution.py:46
  67.0 1.9 %collective-permute-start.1 = (bf16[8,16,640]{2,1,0:T(8,128)(2,1)S(1)}, bf16[8,16,640]{2,1,0:T(8,128)(2,1)S(1)}, u32[]{:S(2)}, u32[]{:S(2)}) collective-permute-start(bf16[8,16,640]{2,1,0:T(8,128)(2,1)S(1)} %get-tuple-element.20), channel_id=1, source_target_pairs={{0,3},{1,0},{2,1},{3,2},{4,7},{5,4},{6,5},{7,6},{8,11},{9,8},{10,9... | collective-permute-start | bytes 491528 | tf_op jit(solution)/shard_map/ppermute | solution.py:20
  69.0 3.9 %collective-permute-start = (bf16[8,16,640]{2,1,0:T(8,128)(2,1)S(1)}, bf16[8,16,640]{2,1,0:T(8,128)(2,1)S(1)}, u32[]{:S(2)}, u32[]{:S(2)}) collective-permute-start(bf16[8,16,640]{2,1,0:T(8,128)(2,1)S(1)} %get-tuple-element.20), channel_id=1, source_target_pairs={{0,1},{1,2},{2,3},{3,0},{4,5},{5,6},{6,7},{7,4},{8,9},{9,10},{10,1... | collective-permute-start | bytes 491528 | tf_op jit(solution)/shard_map/ppermute | solution.py:20
  72.9 2.2 %collective-permute-start.2 = (bf16[8,16,640]{2,1,0:T(8,128)(2,1)S(1)}, bf16[8,16,640]{2,1,0:T(8,128)(2,1)S(1)}, u32[]{:S(2)}, u32[]{:S(2)}) collective-permute-start(bf16[8,16,640]{2,1,0:T(8,128)(2,1)S(1)} %get-tuple-element.20), channel_id=1, source_target_pairs={{0,2},{1,3},{2,0},{3,1},{4,6},{5,7},{6,4},{7,5},{8,10},{9,11},{10,... | collective-permute-start | bytes 491528 | tf_op jit(solution)/shard_map/ppermute | solution.py:20
  75.1 0.4 collective-permute-done.1
  75.6 1.8 %collective-permute-done = bf16[8,16,640]{2,1,0:T(8,128)(2,1)S(1)} collective-permute-done((bf16[8,16,640]{2,1,0:T(8,128)(2,1)S(1)}, bf16[8,16,640]{2,1,0:T(8,128)(2,1)S(1)}, u32[]{:S(2)}, u32[]{:S(2)}) %collective-permute-start) | collective-permute-done | bytes 163872 | tf_op jit(solution)/shard_map/ppermute | solution.py:20
  77.4 4.2 %collective-permute-done.2 = bf16[8,16,640]{2,1,0:T(8,128)(2,1)S(1)} collective-permute-done((bf16[8,16,640]{2,1,0:T(8,128)(2,1)S(1)}, bf16[8,16,640]{2,1,0:T(8,128)(2,1)S(1)}, u32[]{:S(2)}, u32[]{:S(2)}) %collective-permute-start.2) | collective-permute-done | bytes 163872 | tf_op jit(solution)/shard_map/ppermute | solution.py:20
  81.6 0.1 pad_maximum_fusion.refs_6_
  81.7 0.0 all-to-all-done.2.refs_2_
  81.7 2.0 %collective-permute-start.3 = (bf16[4,8,16,640]{3,2,1,0:T(8,128)(2,1)S(1)}, bf16[4,8,16,640]{3,2,1,0:T(8,128)(2,1)S(1)}, u32[]{:S(2)}, u32[]{:S(2)}) collective-permute-start(bf16[4,8,16,640]{3,2,1,0:T(8,128)(2,1)S(1)} %all-to-all-done.2.refs_2_), channel_id=1, source_target_pairs={{0,1},{1,2},{2,3},{3,0},{64,67},{65,64},{66,65},{67,66},{4,5},{5,6... | collective-permute-start | bytes 1966088 | tf_op jit(solution)/shard_map/ppermute | solution.py:38
  83.8 4.6 %collective-permute-start.6 = (bf16[4,8,16,640]{3,2,1,0:T(8,128)(2,1)S(1)}, bf16[4,8,16,640]{3,2,1,0:T(8,128)(2,1)S(1)}, u32[]{:S(2)}, u32[]{:S(2)}) collective-permute-start(bf16[4,8,16,640]{3,2,1,0:T(8,128)(2,1)S(1)} %pad_maximum_fusion.refs_6_), channel_id=1, source_target_pairs={{0,128},{128,256},{256,384},{384,0},{64,448},{192,64},{320,192},{4... | collective-permute-start | bytes 1966088 | tf_op jit(solution)/shard_map/ppermute | solution.py:38
  88.3 4.3 %collective-permute-start.4 = (bf16[4,8,16,640]{3,2,1,0:T(8,128)(2,1)S(1)}, bf16[4,8,16,640]{3,2,1,0:T(8,128)(2,1)S(1)}, u32[]{:S(2)}, u32[]{:S(2)}) collective-permute-start(bf16[4,8,16,640]{3,2,1,0:T(8,128)(2,1)S(1)} %all-to-all-done.2.refs_2_), channel_id=1, source_target_pairs={{0,3},{1,0},{2,1},{3,2},{64,65},{65,66},{66,67},{67,64},{4,7},{5,4... | collective-permute-start | bytes 1966088 | tf_op jit(solution)/shard_map/ppermute | solution.py:39
  92.7 3.2 %collective-permute-start.7 = (bf16[4,8,16,640]{3,2,1,0:T(8,128)(2,1)S(1)}, bf16[4,8,16,640]{3,2,1,0:T(8,128)(2,1)S(1)}, u32[]{:S(2)}, u32[]{:S(2)}) collective-permute-start(bf16[4,8,16,640]{3,2,1,0:T(8,128)(2,1)S(1)} %pad_maximum_fusion.refs_6_), channel_id=1, source_target_pairs={{0,384},{128,0},{256,128},{384,256},{64,192},{192,320},{320,448},{... | collective-permute-start | bytes 1966088 | tf_op jit(solution)/shard_map/ppermute | solution.py:39
  95.9 5.6 %collective-permute-done.3.refs_3_ = bf16[4,8,16,640]{3,2,1,0:T(8,128)(2,1)S(1)} collective-permute-done((bf16[4,8,16,640]{3,2,1,0:T(8,128)(2,1)S(1)}, bf16[4,8,16,640]{3,2,1,0:T(8,128)(2,1)S(1)}, u32[]{:S(2)}, u32[]{:S(2)}) %collective-permute-start.3) | collective-permute-done | bytes 655392 | tf_op jit(solution)/shard_map/ppermute | solution.py:38
  101.4 1.9 %collective-permute-start.5 = (bf16[4,8,16,640]{3,2,1,0:T(8,128)(2,1)S(1)}, bf16[4,8,16,640]{3,2,1,0:T(8,128)(2,1)S(1)}, u32[]{:S(2)}, u32[]{:S(2)}) collective-permute-start(bf16[4,8,16,640]{3,2,1,0:T(8,128)(2,1)S(1)} %collective-permute-done.3.refs_3_), channel_id=1, source_target_pairs={{0,1},{1,2},{2,3},{3,0},{64,67},{65,64},{66,65},{67,66},{4,5},{5,6... | collective-permute-start | bytes 1966088 | tf_op jit(solution)/shard_map/ppermute | solution.py:40
  103.4 1.5 collective-permute-done.6.refs_7_
  104.9 0.0 copy-start.1
  104.9 1.9 %collective-permute-start.8 = (bf16[4,8,16,640]{3,2,1,0:T(8,128)(2,1)S(1)}, bf16[4,8,16,640]{3,2,1,0:T(8,128)(2,1)}, u32[]{:S(2)}, u32[]{:S(2)}) collective-permute-start(bf16[4,8,16,640]{3,2,1,0:T(8,128)(2,1)S(1)} %collective-permute-done.6.refs_7_), channel_id=1, source_target_pairs={{0,128},{128,256},{256,384},{384,0},{64,448},{192,64},{320,192},{4... | collective-permute-start | bytes 1966088 | tf_op jit(solution)/shard_map/ppermute | solution.py:40
  106.8 0.1 pad_add_fusion.1.refs_0_
  106.9 0.0 collective-permute-done.4.refs_4_
  106.9 4.1 %collective-permute-done.7.refs_8_ = bf16[4,8,16,640]{3,2,1,0:T(8,128)(2,1)S(1)} collective-permute-done((bf16[4,8,16,640]{3,2,1,0:T(8,128)(2,1)S(1)}, bf16[4,8,16,640]{3,2,1,0:T(8,128)(2,1)S(1)}, u32[]{:S(2)}, u32[]{:S(2)}) %collective-permute-start.7) | collective-permute-done | bytes 655392 | tf_op jit(solution)/shard_map/ppermute | solution.py:39
  111.0 0.0 copy-start.2
  111.0 4.1 %collective-permute-done.5.refs_5_ = bf16[4,8,16,640]{3,2,1,0:T(8,128)(2,1)S(1)} collective-permute-done((bf16[4,8,16,640]{3,2,1,0:T(8,128)(2,1)S(1)}, bf16[4,8,16,640]{3,2,1,0:T(8,128)(2,1)S(1)}, u32[]{:S(2)}, u32[]{:S(2)}) %collective-permute-start.5) | collective-permute-done | bytes 655392 | tf_op jit(solution)/shard_map/ppermute | solution.py:40
  115.1 0.0 copy-done.1
  115.1 0.0 copy-done.2
  115.1 3.5 %collective-permute-done.8.refs_9_ = bf16[4,8,16,640]{3,2,1,0:T(8,128)(2,1)} collective-permute-done((bf16[4,8,16,640]{3,2,1,0:T(8,128)(2,1)S(1)}, bf16[4,8,16,640]{3,2,1,0:T(8,128)(2,1)}, u32[]{:S(2)}, u32[]{:S(2)}) %collective-permute-start.8) | collective-permute-done | bytes 655392 | tf_op jit(solution)/shard_map/ppermute | solution.py:40
  118.7 0.0 all-gather.2.cloned.1.call-done
  118.7 8.4 %gram.1 = (f32[320,640]{1,0:T(8,128)}, f32[320,640]{1,0:T(8,128)}) custom-call(s32[3]{0:T(128)S(1)} %pad_add_fusion.1.refs_0_, bf16[16,16,16,640]{3,2,1,0:T(8,128)(2,1)} %bitcast.20, bf16[4,8,16,640]{3,2,1,0:T(8,128)(2,1)S(1)} %all-to-all-done.2.refs_2_, bf16[4,8,16,640]{3,2,1,0:T(8,128)(2,1)S(1)} %collective-permute-done.3.refs_3_, ...), custom_call_target="tpu_custom_call" | custom-call | flops 3355443200 | bytes 10485760 | tf_op jit(solution)/shard_map/gram/pallas_call | solution.py:250
  127.0 1.9 %collective-permute-start.9 = (f32[320,640]{1,0:T(8,128)}, f32[320,640]{1,0:T(8,128)S(1)}, u32[]{:S(2)}, u32[]{:S(2)}) collective-permute-start(f32[320,640]{1,0:T(8,128)} %get-tuple-element.18), channel_id=1, source_target_pairs={{0,64},{64,0},{1,65},{65,1},{2,66},{66,2},{3,67},{67,3},{4,68},{68... | collective-permute-start | bytes 2457608 | tf_op jit(solution)/shard_map/ppermute | solution.py:276
  129.0 0.1 pad_add_fusion.refs_0_
  129.0 2.4 %collective-permute-done.9.refs_2_ = f32[320,640]{1,0:T(8,128)S(1)} collective-permute-done((f32[320,640]{1,0:T(8,128)}, f32[320,640]{1,0:T(8,128)S(1)}, u32[]{:S(2)}, u32[]{:S(2)}) %collective-permute-start.9) | collective-permute-done | bytes 819232 | tf_op jit(solution)/shard_map/ppermute | solution.py:276
  131.5 0.0 copy-start
  131.5 1.1 copy-done
  132.6 1.1 finish.1.own_ref
  133.7 1.9 %collective-permute-start.10 = (bf16[320,640]{1,0:T(8,128)(2,1)S(1)}, bf16[320,640]{1,0:T(8,128)(2,1)S(1)}, u32[]{:S(2)}, u32[]{:S(2)}) collective-permute-start(bf16[320,640]{1,0:T(8,128)(2,1)S(1)} %finish.1.own_ref), channel_id=1, source_target_pairs={{0,1},{1,2},{2,3},{3,0},{64,67},{65,64},{66,65},{67,66},{4,5},{5,6... | collective-permute-start | bytes 1228808 | tf_op jit(solution)/shard_map/ppermute | solution.py:38
  135.7 5.1 %collective-permute-start.11 = (bf16[320,640]{1,0:T(8,128)(2,1)S(1)}, bf16[320,640]{1,0:T(8,128)(2,1)S(1)}, u32[]{:S(2)}, u32[]{:S(2)}) collective-permute-start(bf16[320,640]{1,0:T(8,128)(2,1)S(1)} %finish.1.own_ref), channel_id=1, source_target_pairs={{0,3},{1,0},{2,1},{3,2},{64,65},{65,66},{66,67},{67,64},{4,7},{5,4... | collective-permute-start | bytes 1228808 | tf_op jit(solution)/shard_map/ppermute | solution.py:39
  140.8 5.5 %collective-permute-done.10.ahead_ref = bf16[320,640]{1,0:T(8,128)(2,1)S(1)} collective-permute-done((bf16[320,640]{1,0:T(8,128)(2,1)S(1)}, bf16[320,640]{1,0:T(8,128)(2,1)S(1)}, u32[]{:S(2)}, u32[]{:S(2)}) %collective-permute-start.10) | collective-permute-done | bytes 409632 | tf_op jit(solution)/shard_map/ppermute | solution.py:38
  146.3 1.9 %collective-permute-start.12 = (bf16[320,640]{1,0:T(8,128)(2,1)S(1)}, bf16[320,640]{1,0:T(8,128)(2,1)S(1)}, u32[]{:S(2)}, u32[]{:S(2)}) collective-permute-start(bf16[320,640]{1,0:T(8,128)(2,1)S(1)} %collective-permute-done.10.ahead_ref), channel_id=1, source_target_pairs={{0,1},{1,2},{2,3},{3,0},{64,67},{65,64},{66,65},{67,66},{4,5},{5,6... | collective-permute-start | bytes 1228808 | tf_op jit(solution)/shard_map/ppermute | solution.py:40
  148.2 0.0 collective-permute-done.11.behind_ref
  148.2 1.1 place.1.held_ref
  149.3 8.1 %collective-permute-done.12.across_ref = bf16[320,640]{1,0:T(8,128)(2,1)S(1)} collective-permute-done((bf16[320,640]{1,0:T(8,128)(2,1)S(1)}, bf16[320,640]{1,0:T(8,128)(2,1)S(1)}, u32[]{:S(2)}, u32[]{:S(2)}) %collective-permute-start.12) | collective-permute-done | bytes 409632 | tf_op jit(solution)/shard_map/ppermute | solution.py:40
  157.3 0.8 last.1
  (1 shorter events, 0.0 us)
Async XLA Ops:
  6.5 112.1 %all-gather.2.cloned.1.call-start = ((), (), s32[]{:S(2)}) async-start(), calls=%async_computation.3 | async-start | bytes 5570560 | tf_op jit(solution)/shard_map/all_gather | solution.py:238
  63.5 18.2 %all-to-all-start.2 = ((bf16[4,8,16,640]{3,2,1,0:T(8,128)(2,1)}), bf16[4,8,16,640]{3,2,1,0:T(8,128)(2,1)S(1)}, u32[]{:S(2)}, u32[]{:S(2)}) async-start(bf16[4,8,16,640]{3,2,1,0:T(8,128)(2,1)} %broadcast_in_dim.2), calls=%async_computation.2 | async-start | bytes 1310720 | tf_op jit(solution)/shard_map/all_to_all | solution.py:46
  67.0 8.5 %collective-permute-start.1 = (bf16[8,16,640]{2,1,0:T(8,128)(2,1)S(1)}, bf16[8,16,640]{2,1,0:T(8,128)(2,1)S(1)}, u32[]{:S(2)}, u32[]{:S(2)}) collective-permute-start(bf16[8,16,640]{2,1,0:T(8,128)(2,1)S(1)} %get-tuple-element.20), channel_id=1, source_target_pairs={{0,3},{1,0},{2,1},{3,2},{4,7},{5,4},{6,5},{7,6},{8,11},{9,8},{10,9... | collective-permute-start | bytes 491528 | tf_op jit(solution)/shard_map/ppermute | solution.py:20
  69.0 8.4 %collective-permute-start = (bf16[8,16,640]{2,1,0:T(8,128)(2,1)S(1)}, bf16[8,16,640]{2,1,0:T(8,128)(2,1)S(1)}, u32[]{:S(2)}, u32[]{:S(2)}) collective-permute-start(bf16[8,16,640]{2,1,0:T(8,128)(2,1)S(1)} %get-tuple-element.20), channel_id=1, source_target_pairs={{0,1},{1,2},{2,3},{3,0},{4,5},{5,6},{6,7},{7,4},{8,9},{9,10},{10,1... | collective-permute-start | bytes 491528 | tf_op jit(solution)/shard_map/ppermute | solution.py:20
  72.9 8.7 %collective-permute-start.2 = (bf16[8,16,640]{2,1,0:T(8,128)(2,1)S(1)}, bf16[8,16,640]{2,1,0:T(8,128)(2,1)S(1)}, u32[]{:S(2)}, u32[]{:S(2)}) collective-permute-start(bf16[8,16,640]{2,1,0:T(8,128)(2,1)S(1)} %get-tuple-element.20), channel_id=1, source_target_pairs={{0,2},{1,3},{2,0},{3,1},{4,6},{5,7},{6,4},{7,5},{8,10},{9,11},{10,... | collective-permute-start | bytes 491528 | tf_op jit(solution)/shard_map/ppermute | solution.py:20
  81.7 19.7 %collective-permute-start.3 = (bf16[4,8,16,640]{3,2,1,0:T(8,128)(2,1)S(1)}, bf16[4,8,16,640]{3,2,1,0:T(8,128)(2,1)S(1)}, u32[]{:S(2)}, u32[]{:S(2)}) collective-permute-start(bf16[4,8,16,640]{3,2,1,0:T(8,128)(2,1)S(1)} %all-to-all-done.2.refs_2_), channel_id=1, source_target_pairs={{0,1},{1,2},{2,3},{3,0},{64,67},{65,64},{66,65},{67,66},{4,5},{5,6... | collective-permute-start | bytes 1966088 | tf_op jit(solution)/shard_map/ppermute | solution.py:38
  83.8 21.1 %collective-permute-start.6 = (bf16[4,8,16,640]{3,2,1,0:T(8,128)(2,1)S(1)}, bf16[4,8,16,640]{3,2,1,0:T(8,128)(2,1)S(1)}, u32[]{:S(2)}, u32[]{:S(2)}) collective-permute-start(bf16[4,8,16,640]{3,2,1,0:T(8,128)(2,1)S(1)} %pad_maximum_fusion.refs_6_), channel_id=1, source_target_pairs={{0,128},{128,256},{256,384},{384,0},{64,448},{192,64},{320,192},{4... | collective-permute-start | bytes 1966088 | tf_op jit(solution)/shard_map/ppermute | solution.py:38
  88.3 18.5 %collective-permute-start.4 = (bf16[4,8,16,640]{3,2,1,0:T(8,128)(2,1)S(1)}, bf16[4,8,16,640]{3,2,1,0:T(8,128)(2,1)S(1)}, u32[]{:S(2)}, u32[]{:S(2)}) collective-permute-start(bf16[4,8,16,640]{3,2,1,0:T(8,128)(2,1)S(1)} %all-to-all-done.2.refs_2_), channel_id=1, source_target_pairs={{0,3},{1,0},{2,1},{3,2},{64,65},{65,66},{66,67},{67,64},{4,7},{5,4... | collective-permute-start | bytes 1966088 | tf_op jit(solution)/shard_map/ppermute | solution.py:39
  92.7 18.3 %collective-permute-start.7 = (bf16[4,8,16,640]{3,2,1,0:T(8,128)(2,1)S(1)}, bf16[4,8,16,640]{3,2,1,0:T(8,128)(2,1)S(1)}, u32[]{:S(2)}, u32[]{:S(2)}) collective-permute-start(bf16[4,8,16,640]{3,2,1,0:T(8,128)(2,1)S(1)} %pad_maximum_fusion.refs_6_), channel_id=1, source_target_pairs={{0,384},{128,0},{256,128},{384,256},{64,192},{192,320},{320,448},{... | collective-permute-start | bytes 1966088 | tf_op jit(solution)/shard_map/ppermute | solution.py:39
  101.4 13.7 %collective-permute-start.5 = (bf16[4,8,16,640]{3,2,1,0:T(8,128)(2,1)S(1)}, bf16[4,8,16,640]{3,2,1,0:T(8,128)(2,1)S(1)}, u32[]{:S(2)}, u32[]{:S(2)}) collective-permute-start(bf16[4,8,16,640]{3,2,1,0:T(8,128)(2,1)S(1)} %collective-permute-done.3.refs_3_), channel_id=1, source_target_pairs={{0,1},{1,2},{2,3},{3,0},{64,67},{65,64},{66,65},{67,66},{4,5},{5,6... | collective-permute-start | bytes 1966088 | tf_op jit(solution)/shard_map/ppermute | solution.py:40
  104.9 10.3 %copy-start.1 = (bf16[4,8,16,640]{3,2,1,0:T(8,128)(2,1)}, bf16[4,8,16,640]{3,2,1,0:T(8,128)(2,1)S(1)}, u32[]{:S(2)}) copy-start(bf16[4,8,16,640]{3,2,1,0:T(8,128)(2,1)S(1)} %collective-permute-done.6.refs_7_) | copy-start | bytes 1966084
  104.9 13.8 %collective-permute-start.8 = (bf16[4,8,16,640]{3,2,1,0:T(8,128)(2,1)S(1)}, bf16[4,8,16,640]{3,2,1,0:T(8,128)(2,1)}, u32[]{:S(2)}, u32[]{:S(2)}) collective-permute-start(bf16[4,8,16,640]{3,2,1,0:T(8,128)(2,1)S(1)} %collective-permute-done.6.refs_7_), channel_id=1, source_target_pairs={{0,128},{128,256},{256,384},{384,0},{64,448},{192,64},{320,192},{4... | collective-permute-start | bytes 1966088 | tf_op jit(solution)/shard_map/ppermute | solution.py:40
  111.0 4.2 %copy-start.2 = (bf16[4,8,16,640]{3,2,1,0:T(8,128)(2,1)}, bf16[4,8,16,640]{3,2,1,0:T(8,128)(2,1)S(1)}, u32[]{:S(2)}) copy-start(bf16[4,8,16,640]{3,2,1,0:T(8,128)(2,1)S(1)} %collective-permute-done.7.refs_8_) | copy-start | bytes 1966084
  127.0 4.4 %collective-permute-start.9 = (f32[320,640]{1,0:T(8,128)}, f32[320,640]{1,0:T(8,128)S(1)}, u32[]{:S(2)}, u32[]{:S(2)}) collective-permute-start(f32[320,640]{1,0:T(8,128)} %get-tuple-element.18), channel_id=1, source_target_pairs={{0,64},{64,0},{1,65},{65,1},{2,66},{66,2},{3,67},{67,3},{4,68},{68... | collective-permute-start | bytes 2457608 | tf_op jit(solution)/shard_map/ppermute | solution.py:276
  131.5 1.1 copy-start
  133.7 12.5 %collective-permute-start.10 = (bf16[320,640]{1,0:T(8,128)(2,1)S(1)}, bf16[320,640]{1,0:T(8,128)(2,1)S(1)}, u32[]{:S(2)}, u32[]{:S(2)}) collective-permute-start(bf16[320,640]{1,0:T(8,128)(2,1)S(1)} %finish.1.own_ref), channel_id=1, source_target_pairs={{0,1},{1,2},{2,3},{3,0},{64,67},{65,64},{66,65},{67,66},{4,5},{5,6... | collective-permute-start | bytes 1228808 | tf_op jit(solution)/shard_map/ppermute | solution.py:38
  135.7 12.5 %collective-permute-start.11 = (bf16[320,640]{1,0:T(8,128)(2,1)S(1)}, bf16[320,640]{1,0:T(8,128)(2,1)S(1)}, u32[]{:S(2)}, u32[]{:S(2)}) collective-permute-start(bf16[320,640]{1,0:T(8,128)(2,1)S(1)} %finish.1.own_ref), channel_id=1, source_target_pairs={{0,3},{1,0},{2,1},{3,2},{64,65},{65,66},{66,67},{67,64},{4,7},{5,4... | collective-permute-start | bytes 1228808 | tf_op jit(solution)/shard_map/ppermute | solution.py:39
  146.3 11.0 %collective-permute-start.12 = (bf16[320,640]{1,0:T(8,128)(2,1)S(1)}, bf16[320,640]{1,0:T(8,128)(2,1)S(1)}, u32[]{:S(2)}, u32[]{:S(2)}) collective-permute-start(bf16[320,640]{1,0:T(8,128)(2,1)S(1)} %collective-permute-done.10.ahead_ref), channel_id=1, source_target_pairs={{0,1},{1,2},{2,3},{3,0},{64,67},{65,64},{66,65},{67,66},{4,5},{5,6... | collective-permute-start | bytes 1228808 | tf_op jit(solution)/shard_map/ppermute | solution.py:40
Sparse Core Ops, SparseCore 0:
  25.2 90.7 all-gather.1

commit v8 on v7

--- a/solution.py
+++ b/solution.py
@@ -20,24 +20,26 @@
     return [value] + [lax.ppermute(value, axis, around(n, s)) for s in SHIFTS[1:]]
 
 
+def ways_of(axis, n):
+    group = ("x", "core") if axis == "x" else ("core", axis)
+
+    def spot(core, i):
+        return 2 * i + core if axis == "x" else core * n + i
+
+    ways = []
+    for way in (1, -1):
+        pairs = []
+        for core in (0, 1):
+            pairs += [(spot(core, i), spot(core, j)) for i, j in around(n, way * (1 - 2 * core))]
+        ways.append(pairs)
+    return group, ways
+
+
 def relay(values, axes, sizes):
-    groups, ways = [], []
-    for axis, n in zip(axes, sizes):
-        if axis == "x":
-            groups.append(("x", "core"))
-            spot = lambda core, i: 2 * i + core
-        else:
-            groups.append(("core", axis))
-            spot = lambda core, i, n=n: core * n + i
-        ways.append(
-            [
-                [(spot(core, i), spot(core, j)) for core in (0, 1) for i, j in around(n, way * (1 - 2 * core))]
-                for way in (1, -1)
-            ]
-        )
-    ahead = [lax.ppermute(v, g, w[0]) for v, g, w in zip(values, groups, ways)]
-    behind = [lax.ppermute(v, g, w[1]) for v, g, w in zip(values, groups, ways)]
-    across = [lax.ppermute(v, g, w[0]) for v, g, w in zip(ahead, groups, ways)]
+    plans = [ways_of(axis, n) for axis, n in zip(axes, sizes)]
+    ahead = [lax.ppermute(v, g, w[0]) for v, (g, w) in zip(values, plans)]
+    behind = [lax.ppermute(v, g, w[1]) for v, (g, w) in zip(values, plans)]
+    across = [lax.ppermute(v, g, w[0]) for v, (g, w) in zip(ahead, plans)]
     return [list(blocks) for blocks in zip(values, ahead, behind, across)]
 
 
@@ -143,25 +145,6 @@
     def _():
         keep_ref[...] = acc_ref[half:]
         send_ref[...] = acc_ref[:half]
-
-
-def finish_kernel(factor, corner_ref, keep_ref, add_ref, out_ref, held_ref, sems):
-    bands = held_ref.shape[0]
-    rows, width = held_ref.shape[1:]
-    copies = [
-        pltpu.make_async_copy(keep_ref.at[pl.ds(i * rows, rows)], held_ref.at[i], sems.at[i])
-        for i in range(bands)
-    ]
-    for copy in copies:
-        copy.start()
-    for i, copy in enumerate(copies):
-        row_ids = corner_ref[0] + i * rows + lax.broadcasted_iota(jnp.int32, (rows, width), 0)
-        col_ids = corner_ref[1] + lax.broadcasted_iota(jnp.int32, (rows, width), 1)
-        copy.wait()
-        total = (held_ref[i] + add_ref[i * rows : (i + 1) * rows]) * factor
-        out_ref[i * rows : (i + 1) * rows] = jnp.where(
-            row_ids == col_ids, jnp.float32(0.0), total
-        ).astype(jnp.bfloat16)
 
 
 def place_kernel(own_ref, ahead_ref, behind_ref, out_ref, sems):
@@ -274,22 +257,12 @@
         name="gram",
     )(place, rows, *by_y, *by_x)
     add = lax.ppermute(send, "core", [(0, 1), (1, 0)])
-    corner = jnp.stack([((x * nc + c) * ny + y) * half, z * width]).astype(jnp.int32)
-    bands = 2
-    piece = pl.pallas_call(
-        lambda *refs: finish_kernel(factor, *refs),
-        out_shape=jax.ShapeDtypeStruct((half, width), jnp.bfloat16),
-        in_specs=[SMEM, pl.BlockSpec(memory_space=pl.ANY), VMEM],
-        out_specs=VMEM,
-        scratch_shapes=[
-            pltpu.VMEM((bands, half // bands, width), jnp.float32),
-            pltpu.SemaphoreType.DMA((bands,)),
-        ],
-        compiler_params=pltpu.CompilerParams(vmem_limit_bytes=16 << 20),
-        name="finish",
-    )(corner, keep, add)
-    (pieces,) = relay([piece], ["layer"], [ny])
-    return assemble(*pieces).reshape(ny * half, width)
+    total = (keep + add) * factor
+    row_ids = ((x * nc + c) * ny + y) * half + lax.broadcasted_iota(jnp.int32, total.shape, 0)
+    col_ids = z * width + lax.broadcasted_iota(jnp.int32, total.shape, 1)
+    piece = jnp.where(row_ids == col_ids, jnp.float32(0.0), total).astype(jnp.bfloat16)
+    ((own, ahead, behind, across),) = relay([piece], ["layer"], [ny])
+    return assemble(own, ahead, behind, across).reshape(ny * half, width)
 
 
 def solution(mesh):

time: 166 us -> 167 us (level)
  starting transfers between devices: 40.4 us -> 44.4 us
  waiting for transfers between devices: 41.3 us -> 39.3 us
    ppermute x9, starting transfers between devices: 26.9 us -> 29.7 us  [the longest x3 10.8 us: relay(): ahead = [lax.ppermute(v, g, w[0]) for v, (g, w) in zip(values, plans)]]
    ppermute x3, waiting for transfers between devices: 6.48 us -> 3.83 us  [spread(): lax.ppermute(value, axis, around(n, s))]
  transfers between devices with their start and end apart: 15 -> 15, of which waited for: 11 -> 10; matrix products, arithmetic and copies ran while one was open for 1% -> 1% of each run, Pallas kernels for 1% -> 1%
where the time goes in v8:
time: 167 us; the launch traced here: 166 us
  blocking collectives  53.9 us (32%)
  starting transfers between devices  44.4 us (27%)
  waiting for transfers between devices  39.3 us (24%)
  between operations  13.6 us (8%)
  Pallas kernels  12.4 us (7%)
    all_to_all x1, blocking collectives, body(): lax.all_to_all(by_col, 'col', split_axis=0, concat_axis=0, tiled=True)  37.6 us
    ppermute x3, waiting for transfers between devices, relay(): across = [lax.ppermute(v, g, w[0]) for v, (g, w) in zip(ahead, plans)]  16.5 us
    all_to_all x1, blocking collectives, body(): lax.all_to_all(by_chip, ('x', 'layer'), split_axis=0, concat_axis=0, tile...  16.3 us
    ppermute x3, waiting for transfers between devices, relay(): ahead = [lax.ppermute(v, g, w[0]) for v, (g, w) in zip(values, plans)]  13.1 us
    ppermute x3, starting transfers between devices, relay(): ahead = [lax.ppermute(v, g, w[0]) for v, (g, w) in zip(values, plans)]  10.8 us
    ppermute x3, starting transfers between devices, relay(): behind = [lax.ppermute(v, g, w[1]) for v, (g, w) in zip(values, plans)]  10.7 us
    ppermute x3, starting transfers between devices, spread(): lax.ppermute(value, axis, around(n, s))  9.28 us
    pallas_call x1, Pallas kernels, body(): pl.pallas_call(lambda *refs: gram_kernel(half, steps, *refs), out_shape=(...  8.38 us
  transfers between devices with their start and end apart: 15, of which 10 were waited for; matrix products, arithmetic and copies ran while one was open for 1% of the time, Pallas kernels for 1%

profile of v8, /device:TPU:32, one launch (start us, length us, event | category | flops | bytes accessed | tf_op | source)
XLA Modules:
  0.0 165.9 jit_solution(7543656517998555597)
XLA Ops:
  6.5 0.0 all-gather.2.cloned.1.call-start
  6.5 2.2 %weigh.1 = (bf16[16,16,640]{2,1,0:T(8,128)(2,1)}, bf16[16,16,640]{2,1,0:T(8,128)(2,1)}) custom-call(s32[1]{0:T(128)} %bitcast.3.refs_0_, s32[64,80]{1,0:T(8,128)} %refs_1_.1, f32[1,16]{1,0:T(1,128)} %bitcast.17, bf16[16,10240]{1,0:T(8,128)(2,1)} %refs_3_.1), custom_call_target="tpu_custom_call" | custom-call | tf_op jit(solution)/shard_map/weigh/pallas_call | solution.py:208
  8.7 16.3 %all_to_all.15 = bf16[16,16,640]{2,1,0:T(8,128)(2,1)} all-to-all(bf16[16,16,640]{2,1,0:T(8,128)(2,1)} %get-tuple-element.12), channel_id=1, replica_groups=mesh['x'=4,'core'=2,'col'=16,'layer'=4] {'x','layer'}, dimensions={0} | all-to-all | bytes 655360 | tf_op jit(solution)/shard_map/all_to_all | solution.py:219
  25.0 0.0 all-gather.2.cloned.1.call-update
  25.1 37.6 %all_to_all.16 = bf16[16,16,640]{2,1,0:T(8,128)(2,1)S(1)} all-to-all(bf16[16,16,640]{2,1,0:T(8,128)(2,1)} %get-tuple-element.14), channel_id=1, replica_groups=mesh['x'=4,'core'=2,'col'=16,'layer'=4] {'col'}, dimensions={0} | all-to-all | bytes 655360 | tf_op jit(solution)/shard_map/all_to_all | solution.py:223
  62.7 0.9 broadcast_in_dim.11
  63.6 3.5 %all-to-all-start.2 = ((bf16[4,8,16,640]{3,2,1,0:T(8,128)(2,1)}), bf16[4,8,16,640]{3,2,1,0:T(8,128)(2,1)S(1)}, u32[]{:S(2)}, u32[]{:S(2)}) async-start(bf16[4,8,16,640]{3,2,1,0:T(8,128)(2,1)} %broadcast_in_dim.11), calls=%async_computation.2 | async-start | bytes 1310720 | tf_op jit(solution)/shard_map/all_to_all | solution.py:48
  67.0 2.2 %collective-permute-start.2 = (bf16[8,16,640]{2,1,0:T(8,128)(2,1)S(1)}, bf16[8,16,640]{2,1,0:T(8,128)(2,1)S(1)}, u32[]{:S(2)}, u32[]{:S(2)}) collective-permute-start(bf16[8,16,640]{2,1,0:T(8,128)(2,1)S(1)} %get-tuple-element.20), channel_id=1, source_target_pairs={{0,2},{1,3},{2,0},{3,1},{4,6},{5,7},{6,4},{7,5},{8,10},{9,11},{10,... | collective-permute-start | bytes 491528 | tf_op jit(solution)/shard_map/ppermute | solution.py:20
  69.3 2.2 %collective-permute-start = (bf16[8,16,640]{2,1,0:T(8,128)(2,1)S(1)}, bf16[8,16,640]{2,1,0:T(8,128)(2,1)S(1)}, u32[]{:S(2)}, u32[]{:S(2)}) collective-permute-start(bf16[8,16,640]{2,1,0:T(8,128)(2,1)S(1)} %get-tuple-element.20), channel_id=1, source_target_pairs={{0,1},{1,2},{2,3},{3,0},{4,5},{5,6},{6,7},{7,4},{8,9},{9,10},{10,1... | collective-permute-start | bytes 491528 | tf_op jit(solution)/shard_map/ppermute | solution.py:20
  71.5 4.8 %collective-permute-start.1 = (bf16[8,16,640]{2,1,0:T(8,128)(2,1)S(1)}, bf16[8,16,640]{2,1,0:T(8,128)(2,1)S(1)}, u32[]{:S(2)}, u32[]{:S(2)}) collective-permute-start(bf16[8,16,640]{2,1,0:T(8,128)(2,1)S(1)} %get-tuple-element.20), channel_id=1, source_target_pairs={{0,3},{1,0},{2,1},{3,2},{4,7},{5,4},{6,5},{7,6},{8,11},{9,8},{10,9... | collective-permute-start | bytes 491528 | tf_op jit(solution)/shard_map/ppermute | solution.py:20
  76.4 0.0 collective-permute-done.2
  76.4 1.3 collective-permute-done
  77.7 2.5 %collective-permute-done.1 = bf16[8,16,640]{2,1,0:T(8,128)(2,1)S(1)} collective-permute-done((bf16[8,16,640]{2,1,0:T(8,128)(2,1)S(1)}, bf16[8,16,640]{2,1,0:T(8,128)(2,1)S(1)}, u32[]{:S(2)}, u32[]{:S(2)}) %collective-permute-start.1) | collective-permute-done | bytes 163872 | tf_op jit(solution)/shard_map/ppermute | solution.py:20
  80.2 0.1 pad_maximum_fusion.refs_6_
  80.3 0.0 all-to-all-done.2.refs_2_
  80.3 5.0 %collective-permute-start.3 = (bf16[4,8,16,640]{3,2,1,0:T(8,128)(2,1)S(1)}, bf16[4,8,16,640]{3,2,1,0:T(8,128)(2,1)S(1)}, u32[]{:S(2)}, u32[]{:S(2)}) collective-permute-start(bf16[4,8,16,640]{3,2,1,0:T(8,128)(2,1)S(1)} %all-to-all-done.2.refs_2_), channel_id=1, source_target_pairs={{0,1},{1,2},{2,3},{3,0},{64,67},{65,64},{66,65},{67,66},{4,5},{5,6... | collective-permute-start | bytes 1966088 | tf_op jit(solution)/shard_map/ppermute | solution.py:40
  85.3 3.9 %collective-permute-start.6 = (bf16[4,8,16,640]{3,2,1,0:T(8,128)(2,1)S(1)}, bf16[4,8,16,640]{3,2,1,0:T(8,128)(2,1)S(1)}, u32[]{:S(2)}, u32[]{:S(2)}) collective-permute-start(bf16[4,8,16,640]{3,2,1,0:T(8,128)(2,1)S(1)} %pad_maximum_fusion.refs_6_), channel_id=1, source_target_pairs={{0,128},{128,256},{256,384},{384,0},{64,448},{192,64},{320,192},{4... | collective-permute-start | bytes 1966088 | tf_op jit(solution)/shard_map/ppermute | solution.py:40
  89.2 2.5 %collective-permute-start.4 = (bf16[4,8,16,640]{3,2,1,0:T(8,128)(2,1)S(1)}, bf16[4,8,16,640]{3,2,1,0:T(8,128)(2,1)S(1)}, u32[]{:S(2)}, u32[]{:S(2)}) collective-permute-start(bf16[4,8,16,640]{3,2,1,0:T(8,128)(2,1)S(1)} %all-to-all-done.2.refs_2_), channel_id=1, source_target_pairs={{0,3},{1,0},{2,1},{3,2},{64,65},{65,66},{66,67},{67,64},{4,7},{5,4... | collective-permute-start | bytes 1966088 | tf_op jit(solution)/shard_map/ppermute | solution.py:41
  91.7 3.1 %collective-permute-start.7 = (bf16[4,8,16,640]{3,2,1,0:T(8,128)(2,1)S(1)}, bf16[4,8,16,640]{3,2,1,0:T(8,128)(2,1)S(1)}, u32[]{:S(2)}, u32[]{:S(2)}) collective-permute-start(bf16[4,8,16,640]{3,2,1,0:T(8,128)(2,1)S(1)} %pad_maximum_fusion.refs_6_), channel_id=1, source_target_pairs={{0,384},{128,0},{256,128},{384,256},{64,192},{192,320},{320,448},{... | collective-permute-start | bytes 1966088 | tf_op jit(solution)/shard_map/ppermute | solution.py:41
  94.8 5.5 %collective-permute-done.3.refs_3_ = bf16[4,8,16,640]{3,2,1,0:T(8,128)(2,1)S(1)} collective-permute-done((bf16[4,8,16,640]{3,2,1,0:T(8,128)(2,1)S(1)}, bf16[4,8,16,640]{3,2,1,0:T(8,128)(2,1)S(1)}, u32[]{:S(2)}, u32[]{:S(2)}) %collective-permute-start.3) | collective-permute-done | bytes 655392 | tf_op jit(solution)/shard_map/ppermute | solution.py:40
  100.3 4.4 %collective-permute-start.5 = (bf16[4,8,16,640]{3,2,1,0:T(8,128)(2,1)S(1)}, bf16[4,8,16,640]{3,2,1,0:T(8,128)(2,1)S(1)}, u32[]{:S(2)}, u32[]{:S(2)}) collective-permute-start(bf16[4,8,16,640]{3,2,1,0:T(8,128)(2,1)S(1)} %collective-permute-done.3.refs_3_), channel_id=1, source_target_pairs={{0,1},{1,2},{2,3},{3,0},{64,67},{65,64},{66,65},{67,66},{4,5},{5,6... | collective-permute-start | bytes 1966088 | tf_op jit(solution)/shard_map/ppermute | solution.py:42
  104.7 0.9 collective-permute-done.6.refs_7_
  105.6 0.0 copy-start
  105.6 1.9 %collective-permute-start.8 = (bf16[4,8,16,640]{3,2,1,0:T(8,128)(2,1)S(1)}, bf16[4,8,16,640]{3,2,1,0:T(8,128)(2,1)}, u32[]{:S(2)}, u32[]{:S(2)}) collective-permute-start(bf16[4,8,16,640]{3,2,1,0:T(8,128)(2,1)S(1)} %collective-permute-done.6.refs_7_), channel_id=1, source_target_pairs={{0,128},{128,256},{256,384},{384,0},{64,448},{192,64},{320,192},{4... | collective-permute-start | bytes 1966088 | tf_op jit(solution)/shard_map/ppermute | solution.py:42
  107.6 0.1 pad_add_fusion.refs_0_
  107.6 0.0 collective-permute-done.4.refs_4_
  107.6 3.3 %collective-permute-done.7.refs_8_ = bf16[4,8,16,640]{3,2,1,0:T(8,128)(2,1)S(1)} collective-permute-done((bf16[4,8,16,640]{3,2,1,0:T(8,128)(2,1)S(1)}, bf16[4,8,16,640]{3,2,1,0:T(8,128)(2,1)S(1)}, u32[]{:S(2)}, u32[]{:S(2)}) %collective-permute-start.7) | collective-permute-done | bytes 655392 | tf_op jit(solution)/shard_map/ppermute | solution.py:41
  111.0 0.0 copy-start.1
  111.0 3.0 %collective-permute-done.5.refs_5_ = bf16[4,8,16,640]{3,2,1,0:T(8,128)(2,1)S(1)} collective-permute-done((bf16[4,8,16,640]{3,2,1,0:T(8,128)(2,1)S(1)}, bf16[4,8,16,640]{3,2,1,0:T(8,128)(2,1)S(1)}, u32[]{:S(2)}, u32[]{:S(2)}) %collective-permute-start.5) | collective-permute-done | bytes 655392 | tf_op jit(solution)/shard_map/ppermute | solution.py:42
  114.0 0.0 copy-done
  114.0 0.0 copy-done.1
  114.0 5.4 %collective-permute-done.8.refs_9_ = bf16[4,8,16,640]{3,2,1,0:T(8,128)(2,1)} collective-permute-done((bf16[4,8,16,640]{3,2,1,0:T(8,128)(2,1)S(1)}, bf16[4,8,16,640]{3,2,1,0:T(8,128)(2,1)}, u32[]{:S(2)}, u32[]{:S(2)}) %collective-permute-start.8) | collective-permute-done | bytes 655392 | tf_op jit(solution)/shard_map/ppermute | solution.py:42
  119.4 0.0 all-gather.2.cloned.1.call-done
  119.4 8.4 %gram.1 = (f32[320,640]{1,0:T(8,128)}, f32[320,640]{1,0:T(8,128)}) custom-call(s32[3]{0:T(128)S(1)} %pad_add_fusion.refs_0_, bf16[16,16,16,640]{3,2,1,0:T(8,128)(2,1)} %bitcast.18, bf16[4,8,16,640]{3,2,1,0:T(8,128)(2,1)S(1)} %all-to-all-done.2.refs_2_, bf16[4,8,16,640]{3,2,1,0:T(8,128)(2,1)S(1)} %collective-permute-done.3.refs_3_, ...), custom_call_target="tpu_custom_call" | custom-call | flops 3355443200 | bytes 10485760 | tf_op jit(solution)/shard_map/gram/pallas_call | solution.py:233
  127.8 1.9 %collective-permute-start.9 = (f32[320,640]{1,0:T(8,128)}, f32[320,640]{1,0:T(8,128)S(1)}, u32[]{:S(2)}, u32[]{:S(2)}) collective-permute-start(f32[320,640]{1,0:T(8,128)} %get-tuple-element.18), channel_id=1, source_target_pairs={{0,64},{64,0},{1,65},{65,1},{2,66},{66,2},{3,67},{67,3},{4,68},{68... | collective-permute-start | bytes 2457608 | tf_op jit(solution)/shard_map/ppermute | solution.py:259
  129.8 2.5 %collective-permute-done.9 = f32[320,640]{1,0:T(8,128)S(1)} collective-permute-done((f32[320,640]{1,0:T(8,128)}, f32[320,640]{1,0:T(8,128)S(1)}, u32[]{:S(2)}, u32[]{:S(2)}) %collective-permute-start.9) | collective-permute-done | bytes 819232 | tf_op jit(solution)/shard_map/ppermute | solution.py:259
  132.2 1.3 select_convert_fusion.own_ref
  133.6 1.9 %collective-permute-start.10 = (bf16[320,640]{1,0:T(8,128)(2,1)S(1)}, bf16[320,640]{1,0:T(8,128)(2,1)S(1)}, u32[]{:S(2)}, u32[]{:S(2)}) collective-permute-start(bf16[320,640]{1,0:T(8,128)(2,1)S(1)} %select_convert_fusion.own_ref), channel_id=1, source_target_pairs={{0,1},{1,2},{2,3},{3,0},{64,67},{65,64},{66,65},{67,66},{4,5},{5,6... | collective-permute-start | bytes 1228808 | tf_op jit(solution)/shard_map/ppermute | solution.py:40
  135.5 5.1 %collective-permute-start.11 = (bf16[320,640]{1,0:T(8,128)(2,1)S(1)}, bf16[320,640]{1,0:T(8,128)(2,1)S(1)}, u32[]{:S(2)}, u32[]{:S(2)}) collective-permute-start(bf16[320,640]{1,0:T(8,128)(2,1)S(1)} %select_convert_fusion.own_ref), channel_id=1, source_target_pairs={{0,3},{1,0},{2,1},{3,2},{64,65},{65,66},{66,67},{67,64},{4,7},{5,4... | collective-permute-start | bytes 1228808 | tf_op jit(solution)/shard_map/ppermute | solution.py:41
  140.6 6.6 %collective-permute-done.10.ahead_ref = bf16[320,640]{1,0:T(8,128)(2,1)S(1)} collective-permute-done((bf16[320,640]{1,0:T(8,128)(2,1)S(1)}, bf16[320,640]{1,0:T(8,128)(2,1)S(1)}, u32[]{:S(2)}, u32[]{:S(2)}) %collective-permute-start.10) | collective-permute-done | bytes 409632 | tf_op jit(solution)/shard_map/ppermute | solution.py:40
  147.3 1.9 %collective-permute-start.12 = (bf16[320,640]{1,0:T(8,128)(2,1)S(1)}, bf16[320,640]{1,0:T(8,128)(2,1)S(1)}, u32[]{:S(2)}, u32[]{:S(2)}) collective-permute-start(bf16[320,640]{1,0:T(8,128)(2,1)S(1)} %collective-permute-done.10.ahead_ref), channel_id=1, source_target_pairs={{0,1},{1,2},{2,3},{3,0},{64,67},{65,64},{66,65},{67,66},{4,5},{5,6... | collective-permute-start | bytes 1228808 | tf_op jit(solution)/shard_map/ppermute | solution.py:42
  149.2 0.0 collective-permute-done.11.behind_ref
  149.2 1.1 place.1.held_ref
  150.3 8.1 %collective-permute-done.12.across_ref = bf16[320,640]{1,0:T(8,128)(2,1)S(1)} collective-permute-done((bf16[320,640]{1,0:T(8,128)(2,1)S(1)}, bf16[320,640]{1,0:T(8,128)(2,1)S(1)}, u32[]{:S(2)}, u32[]{:S(2)}) %collective-permute-start.12) | collective-permute-done | bytes 409632 | tf_op jit(solution)/shard_map/ppermute | solution.py:42
  158.3 0.8 last.1
  (3 shorter events, 0.0 us)
Async XLA Ops:
  6.5 112.9 %all-gather.2.cloned.1.call-start = ((), (), s32[]{:S(2)}) async-start(), calls=%async_computation.3 | async-start | bytes 5570560 | tf_op jit(solution)/shard_map/all_gather | solution.py:221
  63.6 16.8 %all-to-all-start.2 = ((bf16[4,8,16,640]{3,2,1,0:T(8,128)(2,1)}), bf16[4,8,16,640]{3,2,1,0:T(8,128)(2,1)S(1)}, u32[]{:S(2)}, u32[]{:S(2)}) async-start(bf16[4,8,16,640]{3,2,1,0:T(8,128)(2,1)} %broadcast_in_dim.11), calls=%async_computation.2 | async-start | bytes 1310720 | tf_op jit(solution)/shard_map/all_to_all | solution.py:48
  67.0 9.3 %collective-permute-start.2 = (bf16[8,16,640]{2,1,0:T(8,128)(2,1)S(1)}, bf16[8,16,640]{2,1,0:T(8,128)(2,1)S(1)}, u32[]{:S(2)}, u32[]{:S(2)}) collective-permute-start(bf16[8,16,640]{2,1,0:T(8,128)(2,1)S(1)} %get-tuple-element.20), channel_id=1, source_target_pairs={{0,2},{1,3},{2,0},{3,1},{4,6},{5,7},{6,4},{7,5},{8,10},{9,11},{10,... | collective-permute-start | bytes 491528 | tf_op jit(solution)/shard_map/ppermute | solution.py:20
  69.3 8.4 %collective-permute-start = (bf16[8,16,640]{2,1,0:T(8,128)(2,1)S(1)}, bf16[8,16,640]{2,1,0:T(8,128)(2,1)S(1)}, u32[]{:S(2)}, u32[]{:S(2)}) collective-permute-start(bf16[8,16,640]{2,1,0:T(8,128)(2,1)S(1)} %get-tuple-element.20), channel_id=1, source_target_pairs={{0,1},{1,2},{2,3},{3,0},{4,5},{5,6},{6,7},{7,4},{8,9},{9,10},{10,1... | collective-permute-start | bytes 491528 | tf_op jit(solution)/shard_map/ppermute | solution.py:20
  71.5 8.7 %collective-permute-start.1 = (bf16[8,16,640]{2,1,0:T(8,128)(2,1)S(1)}, bf16[8,16,640]{2,1,0:T(8,128)(2,1)S(1)}, u32[]{:S(2)}, u32[]{:S(2)}) collective-permute-start(bf16[8,16,640]{2,1,0:T(8,128)(2,1)S(1)} %get-tuple-element.20), channel_id=1, source_target_pairs={{0,3},{1,0},{2,1},{3,2},{4,7},{5,4},{6,5},{7,6},{8,11},{9,8},{10,9... | collective-permute-start | bytes 491528 | tf_op jit(solution)/shard_map/ppermute | solution.py:20
  80.3 20.0 %collective-permute-start.3 = (bf16[4,8,16,640]{3,2,1,0:T(8,128)(2,1)S(1)}, bf16[4,8,16,640]{3,2,1,0:T(8,128)(2,1)S(1)}, u32[]{:S(2)}, u32[]{:S(2)}) collective-permute-start(bf16[4,8,16,640]{3,2,1,0:T(8,128)(2,1)S(1)} %all-to-all-done.2.refs_2_), channel_id=1, source_target_pairs={{0,1},{1,2},{2,3},{3,0},{64,67},{65,64},{66,65},{67,66},{4,5},{5,6... | collective-permute-start | bytes 1966088 | tf_op jit(solution)/shard_map/ppermute | solution.py:40
  85.3 20.3 %collective-permute-start.6 = (bf16[4,8,16,640]{3,2,1,0:T(8,128)(2,1)S(1)}, bf16[4,8,16,640]{3,2,1,0:T(8,128)(2,1)S(1)}, u32[]{:S(2)}, u32[]{:S(2)}) collective-permute-start(bf16[4,8,16,640]{3,2,1,0:T(8,128)(2,1)S(1)} %pad_maximum_fusion.refs_6_), channel_id=1, source_target_pairs={{0,128},{128,256},{256,384},{384,0},{64,448},{192,64},{320,192},{4... | collective-permute-start | bytes 1966088 | tf_op jit(solution)/shard_map/ppermute | solution.py:40
  89.2 18.4 %collective-permute-start.4 = (bf16[4,8,16,640]{3,2,1,0:T(8,128)(2,1)S(1)}, bf16[4,8,16,640]{3,2,1,0:T(8,128)(2,1)S(1)}, u32[]{:S(2)}, u32[]{:S(2)}) collective-permute-start(bf16[4,8,16,640]{3,2,1,0:T(8,128)(2,1)S(1)} %all-to-all-done.2.refs_2_), channel_id=1, source_target_pairs={{0,3},{1,0},{2,1},{3,2},{64,65},{65,66},{66,67},{67,64},{4,7},{5,4... | collective-permute-start | bytes 1966088 | tf_op jit(solution)/shard_map/ppermute | solution.py:41
  91.7 19.3 %collective-permute-start.7 = (bf16[4,8,16,640]{3,2,1,0:T(8,128)(2,1)S(1)}, bf16[4,8,16,640]{3,2,1,0:T(8,128)(2,1)S(1)}, u32[]{:S(2)}, u32[]{:S(2)}) collective-permute-start(bf16[4,8,16,640]{3,2,1,0:T(8,128)(2,1)S(1)} %pad_maximum_fusion.refs_6_), channel_id=1, source_target_pairs={{0,384},{128,0},{256,128},{384,256},{64,192},{192,320},{320,448},{... | collective-permute-start | bytes 1966088 | tf_op jit(solution)/shard_map/ppermute | solution.py:41
  100.3 13.7 %collective-permute-start.5 = (bf16[4,8,16,640]{3,2,1,0:T(8,128)(2,1)S(1)}, bf16[4,8,16,640]{3,2,1,0:T(8,128)(2,1)S(1)}, u32[]{:S(2)}, u32[]{:S(2)}) collective-permute-start(bf16[4,8,16,640]{3,2,1,0:T(8,128)(2,1)S(1)} %collective-permute-done.3.refs_3_), channel_id=1, source_target_pairs={{0,1},{1,2},{2,3},{3,0},{64,67},{65,64},{66,65},{67,66},{4,5},{5,6... | collective-permute-start | bytes 1966088 | tf_op jit(solution)/shard_map/ppermute | solution.py:42
  105.6 8.4 %copy-start = (bf16[4,8,16,640]{3,2,1,0:T(8,128)(2,1)}, bf16[4,8,16,640]{3,2,1,0:T(8,128)(2,1)S(1)}, u32[]{:S(2)}) copy-start(bf16[4,8,16,640]{3,2,1,0:T(8,128)(2,1)S(1)} %collective-permute-done.6.refs_7_) | copy-start | bytes 1966084
  105.6 13.8 %collective-permute-start.8 = (bf16[4,8,16,640]{3,2,1,0:T(8,128)(2,1)S(1)}, bf16[4,8,16,640]{3,2,1,0:T(8,128)(2,1)}, u32[]{:S(2)}, u32[]{:S(2)}) collective-permute-start(bf16[4,8,16,640]{3,2,1,0:T(8,128)(2,1)S(1)} %collective-permute-done.6.refs_7_), channel_id=1, source_target_pairs={{0,128},{128,256},{256,384},{384,0},{64,448},{192,64},{320,192},{4... | collective-permute-start | bytes 1966088 | tf_op jit(solution)/shard_map/ppermute | solution.py:42
  111.0 3.0 %copy-start.1 = (bf16[4,8,16,640]{3,2,1,0:T(8,128)(2,1)}, bf16[4,8,16,640]{3,2,1,0:T(8,128)(2,1)S(1)}, u32[]{:S(2)}) copy-start(bf16[4,8,16,640]{3,2,1,0:T(8,128)(2,1)S(1)} %collective-permute-done.7.refs_8_) | copy-start | bytes 1966084
  127.8 4.4 %collective-permute-start.9 = (f32[320,640]{1,0:T(8,128)}, f32[320,640]{1,0:T(8,128)S(1)}, u32[]{:S(2)}, u32[]{:S(2)}) collective-permute-start(f32[320,640]{1,0:T(8,128)} %get-tuple-element.18), channel_id=1, source_target_pairs={{0,64},{64,0},{1,65},{65,1},{2,66},{66,2},{3,67},{67,3},{4,68},{68... | collective-permute-start | bytes 2457608 | tf_op jit(solution)/shard_map/ppermute | solution.py:259
  133.6 13.7 %collective-permute-start.10 = (bf16[320,640]{1,0:T(8,128)(2,1)S(1)}, bf16[320,640]{1,0:T(8,128)(2,1)S(1)}, u32[]{:S(2)}, u32[]{:S(2)}) collective-permute-start(bf16[320,640]{1,0:T(8,128)(2,1)S(1)} %select_convert_fusion.own_ref), channel_id=1, source_target_pairs={{0,1},{1,2},{2,3},{3,0},{64,67},{65,64},{66,65},{67,66},{4,5},{5,6... | collective-permute-start | bytes 1228808 | tf_op jit(solution)/shard_map/ppermute | solution.py:40
  135.5 13.7 %collective-permute-start.11 = (bf16[320,640]{1,0:T(8,128)(2,1)S(1)}, bf16[320,640]{1,0:T(8,128)(2,1)S(1)}, u32[]{:S(2)}, u32[]{:S(2)}) collective-permute-start(bf16[320,640]{1,0:T(8,128)(2,1)S(1)} %select_convert_fusion.own_ref), channel_id=1, source_target_pairs={{0,3},{1,0},{2,1},{3,2},{64,65},{65,66},{66,67},{67,64},{4,7},{5,4... | collective-permute-start | bytes 1228808 | tf_op jit(solution)/shard_map/ppermute | solution.py:41
  147.3 11.0 %collective-permute-start.12 = (bf16[320,640]{1,0:T(8,128)(2,1)S(1)}, bf16[320,640]{1,0:T(8,128)(2,1)S(1)}, u32[]{:S(2)}, u32[]{:S(2)}) collective-permute-start(bf16[320,640]{1,0:T(8,128)(2,1)S(1)} %collective-permute-done.10.ahead_ref), channel_id=1, source_target_pairs={{0,1},{1,2},{2,3},{3,0},{64,67},{65,64},{66,65},{67,66},{4,5},{5,6... | collective-permute-start | bytes 1228808 | tf_op jit(solution)/shard_map/ppermute | solution.py:42
Sparse Core Ops, SparseCore 0:
  25.2 90.5 all-gather.1

commit v9 on v8

--- a/solution.py
+++ b/solution.py
@@ -49,39 +49,46 @@
 
 
 SHIFTS = (0, 1, 3, 2)
-GROUP = 4
-
-
-def weigh_kernel(owned, nz, place_ref, pattern_ref, weight_ref, block_ref, by_col_ref, by_chip_ref):
+GROUP = 8
+
+
+def strips(nz, place_ref, pattern_ref, weight_ref, block_ref):
     lanes = 128
+    owned, reads = block_ref.shape
     row = place_ref[0]
     diagonal = lax.broadcasted_iota(jnp.int32, (owned, owned), 0) == lax.broadcasted_iota(
         jnp.int32, (owned, owned), 1
     )
     spread_weight = jnp.broadcast_to(weight_ref[...], (owned, owned))
     weight = jnp.sum(jnp.where(diagonal, spread_weight, 0.0), axis=1, keepdims=True)
-    width = by_col_ref.shape[2]
-    count = width // lanes
-    chips, _, tile = by_chip_ref.shape
-    half = tile // 2
-    strips = []
+    count = reads // nz // lanes
     for z in range(nz):
         parts = []
-        for i in range(count):
-            j = z * count + i
+        for j in range(z * count, (z + 1) * count):
             flag = pattern_ref[row, j].astype(jnp.float32)
             block = block_ref[:, j * lanes : (j + 1) * lanes].astype(jnp.float32)
             parts.append((block * weight * flag).astype(jnp.bfloat16))
-        strip = jnp.concatenate(parts, 1)
-        by_col_ref[z] = strip
-        strips.append(strip)
-    for x in range(4):
-        for core in range(2):
-            pair = jnp.concatenate(strips[x * 4 + core * 2 : x * 4 + core * 2 + 2], 1)
-            for y in range(4):
-                by_chip_ref[x * 4 + y, :, core * half : (core + 1) * half] = pair[
-                    :, y * half : (y + 1) * half
-                ]
+        yield jnp.concatenate(parts, 1)
+
+
+def cols_kernel(nz, place_ref, pattern_ref, weight_ref, block_ref, out_ref):
+    for z, strip in enumerate(strips(nz, place_ref, pattern_ref, weight_ref, block_ref)):
+        out_ref[z] = strip
+
+
+def chips_kernel(nz, place_ref, pattern_ref, weight_ref, block_ref, out_ref):
+    half = out_ref.shape[2] // 2
+    held = []
+    for z, strip in enumerate(strips(nz, place_ref, pattern_ref, weight_ref, block_ref)):
+        held.append(strip)
+        if z % 2 == 0:
+            continue
+        pair = jnp.concatenate(held[-2:], 1)
+        x, core = z // 4, z // 2 % 2
+        for y in range(4):
+            out_ref[x * 4 + y, :, core * half : (core + 1) * half] = pair[
+                :, y * half : (y + 1) * half
+            ]
 
 
 def gram_kernel(half, steps, place_ref, rows_ref, *refs):
@@ -205,21 +212,27 @@
     tile = nc * half
     chips = nx * ny
     block_row = jnp.reshape(owner * owned // 128, (1,)).astype(jnp.int32)
-    by_col, by_chip = pl.pallas_call(
-        lambda *refs: weigh_kernel(owned, nz, *refs),
-        out_shape=(
-            jax.ShapeDtypeStruct((nz, owned, width), jnp.bfloat16),
-            jax.ShapeDtypeStruct((chips, owned, tile), jnp.bfloat16),
-        ),
-        in_specs=[SMEM, SMEM, VMEM, VMEM],
-        out_specs=(VMEM, VMEM),
-        compiler_params=pltpu.CompilerParams(vmem_limit_bytes=58 << 20),
-        name="weigh",
-    )(block_row, pattern, idf_weight.reshape(1, owned), occurrences)
+    by_col, by_chip = [
+        pl.pallas_call(
+            lambda *refs, kernel=kernel: kernel(nz, *refs),
+            out_shape=jax.ShapeDtypeStruct((count, owned, across), jnp.bfloat16),
+            in_specs=[SMEM, SMEM, VMEM, VMEM],
+            out_specs=VMEM,
+            compiler_params=pltpu.CompilerParams(vmem_limit_bytes=58 << 20),
+            cost_estimate=pl.CostEstimate(
+                flops=4 * owned * reads, bytes_accessed=4 * owned * reads, transcendentals=0
+            ),
+            name=name,
+        )(block_row, pattern, idf_weight.reshape(1, owned), occurrences)
+        for kernel, count, across, name in (
+            (cols_kernel, nz, width, "weigh_cols"),
+            (chips_kernel, chips, tile, "weigh_chips"),
+        )
+    ]
     own = lax.all_to_all(by_chip, ("x", "layer"), split_axis=0, concat_axis=0, tiled=True)
     own = own.reshape(chips * owned, tile)
+    by_col, own = lax.optimization_barrier((by_col, own))
     rows = lax.all_gather(own, "col", axis=0, tiled=True).reshape(nz, chips, owned, tile)
-    by_col, own = lax.optimization_barrier((by_col, own))
     part = lax.all_to_all(by_col, "col", split_axis=0, concat_axis=0, tiled=True)
     upper, lower = part[: nz // 2], part[nz // 2 :]
     along_x = collect(upper, "x", nx)

time: 167 us -> 167 us (level)
  blocking collectives: 53.9 us -> 37.6 us
  starting transfers between devices: 44.4 us -> 51.4 us
  waiting for transfers between devices: 39.3 us -> 46.3 us
  Pallas kernels: 12.4 us -> 14.3 us
    all_to_all x1 -> x0, blocking collectives: 16.3 us -> none  [body(): lax.all_to_all(by_chip, ('x', 'layer'), split_axis=0, concat_axis=0, tile...]
    all_to_all x0 -> x1, starting transfers between devices: none -> 7.03 us  [body(): lax.all_to_all(by_chip, ('x', 'layer'), split_axis=0, concat_axis=0, tile...]
    all_to_all x0 -> x1, waiting for transfers between devices: none -> 7.01 us  [body(): lax.all_to_all(by_chip, ('x', 'layer'), split_axis=0, concat_axis=0, tile...]
    pallas_call x1 -> x2, Pallas kernels: 2.21 us -> 4.27 us  [body(): pl.pallas_call(lambda *refs, kernel=kernel: kernel(nz, *refs), out_shape=...]
  transfers between devices with their start and end apart: 15 -> 16, of which waited for: 10 -> 11; matrix products, arithmetic and copies ran while one was open for 1% -> 1% of each run, Pallas kernels for 1% -> 2%
where the time goes in v9:
time: 167 us; the launch traced here: 166 us
  starting transfers between devices  51.4 us (31%)
  waiting for transfers between devices  46.3 us (28%)
  blocking collectives  37.6 us (23%)
  Pallas kernels  14.3 us (9%)
  between operations  13.6 us (8%)
  local copies, waits for them, and re-layouts  1.68 us (1%)
    all_to_all x1, blocking collectives, body(): lax.all_to_all(by_col, 'col', split_axis=0, concat_axis=0, tiled=True)  37.6 us
    ppermute x3, waiting for transfers between devices, relay(): across = [lax.ppermute(v, g, w[0]) for v, (g, w) in zip(ahead, plans)]  16.5 us
    ppermute x3, waiting for transfers between devices, relay(): ahead = [lax.ppermute(v, g, w[0]) for v, (g, w) in zip(values, plans)]  13.1 us
    ppermute x3, starting transfers between devices, relay(): ahead = [lax.ppermute(v, g, w[0]) for v, (g, w) in zip(values, plans)]  10.8 us
    ppermute x3, starting transfers between devices, relay(): behind = [lax.ppermute(v, g, w[1]) for v, (g, w) in zip(values, plans)]  10.7 us
    ppermute x3, starting transfers between devices, spread(): lax.ppermute(value, axis, around(n, s))  9.28 us
    ppermute x3, starting transfers between devices, relay(): across = [lax.ppermute(v, g, w[0]) for v, (g, w) in zip(ahead, plans)]  8.2 us
    pallas_call x1, Pallas kernels, body(): pl.pallas_call(lambda *refs: gram_kernel(half, steps, *refs), out_shape=(...  8.19 us
  transfers between devices with their start and end apart: 16, of which 11 were waited for; matrix products, arithmetic and copies ran while one was open for 1% of the time, Pallas kernels for 2%

profile of v9, /device:TPU:32, one launch (start us, length us, event | category | flops | bytes accessed | tf_op | source)
XLA Modules:
  0.0 166.3 jit_solution(16994295096453514070)
XLA Ops:
  6.5 2.2 %weigh_chips.1 = bf16[16,16,640]{2,1,0:T(8,128)(2,1)} custom-call(s32[1]{0:T(128)} %bitcast.3.refs_0_, s32[64,80]{1,0:T(8,128)} %refs_1_.3, f32[1,16]{1,0:T(1,128)} %bitcast.17, bf16[16,10240]{1,0:T(8,128)(2,1)} %refs_3_.3), custom_call_target="tpu_custom_call" | custom-call | flops 655360 | bytes 655360 | tf_op jit(solution)/shard_map/weigh_chips/pallas_call | solution.py:216
  8.7 7.0 %all-to-all-start = ((bf16[16,16,640]{2,1,0:T(8,128)(2,1)}), bf16[16,16,640]{2,1,0:T(8,128)(2,1)S(1)}, u32[]{:S(2)}, u32[]{:S(2)}) async-start(bf16[16,16,640]{2,1,0:T(8,128)(2,1)} %weigh_chips.1), calls=%async_computation | async-start | bytes 655360 | tf_op jit(solution)/shard_map/all_to_all | solution.py:232
  15.7 0.0 all-gather.2.cloned.1.call-start
  15.8 2.1 %weigh_cols.1 = bf16[16,16,640]{2,1,0:T(8,128)(2,1)} custom-call(s32[1]{0:T(128)} %bitcast.3.refs_0_, s32[64,80]{1,0:T(8,128)} %refs_1_.3, f32[1,16]{1,0:T(1,128)} %bitcast.18, bf16[16,10240]{1,0:T(8,128)(2,1)} %refs_3_.3), custom_call_target="tpu_custom_call" | custom-call | flops 655360 | bytes 655360 | tf_op jit(solution)/shard_map/weigh_cols/pallas_call | solution.py:216
  17.9 7.0 %all-to-all-done = bf16[16,16,640]{2,1,0:T(8,128)(2,1)S(1)} async-done(((bf16[16,16,640]{2,1,0:T(8,128)(2,1)}), bf16[16,16,640]{2,1,0:T(8,128)(2,1)S(1)}, u32[]{:S(2)}, u32[]{:S(2)}) %all-to-all-start) | async-done | bytes 327712 | tf_op jit(solution)/shard_map/all_to_all | solution.py:232
  24.9 0.0 copy-start
  24.9 0.7 copy-done
  25.7 0.0 all-gather.2.cloned.1.call-update
  25.7 37.6 %all_to_all.15 = bf16[16,16,640]{2,1,0:T(8,128)(2,1)S(1)} all-to-all(bf16[16,16,640]{2,1,0:T(8,128)(2,1)} %weigh_cols.1), channel_id=1, replica_groups=mesh['x'=4,'core'=2,'col'=16,'layer'=4] {'col'}, dimensions={0} | all-to-all | bytes 655360 | tf_op jit(solution)/shard_map/all_to_all | solution.py:236
  63.3 0.9 broadcast_in_dim.11
  64.2 3.5 %all-to-all-start.2 = ((bf16[4,8,16,640]{3,2,1,0:T(8,128)(2,1)}), bf16[4,8,16,640]{3,2,1,0:T(8,128)(2,1)S(1)}, u32[]{:S(2)}, u32[]{:S(2)}) async-start(bf16[4,8,16,640]{3,2,1,0:T(8,128)(2,1)} %broadcast_in_dim.11), calls=%async_computation.2 | async-start | bytes 1310720 | tf_op jit(solution)/shard_map/all_to_all | solution.py:48
  67.7 2.2 %collective-permute-start.2 = (bf16[8,16,640]{2,1,0:T(8,128)(2,1)S(1)}, bf16[8,16,640]{2,1,0:T(8,128)(2,1)S(1)}, u32[]{:S(2)}, u32[]{:S(2)}) collective-permute-start(bf16[8,16,640]{2,1,0:T(8,128)(2,1)S(1)} %get-tuple-element.18), channel_id=1, source_target_pairs={{0,2},{1,3},{2,0},{3,1},{4,6},{5,7},{6,4},{7,5},{8,10},{9,11},{10,... | collective-permute-start | bytes 491528 | tf_op jit(solution)/shard_map/ppermute | solution.py:20
  69.9 2.2 %collective-permute-start = (bf16[8,16,640]{2,1,0:T(8,128)(2,1)S(1)}, bf16[8,16,640]{2,1,0:T(8,128)(2,1)S(1)}, u32[]{:S(2)}, u32[]{:S(2)}) collective-permute-start(bf16[8,16,640]{2,1,0:T(8,128)(2,1)S(1)} %get-tuple-element.18), channel_id=1, source_target_pairs={{0,1},{1,2},{2,3},{3,0},{4,5},{5,6},{6,7},{7,4},{8,9},{9,10},{10,1... | collective-permute-start | bytes 491528 | tf_op jit(solution)/shard_map/ppermute | solution.py:20
  72.1 4.8 %collective-permute-start.1 = (bf16[8,16,640]{2,1,0:T(8,128)(2,1)S(1)}, bf16[8,16,640]{2,1,0:T(8,128)(2,1)S(1)}, u32[]{:S(2)}, u32[]{:S(2)}) collective-permute-start(bf16[8,16,640]{2,1,0:T(8,128)(2,1)S(1)} %get-tuple-element.18), channel_id=1, source_target_pairs={{0,3},{1,0},{2,1},{3,2},{4,7},{5,4},{6,5},{7,6},{8,11},{9,8},{10,9... | collective-permute-start | bytes 491528 | tf_op jit(solution)/shard_map/ppermute | solution.py:20
  77.0 0.0 collective-permute-done.2
  77.0 1.3 collective-permute-done
  78.3 2.5 %collective-permute-done.1 = bf16[8,16,640]{2,1,0:T(8,128)(2,1)S(1)} collective-permute-done((bf16[8,16,640]{2,1,0:T(8,128)(2,1)S(1)}, bf16[8,16,640]{2,1,0:T(8,128)(2,1)S(1)}, u32[]{:S(2)}, u32[]{:S(2)}) %collective-permute-start.1) | collective-permute-done | bytes 163872 | tf_op jit(solution)/shard_map/ppermute | solution.py:20
  80.8 0.1 pad_maximum_fusion.refs_6_
  80.9 0.0 all-to-all-done.2.refs_2_
  80.9 5.0 %collective-permute-start.3 = (bf16[4,8,16,640]{3,2,1,0:T(8,128)(2,1)S(1)}, bf16[4,8,16,640]{3,2,1,0:T(8,128)(2,1)S(1)}, u32[]{:S(2)}, u32[]{:S(2)}) collective-permute-start(bf16[4,8,16,640]{3,2,1,0:T(8,128)(2,1)S(1)} %all-to-all-done.2.refs_2_), channel_id=1, source_target_pairs={{0,1},{1,2},{2,3},{3,0},{64,67},{65,64},{66,65},{67,66},{4,5},{5,6... | collective-permute-start | bytes 1966088 | tf_op jit(solution)/shard_map/ppermute | solution.py:40
  85.9 3.9 %collective-permute-start.6 = (bf16[4,8,16,640]{3,2,1,0:T(8,128)(2,1)S(1)}, bf16[4,8,16,640]{3,2,1,0:T(8,128)(2,1)S(1)}, u32[]{:S(2)}, u32[]{:S(2)}) collective-permute-start(bf16[4,8,16,640]{3,2,1,0:T(8,128)(2,1)S(1)} %pad_maximum_fusion.refs_6_), channel_id=1, source_target_pairs={{0,128},{128,256},{256,384},{384,0},{64,448},{192,64},{320,192},{4... | collective-permute-start | bytes 1966088 | tf_op jit(solution)/shard_map/ppermute | solution.py:40
  89.8 2.5 %collective-permute-start.4 = (bf16[4,8,16,640]{3,2,1,0:T(8,128)(2,1)S(1)}, bf16[4,8,16,640]{3,2,1,0:T(8,128)(2,1)S(1)}, u32[]{:S(2)}, u32[]{:S(2)}) collective-permute-start(bf16[4,8,16,640]{3,2,1,0:T(8,128)(2,1)S(1)} %all-to-all-done.2.refs_2_), channel_id=1, source_target_pairs={{0,3},{1,0},{2,1},{3,2},{64,65},{65,66},{66,67},{67,64},{4,7},{5,4... | collective-permute-start | bytes 1966088 | tf_op jit(solution)/shard_map/ppermute | solution.py:41
  92.3 3.1 %collective-permute-start.7 = (bf16[4,8,16,640]{3,2,1,0:T(8,128)(2,1)S(1)}, bf16[4,8,16,640]{3,2,1,0:T(8,128)(2,1)S(1)}, u32[]{:S(2)}, u32[]{:S(2)}) collective-permute-start(bf16[4,8,16,640]{3,2,1,0:T(8,128)(2,1)S(1)} %pad_maximum_fusion.refs_6_), channel_id=1, source_target_pairs={{0,384},{128,0},{256,128},{384,256},{64,192},{192,320},{320,448},{... | collective-permute-start | bytes 1966088 | tf_op jit(solution)/shard_map/ppermute | solution.py:41
  95.4 5.5 %collective-permute-done.3.refs_3_ = bf16[4,8,16,640]{3,2,1,0:T(8,128)(2,1)S(1)} collective-permute-done((bf16[4,8,16,640]{3,2,1,0:T(8,128)(2,1)S(1)}, bf16[4,8,16,640]{3,2,1,0:T(8,128)(2,1)S(1)}, u32[]{:S(2)}, u32[]{:S(2)}) %collective-permute-start.3) | collective-permute-done | bytes 655392 | tf_op jit(solution)/shard_map/ppermute | solution.py:40
  100.9 4.4 %collective-permute-start.5 = (bf16[4,8,16,640]{3,2,1,0:T(8,128)(2,1)S(1)}, bf16[4,8,16,640]{3,2,1,0:T(8,128)(2,1)S(1)}, u32[]{:S(2)}, u32[]{:S(2)}) collective-permute-start(bf16[4,8,16,640]{3,2,1,0:T(8,128)(2,1)S(1)} %collective-permute-done.3.refs_3_), channel_id=1, source_target_pairs={{0,1},{1,2},{2,3},{3,0},{64,67},{65,64},{66,65},{67,66},{4,5},{5,6... | collective-permute-start | bytes 1966088 | tf_op jit(solution)/shard_map/ppermute | solution.py:42
  105.3 0.9 collective-permute-done.6.refs_7_
  106.2 0.0 copy-start.1
  106.2 1.9 %collective-permute-start.8 = (bf16[4,8,16,640]{3,2,1,0:T(8,128)(2,1)S(1)}, bf16[4,8,16,640]{3,2,1,0:T(8,128)(2,1)}, u32[]{:S(2)}, u32[]{:S(2)}) collective-permute-start(bf16[4,8,16,640]{3,2,1,0:T(8,128)(2,1)S(1)} %collective-permute-done.6.refs_7_), channel_id=1, source_target_pairs={{0,128},{128,256},{256,384},{384,0},{64,448},{192,64},{320,192},{4... | collective-permute-start | bytes 1966088 | tf_op jit(solution)/shard_map/ppermute | solution.py:42
  108.2 0.1 pad_add_fusion.refs_0_
  108.2 0.0 collective-permute-done.4.refs_4_
  108.2 3.3 %collective-permute-done.7.refs_8_ = bf16[4,8,16,640]{3,2,1,0:T(8,128)(2,1)S(1)} collective-permute-done((bf16[4,8,16,640]{3,2,1,0:T(8,128)(2,1)S(1)}, bf16[4,8,16,640]{3,2,1,0:T(8,128)(2,1)S(1)}, u32[]{:S(2)}, u32[]{:S(2)}) %collective-permute-start.7) | collective-permute-done | bytes 655392 | tf_op jit(solution)/shard_map/ppermute | solution.py:41
  111.6 0.0 copy-start.2
  111.6 3.0 %collective-permute-done.5.refs_5_ = bf16[4,8,16,640]{3,2,1,0:T(8,128)(2,1)S(1)} collective-permute-done((bf16[4,8,16,640]{3,2,1,0:T(8,128)(2,1)S(1)}, bf16[4,8,16,640]{3,2,1,0:T(8,128)(2,1)S(1)}, u32[]{:S(2)}, u32[]{:S(2)}) %collective-permute-start.5) | collective-permute-done | bytes 655392 | tf_op jit(solution)/shard_map/ppermute | solution.py:42
  114.6 0.0 copy-done.1
  114.6 0.0 copy-done.2
  114.6 5.4 %collective-permute-done.8.refs_9_ = bf16[4,8,16,640]{3,2,1,0:T(8,128)(2,1)} collective-permute-done((bf16[4,8,16,640]{3,2,1,0:T(8,128)(2,1)S(1)}, bf16[4,8,16,640]{3,2,1,0:T(8,128)(2,1)}, u32[]{:S(2)}, u32[]{:S(2)}) %collective-permute-start.8) | collective-permute-done | bytes 655392 | tf_op jit(solution)/shard_map/ppermute | solution.py:42
  120.0 0.0 all-gather.2.cloned.1.call-done
  120.0 8.2 %gram.1 = (f32[320,640]{1,0:T(8,128)}, f32[320,640]{1,0:T(8,128)}) custom-call(s32[3]{0:T(128)S(1)} %pad_add_fusion.refs_0_, bf16[16,16,16,640]{3,2,1,0:T(8,128)(2,1)} %bitcast.19, bf16[4,8,16,640]{3,2,1,0:T(8,128)(2,1)S(1)} %all-to-all-done.2.refs_2_, bf16[4,8,16,640]{3,2,1,0:T(8,128)(2,1)S(1)} %collective-permute-done.3.refs_3_, ...), custom_call_target="tpu_custom_call" | custom-call | flops 3355443200 | bytes 10485760 | tf_op jit(solution)/shard_map/gram/pallas_call | solution.py:246
  128.2 1.9 %collective-permute-start.9 = (f32[320,640]{1,0:T(8,128)}, f32[320,640]{1,0:T(8,128)S(1)}, u32[]{:S(2)}, u32[]{:S(2)}) collective-permute-start(f32[320,640]{1,0:T(8,128)} %get-tuple-element.16), channel_id=1, source_target_pairs={{0,64},{64,0},{1,65},{65,1},{2,66},{66,2},{3,67},{67,3},{4,68},{68... | collective-permute-start | bytes 2457608 | tf_op jit(solution)/shard_map/ppermute | solution.py:272
  130.2 2.5 %collective-permute-done.9 = f32[320,640]{1,0:T(8,128)S(1)} collective-permute-done((f32[320,640]{1,0:T(8,128)}, f32[320,640]{1,0:T(8,128)S(1)}, u32[]{:S(2)}, u32[]{:S(2)}) %collective-permute-start.9) | collective-permute-done | bytes 819232 | tf_op jit(solution)/shard_map/ppermute | solution.py:272
  132.6 1.3 select_convert_fusion.own_ref
  134.0 1.9 %collective-permute-start.10 = (bf16[320,640]{1,0:T(8,128)(2,1)S(1)}, bf16[320,640]{1,0:T(8,128)(2,1)S(1)}, u32[]{:S(2)}, u32[]{:S(2)}) collective-permute-start(bf16[320,640]{1,0:T(8,128)(2,1)S(1)} %select_convert_fusion.own_ref), channel_id=1, source_target_pairs={{0,1},{1,2},{2,3},{3,0},{64,67},{65,64},{66,65},{67,66},{4,5},{5,6... | collective-permute-start | bytes 1228808 | tf_op jit(solution)/shard_map/ppermute | solution.py:40
  135.9 5.1 %collective-permute-start.11 = (bf16[320,640]{1,0:T(8,128)(2,1)S(1)}, bf16[320,640]{1,0:T(8,128)(2,1)S(1)}, u32[]{:S(2)}, u32[]{:S(2)}) collective-permute-start(bf16[320,640]{1,0:T(8,128)(2,1)S(1)} %select_convert_fusion.own_ref), channel_id=1, source_target_pairs={{0,3},{1,0},{2,1},{3,2},{64,65},{65,66},{66,67},{67,64},{4,7},{5,4... | collective-permute-start | bytes 1228808 | tf_op jit(solution)/shard_map/ppermute | solution.py:41
  141.0 6.6 %collective-permute-done.10.ahead_ref = bf16[320,640]{1,0:T(8,128)(2,1)S(1)} collective-permute-done((bf16[320,640]{1,0:T(8,128)(2,1)S(1)}, bf16[320,640]{1,0:T(8,128)(2,1)S(1)}, u32[]{:S(2)}, u32[]{:S(2)}) %collective-permute-start.10) | collective-permute-done | bytes 409632 | tf_op jit(solution)/shard_map/ppermute | solution.py:40
  147.7 1.9 %collective-permute-start.12 = (bf16[320,640]{1,0:T(8,128)(2,1)S(1)}, bf16[320,640]{1,0:T(8,128)(2,1)S(1)}, u32[]{:S(2)}, u32[]{:S(2)}) collective-permute-start(bf16[320,640]{1,0:T(8,128)(2,1)S(1)} %collective-permute-done.10.ahead_ref), channel_id=1, source_target_pairs={{0,1},{1,2},{2,3},{3,0},{64,67},{65,64},{66,65},{67,66},{4,5},{5,6... | collective-permute-start | bytes 1228808 | tf_op jit(solution)/shard_map/ppermute | solution.py:42
  149.6 0.0 collective-permute-done.11.behind_ref
  149.6 1.1 place.1.held_ref
  150.7 8.1 %collective-permute-done.12.across_ref = bf16[320,640]{1,0:T(8,128)(2,1)S(1)} collective-permute-done((bf16[320,640]{1,0:T(8,128)(2,1)S(1)}, bf16[320,640]{1,0:T(8,128)(2,1)S(1)}, u32[]{:S(2)}, u32[]{:S(2)}) %collective-permute-start.12) | collective-permute-done | bytes 409632 | tf_op jit(solution)/shard_map/ppermute | solution.py:42
  158.7 0.8 last.1
  (3 shorter events, 0.0 us)
Async XLA Ops:
  8.7 16.2 %all-to-all-start = ((bf16[16,16,640]{2,1,0:T(8,128)(2,1)}), bf16[16,16,640]{2,1,0:T(8,128)(2,1)S(1)}, u32[]{:S(2)}, u32[]{:S(2)}) async-start(bf16[16,16,640]{2,1,0:T(8,128)(2,1)} %weigh_chips.1), calls=%async_computation | async-start | bytes 655360 | tf_op jit(solution)/shard_map/all_to_all | solution.py:232
  15.7 104.3 %all-gather.2.cloned.1.call-start = ((), (), s32[]{:S(2)}) async-start(), calls=%async_computation.3 | async-start | bytes 5570560 | tf_op jit(solution)/shard_map/all_gather | solution.py:235
  24.9 0.7 copy-start
  64.2 16.8 %all-to-all-start.2 = ((bf16[4,8,16,640]{3,2,1,0:T(8,128)(2,1)}), bf16[4,8,16,640]{3,2,1,0:T(8,128)(2,1)S(1)}, u32[]{:S(2)}, u32[]{:S(2)}) async-start(bf16[4,8,16,640]{3,2,1,0:T(8,128)(2,1)} %broadcast_in_dim.11), calls=%async_computation.2 | async-start | bytes 1310720 | tf_op jit(solution)/shard_map/all_to_all | solution.py:48
  67.7 9.3 %collective-permute-start.2 = (bf16[8,16,640]{2,1,0:T(8,128)(2,1)S(1)}, bf16[8,16,640]{2,1,0:T(8,128)(2,1)S(1)}, u32[]{:S(2)}, u32[]{:S(2)}) collective-permute-start(bf16[8,16,640]{2,1,0:T(8,128)(2,1)S(1)} %get-tuple-element.18), channel_id=1, source_target_pairs={{0,2},{1,3},{2,0},{3,1},{4,6},{5,7},{6,4},{7,5},{8,10},{9,11},{10,... | collective-permute-start | bytes 491528 | tf_op jit(solution)/shard_map/ppermute | solution.py:20
  69.9 8.4 %collective-permute-start = (bf16[8,16,640]{2,1,0:T(8,128)(2,1)S(1)}, bf16[8,16,640]{2,1,0:T(8,128)(2,1)S(1)}, u32[]{:S(2)}, u32[]{:S(2)}) collective-permute-start(bf16[8,16,640]{2,1,0:T(8,128)(2,1)S(1)} %get-tuple-element.18), channel_id=1, source_target_pairs={{0,1},{1,2},{2,3},{3,0},{4,5},{5,6},{6,7},{7,4},{8,9},{9,10},{10,1... | collective-permute-start | bytes 491528 | tf_op jit(solution)/shard_map/ppermute | solution.py:20
  72.1 8.7 %collective-permute-start.1 = (bf16[8,16,640]{2,1,0:T(8,128)(2,1)S(1)}, bf16[8,16,640]{2,1,0:T(8,128)(2,1)S(1)}, u32[]{:S(2)}, u32[]{:S(2)}) collective-permute-start(bf16[8,16,640]{2,1,0:T(8,128)(2,1)S(1)} %get-tuple-element.18), channel_id=1, source_target_pairs={{0,3},{1,0},{2,1},{3,2},{4,7},{5,4},{6,5},{7,6},{8,11},{9,8},{10,9... | collective-permute-start | bytes 491528 | tf_op jit(solution)/shard_map/ppermute | solution.py:20
  80.9 20.0 %collective-permute-start.3 = (bf16[4,8,16,640]{3,2,1,0:T(8,128)(2,1)S(1)}, bf16[4,8,16,640]{3,2,1,0:T(8,128)(2,1)S(1)}, u32[]{:S(2)}, u32[]{:S(2)}) collective-permute-start(bf16[4,8,16,640]{3,2,1,0:T(8,128)(2,1)S(1)} %all-to-all-done.2.refs_2_), channel_id=1, source_target_pairs={{0,1},{1,2},{2,3},{3,0},{64,67},{65,64},{66,65},{67,66},{4,5},{5,6... | collective-permute-start | bytes 1966088 | tf_op jit(solution)/shard_map/ppermute | solution.py:40
  85.9 20.3 %collective-permute-start.6 = (bf16[4,8,16,640]{3,2,1,0:T(8,128)(2,1)S(1)}, bf16[4,8,16,640]{3,2,1,0:T(8,128)(2,1)S(1)}, u32[]{:S(2)}, u32[]{:S(2)}) collective-permute-start(bf16[4,8,16,640]{3,2,1,0:T(8,128)(2,1)S(1)} %pad_maximum_fusion.refs_6_), channel_id=1, source_target_pairs={{0,128},{128,256},{256,384},{384,0},{64,448},{192,64},{320,192},{4... | collective-permute-start | bytes 1966088 | tf_op jit(solution)/shard_map/ppermute | solution.py:40
  89.8 18.4 %collective-permute-start.4 = (bf16[4,8,16,640]{3,2,1,0:T(8,128)(2,1)S(1)}, bf16[4,8,16,640]{3,2,1,0:T(8,128)(2,1)S(1)}, u32[]{:S(2)}, u32[]{:S(2)}) collective-permute-start(bf16[4,8,16,640]{3,2,1,0:T(8,128)(2,1)S(1)} %all-to-all-done.2.refs_2_), channel_id=1, source_target_pairs={{0,3},{1,0},{2,1},{3,2},{64,65},{65,66},{66,67},{67,64},{4,7},{5,4... | collective-permute-start | bytes 1966088 | tf_op jit(solution)/shard_map/ppermute | solution.py:41
  92.3 19.3 %collective-permute-start.7 = (bf16[4,8,16,640]{3,2,1,0:T(8,128)(2,1)S(1)}, bf16[4,8,16,640]{3,2,1,0:T(8,128)(2,1)S(1)}, u32[]{:S(2)}, u32[]{:S(2)}) collective-permute-start(bf16[4,8,16,640]{3,2,1,0:T(8,128)(2,1)S(1)} %pad_maximum_fusion.refs_6_), channel_id=1, source_target_pairs={{0,384},{128,0},{256,128},{384,256},{64,192},{192,320},{320,448},{... | collective-permute-start | bytes 1966088 | tf_op jit(solution)/shard_map/ppermute | solution.py:41
  100.9 13.7 %collective-permute-start.5 = (bf16[4,8,16,640]{3,2,1,0:T(8,128)(2,1)S(1)}, bf16[4,8,16,640]{3,2,1,0:T(8,128)(2,1)S(1)}, u32[]{:S(2)}, u32[]{:S(2)}) collective-permute-start(bf16[4,8,16,640]{3,2,1,0:T(8,128)(2,1)S(1)} %collective-permute-done.3.refs_3_), channel_id=1, source_target_pairs={{0,1},{1,2},{2,3},{3,0},{64,67},{65,64},{66,65},{67,66},{4,5},{5,6... | collective-permute-start | bytes 1966088 | tf_op jit(solution)/shard_map/ppermute | solution.py:42
  106.2 8.4 %copy-start.1 = (bf16[4,8,16,640]{3,2,1,0:T(8,128)(2,1)}, bf16[4,8,16,640]{3,2,1,0:T(8,128)(2,1)S(1)}, u32[]{:S(2)}) copy-start(bf16[4,8,16,640]{3,2,1,0:T(8,128)(2,1)S(1)} %collective-permute-done.6.refs_7_) | copy-start | bytes 1966084
  106.2 13.8 %collective-permute-start.8 = (bf16[4,8,16,640]{3,2,1,0:T(8,128)(2,1)S(1)}, bf16[4,8,16,640]{3,2,1,0:T(8,128)(2,1)}, u32[]{:S(2)}, u32[]{:S(2)}) collective-permute-start(bf16[4,8,16,640]{3,2,1,0:T(8,128)(2,1)S(1)} %collective-permute-done.6.refs_7_), channel_id=1, source_target_pairs={{0,128},{128,256},{256,384},{384,0},{64,448},{192,64},{320,192},{4... | collective-permute-start | bytes 1966088 | tf_op jit(solution)/shard_map/ppermute | solution.py:42
  111.6 3.0 %copy-start.2 = (bf16[4,8,16,640]{3,2,1,0:T(8,128)(2,1)}, bf16[4,8,16,640]{3,2,1,0:T(8,128)(2,1)S(1)}, u32[]{:S(2)}) copy-start(bf16[4,8,16,640]{3,2,1,0:T(8,128)(2,1)S(1)} %collective-permute-done.7.refs_8_) | copy-start | bytes 1966084
  128.2 4.4 %collective-permute-start.9 = (f32[320,640]{1,0:T(8,128)}, f32[320,640]{1,0:T(8,128)S(1)}, u32[]{:S(2)}, u32[]{:S(2)}) collective-permute-start(f32[320,640]{1,0:T(8,128)} %get-tuple-element.16), channel_id=1, source_target_pairs={{0,64},{64,0},{1,65},{65,1},{2,66},{66,2},{3,67},{67,3},{4,68},{68... | collective-permute-start | bytes 2457608 | tf_op jit(solution)/shard_map/ppermute | solution.py:272
  134.0 13.7 %collective-permute-start.10 = (bf16[320,640]{1,0:T(8,128)(2,1)S(1)}, bf16[320,640]{1,0:T(8,128)(2,1)S(1)}, u32[]{:S(2)}, u32[]{:S(2)}) collective-permute-start(bf16[320,640]{1,0:T(8,128)(2,1)S(1)} %select_convert_fusion.own_ref), channel_id=1, source_target_pairs={{0,1},{1,2},{2,3},{3,0},{64,67},{65,64},{66,65},{67,66},{4,5},{5,6... | collective-permute-start | bytes 1228808 | tf_op jit(solution)/shard_map/ppermute | solution.py:40
  135.9 13.7 %collective-permute-start.11 = (bf16[320,640]{1,0:T(8,128)(2,1)S(1)}, bf16[320,640]{1,0:T(8,128)(2,1)S(1)}, u32[]{:S(2)}, u32[]{:S(2)}) collective-permute-start(bf16[320,640]{1,0:T(8,128)(2,1)S(1)} %select_convert_fusion.own_ref), channel_id=1, source_target_pairs={{0,3},{1,0},{2,1},{3,2},{64,65},{65,66},{66,67},{67,64},{4,7},{5,4... | collective-permute-start | bytes 1228808 | tf_op jit(solution)/shard_map/ppermute | solution.py:41
  147.7 11.0 %collective-permute-start.12 = (bf16[320,640]{1,0:T(8,128)(2,1)S(1)}, bf16[320,640]{1,0:T(8,128)(2,1)S(1)}, u32[]{:S(2)}, u32[]{:S(2)}) collective-permute-start(bf16[320,640]{1,0:T(8,128)(2,1)S(1)} %collective-permute-done.10.ahead_ref), channel_id=1, source_target_pairs={{0,1},{1,2},{2,3},{3,0},{64,67},{65,64},{66,65},{67,66},{4,5},{5,6... | collective-permute-start | bytes 1228808 | tf_op jit(solution)/shard_map/ppermute | solution.py:42
Sparse Core Ops, SparseCore 0:
  25.8 90.5 all-gather.1

commit v10 on v7

--- a/solution.py
+++ b/solution.py
@@ -14,10 +14,6 @@
 
 def around(n, shift):
     return [(i, (i + shift) % n) for i in range(n)]
-
-
-def spread(value, axis, n):
-    return [value] + [lax.ppermute(value, axis, around(n, s)) for s in SHIFTS[1:]]
 
 
 def relay(values, axes, sizes):
@@ -41,12 +37,6 @@
     return [list(blocks) for blocks in zip(values, ahead, behind, across)]
 
 
-def collect(value, axis, n):
-    copies = jnp.broadcast_to(value[None], (n,) + value.shape)
-    return lax.all_to_all(copies, axis, split_axis=0, concat_axis=0, tiled=True)
-
-
-SHIFTS = (0, 1, 3, 2)
 GROUP = 4
 
 
@@ -100,25 +90,20 @@
             preferred_element_type=jnp.float32,
         )
 
-    def first():
+    def part(pick):
         left, right = [], []
         for p in range(GROUP):
             for i in range(4):
                 for j in range(4):
-                    left.append(rows_ref[p, i * 4 + before(y, offsets[j])])
-                    right.append(by_y[j][i, p])
+                    left.append(rows_ref[p, before(x, offsets[i]) * 4 + before(y, offsets[j])])
+                    right.append(pick(i, j, p))
         return product(left, right)
 
+    def first():
+        return part(lambda i, j, p: by_y[j][i, p])
+
     def second():
-        left, right = [], []
-        for p in range(GROUP):
-            for i in range(4):
-                for j in range(4):
-                    left.append(
-                        rows_ref[p, before(x, offsets[i]) * 4 + before(y, SHIFTS[j])]
-                    )
-                    right.append(by_x[i][j, p])
-        return product(left, right)
+        return part(lambda i, j, p: by_x[i][j, p])
 
     @pl.when(k == 0)
     def _():
@@ -239,8 +224,7 @@
     by_col, own = lax.optimization_barrier((by_col, own))
     part = lax.all_to_all(by_col, "col", split_axis=0, concat_axis=0, tiled=True)
     upper, lower = part[: nz // 2], part[nz // 2 :]
-    along_x = collect(upper, "x", nx)
-    along_y = jnp.stack(spread(lower, "layer", ny))
+    along_x, along_y = map(jnp.stack, relay([upper, lower], ["x", "layer"], [nx, ny]))
     along_x, along_y = lax.optimization_barrier((along_x, along_y))
     by_x, by_y = relay([along_y, along_x], ["x", "layer"], [nx, ny])
 

time: 166 us -> 168 us (1.012)
  starting transfers between devices: 40.4 us -> 47 us
  waiting for transfers between devices: 41.3 us -> 37.9 us
    ppermute x3 -> x5, starting transfers between devices: 12.7 us -> 25.4 us  [relay(): behind = [lax.ppermute(v, g, w[1]) for v, g, w in zip(values, groups, ways)]]
    ppermute x3 -> x0, starting transfers between devices: 8.07 us -> none  [spread(): lax.ppermute(value, axis, around(n, s))]
    ppermute x3 -> x5, waiting for transfers between devices: 15.7 us -> 22.8 us  [relay(): across = [lax.ppermute(v, g, w[0]) for v, g, w in zip(ahead, groups, ways)]]
    ppermute x3 -> x0, waiting for transfers between devices: 6.48 us -> none  [spread(): lax.ppermute(value, axis, around(n, s))]
    ppermute x3 -> x5, starting transfers between devices: 5.73 us -> 9.79 us  [relay(): across = [lax.ppermute(v, g, w[0]) for v, g, w in zip(ahead, groups, ways)]]
    all_to_all x1 -> x0, starting transfers between devices: 3.49 us -> none  [collect(): return lax.all_to_all(copies, axis, split_axis=0, concat_axis=0, tiled=True)]
    ppermute x3 -> x5, waiting for transfers between devices: 12.6 us -> 9.26 us  [relay(): ahead = [lax.ppermute(v, g, w[0]) for v, g, w in zip(values, groups, ways)]]
    ppermute x3 -> x5, starting transfers between devices: 8.51 us -> 9.87 us  [relay(): ahead = [lax.ppermute(v, g, w[0]) for v, g, w in zip(values, groups, ways)]]
  transfers between devices with their start and end apart: 15 -> 17, of which waited for: 11 -> 10; matrix products, arithmetic and copies ran while one was open for 1% -> 0% of each run, Pallas kernels for 1% -> 1%
where the time goes in v10:
time: 168 us; the launch traced here: 167 us
  blocking collectives  53.9 us (32%)
  starting transfers between devices  47 us (28%)
  waiting for transfers between devices  37.9 us (23%)
  Pallas kernels  13.6 us (8%)
  between operations  13.6 us (8%)
    all_to_all x1, blocking collectives, body(): lax.all_to_all(by_col, 'col', split_axis=0, concat_axis=0, tiled=True)  37.6 us
    ppermute x5, starting transfers between devices, relay(): behind = [lax.ppermute(v, g, w[1]) for v, g, w in zip(values, groups, ways)]  25.4 us
    ppermute x5, waiting for transfers between devices, relay(): across = [lax.ppermute(v, g, w[0]) for v, g, w in zip(ahead, groups, ways)]  22.8 us
    all_to_all x1, blocking collectives, body(): lax.all_to_all(by_chip, ('x', 'layer'), split_axis=0, concat_axis=0, tile...  16.3 us
    ppermute x5, starting transfers between devices, relay(): ahead = [lax.ppermute(v, g, w[0]) for v, g, w in zip(values, groups, ways)]  9.87 us
    ppermute x5, starting transfers between devices, relay(): across = [lax.ppermute(v, g, w[0]) for v, g, w in zip(ahead, groups, ways)]  9.79 us
    ppermute x5, waiting for transfers between devices, relay(): ahead = [lax.ppermute(v, g, w[0]) for v, g, w in zip(values, groups, ways)]  9.26 us
    pallas_call x1, Pallas kernels, body(): pl.pallas_call(lambda *refs: gram_kernel(half, steps, *refs), out_shape=(...  8.41 us
  transfers between devices with their start and end apart: 17, of which 10 were waited for; matrix products, arithmetic and copies ran while one was open for 0% of the time, Pallas kernels for 1%

profile of v10, /device:TPU:32, one launch (start us, length us, event | category | flops | bytes accessed | tf_op | source)
XLA Modules:
  0.0 167.5 jit_solution(9104893368301269439)
XLA Ops:
  6.5 0.0 all-gather.2.cloned.1.call-start
  6.5 2.2 %weigh.1 = (bf16[16,16,640]{2,1,0:T(8,128)(2,1)}, bf16[16,16,640]{2,1,0:T(8,128)(2,1)}) custom-call(s32[1]{0:T(128)} %bitcast.5.refs_0_, s32[64,80]{1,0:T(8,128)} %refs_1_.1, f32[1,16]{1,0:T(1,128)} %bitcast.27, bf16[16,10240]{1,0:T(8,128)(2,1)} %refs_3_.1), custom_call_target="tpu_custom_call" | custom-call | tf_op jit(solution)/shard_map/weigh/pallas_call | solution.py:210
  8.8 16.3 %all_to_all.10 = bf16[16,16,640]{2,1,0:T(8,128)(2,1)} all-to-all(bf16[16,16,640]{2,1,0:T(8,128)(2,1)} %get-tuple-element.12), channel_id=1, replica_groups=mesh['x'=4,'core'=2,'col'=16,'layer'=4] {'x','layer'}, dimensions={0} | all-to-all | bytes 655360 | tf_op jit(solution)/shard_map/all_to_all | solution.py:221
  25.1 0.0 all-gather.2.cloned.1.call-update
  25.1 37.6 %all_to_all.11 = bf16[16,16,640]{2,1,0:T(8,128)(2,1)S(1)} all-to-all(bf16[16,16,640]{2,1,0:T(8,128)(2,1)} %get-tuple-element.14), channel_id=1, replica_groups=mesh['x'=4,'core'=2,'col'=16,'layer'=4] {'col'}, dimensions={0} | all-to-all | bytes 655360 | tf_op jit(solution)/shard_map/all_to_all | solution.py:225
  62.6 0.1 slice_bitcast_fusion
  62.7 1.9 %collective-permute-start.3 = (bf16[8,16,640]{2,1,0:T(8,128)(2,1)S(1)}, bf16[8,16,640]{2,1,0:T(8,128)(2,1)S(1)}, u32[]{:S(2)}, u32[]{:S(2)}) collective-permute-start(bf16[8,16,640]{2,1,0:T(8,128)(2,1)S(1)} %get-tuple-element.21), channel_id=1, source_target_pairs={{0,1},{1,2},{2,3},{3,0},{64,67},{65,64},{66,65},{67,66},{4,5},{5,6... | collective-permute-start | bytes 491528 | tf_op jit(solution)/shard_map/ppermute | solution.py:34
  64.6 1.9 %collective-permute-start = (bf16[8,16,640]{2,1,0:T(8,128)(2,1)S(1)}, bf16[8,16,640]{2,1,0:T(8,128)(2,1)S(1)}, u32[]{:S(2)}, u32[]{:S(2)}) collective-permute-start(bf16[8,16,640]{2,1,0:T(8,128)(2,1)S(1)} %get-tuple-element.22), channel_id=1, source_target_pairs={{0,128},{128,256},{256,384},{384,0},{64,448},{192,64},{320,192},{4... | collective-permute-start | bytes 491528 | tf_op jit(solution)/shard_map/ppermute | solution.py:34
  66.5 5.1 %collective-permute-start.4 = (bf16[8,16,640]{2,1,0:T(8,128)(2,1)S(1)}, bf16[8,16,640]{2,1,0:T(8,128)(2,1)S(1)}, u32[]{:S(2)}, u32[]{:S(2)}) collective-permute-start(bf16[8,16,640]{2,1,0:T(8,128)(2,1)S(1)} %get-tuple-element.21), channel_id=1, source_target_pairs={{0,3},{1,0},{2,1},{3,2},{64,65},{65,66},{66,67},{67,64},{4,7},{5,4... | collective-permute-start | bytes 491528 | tf_op jit(solution)/shard_map/ppermute | solution.py:35
  71.7 0.0 collective-permute-done.3
  71.7 1.9 %collective-permute-start.5 = (bf16[8,16,640]{2,1,0:T(8,128)(2,1)S(1)}, bf16[8,16,640]{2,1,0:T(8,128)(2,1)S(1)}, u32[]{:S(2)}, u32[]{:S(2)}) collective-permute-start(bf16[8,16,640]{2,1,0:T(8,128)(2,1)S(1)} %collective-permute-done.3), channel_id=1, source_target_pairs={{0,1},{1,2},{2,3},{3,0},{64,67},{65,64},{66,65},{67,66},{4,5},{5,6... | collective-permute-start | bytes 491528 | tf_op jit(solution)/shard_map/ppermute | solution.py:36
  73.6 5.1 %collective-permute-start.1 = (bf16[8,16,640]{2,1,0:T(8,128)(2,1)S(1)}, bf16[8,16,640]{2,1,0:T(8,128)(2,1)S(1)}, u32[]{:S(2)}, u32[]{:S(2)}) collective-permute-start(bf16[8,16,640]{2,1,0:T(8,128)(2,1)S(1)} %get-tuple-element.22), channel_id=1, source_target_pairs={{0,384},{128,0},{256,128},{384,256},{64,192},{192,320},{320,448},{... | collective-permute-start | bytes 491528 | tf_op jit(solution)/shard_map/ppermute | solution.py:35
  78.8 0.0 collective-permute-done
  78.8 1.9 %collective-permute-start.2 = (bf16[8,16,640]{2,1,0:T(8,128)(2,1)S(1)}, bf16[8,16,640]{2,1,0:T(8,128)(2,1)S(1)}, u32[]{:S(2)}, u32[]{:S(2)}) collective-permute-start(bf16[8,16,640]{2,1,0:T(8,128)(2,1)S(1)} %collective-permute-done), channel_id=1, source_target_pairs={{0,128},{128,256},{256,384},{384,0},{64,448},{192,64},{320,192},{4... | collective-permute-start | bytes 491528 | tf_op jit(solution)/shard_map/ppermute | solution.py:36
  80.7 0.0 collective-permute-done.4
  80.7 0.0 collective-permute-done.5
  80.7 0.1 pad_maximum_fusion.1.refs_6_
  80.8 0.7 collective-permute-done.1
  81.6 5.6 %collective-permute-done.2 = bf16[8,16,640]{2,1,0:T(8,128)(2,1)S(1)} collective-permute-done((bf16[8,16,640]{2,1,0:T(8,128)(2,1)S(1)}, bf16[8,16,640]{2,1,0:T(8,128)(2,1)S(1)}, u32[]{:S(2)}, u32[]{:S(2)}) %collective-permute-start.2) | collective-permute-done | bytes 163872 | tf_op jit(solution)/shard_map/ppermute | solution.py:36
  87.2 0.1 pad_maximum_fusion.refs_2_
  87.3 1.9 %collective-permute-start.6 = (bf16[4,8,16,640]{3,2,1,0:T(8,128)(2,1)S(1)}, bf16[4,8,16,640]{3,2,1,0:T(8,128)(2,1)S(1)}, u32[]{:S(2)}, u32[]{:S(2)}) collective-permute-start(bf16[4,8,16,640]{3,2,1,0:T(8,128)(2,1)S(1)} %pad_maximum_fusion.refs_2_), channel_id=1, source_target_pairs={{0,1},{1,2},{2,3},{3,0},{64,67},{65,64},{66,65},{67,66},{4,5},{5,6... | collective-permute-start | bytes 1966088 | tf_op jit(solution)/shard_map/ppermute | solution.py:34
  89.2 1.9 %collective-permute-start.9 = (bf16[4,8,16,640]{3,2,1,0:T(8,128)(2,1)S(1)}, bf16[4,8,16,640]{3,2,1,0:T(8,128)(2,1)S(1)}, u32[]{:S(2)}, u32[]{:S(2)}) collective-permute-start(bf16[4,8,16,640]{3,2,1,0:T(8,128)(2,1)S(1)} %pad_maximum_fusion.1.refs_6_), channel_id=1, source_target_pairs={{0,128},{128,256},{256,384},{384,0},{64,448},{192,64},{320,192},{4... | collective-permute-start | bytes 1966088 | tf_op jit(solution)/shard_map/ppermute | solution.py:34
  91.2 5.1 %collective-permute-start.7 = (bf16[4,8,16,640]{3,2,1,0:T(8,128)(2,1)S(1)}, bf16[4,8,16,640]{3,2,1,0:T(8,128)(2,1)S(1)}, u32[]{:S(2)}, u32[]{:S(2)}) collective-permute-start(bf16[4,8,16,640]{3,2,1,0:T(8,128)(2,1)S(1)} %pad_maximum_fusion.refs_2_), channel_id=1, source_target_pairs={{0,3},{1,0},{2,1},{3,2},{64,65},{65,66},{66,67},{67,64},{4,7},{5,4... | collective-permute-start | bytes 1966088 | tf_op jit(solution)/shard_map/ppermute | solution.py:35
  96.3 5.1 %collective-permute-start.10 = (bf16[4,8,16,640]{3,2,1,0:T(8,128)(2,1)S(1)}, bf16[4,8,16,640]{3,2,1,0:T(8,128)(2,1)S(1)}, u32[]{:S(2)}, u32[]{:S(2)}) collective-permute-start(bf16[4,8,16,640]{3,2,1,0:T(8,128)(2,1)S(1)} %pad_maximum_fusion.1.refs_6_), channel_id=1, source_target_pairs={{0,384},{128,0},{256,128},{384,256},{64,192},{192,320},{320,448},{... | collective-permute-start | bytes 1966088 | tf_op jit(solution)/shard_map/ppermute | solution.py:35
  101.4 2.9 %collective-permute-done.6.refs_3_ = bf16[4,8,16,640]{3,2,1,0:T(8,128)(2,1)S(1)} collective-permute-done((bf16[4,8,16,640]{3,2,1,0:T(8,128)(2,1)S(1)}, bf16[4,8,16,640]{3,2,1,0:T(8,128)(2,1)S(1)}, u32[]{:S(2)}, u32[]{:S(2)}) %collective-permute-start.6) | collective-permute-done | bytes 655392 | tf_op jit(solution)/shard_map/ppermute | solution.py:34
  104.3 2.1 %collective-permute-start.8 = (bf16[4,8,16,640]{3,2,1,0:T(8,128)(2,1)S(1)}, bf16[4,8,16,640]{3,2,1,0:T(8,128)(2,1)S(1)}, u32[]{:S(2)}, u32[]{:S(2)}) collective-permute-start(bf16[4,8,16,640]{3,2,1,0:T(8,128)(2,1)S(1)} %collective-permute-done.6.refs_3_), channel_id=1, source_target_pairs={{0,1},{1,2},{2,3},{3,0},{64,67},{65,64},{66,65},{67,66},{4,5},{5,6... | collective-permute-start | bytes 1966088 | tf_op jit(solution)/shard_map/ppermute | solution.py:36
  106.5 0.9 collective-permute-done.9.refs_7_
  107.4 0.0 copy-start.1
  107.4 1.9 %collective-permute-start.11 = (bf16[4,8,16,640]{3,2,1,0:T(8,128)(2,1)S(1)}, bf16[4,8,16,640]{3,2,1,0:T(8,128)(2,1)}, u32[]{:S(2)}, u32[]{:S(2)}) collective-permute-start(bf16[4,8,16,640]{3,2,1,0:T(8,128)(2,1)S(1)} %collective-permute-done.9.refs_7_), channel_id=1, source_target_pairs={{0,128},{128,256},{256,384},{384,0},{64,448},{192,64},{320,192},{4... | collective-permute-start | bytes 1966088 | tf_op jit(solution)/shard_map/ppermute | solution.py:36
  109.3 0.1 pad_add_fusion.1.refs_0_
  109.4 0.0 collective-permute-done.7.refs_4_
  109.4 2.6 %collective-permute-done.10.refs_8_ = bf16[4,8,16,640]{3,2,1,0:T(8,128)(2,1)S(1)} collective-permute-done((bf16[4,8,16,640]{3,2,1,0:T(8,128)(2,1)S(1)}, bf16[4,8,16,640]{3,2,1,0:T(8,128)(2,1)S(1)}, u32[]{:S(2)}, u32[]{:S(2)}) %collective-permute-start.10) | collective-permute-done | bytes 655392 | tf_op jit(solution)/shard_map/ppermute | solution.py:35
  112.1 0.0 copy-start.2
  112.1 6.0 %collective-permute-done.8.refs_5_ = bf16[4,8,16,640]{3,2,1,0:T(8,128)(2,1)S(1)} collective-permute-done((bf16[4,8,16,640]{3,2,1,0:T(8,128)(2,1)S(1)}, bf16[4,8,16,640]{3,2,1,0:T(8,128)(2,1)S(1)}, u32[]{:S(2)}, u32[]{:S(2)}) %collective-permute-start.8) | collective-permute-done | bytes 655392 | tf_op jit(solution)/shard_map/ppermute | solution.py:36
  118.0 0.0 copy-done.1
  118.0 0.0 copy-done.2
  118.0 3.2 %collective-permute-done.11.refs_9_ = bf16[4,8,16,640]{3,2,1,0:T(8,128)(2,1)} collective-permute-done((bf16[4,8,16,640]{3,2,1,0:T(8,128)(2,1)S(1)}, bf16[4,8,16,640]{3,2,1,0:T(8,128)(2,1)}, u32[]{:S(2)}, u32[]{:S(2)}) %collective-permute-start.11) | collective-permute-done | bytes 655392 | tf_op jit(solution)/shard_map/ppermute | solution.py:36
  121.2 0.0 all-gather.2.cloned.1.call-done
  121.2 8.4 %gram.1 = (f32[320,640]{1,0:T(8,128)}, f32[320,640]{1,0:T(8,128)}) custom-call(s32[3]{0:T(128)S(1)} %pad_add_fusion.1.refs_0_, bf16[16,16,16,640]{3,2,1,0:T(8,128)(2,1)} %bitcast.28, bf16[4,8,16,640]{3,2,1,0:T(8,128)(2,1)S(1)} %pad_maximum_fusion.refs_2_, bf16[4,8,16,640]{3,2,1,0:T(8,128)(2,1)S(1)} %collective-permute-done.6.refs_3_, ...), custom_call_target="tpu_custom_call" | custom-call | flops 3355443200 | bytes 10485760 | tf_op jit(solution)/shard_map/gram/pallas_call | solution.py:234
  129.6 1.9 %collective-permute-start.12 = (f32[320,640]{1,0:T(8,128)}, f32[320,640]{1,0:T(8,128)S(1)}, u32[]{:S(2)}, u32[]{:S(2)}) collective-permute-start(f32[320,640]{1,0:T(8,128)} %get-tuple-element.18), channel_id=1, source_target_pairs={{0,64},{64,0},{1,65},{65,1},{2,66},{66,2},{3,67},{67,3},{4,68},{68... | collective-permute-start | bytes 2457608 | tf_op jit(solution)/shard_map/ppermute | solution.py:260
  131.5 0.1 pad_add_fusion.refs_0_
  131.6 2.4 %collective-permute-done.12.refs_2_ = f32[320,640]{1,0:T(8,128)S(1)} collective-permute-done((f32[320,640]{1,0:T(8,128)}, f32[320,640]{1,0:T(8,128)S(1)}, u32[]{:S(2)}, u32[]{:S(2)}) %collective-permute-start.12) | collective-permute-done | bytes 819232 | tf_op jit(solution)/shard_map/ppermute | solution.py:260
  134.0 0.0 copy-start
  134.0 1.1 copy-done
  135.2 1.1 finish.1.own_ref
  136.3 2.2 %collective-permute-start.13 = (bf16[320,640]{1,0:T(8,128)(2,1)S(1)}, bf16[320,640]{1,0:T(8,128)(2,1)S(1)}, u32[]{:S(2)}, u32[]{:S(2)}) collective-permute-start(bf16[320,640]{1,0:T(8,128)(2,1)S(1)} %finish.1.own_ref), channel_id=1, source_target_pairs={{0,1},{1,2},{2,3},{3,0},{64,67},{65,64},{66,65},{67,66},{4,5},{5,6... | collective-permute-start | bytes 1228808 | tf_op jit(solution)/shard_map/ppermute | solution.py:34
  138.5 4.9 %collective-permute-start.14 = (bf16[320,640]{1,0:T(8,128)(2,1)S(1)}, bf16[320,640]{1,0:T(8,128)(2,1)S(1)}, u32[]{:S(2)}, u32[]{:S(2)}) collective-permute-start(bf16[320,640]{1,0:T(8,128)(2,1)S(1)} %finish.1.own_ref), channel_id=1, source_target_pairs={{0,3},{1,0},{2,1},{3,2},{64,65},{65,66},{66,67},{67,64},{4,7},{5,4... | collective-permute-start | bytes 1228808 | tf_op jit(solution)/shard_map/ppermute | solution.py:35
  143.4 5.4 %collective-permute-done.13.ahead_ref = bf16[320,640]{1,0:T(8,128)(2,1)S(1)} collective-permute-done((bf16[320,640]{1,0:T(8,128)(2,1)S(1)}, bf16[320,640]{1,0:T(8,128)(2,1)S(1)}, u32[]{:S(2)}, u32[]{:S(2)}) %collective-permute-start.13) | collective-permute-done | bytes 409632 | tf_op jit(solution)/shard_map/ppermute | solution.py:34
  148.8 1.9 %collective-permute-start.15 = (bf16[320,640]{1,0:T(8,128)(2,1)S(1)}, bf16[320,640]{1,0:T(8,128)(2,1)S(1)}, u32[]{:S(2)}, u32[]{:S(2)}) collective-permute-start(bf16[320,640]{1,0:T(8,128)(2,1)S(1)} %collective-permute-done.13.ahead_ref), channel_id=1, source_target_pairs={{0,1},{1,2},{2,3},{3,0},{64,67},{65,64},{66,65},{67,66},{4,5},{5,6... | collective-permute-start | bytes 1228808 | tf_op jit(solution)/shard_map/ppermute | solution.py:36
  150.7 0.0 collective-permute-done.14.behind_ref
  150.7 1.1 place.1.held_ref
  151.8 8.1 %collective-permute-done.15.across_ref = bf16[320,640]{1,0:T(8,128)(2,1)S(1)} collective-permute-done((bf16[320,640]{1,0:T(8,128)(2,1)S(1)}, bf16[320,640]{1,0:T(8,128)(2,1)S(1)}, u32[]{:S(2)}, u32[]{:S(2)}) %collective-permute-start.15) | collective-permute-done | bytes 409632 | tf_op jit(solution)/shard_map/ppermute | solution.py:36
  159.8 0.8 last.1
Async XLA Ops:
  6.5 114.7 %all-gather.2.cloned.1.call-start = ((), (), s32[]{:S(2)}) async-start(), calls=%async_computation.2 | async-start | bytes 5570560 | tf_op jit(solution)/shard_map/all_gather | solution.py:223
  62.7 9.0 %collective-permute-start.3 = (bf16[8,16,640]{2,1,0:T(8,128)(2,1)S(1)}, bf16[8,16,640]{2,1,0:T(8,128)(2,1)S(1)}, u32[]{:S(2)}, u32[]{:S(2)}) collective-permute-start(bf16[8,16,640]{2,1,0:T(8,128)(2,1)S(1)} %get-tuple-element.21), channel_id=1, source_target_pairs={{0,1},{1,2},{2,3},{3,0},{64,67},{65,64},{66,65},{67,66},{4,5},{5,6... | collective-permute-start | bytes 491528 | tf_op jit(solution)/shard_map/ppermute | solution.py:34
  64.6 14.2 %collective-permute-start = (bf16[8,16,640]{2,1,0:T(8,128)(2,1)S(1)}, bf16[8,16,640]{2,1,0:T(8,128)(2,1)S(1)}, u32[]{:S(2)}, u32[]{:S(2)}) collective-permute-start(bf16[8,16,640]{2,1,0:T(8,128)(2,1)S(1)} %get-tuple-element.22), channel_id=1, source_target_pairs={{0,128},{128,256},{256,384},{384,0},{64,448},{192,64},{320,192},{4... | collective-permute-start | bytes 491528 | tf_op jit(solution)/shard_map/ppermute | solution.py:34
  66.5 14.2 %collective-permute-start.4 = (bf16[8,16,640]{2,1,0:T(8,128)(2,1)S(1)}, bf16[8,16,640]{2,1,0:T(8,128)(2,1)S(1)}, u32[]{:S(2)}, u32[]{:S(2)}) collective-permute-start(bf16[8,16,640]{2,1,0:T(8,128)(2,1)S(1)} %get-tuple-element.21), channel_id=1, source_target_pairs={{0,3},{1,0},{2,1},{3,2},{64,65},{65,66},{66,67},{67,64},{4,7},{5,4... | collective-permute-start | bytes 491528 | tf_op jit(solution)/shard_map/ppermute | solution.py:35
  71.7 9.0 %collective-permute-start.5 = (bf16[8,16,640]{2,1,0:T(8,128)(2,1)S(1)}, bf16[8,16,640]{2,1,0:T(8,128)(2,1)S(1)}, u32[]{:S(2)}, u32[]{:S(2)}) collective-permute-start(bf16[8,16,640]{2,1,0:T(8,128)(2,1)S(1)} %collective-permute-done.3), channel_id=1, source_target_pairs={{0,1},{1,2},{2,3},{3,0},{64,67},{65,64},{66,65},{67,66},{4,5},{5,6... | collective-permute-start | bytes 491528 | tf_op jit(solution)/shard_map/ppermute | solution.py:36
  73.6 8.0 %collective-permute-start.1 = (bf16[8,16,640]{2,1,0:T(8,128)(2,1)S(1)}, bf16[8,16,640]{2,1,0:T(8,128)(2,1)S(1)}, u32[]{:S(2)}, u32[]{:S(2)}) collective-permute-start(bf16[8,16,640]{2,1,0:T(8,128)(2,1)S(1)} %get-tuple-element.22), channel_id=1, source_target_pairs={{0,384},{128,0},{256,128},{384,256},{64,192},{192,320},{320,448},{... | collective-permute-start | bytes 491528 | tf_op jit(solution)/shard_map/ppermute | solution.py:35
  78.8 8.4 %collective-permute-start.2 = (bf16[8,16,640]{2,1,0:T(8,128)(2,1)S(1)}, bf16[8,16,640]{2,1,0:T(8,128)(2,1)S(1)}, u32[]{:S(2)}, u32[]{:S(2)}) collective-permute-start(bf16[8,16,640]{2,1,0:T(8,128)(2,1)S(1)} %collective-permute-done), channel_id=1, source_target_pairs={{0,128},{128,256},{256,384},{384,0},{64,448},{192,64},{320,192},{4... | collective-permute-start | bytes 491528 | tf_op jit(solution)/shard_map/ppermute | solution.py:36
  87.3 17.0 %collective-permute-start.6 = (bf16[4,8,16,640]{3,2,1,0:T(8,128)(2,1)S(1)}, bf16[4,8,16,640]{3,2,1,0:T(8,128)(2,1)S(1)}, u32[]{:S(2)}, u32[]{:S(2)}) collective-permute-start(bf16[4,8,16,640]{3,2,1,0:T(8,128)(2,1)S(1)} %pad_maximum_fusion.refs_2_), channel_id=1, source_target_pairs={{0,1},{1,2},{2,3},{3,0},{64,67},{65,64},{66,65},{67,66},{4,5},{5,6... | collective-permute-start | bytes 1966088 | tf_op jit(solution)/shard_map/ppermute | solution.py:34
  89.2 18.2 %collective-permute-start.9 = (bf16[4,8,16,640]{3,2,1,0:T(8,128)(2,1)S(1)}, bf16[4,8,16,640]{3,2,1,0:T(8,128)(2,1)S(1)}, u32[]{:S(2)}, u32[]{:S(2)}) collective-permute-start(bf16[4,8,16,640]{3,2,1,0:T(8,128)(2,1)S(1)} %pad_maximum_fusion.1.refs_6_), channel_id=1, source_target_pairs={{0,128},{128,256},{256,384},{384,0},{64,448},{192,64},{320,192},{4... | collective-permute-start | bytes 1966088 | tf_op jit(solution)/shard_map/ppermute | solution.py:34
  91.2 18.3 %collective-permute-start.7 = (bf16[4,8,16,640]{3,2,1,0:T(8,128)(2,1)S(1)}, bf16[4,8,16,640]{3,2,1,0:T(8,128)(2,1)S(1)}, u32[]{:S(2)}, u32[]{:S(2)}) collective-permute-start(bf16[4,8,16,640]{3,2,1,0:T(8,128)(2,1)S(1)} %pad_maximum_fusion.refs_2_), channel_id=1, source_target_pairs={{0,3},{1,0},{2,1},{3,2},{64,65},{65,66},{66,67},{67,64},{4,7},{5,4... | collective-permute-start | bytes 1966088 | tf_op jit(solution)/shard_map/ppermute | solution.py:35
  96.3 15.8 %collective-permute-start.10 = (bf16[4,8,16,640]{3,2,1,0:T(8,128)(2,1)S(1)}, bf16[4,8,16,640]{3,2,1,0:T(8,128)(2,1)S(1)}, u32[]{:S(2)}, u32[]{:S(2)}) collective-permute-start(bf16[4,8,16,640]{3,2,1,0:T(8,128)(2,1)S(1)} %pad_maximum_fusion.1.refs_6_), channel_id=1, source_target_pairs={{0,384},{128,0},{256,128},{384,256},{64,192},{192,320},{320,448},{... | collective-permute-start | bytes 1966088 | tf_op jit(solution)/shard_map/ppermute | solution.py:35
  104.3 13.7 %collective-permute-start.8 = (bf16[4,8,16,640]{3,2,1,0:T(8,128)(2,1)S(1)}, bf16[4,8,16,640]{3,2,1,0:T(8,128)(2,1)S(1)}, u32[]{:S(2)}, u32[]{:S(2)}) collective-permute-start(bf16[4,8,16,640]{3,2,1,0:T(8,128)(2,1)S(1)} %collective-permute-done.6.refs_3_), channel_id=1, source_target_pairs={{0,1},{1,2},{2,3},{3,0},{64,67},{65,64},{66,65},{67,66},{4,5},{5,6... | collective-permute-start | bytes 1966088 | tf_op jit(solution)/shard_map/ppermute | solution.py:36
  107.4 10.6 %copy-start.1 = (bf16[4,8,16,640]{3,2,1,0:T(8,128)(2,1)}, bf16[4,8,16,640]{3,2,1,0:T(8,128)(2,1)S(1)}, u32[]{:S(2)}) copy-start(bf16[4,8,16,640]{3,2,1,0:T(8,128)(2,1)S(1)} %collective-permute-done.9.refs_7_) | copy-start | bytes 1966084
  107.4 13.8 %collective-permute-start.11 = (bf16[4,8,16,640]{3,2,1,0:T(8,128)(2,1)S(1)}, bf16[4,8,16,640]{3,2,1,0:T(8,128)(2,1)}, u32[]{:S(2)}, u32[]{:S(2)}) collective-permute-start(bf16[4,8,16,640]{3,2,1,0:T(8,128)(2,1)S(1)} %collective-permute-done.9.refs_7_), channel_id=1, source_target_pairs={{0,128},{128,256},{256,384},{384,0},{64,448},{192,64},{320,192},{4... | collective-permute-start | bytes 1966088 | tf_op jit(solution)/shard_map/ppermute | solution.py:36
  112.1 6.0 %copy-start.2 = (bf16[4,8,16,640]{3,2,1,0:T(8,128)(2,1)}, bf16[4,8,16,640]{3,2,1,0:T(8,128)(2,1)S(1)}, u32[]{:S(2)}) copy-start(bf16[4,8,16,640]{3,2,1,0:T(8,128)(2,1)S(1)} %collective-permute-done.10.refs_8_) | copy-start | bytes 1966084
  129.6 4.4 %collective-permute-start.12 = (f32[320,640]{1,0:T(8,128)}, f32[320,640]{1,0:T(8,128)S(1)}, u32[]{:S(2)}, u32[]{:S(2)}) collective-permute-start(f32[320,640]{1,0:T(8,128)} %get-tuple-element.18), channel_id=1, source_target_pairs={{0,64},{64,0},{1,65},{65,1},{2,66},{66,2},{3,67},{67,3},{4,68},{68... | collective-permute-start | bytes 2457608 | tf_op jit(solution)/shard_map/ppermute | solution.py:260
  134.0 1.1 copy-start
  136.3 12.5 %collective-permute-start.13 = (bf16[320,640]{1,0:T(8,128)(2,1)S(1)}, bf16[320,640]{1,0:T(8,128)(2,1)S(1)}, u32[]{:S(2)}, u32[]{:S(2)}) collective-permute-start(bf16[320,640]{1,0:T(8,128)(2,1)S(1)} %finish.1.own_ref), channel_id=1, source_target_pairs={{0,1},{1,2},{2,3},{3,0},{64,67},{65,64},{66,65},{67,66},{4,5},{5,6... | collective-permute-start | bytes 1228808 | tf_op jit(solution)/shard_map/ppermute | solution.py:34
  138.5 12.2 %collective-permute-start.14 = (bf16[320,640]{1,0:T(8,128)(2,1)S(1)}, bf16[320,640]{1,0:T(8,128)(2,1)S(1)}, u32[]{:S(2)}, u32[]{:S(2)}) collective-permute-start(bf16[320,640]{1,0:T(8,128)(2,1)S(1)} %finish.1.own_ref), channel_id=1, source_target_pairs={{0,3},{1,0},{2,1},{3,2},{64,65},{65,66},{66,67},{67,64},{4,7},{5,4... | collective-permute-start | bytes 1228808 | tf_op jit(solution)/shard_map/ppermute | solution.py:35
  148.8 11.0 %collective-permute-start.15 = (bf16[320,640]{1,0:T(8,128)(2,1)S(1)}, bf16[320,640]{1,0:T(8,128)(2,1)S(1)}, u32[]{:S(2)}, u32[]{:S(2)}) collective-permute-start(bf16[320,640]{1,0:T(8,128)(2,1)S(1)} %collective-permute-done.13.ahead_ref), channel_id=1, source_target_pairs={{0,1},{1,2},{2,3},{3,0},{64,67},{65,64},{66,65},{67,66},{4,5},{5,6... | collective-permute-start | bytes 1228808 | tf_op jit(solution)/shard_map/ppermute | solution.py:36
Sparse Core Ops, SparseCore 0:
  25.2 90.7 all-gather.1

commit v11 on v7

--- a/solution.py
+++ b/solution.py
@@ -50,9 +50,21 @@
 GROUP = 4
 
 
-def weigh_kernel(owned, nz, place_ref, pattern_ref, weight_ref, block_ref, by_col_ref, by_chip_ref):
+def weigh_kernel(
+    owned, nz, place_ref, pattern_hbm, weight_ref, block_hbm, by_col_ref, by_chip_ref, pattern_ref, block_ref, sems
+):
     lanes = 128
-    row = place_ref[0]
+    whole = place_ref[0]
+    row = lax.rem(whole, 8)
+    first = pl.multiple_of(whole - row, 8)
+    flags = pltpu.make_async_copy(pattern_hbm.at[pl.ds(first, 8)], pattern_ref, sems.at[4])
+    flags.start()
+    span = block_hbm.shape[1] // 4
+    loads = []
+    for i in range(4):
+        part = pl.ds(i * span, span)
+        loads.append(pltpu.make_async_copy(block_hbm.at[:, part], block_ref.at[:, part], sems.at[i]))
+        loads[-1].start()
     diagonal = lax.broadcasted_iota(jnp.int32, (owned, owned), 0) == lax.broadcasted_iota(
         jnp.int32, (owned, owned), 1
     )
@@ -63,7 +75,10 @@
     chips, _, tile = by_chip_ref.shape
     half = tile // 2
     strips = []
+    flags.wait()
     for z in range(nz):
+        if z % (nz // 4) == 0:
+            loads[z // (nz // 4)].wait()
         parts = []
         for i in range(count):
             j = z * count + i
@@ -228,8 +243,13 @@
             jax.ShapeDtypeStruct((nz, owned, width), jnp.bfloat16),
             jax.ShapeDtypeStruct((chips, owned, tile), jnp.bfloat16),
         ),
-        in_specs=[SMEM, SMEM, VMEM, VMEM],
+        in_specs=[SMEM, pl.BlockSpec(memory_space=pl.ANY), VMEM, pl.BlockSpec(memory_space=pl.ANY)],
         out_specs=(VMEM, VMEM),
+        scratch_shapes=[
+            pltpu.SMEM((8, pattern.shape[1]), jnp.int32),
+            pltpu.VMEM((owned, reads), jnp.bfloat16),
+            pltpu.SemaphoreType.DMA((5,)),
+        ],
         compiler_params=pltpu.CompilerParams(vmem_limit_bytes=58 << 20),
         name="weigh",
     )(block_row, pattern, idf_weight.reshape(1, owned), occurrences)

time: 166 us -> 166 us (level)
  no operation moved by 1% of the time
where the time goes in v11:
time: 166 us; the launch traced here: 165 us
  blocking collectives  53.9 us (32%)
  waiting for transfers between devices  41.3 us (25%)
  starting transfers between devices  40.4 us (24%)
  Pallas kernels  13.9 us (8%)
  between operations  13.6 us (8%)
  local copies, waits for them, and re-layouts  2.08 us (1%)
    all_to_all x1, blocking collectives, body(): lax.all_to_all(by_col, 'col', split_axis=0, concat_axis=0, tiled=True)  37.6 us
    all_to_all x1, blocking collectives, body(): lax.all_to_all(by_chip, ('x', 'layer'), split_axis=0, concat_axis=0, tile...  16.3 us
    ppermute x3, waiting for transfers between devices, relay(): across = [lax.ppermute(v, g, w[0]) for v, g, w in zip(ahead, groups, ways)]  15.7 us
    ppermute x3, starting transfers between devices, relay(): behind = [lax.ppermute(v, g, w[1]) for v, g, w in zip(values, groups, ways)]  12.7 us
    ppermute x3, waiting for transfers between devices, relay(): ahead = [lax.ppermute(v, g, w[0]) for v, g, w in zip(values, groups, ways)]  12.6 us
    ppermute x3, starting transfers between devices, relay(): ahead = [lax.ppermute(v, g, w[0]) for v, g, w in zip(values, groups, ways)]  8.51 us
    pallas_call x1, Pallas kernels, body(): pl.pallas_call(lambda *refs: gram_kernel(half, steps, *refs), out_shape=(...  8.37 us
    ppermute x3, starting transfers between devices, spread(): lax.ppermute(value, axis, around(n, s))  8.07 us
  transfers between devices with their start and end apart: 15, of which 11 were waited for; matrix products, arithmetic and copies ran while one was open for 1% of the time, Pallas kernels for 1%

profile of v11, /device:TPU:32, one launch (start us, length us, event | category | flops | bytes accessed | tf_op | source)
XLA Modules:
  0.0 165.4 jit_solution(4132775710998546105)
XLA Ops:
  6.5 0.0 all-gather.2.cloned.1.call-start
  6.5 2.6 %weigh.1 = (bf16[16,16,640]{2,1,0:T(8,128)(2,1)}, bf16[16,16,640]{2,1,0:T(8,128)(2,1)}) custom-call(s32[1]{0:T(128)} %bitcast.5.refs_0_, s32[64,80]{1,0:T(8,128)} %refs_1_.1, f32[1,16]{1,0:T(1,128)} %bitcast.19, bf16[16,10240]{1,0:T(8,128)(2,1)} %refs_3_.1), custom_call_target="tpu_custom_call" | custom-call | tf_op jit(solution)/shard_map/weigh/pallas_call | solution.py:240
  9.1 16.3 %all_to_all.15 = bf16[16,16,640]{2,1,0:T(8,128)(2,1)} all-to-all(bf16[16,16,640]{2,1,0:T(8,128)(2,1)} %get-tuple-element.12), channel_id=1, replica_groups=mesh['x'=4,'core'=2,'col'=16,'layer'=4] {'x','layer'}, dimensions={0} | all-to-all | bytes 655360 | tf_op jit(solution)/shard_map/all_to_all | solution.py:256
  25.5 0.0 all-gather.2.cloned.1.call-update
  25.5 37.6 %all_to_all.16 = bf16[16,16,640]{2,1,0:T(8,128)(2,1)S(1)} all-to-all(bf16[16,16,640]{2,1,0:T(8,128)(2,1)} %get-tuple-element.14), channel_id=1, replica_groups=mesh['x'=4,'core'=2,'col'=16,'layer'=4] {'col'}, dimensions={0} | all-to-all | bytes 655360 | tf_op jit(solution)/shard_map/all_to_all | solution.py:260
  63.1 0.9 broadcast_in_dim.2
  64.0 3.5 %all-to-all-start.2 = ((bf16[4,8,16,640]{3,2,1,0:T(8,128)(2,1)}), bf16[4,8,16,640]{3,2,1,0:T(8,128)(2,1)S(1)}, u32[]{:S(2)}, u32[]{:S(2)}) async-start(bf16[4,8,16,640]{3,2,1,0:T(8,128)(2,1)} %broadcast_in_dim.2), calls=%async_computation.2 | async-start | bytes 1310720 | tf_op jit(solution)/shard_map/all_to_all | solution.py:46
  67.5 1.9 %collective-permute-start.1 = (bf16[8,16,640]{2,1,0:T(8,128)(2,1)S(1)}, bf16[8,16,640]{2,1,0:T(8,128)(2,1)S(1)}, u32[]{:S(2)}, u32[]{:S(2)}) collective-permute-start(bf16[8,16,640]{2,1,0:T(8,128)(2,1)S(1)} %get-tuple-element.20), channel_id=1, source_target_pairs={{0,3},{1,0},{2,1},{3,2},{4,7},{5,4},{6,5},{7,6},{8,11},{9,8},{10,9... | collective-permute-start | bytes 491528 | tf_op jit(solution)/shard_map/ppermute | solution.py:20
  69.4 3.9 %collective-permute-start = (bf16[8,16,640]{2,1,0:T(8,128)(2,1)S(1)}, bf16[8,16,640]{2,1,0:T(8,128)(2,1)S(1)}, u32[]{:S(2)}, u32[]{:S(2)}) collective-permute-start(bf16[8,16,640]{2,1,0:T(8,128)(2,1)S(1)} %get-tuple-element.20), channel_id=1, source_target_pairs={{0,1},{1,2},{2,3},{3,0},{4,5},{5,6},{6,7},{7,4},{8,9},{9,10},{10,1... | collective-permute-start | bytes 491528 | tf_op jit(solution)/shard_map/ppermute | solution.py:20
  73.3 2.2 %collective-permute-start.2 = (bf16[8,16,640]{2,1,0:T(8,128)(2,1)S(1)}, bf16[8,16,640]{2,1,0:T(8,128)(2,1)S(1)}, u32[]{:S(2)}, u32[]{:S(2)}) collective-permute-start(bf16[8,16,640]{2,1,0:T(8,128)(2,1)S(1)} %get-tuple-element.20), channel_id=1, source_target_pairs={{0,2},{1,3},{2,0},{3,1},{4,6},{5,7},{6,4},{7,5},{8,10},{9,11},{10,... | collective-permute-start | bytes 491528 | tf_op jit(solution)/shard_map/ppermute | solution.py:20
  75.6 0.4 collective-permute-done.1
  76.0 1.8 %collective-permute-done = bf16[8,16,640]{2,1,0:T(8,128)(2,1)S(1)} collective-permute-done((bf16[8,16,640]{2,1,0:T(8,128)(2,1)S(1)}, bf16[8,16,640]{2,1,0:T(8,128)(2,1)S(1)}, u32[]{:S(2)}, u32[]{:S(2)}) %collective-permute-start) | collective-permute-done | bytes 163872 | tf_op jit(solution)/shard_map/ppermute | solution.py:20
  77.8 4.2 %collective-permute-done.2 = bf16[8,16,640]{2,1,0:T(8,128)(2,1)S(1)} collective-permute-done((bf16[8,16,640]{2,1,0:T(8,128)(2,1)S(1)}, bf16[8,16,640]{2,1,0:T(8,128)(2,1)S(1)}, u32[]{:S(2)}, u32[]{:S(2)}) %collective-permute-start.2) | collective-permute-done | bytes 163872 | tf_op jit(solution)/shard_map/ppermute | solution.py:20
  82.0 0.1 pad_maximum_fusion.refs_6_
  82.1 0.0 all-to-all-done.2.refs_2_
  82.2 2.0 %collective-permute-start.3 = (bf16[4,8,16,640]{3,2,1,0:T(8,128)(2,1)S(1)}, bf16[4,8,16,640]{3,2,1,0:T(8,128)(2,1)S(1)}, u32[]{:S(2)}, u32[]{:S(2)}) collective-permute-start(bf16[4,8,16,640]{3,2,1,0:T(8,128)(2,1)S(1)} %all-to-all-done.2.refs_2_), channel_id=1, source_target_pairs={{0,1},{1,2},{2,3},{3,0},{64,67},{65,64},{66,65},{67,66},{4,5},{5,6... | collective-permute-start | bytes 1966088 | tf_op jit(solution)/shard_map/ppermute | solution.py:38
  84.2 4.6 %collective-permute-start.6 = (bf16[4,8,16,640]{3,2,1,0:T(8,128)(2,1)S(1)}, bf16[4,8,16,640]{3,2,1,0:T(8,128)(2,1)S(1)}, u32[]{:S(2)}, u32[]{:S(2)}) collective-permute-start(bf16[4,8,16,640]{3,2,1,0:T(8,128)(2,1)S(1)} %pad_maximum_fusion.refs_6_), channel_id=1, source_target_pairs={{0,128},{128,256},{256,384},{384,0},{64,448},{192,64},{320,192},{4... | collective-permute-start | bytes 1966088 | tf_op jit(solution)/shard_map/ppermute | solution.py:38
  88.8 4.3 %collective-permute-start.4 = (bf16[4,8,16,640]{3,2,1,0:T(8,128)(2,1)S(1)}, bf16[4,8,16,640]{3,2,1,0:T(8,128)(2,1)S(1)}, u32[]{:S(2)}, u32[]{:S(2)}) collective-permute-start(bf16[4,8,16,640]{3,2,1,0:T(8,128)(2,1)S(1)} %all-to-all-done.2.refs_2_), channel_id=1, source_target_pairs={{0,3},{1,0},{2,1},{3,2},{64,65},{65,66},{66,67},{67,64},{4,7},{5,4... | collective-permute-start | bytes 1966088 | tf_op jit(solution)/shard_map/ppermute | solution.py:39
  93.1 3.2 %collective-permute-start.7 = (bf16[4,8,16,640]{3,2,1,0:T(8,128)(2,1)S(1)}, bf16[4,8,16,640]{3,2,1,0:T(8,128)(2,1)S(1)}, u32[]{:S(2)}, u32[]{:S(2)}) collective-permute-start(bf16[4,8,16,640]{3,2,1,0:T(8,128)(2,1)S(1)} %pad_maximum_fusion.refs_6_), channel_id=1, source_target_pairs={{0,384},{128,0},{256,128},{384,256},{64,192},{192,320},{320,448},{... | collective-permute-start | bytes 1966088 | tf_op jit(solution)/shard_map/ppermute | solution.py:39
  96.3 5.6 %collective-permute-done.3.refs_3_ = bf16[4,8,16,640]{3,2,1,0:T(8,128)(2,1)S(1)} collective-permute-done((bf16[4,8,16,640]{3,2,1,0:T(8,128)(2,1)S(1)}, bf16[4,8,16,640]{3,2,1,0:T(8,128)(2,1)S(1)}, u32[]{:S(2)}, u32[]{:S(2)}) %collective-permute-start.3) | collective-permute-done | bytes 655392 | tf_op jit(solution)/shard_map/ppermute | solution.py:38
  101.9 1.9 %collective-permute-start.5 = (bf16[4,8,16,640]{3,2,1,0:T(8,128)(2,1)S(1)}, bf16[4,8,16,640]{3,2,1,0:T(8,128)(2,1)S(1)}, u32[]{:S(2)}, u32[]{:S(2)}) collective-permute-start(bf16[4,8,16,640]{3,2,1,0:T(8,128)(2,1)S(1)} %collective-permute-done.3.refs_3_), channel_id=1, source_target_pairs={{0,1},{1,2},{2,3},{3,0},{64,67},{65,64},{66,65},{67,66},{4,5},{5,6... | collective-permute-start | bytes 1966088 | tf_op jit(solution)/shard_map/ppermute | solution.py:40
  103.8 1.5 collective-permute-done.6.refs_7_
  105.3 0.0 copy-start.1
  105.3 1.9 %collective-permute-start.8 = (bf16[4,8,16,640]{3,2,1,0:T(8,128)(2,1)S(1)}, bf16[4,8,16,640]{3,2,1,0:T(8,128)(2,1)}, u32[]{:S(2)}, u32[]{:S(2)}) collective-permute-start(bf16[4,8,16,640]{3,2,1,0:T(8,128)(2,1)S(1)} %collective-permute-done.6.refs_7_), channel_id=1, source_target_pairs={{0,128},{128,256},{256,384},{384,0},{64,448},{192,64},{320,192},{4... | collective-permute-start | bytes 1966088 | tf_op jit(solution)/shard_map/ppermute | solution.py:40
  107.2 0.1 pad_add_fusion.1.refs_0_
  107.3 0.0 collective-permute-done.4.refs_4_
  107.3 4.1 %collective-permute-done.7.refs_8_ = bf16[4,8,16,640]{3,2,1,0:T(8,128)(2,1)S(1)} collective-permute-done((bf16[4,8,16,640]{3,2,1,0:T(8,128)(2,1)S(1)}, bf16[4,8,16,640]{3,2,1,0:T(8,128)(2,1)S(1)}, u32[]{:S(2)}, u32[]{:S(2)}) %collective-permute-start.7) | collective-permute-done | bytes 655392 | tf_op jit(solution)/shard_map/ppermute | solution.py:39
  111.4 0.0 copy-start.2
  111.4 4.1 %collective-permute-done.5.refs_5_ = bf16[4,8,16,640]{3,2,1,0:T(8,128)(2,1)S(1)} collective-permute-done((bf16[4,8,16,640]{3,2,1,0:T(8,128)(2,1)S(1)}, bf16[4,8,16,640]{3,2,1,0:T(8,128)(2,1)S(1)}, u32[]{:S(2)}, u32[]{:S(2)}) %collective-permute-start.5) | collective-permute-done | bytes 655392 | tf_op jit(solution)/shard_map/ppermute | solution.py:40
  115.5 0.0 copy-done.1
  115.5 0.0 copy-done.2
  115.5 3.5 %collective-permute-done.8.refs_9_ = bf16[4,8,16,640]{3,2,1,0:T(8,128)(2,1)} collective-permute-done((bf16[4,8,16,640]{3,2,1,0:T(8,128)(2,1)S(1)}, bf16[4,8,16,640]{3,2,1,0:T(8,128)(2,1)}, u32[]{:S(2)}, u32[]{:S(2)}) %collective-permute-start.8) | collective-permute-done | bytes 655392 | tf_op jit(solution)/shard_map/ppermute | solution.py:40
  119.1 0.0 all-gather.2.cloned.1.call-done
  119.1 8.4 %gram.1 = (f32[320,640]{1,0:T(8,128)}, f32[320,640]{1,0:T(8,128)}) custom-call(s32[3]{0:T(128)S(1)} %pad_add_fusion.1.refs_0_, bf16[16,16,16,640]{3,2,1,0:T(8,128)(2,1)} %bitcast.20, bf16[4,8,16,640]{3,2,1,0:T(8,128)(2,1)S(1)} %all-to-all-done.2.refs_2_, bf16[4,8,16,640]{3,2,1,0:T(8,128)(2,1)S(1)} %collective-permute-done.3.refs_3_, ...), custom_call_target="tpu_custom_call" | custom-call | flops 3355443200 | bytes 10485760 | tf_op jit(solution)/shard_map/gram/pallas_call | solution.py:270
  127.4 1.9 %collective-permute-start.9 = (f32[320,640]{1,0:T(8,128)}, f32[320,640]{1,0:T(8,128)S(1)}, u32[]{:S(2)}, u32[]{:S(2)}) collective-permute-start(f32[320,640]{1,0:T(8,128)} %get-tuple-element.18), channel_id=1, source_target_pairs={{0,64},{64,0},{1,65},{65,1},{2,66},{66,2},{3,67},{67,3},{4,68},{68... | collective-permute-start | bytes 2457608 | tf_op jit(solution)/shard_map/ppermute | solution.py:296
  129.4 0.1 pad_add_fusion.refs_0_
  129.5 2.4 %collective-permute-done.9.refs_2_ = f32[320,640]{1,0:T(8,128)S(1)} collective-permute-done((f32[320,640]{1,0:T(8,128)}, f32[320,640]{1,0:T(8,128)S(1)}, u32[]{:S(2)}, u32[]{:S(2)}) %collective-permute-start.9) | collective-permute-done | bytes 819232 | tf_op jit(solution)/shard_map/ppermute | solution.py:296
  131.9 0.0 copy-start
  131.9 1.1 copy-done
  133.0 1.1 finish.1.own_ref
  134.1 1.9 %collective-permute-start.10 = (bf16[320,640]{1,0:T(8,128)(2,1)S(1)}, bf16[320,640]{1,0:T(8,128)(2,1)S(1)}, u32[]{:S(2)}, u32[]{:S(2)}) collective-permute-start(bf16[320,640]{1,0:T(8,128)(2,1)S(1)} %finish.1.own_ref), channel_id=1, source_target_pairs={{0,1},{1,2},{2,3},{3,0},{64,67},{65,64},{66,65},{67,66},{4,5},{5,6... | collective-permute-start | bytes 1228808 | tf_op jit(solution)/shard_map/ppermute | solution.py:38
  136.1 5.1 %collective-permute-start.11 = (bf16[320,640]{1,0:T(8,128)(2,1)S(1)}, bf16[320,640]{1,0:T(8,128)(2,1)S(1)}, u32[]{:S(2)}, u32[]{:S(2)}) collective-permute-start(bf16[320,640]{1,0:T(8,128)(2,1)S(1)} %finish.1.own_ref), channel_id=1, source_target_pairs={{0,3},{1,0},{2,1},{3,2},{64,65},{65,66},{66,67},{67,64},{4,7},{5,4... | collective-permute-start | bytes 1228808 | tf_op jit(solution)/shard_map/ppermute | solution.py:39
  141.2 5.5 %collective-permute-done.10.ahead_ref = bf16[320,640]{1,0:T(8,128)(2,1)S(1)} collective-permute-done((bf16[320,640]{1,0:T(8,128)(2,1)S(1)}, bf16[320,640]{1,0:T(8,128)(2,1)S(1)}, u32[]{:S(2)}, u32[]{:S(2)}) %collective-permute-start.10) | collective-permute-done | bytes 409632 | tf_op jit(solution)/shard_map/ppermute | solution.py:38
  146.7 1.9 %collective-permute-start.12 = (bf16[320,640]{1,0:T(8,128)(2,1)S(1)}, bf16[320,640]{1,0:T(8,128)(2,1)S(1)}, u32[]{:S(2)}, u32[]{:S(2)}) collective-permute-start(bf16[320,640]{1,0:T(8,128)(2,1)S(1)} %collective-permute-done.10.ahead_ref), channel_id=1, source_target_pairs={{0,1},{1,2},{2,3},{3,0},{64,67},{65,64},{66,65},{67,66},{4,5},{5,6... | collective-permute-start | bytes 1228808 | tf_op jit(solution)/shard_map/ppermute | solution.py:40
  148.6 0.0 collective-permute-done.11.behind_ref
  148.6 1.1 place.1.held_ref
  149.7 8.1 %collective-permute-done.12.across_ref = bf16[320,640]{1,0:T(8,128)(2,1)S(1)} collective-permute-done((bf16[320,640]{1,0:T(8,128)(2,1)S(1)}, bf16[320,640]{1,0:T(8,128)(2,1)S(1)}, u32[]{:S(2)}, u32[]{:S(2)}) %collective-permute-start.12) | collective-permute-done | bytes 409632 | tf_op jit(solution)/shard_map/ppermute | solution.py:40
  157.7 0.8 last.1
  (1 shorter events, 0.0 us)
Async XLA Ops:
  6.5 112.5 %all-gather.2.cloned.1.call-start = ((), (), s32[]{:S(2)}) async-start(), calls=%async_computation.3 | async-start | bytes 5570560 | tf_op jit(solution)/shard_map/all_gather | solution.py:258
  64.0 18.2 %all-to-all-start.2 = ((bf16[4,8,16,640]{3,2,1,0:T(8,128)(2,1)}), bf16[4,8,16,640]{3,2,1,0:T(8,128)(2,1)S(1)}, u32[]{:S(2)}, u32[]{:S(2)}) async-start(bf16[4,8,16,640]{3,2,1,0:T(8,128)(2,1)} %broadcast_in_dim.2), calls=%async_computation.2 | async-start | bytes 1310720 | tf_op jit(solution)/shard_map/all_to_all | solution.py:46
  67.5 8.5 %collective-permute-start.1 = (bf16[8,16,640]{2,1,0:T(8,128)(2,1)S(1)}, bf16[8,16,640]{2,1,0:T(8,128)(2,1)S(1)}, u32[]{:S(2)}, u32[]{:S(2)}) collective-permute-start(bf16[8,16,640]{2,1,0:T(8,128)(2,1)S(1)} %get-tuple-element.20), channel_id=1, source_target_pairs={{0,3},{1,0},{2,1},{3,2},{4,7},{5,4},{6,5},{7,6},{8,11},{9,8},{10,9... | collective-permute-start | bytes 491528 | tf_op jit(solution)/shard_map/ppermute | solution.py:20
  69.4 8.4 %collective-permute-start = (bf16[8,16,640]{2,1,0:T(8,128)(2,1)S(1)}, bf16[8,16,640]{2,1,0:T(8,128)(2,1)S(1)}, u32[]{:S(2)}, u32[]{:S(2)}) collective-permute-start(bf16[8,16,640]{2,1,0:T(8,128)(2,1)S(1)} %get-tuple-element.20), channel_id=1, source_target_pairs={{0,1},{1,2},{2,3},{3,0},{4,5},{5,6},{6,7},{7,4},{8,9},{9,10},{10,1... | collective-permute-start | bytes 491528 | tf_op jit(solution)/shard_map/ppermute | solution.py:20
  73.3 8.7 %collective-permute-start.2 = (bf16[8,16,640]{2,1,0:T(8,128)(2,1)S(1)}, bf16[8,16,640]{2,1,0:T(8,128)(2,1)S(1)}, u32[]{:S(2)}, u32[]{:S(2)}) collective-permute-start(bf16[8,16,640]{2,1,0:T(8,128)(2,1)S(1)} %get-tuple-element.20), channel_id=1, source_target_pairs={{0,2},{1,3},{2,0},{3,1},{4,6},{5,7},{6,4},{7,5},{8,10},{9,11},{10,... | collective-permute-start | bytes 491528 | tf_op jit(solution)/shard_map/ppermute | solution.py:20
  82.2 19.7 %collective-permute-start.3 = (bf16[4,8,16,640]{3,2,1,0:T(8,128)(2,1)S(1)}, bf16[4,8,16,640]{3,2,1,0:T(8,128)(2,1)S(1)}, u32[]{:S(2)}, u32[]{:S(2)}) collective-permute-start(bf16[4,8,16,640]{3,2,1,0:T(8,128)(2,1)S(1)} %all-to-all-done.2.refs_2_), channel_id=1, source_target_pairs={{0,1},{1,2},{2,3},{3,0},{64,67},{65,64},{66,65},{67,66},{4,5},{5,6... | collective-permute-start | bytes 1966088 | tf_op jit(solution)/shard_map/ppermute | solution.py:38
  84.2 21.1 %collective-permute-start.6 = (bf16[4,8,16,640]{3,2,1,0:T(8,128)(2,1)S(1)}, bf16[4,8,16,640]{3,2,1,0:T(8,128)(2,1)S(1)}, u32[]{:S(2)}, u32[]{:S(2)}) collective-permute-start(bf16[4,8,16,640]{3,2,1,0:T(8,128)(2,1)S(1)} %pad_maximum_fusion.refs_6_), channel_id=1, source_target_pairs={{0,128},{128,256},{256,384},{384,0},{64,448},{192,64},{320,192},{4... | collective-permute-start | bytes 1966088 | tf_op jit(solution)/shard_map/ppermute | solution.py:38
  88.8 18.5 %collective-permute-start.4 = (bf16[4,8,16,640]{3,2,1,0:T(8,128)(2,1)S(1)}, bf16[4,8,16,640]{3,2,1,0:T(8,128)(2,1)S(1)}, u32[]{:S(2)}, u32[]{:S(2)}) collective-permute-start(bf16[4,8,16,640]{3,2,1,0:T(8,128)(2,1)S(1)} %all-to-all-done.2.refs_2_), channel_id=1, source_target_pairs={{0,3},{1,0},{2,1},{3,2},{64,65},{65,66},{66,67},{67,64},{4,7},{5,4... | collective-permute-start | bytes 1966088 | tf_op jit(solution)/shard_map/ppermute | solution.py:39
  93.1 18.3 %collective-permute-start.7 = (bf16[4,8,16,640]{3,2,1,0:T(8,128)(2,1)S(1)}, bf16[4,8,16,640]{3,2,1,0:T(8,128)(2,1)S(1)}, u32[]{:S(2)}, u32[]{:S(2)}) collective-permute-start(bf16[4,8,16,640]{3,2,1,0:T(8,128)(2,1)S(1)} %pad_maximum_fusion.refs_6_), channel_id=1, source_target_pairs={{0,384},{128,0},{256,128},{384,256},{64,192},{192,320},{320,448},{... | collective-permute-start | bytes 1966088 | tf_op jit(solution)/shard_map/ppermute | solution.py:39
  101.9 13.7 %collective-permute-start.5 = (bf16[4,8,16,640]{3,2,1,0:T(8,128)(2,1)S(1)}, bf16[4,8,16,640]{3,2,1,0:T(8,128)(2,1)S(1)}, u32[]{:S(2)}, u32[]{:S(2)}) collective-permute-start(bf16[4,8,16,640]{3,2,1,0:T(8,128)(2,1)S(1)} %collective-permute-done.3.refs_3_), channel_id=1, source_target_pairs={{0,1},{1,2},{2,3},{3,0},{64,67},{65,64},{66,65},{67,66},{4,5},{5,6... | collective-permute-start | bytes 1966088 | tf_op jit(solution)/shard_map/ppermute | solution.py:40
  105.3 10.3 %copy-start.1 = (bf16[4,8,16,640]{3,2,1,0:T(8,128)(2,1)}, bf16[4,8,16,640]{3,2,1,0:T(8,128)(2,1)S(1)}, u32[]{:S(2)}) copy-start(bf16[4,8,16,640]{3,2,1,0:T(8,128)(2,1)S(1)} %collective-permute-done.6.refs_7_) | copy-start | bytes 1966084
  105.3 13.8 %collective-permute-start.8 = (bf16[4,8,16,640]{3,2,1,0:T(8,128)(2,1)S(1)}, bf16[4,8,16,640]{3,2,1,0:T(8,128)(2,1)}, u32[]{:S(2)}, u32[]{:S(2)}) collective-permute-start(bf16[4,8,16,640]{3,2,1,0:T(8,128)(2,1)S(1)} %collective-permute-done.6.refs_7_), channel_id=1, source_target_pairs={{0,128},{128,256},{256,384},{384,0},{64,448},{192,64},{320,192},{4... | collective-permute-start | bytes 1966088 | tf_op jit(solution)/shard_map/ppermute | solution.py:40
  111.4 4.2 %copy-start.2 = (bf16[4,8,16,640]{3,2,1,0:T(8,128)(2,1)}, bf16[4,8,16,640]{3,2,1,0:T(8,128)(2,1)S(1)}, u32[]{:S(2)}) copy-start(bf16[4,8,16,640]{3,2,1,0:T(8,128)(2,1)S(1)} %collective-permute-done.7.refs_8_) | copy-start | bytes 1966084
  127.4 4.4 %collective-permute-start.9 = (f32[320,640]{1,0:T(8,128)}, f32[320,640]{1,0:T(8,128)S(1)}, u32[]{:S(2)}, u32[]{:S(2)}) collective-permute-start(f32[320,640]{1,0:T(8,128)} %get-tuple-element.18), channel_id=1, source_target_pairs={{0,64},{64,0},{1,65},{65,1},{2,66},{66,2},{3,67},{67,3},{4,68},{68... | collective-permute-start | bytes 2457608 | tf_op jit(solution)/shard_map/ppermute | solution.py:296
  131.9 1.1 copy-start
  134.1 12.5 %collective-permute-start.10 = (bf16[320,640]{1,0:T(8,128)(2,1)S(1)}, bf16[320,640]{1,0:T(8,128)(2,1)S(1)}, u32[]{:S(2)}, u32[]{:S(2)}) collective-permute-start(bf16[320,640]{1,0:T(8,128)(2,1)S(1)} %finish.1.own_ref), channel_id=1, source_target_pairs={{0,1},{1,2},{2,3},{3,0},{64,67},{65,64},{66,65},{67,66},{4,5},{5,6... | collective-permute-start | bytes 1228808 | tf_op jit(solution)/shard_map/ppermute | solution.py:38
  136.1 12.5 %collective-permute-start.11 = (bf16[320,640]{1,0:T(8,128)(2,1)S(1)}, bf16[320,640]{1,0:T(8,128)(2,1)S(1)}, u32[]{:S(2)}, u32[]{:S(2)}) collective-permute-start(bf16[320,640]{1,0:T(8,128)(2,1)S(1)} %finish.1.own_ref), channel_id=1, source_target_pairs={{0,3},{1,0},{2,1},{3,2},{64,65},{65,66},{66,67},{67,64},{4,7},{5,4... | collective-permute-start | bytes 1228808 | tf_op jit(solution)/shard_map/ppermute | solution.py:39
  146.7 11.0 %collective-permute-start.12 = (bf16[320,640]{1,0:T(8,128)(2,1)S(1)}, bf16[320,640]{1,0:T(8,128)(2,1)S(1)}, u32[]{:S(2)}, u32[]{:S(2)}) collective-permute-start(bf16[320,640]{1,0:T(8,128)(2,1)S(1)} %collective-permute-done.10.ahead_ref), channel_id=1, source_target_pairs={{0,1},{1,2},{2,3},{3,0},{64,67},{65,64},{66,65},{67,66},{4,5},{5,6... | collective-permute-start | bytes 1228808 | tf_op jit(solution)/shard_map/ppermute | solution.py:40
Sparse Core Ops, SparseCore 0:
  25.6 90.7 all-gather.1

commit v12 on v7

--- a/solution.py
+++ b/solution.py
@@ -47,7 +47,7 @@
 
 
 SHIFTS = (0, 1, 3, 2)
-GROUP = 4
+GROUP = 8
 
 
 def weigh_kernel(owned, nz, place_ref, pattern_ref, weight_ref, block_ref, by_col_ref, by_chip_ref):
@@ -241,7 +241,6 @@
     upper, lower = part[: nz // 2], part[nz // 2 :]
     along_x = collect(upper, "x", nx)
     along_y = jnp.stack(spread(lower, "layer", ny))
-    along_x, along_y = lax.optimization_barrier((along_x, along_y))
     by_x, by_y = relay([along_y, along_x], ["x", "layer"], [nx, ny])
 
     place = jnp.stack([x, y, c]).astype(jnp.int32)

time: 166 us -> 168 us (1.012)
  no operation moved by 1% of the time
where the time goes in v12:
time: 168 us; the launch traced here: 167 us
  blocking collectives  53.9 us (32%)
  starting transfers between devices  41.5 us (25%)
  waiting for transfers between devices  41.5 us (25%)
  between operations  13.6 us (8%)
  Pallas kernels  13.3 us (8%)
  local copies, waits for them, and re-layouts  2.93 us (2%)
    all_to_all x1, blocking collectives, body(): lax.all_to_all(by_col, 'col', split_axis=0, concat_axis=0, tiled=True)  37.6 us
    all_to_all x1, blocking collectives, body(): lax.all_to_all(by_chip, ('x', 'layer'), split_axis=0, concat_axis=0, tile...  16.3 us
    ppermute x3, waiting for transfers between devices, relay(): across = [lax.ppermute(v, g, w[0]) for v, g, w in zip(ahead, groups, ways)]  15.4 us
    ppermute x3, waiting for transfers between devices, relay(): ahead = [lax.ppermute(v, g, w[0]) for v, g, w in zip(values, groups, ways)]  13.8 us
    ppermute x3, starting transfers between devices, relay(): behind = [lax.ppermute(v, g, w[1]) for v, g, w in zip(values, groups, ways)]  13.4 us
    pallas_call x1, Pallas kernels, body(): pl.pallas_call(lambda *refs: gram_kernel(half, steps, *refs), out_shape=(...  8.17 us
    ppermute x3, starting transfers between devices, spread(): lax.ppermute(value, axis, around(n, s))  8.07 us
    ppermute x3, starting transfers between devices, relay(): ahead = [lax.ppermute(v, g, w[0]) for v, g, w in zip(values, groups, ways)]  7.72 us
  transfers between devices with their start and end apart: 15, of which 11 were waited for; matrix products, arithmetic and copies ran while one was open for 1% of the time, Pallas kernels for 1%

profile of v12, /device:TPU:32, one launch (start us, length us, event | category | flops | bytes accessed | tf_op | source)
XLA Modules:
  0.0 166.9 jit_solution(10676661711207288485)
XLA Ops:
  6.5 0.0 all-gather.2.cloned.1.call-start
  6.5 2.2 %weigh.1 = (bf16[16,16,640]{2,1,0:T(8,128)(2,1)}, bf16[16,16,640]{2,1,0:T(8,128)(2,1)}) custom-call(s32[1]{0:T(128)} %bitcast.5.refs_0_, s32[64,80]{1,0:T(8,128)} %refs_1_.1, f32[1,16]{1,0:T(1,128)} %bitcast.19, bf16[16,10240]{1,0:T(8,128)(2,1)} %refs_3_.1), custom_call_target="tpu_custom_call" | custom-call | tf_op jit(solution)/shard_map/weigh/pallas_call | solution.py:225
  8.7 16.3 %all_to_all.15 = bf16[16,16,640]{2,1,0:T(8,128)(2,1)} all-to-all(bf16[16,16,640]{2,1,0:T(8,128)(2,1)} %get-tuple-element.10), channel_id=1, replica_groups=mesh['x'=4,'core'=2,'col'=16,'layer'=4] {'x','layer'}, dimensions={0} | all-to-all | bytes 655360 | tf_op jit(solution)/shard_map/all_to_all | solution.py:236
  25.0 0.0 all-gather.2.cloned.1.call-update
  25.1 37.6 %all_to_all.16 = bf16[16,16,640]{2,1,0:T(8,128)(2,1)S(1)} all-to-all(bf16[16,16,640]{2,1,0:T(8,128)(2,1)} %get-tuple-element.12), channel_id=1, replica_groups=mesh['x'=4,'core'=2,'col'=16,'layer'=4] {'col'}, dimensions={0} | all-to-all | bytes 655360 | tf_op jit(solution)/shard_map/all_to_all | solution.py:240
  62.7 0.9 broadcast_in_dim.2
  63.5 3.5 %all-to-all-start.2 = ((bf16[4,8,16,640]{3,2,1,0:T(8,128)(2,1)}), bf16[4,8,16,640]{3,2,1,0:T(8,128)(2,1)S(1)}, u32[]{:S(2)}, u32[]{:S(2)}) async-start(bf16[4,8,16,640]{3,2,1,0:T(8,128)(2,1)} %broadcast_in_dim.2), calls=%async_computation.2 | async-start | bytes 1310720 | tf_op jit(solution)/shard_map/all_to_all | solution.py:46
  67.0 1.9 %collective-permute-start.4 = (bf16[8,16,640]{2,1,0:T(8,128)(2,1)S(1)}, bf16[8,16,640]{2,1,0:T(8,128)(2,1)S(1)}, u32[]{:S(2)}, u32[]{:S(2)}) collective-permute-start(bf16[8,16,640]{2,1,0:T(8,128)(2,1)S(1)} %get-tuple-element.16), channel_id=1, source_target_pairs={{0,3},{1,0},{2,1},{3,2},{4,7},{5,4},{6,5},{7,6},{8,11},{9,8},{10,9... | collective-permute-start | bytes 491528 | tf_op jit(solution)/shard_map/ppermute | solution.py:20
  69.0 3.9 %collective-permute-start.3 = (bf16[8,16,640]{2,1,0:T(8,128)(2,1)S(1)}, bf16[8,16,640]{2,1,0:T(8,128)(2,1)S(1)}, u32[]{:S(2)}, u32[]{:S(2)}) collective-permute-start(bf16[8,16,640]{2,1,0:T(8,128)(2,1)S(1)} %get-tuple-element.16), channel_id=1, source_target_pairs={{0,1},{1,2},{2,3},{3,0},{4,5},{5,6},{6,7},{7,4},{8,9},{9,10},{10,1... | collective-permute-start | bytes 491528 | tf_op jit(solution)/shard_map/ppermute | solution.py:20
  72.9 2.2 %collective-permute-start.5 = (bf16[8,16,640]{2,1,0:T(8,128)(2,1)S(1)}, bf16[8,16,640]{2,1,0:T(8,128)(2,1)S(1)}, u32[]{:S(2)}, u32[]{:S(2)}) collective-permute-start(bf16[8,16,640]{2,1,0:T(8,128)(2,1)S(1)} %get-tuple-element.16), channel_id=1, source_target_pairs={{0,2},{1,3},{2,0},{3,1},{4,6},{5,7},{6,4},{7,5},{8,10},{9,11},{10,... | collective-permute-start | bytes 491528 | tf_op jit(solution)/shard_map/ppermute | solution.py:20
  75.1 0.4 collective-permute-done.4
  75.6 1.8 %collective-permute-done.3 = bf16[8,16,640]{2,1,0:T(8,128)(2,1)S(1)} collective-permute-done((bf16[8,16,640]{2,1,0:T(8,128)(2,1)S(1)}, bf16[8,16,640]{2,1,0:T(8,128)(2,1)S(1)}, u32[]{:S(2)}, u32[]{:S(2)}) %collective-permute-start.3) | collective-permute-done | bytes 163872 | tf_op jit(solution)/shard_map/ppermute | solution.py:20
  77.4 4.2 %collective-permute-done.5 = bf16[8,16,640]{2,1,0:T(8,128)(2,1)S(1)} collective-permute-done((bf16[8,16,640]{2,1,0:T(8,128)(2,1)S(1)}, bf16[8,16,640]{2,1,0:T(8,128)(2,1)S(1)}, u32[]{:S(2)}, u32[]{:S(2)}) %collective-permute-start.5) | collective-permute-done | bytes 163872 | tf_op jit(solution)/shard_map/ppermute | solution.py:20
  81.6 0.1 pad_maximum_fusion.refs_6_
  81.7 3.9 %collective-permute-start.6 = (bf16[4,8,16,640]{3,2,1,0:T(8,128)(2,1)S(1)}, bf16[4,8,16,640]{3,2,1,0:T(8,128)(2,1)}, u32[]{:S(2)}, u32[]{:S(2)}) collective-permute-start(bf16[4,8,16,640]{3,2,1,0:T(8,128)(2,1)S(1)} %pad_maximum_fusion.refs_6_), channel_id=1, source_target_pairs={{0,128},{128,256},{256,384},{384,0},{64,448},{192,64},{320,192},{4... | collective-permute-start | bytes 1966088 | tf_op jit(solution)/shard_map/ppermute | solution.py:38
  85.6 0.0 all-to-all-done.2.refs_2_
  85.6 1.9 %collective-permute-start = (bf16[4,8,16,640]{3,2,1,0:T(8,128)(2,1)S(1)}, bf16[4,8,16,640]{3,2,1,0:T(8,128)(2,1)S(1)}, u32[]{:S(2)}, u32[]{:S(2)}) collective-permute-start(bf16[4,8,16,640]{3,2,1,0:T(8,128)(2,1)S(1)} %all-to-all-done.2.refs_2_), channel_id=1, source_target_pairs={{0,1},{1,2},{2,3},{3,0},{64,67},{65,64},{66,65},{67,66},{4,5},{5,6... | collective-permute-start | bytes 1966088 | tf_op jit(solution)/shard_map/ppermute | solution.py:38
  87.6 3.2 %collective-permute-start.7 = (bf16[4,8,16,640]{3,2,1,0:T(8,128)(2,1)S(1)}, bf16[4,8,16,640]{3,2,1,0:T(8,128)(2,1)S(1)}, u32[]{:S(2)}, u32[]{:S(2)}) collective-permute-start(bf16[4,8,16,640]{3,2,1,0:T(8,128)(2,1)S(1)} %pad_maximum_fusion.refs_6_), channel_id=1, source_target_pairs={{0,384},{128,0},{256,128},{384,256},{64,192},{192,320},{320,448},{... | collective-permute-start | bytes 1966088 | tf_op jit(solution)/shard_map/ppermute | solution.py:39
  90.7 5.1 %collective-permute-start.1 = (bf16[4,8,16,640]{3,2,1,0:T(8,128)(2,1)S(1)}, bf16[4,8,16,640]{3,2,1,0:T(8,128)(2,1)S(1)}, u32[]{:S(2)}, u32[]{:S(2)}) collective-permute-start(bf16[4,8,16,640]{3,2,1,0:T(8,128)(2,1)S(1)} %all-to-all-done.2.refs_2_), channel_id=1, source_target_pairs={{0,3},{1,0},{2,1},{3,2},{64,65},{65,66},{66,67},{67,64},{4,7},{5,4... | collective-permute-start | bytes 1966088 | tf_op jit(solution)/shard_map/ppermute | solution.py:39
  95.9 5.7 %collective-permute-done.6.refs_7_ = bf16[4,8,16,640]{3,2,1,0:T(8,128)(2,1)} collective-permute-done((bf16[4,8,16,640]{3,2,1,0:T(8,128)(2,1)S(1)}, bf16[4,8,16,640]{3,2,1,0:T(8,128)(2,1)}, u32[]{:S(2)}, u32[]{:S(2)}) %collective-permute-start.6) | collective-permute-done | bytes 655392 | tf_op jit(solution)/shard_map/ppermute | solution.py:38
  101.5 3.0 %collective-permute-start.8 = (bf16[4,8,16,640]{3,2,1,0:T(8,128)(2,1)}, bf16[4,8,16,640]{3,2,1,0:T(8,128)(2,1)S(1)}, u32[]{:S(2)}, u32[]{:S(2)}) collective-permute-start(bf16[4,8,16,640]{3,2,1,0:T(8,128)(2,1)} %collective-permute-done.6.refs_7_), channel_id=1, source_target_pairs={{0,128},{128,256},{256,384},{384,0},{64,448},{192,64},{320,192},{4... | collective-permute-start | bytes 1966088 | tf_op jit(solution)/shard_map/ppermute | solution.py:40
  104.5 0.8 collective-permute-done.refs_3_
  105.4 1.9 %collective-permute-start.2 = (bf16[4,8,16,640]{3,2,1,0:T(8,128)(2,1)S(1)}, bf16[4,8,16,640]{3,2,1,0:T(8,128)(2,1)S(1)}, u32[]{:S(2)}, u32[]{:S(2)}) collective-permute-start(bf16[4,8,16,640]{3,2,1,0:T(8,128)(2,1)S(1)} %collective-permute-done.refs_3_), channel_id=1, source_target_pairs={{0,1},{1,2},{2,3},{3,0},{64,67},{65,64},{66,65},{67,66},{4,5},{5,6... | collective-permute-start | bytes 1966088 | tf_op jit(solution)/shard_map/ppermute | solution.py:40
  107.3 0.1 pad_add_fusion.1.refs_0_
  107.4 0.0 collective-permute-done.7.refs_8_
  107.4 0.0 copy-start.1
  107.4 3.4 %collective-permute-done.1.refs_4_ = bf16[4,8,16,640]{3,2,1,0:T(8,128)(2,1)S(1)} collective-permute-done((bf16[4,8,16,640]{3,2,1,0:T(8,128)(2,1)S(1)}, bf16[4,8,16,640]{3,2,1,0:T(8,128)(2,1)S(1)}, u32[]{:S(2)}, u32[]{:S(2)}) %collective-permute-start.1) | collective-permute-done | bytes 655392 | tf_op jit(solution)/shard_map/ppermute | solution.py:39
  110.8 0.0 copy-done.1
  110.8 4.6 %collective-permute-done.8.refs_9_ = bf16[4,8,16,640]{3,2,1,0:T(8,128)(2,1)S(1)} collective-permute-done((bf16[4,8,16,640]{3,2,1,0:T(8,128)(2,1)}, bf16[4,8,16,640]{3,2,1,0:T(8,128)(2,1)S(1)}, u32[]{:S(2)}, u32[]{:S(2)}) %collective-permute-start.8) | collective-permute-done | bytes 655392 | tf_op jit(solution)/shard_map/ppermute | solution.py:40
  115.4 0.0 copy-start.2
  115.4 0.9 copy-done.2
  116.3 2.8 %collective-permute-done.2.refs_5_ = bf16[4,8,16,640]{3,2,1,0:T(8,128)(2,1)S(1)} collective-permute-done((bf16[4,8,16,640]{3,2,1,0:T(8,128)(2,1)S(1)}, bf16[4,8,16,640]{3,2,1,0:T(8,128)(2,1)S(1)}, u32[]{:S(2)}, u32[]{:S(2)}) %collective-permute-start.2) | collective-permute-done | bytes 655392 | tf_op jit(solution)/shard_map/ppermute | solution.py:40
  119.1 0.0 all-gather.2.cloned.1.call-done
  119.1 8.2 %gram.1 = (f32[320,640]{1,0:T(8,128)}, f32[320,640]{1,0:T(8,128)}) custom-call(s32[3]{0:T(128)S(1)} %pad_add_fusion.1.refs_0_, bf16[16,16,16,640]{3,2,1,0:T(8,128)(2,1)} %bitcast.20, bf16[4,8,16,640]{3,2,1,0:T(8,128)(2,1)S(1)} %all-to-all-done.2.refs_2_, bf16[4,8,16,640]{3,2,1,0:T(8,128)(2,1)S(1)} %collective-permute-done.refs_3_, ...), custom_call_target="tpu_custom_call" | custom-call | flops 3355443200 | bytes 10485760 | tf_op jit(solution)/shard_map/gram/pallas_call | solution.py:249
  127.2 1.9 %collective-permute-start.9 = (f32[320,640]{1,0:T(8,128)}, f32[320,640]{1,0:T(8,128)S(1)}, u32[]{:S(2)}, u32[]{:S(2)}) collective-permute-start(f32[320,640]{1,0:T(8,128)} %get-tuple-element.14), channel_id=1, source_target_pairs={{0,64},{64,0},{1,65},{65,1},{2,66},{66,2},{3,67},{67,3},{4,68},{68... | collective-permute-start | bytes 2457608 | tf_op jit(solution)/shard_map/ppermute | solution.py:275
  129.2 0.1 pad_add_fusion.refs_0_
  129.2 2.4 %collective-permute-done.9.refs_2_ = f32[320,640]{1,0:T(8,128)S(1)} collective-permute-done((f32[320,640]{1,0:T(8,128)}, f32[320,640]{1,0:T(8,128)S(1)}, u32[]{:S(2)}, u32[]{:S(2)}) %collective-permute-start.9) | collective-permute-done | bytes 819232 | tf_op jit(solution)/shard_map/ppermute | solution.py:275
  131.6 0.0 copy-start
  131.7 1.1 copy-done
  132.8 1.1 finish.1.own_ref
  133.9 1.9 %collective-permute-start.10 = (bf16[320,640]{1,0:T(8,128)(2,1)S(1)}, bf16[320,640]{1,0:T(8,128)(2,1)S(1)}, u32[]{:S(2)}, u32[]{:S(2)}) collective-permute-start(bf16[320,640]{1,0:T(8,128)(2,1)S(1)} %finish.1.own_ref), channel_id=1, source_target_pairs={{0,1},{1,2},{2,3},{3,0},{64,67},{65,64},{66,65},{67,66},{4,5},{5,6... | collective-permute-start | bytes 1228808 | tf_op jit(solution)/shard_map/ppermute | solution.py:38
  135.8 5.1 %collective-permute-start.11 = (bf16[320,640]{1,0:T(8,128)(2,1)S(1)}, bf16[320,640]{1,0:T(8,128)(2,1)S(1)}, u32[]{:S(2)}, u32[]{:S(2)}) collective-permute-start(bf16[320,640]{1,0:T(8,128)(2,1)S(1)} %finish.1.own_ref), channel_id=1, source_target_pairs={{0,3},{1,0},{2,1},{3,2},{64,65},{65,66},{66,67},{67,64},{4,7},{5,4... | collective-permute-start | bytes 1228808 | tf_op jit(solution)/shard_map/ppermute | solution.py:39
  141.0 7.3 %collective-permute-done.10.ahead_ref = bf16[320,640]{1,0:T(8,128)(2,1)S(1)} collective-permute-done((bf16[320,640]{1,0:T(8,128)(2,1)S(1)}, bf16[320,640]{1,0:T(8,128)(2,1)S(1)}, u32[]{:S(2)}, u32[]{:S(2)}) %collective-permute-start.10) | collective-permute-done | bytes 409632 | tf_op jit(solution)/shard_map/ppermute | solution.py:38
  148.3 1.9 %collective-permute-start.12 = (bf16[320,640]{1,0:T(8,128)(2,1)S(1)}, bf16[320,640]{1,0:T(8,128)(2,1)S(1)}, u32[]{:S(2)}, u32[]{:S(2)}) collective-permute-start(bf16[320,640]{1,0:T(8,128)(2,1)S(1)} %collective-permute-done.10.ahead_ref), channel_id=1, source_target_pairs={{0,1},{1,2},{2,3},{3,0},{64,67},{65,64},{66,65},{67,66},{4,5},{5,6... | collective-permute-start | bytes 1228808 | tf_op jit(solution)/shard_map/ppermute | solution.py:40
  150.2 0.0 collective-permute-done.11.behind_ref
  150.2 1.1 place.1.held_ref
  151.2 8.1 %collective-permute-done.12.across_ref = bf16[320,640]{1,0:T(8,128)(2,1)S(1)} collective-permute-done((bf16[320,640]{1,0:T(8,128)(2,1)S(1)}, bf16[320,640]{1,0:T(8,128)(2,1)S(1)}, u32[]{:S(2)}, u32[]{:S(2)}) %collective-permute-start.12) | collective-permute-done | bytes 409632 | tf_op jit(solution)/shard_map/ppermute | solution.py:40
  159.3 0.8 last.1
  (1 shorter events, 0.0 us)
Async XLA Ops:
  6.5 112.5 %all-gather.2.cloned.1.call-start = ((), (), s32[]{:S(2)}) async-start(), calls=%async_computation.3 | async-start | bytes 5570560 | tf_op jit(solution)/shard_map/all_gather | solution.py:238
  63.5 22.1 %all-to-all-start.2 = ((bf16[4,8,16,640]{3,2,1,0:T(8,128)(2,1)}), bf16[4,8,16,640]{3,2,1,0:T(8,128)(2,1)S(1)}, u32[]{:S(2)}, u32[]{:S(2)}) async-start(bf16[4,8,16,640]{3,2,1,0:T(8,128)(2,1)} %broadcast_in_dim.2), calls=%async_computation.2 | async-start | bytes 1310720 | tf_op jit(solution)/shard_map/all_to_all | solution.py:46
  67.0 8.5 %collective-permute-start.4 = (bf16[8,16,640]{2,1,0:T(8,128)(2,1)S(1)}, bf16[8,16,640]{2,1,0:T(8,128)(2,1)S(1)}, u32[]{:S(2)}, u32[]{:S(2)}) collective-permute-start(bf16[8,16,640]{2,1,0:T(8,128)(2,1)S(1)} %get-tuple-element.16), channel_id=1, source_target_pairs={{0,3},{1,0},{2,1},{3,2},{4,7},{5,4},{6,5},{7,6},{8,11},{9,8},{10,9... | collective-permute-start | bytes 491528 | tf_op jit(solution)/shard_map/ppermute | solution.py:20
  69.0 8.4 %collective-permute-start.3 = (bf16[8,16,640]{2,1,0:T(8,128)(2,1)S(1)}, bf16[8,16,640]{2,1,0:T(8,128)(2,1)S(1)}, u32[]{:S(2)}, u32[]{:S(2)}) collective-permute-start(bf16[8,16,640]{2,1,0:T(8,128)(2,1)S(1)} %get-tuple-element.16), channel_id=1, source_target_pairs={{0,1},{1,2},{2,3},{3,0},{4,5},{5,6},{6,7},{7,4},{8,9},{9,10},{10,1... | collective-permute-start | bytes 491528 | tf_op jit(solution)/shard_map/ppermute | solution.py:20
  72.9 8.7 %collective-permute-start.5 = (bf16[8,16,640]{2,1,0:T(8,128)(2,1)S(1)}, bf16[8,16,640]{2,1,0:T(8,128)(2,1)S(1)}, u32[]{:S(2)}, u32[]{:S(2)}) collective-permute-start(bf16[8,16,640]{2,1,0:T(8,128)(2,1)S(1)} %get-tuple-element.16), channel_id=1, source_target_pairs={{0,2},{1,3},{2,0},{3,1},{4,6},{5,7},{6,4},{7,5},{8,10},{9,11},{10,... | collective-permute-start | bytes 491528 | tf_op jit(solution)/shard_map/ppermute | solution.py:20
  81.7 19.8 %collective-permute-start.6 = (bf16[4,8,16,640]{3,2,1,0:T(8,128)(2,1)S(1)}, bf16[4,8,16,640]{3,2,1,0:T(8,128)(2,1)}, u32[]{:S(2)}, u32[]{:S(2)}) collective-permute-start(bf16[4,8,16,640]{3,2,1,0:T(8,128)(2,1)S(1)} %pad_maximum_fusion.refs_6_), channel_id=1, source_target_pairs={{0,128},{128,256},{256,384},{384,0},{64,448},{192,64},{320,192},{4... | collective-permute-start | bytes 1966088 | tf_op jit(solution)/shard_map/ppermute | solution.py:38
  85.6 19.8 %collective-permute-start = (bf16[4,8,16,640]{3,2,1,0:T(8,128)(2,1)S(1)}, bf16[4,8,16,640]{3,2,1,0:T(8,128)(2,1)S(1)}, u32[]{:S(2)}, u32[]{:S(2)}) collective-permute-start(bf16[4,8,16,640]{3,2,1,0:T(8,128)(2,1)S(1)} %all-to-all-done.2.refs_2_), channel_id=1, source_target_pairs={{0,1},{1,2},{2,3},{3,0},{64,67},{65,64},{66,65},{67,66},{4,5},{5,6... | collective-permute-start | bytes 1966088 | tf_op jit(solution)/shard_map/ppermute | solution.py:38
  87.6 19.8 %collective-permute-start.7 = (bf16[4,8,16,640]{3,2,1,0:T(8,128)(2,1)S(1)}, bf16[4,8,16,640]{3,2,1,0:T(8,128)(2,1)S(1)}, u32[]{:S(2)}, u32[]{:S(2)}) collective-permute-start(bf16[4,8,16,640]{3,2,1,0:T(8,128)(2,1)S(1)} %pad_maximum_fusion.refs_6_), channel_id=1, source_target_pairs={{0,384},{128,0},{256,128},{384,256},{64,192},{192,320},{320,448},{... | collective-permute-start | bytes 1966088 | tf_op jit(solution)/shard_map/ppermute | solution.py:39
  90.7 20.1 %collective-permute-start.1 = (bf16[4,8,16,640]{3,2,1,0:T(8,128)(2,1)S(1)}, bf16[4,8,16,640]{3,2,1,0:T(8,128)(2,1)S(1)}, u32[]{:S(2)}, u32[]{:S(2)}) collective-permute-start(bf16[4,8,16,640]{3,2,1,0:T(8,128)(2,1)S(1)} %all-to-all-done.2.refs_2_), channel_id=1, source_target_pairs={{0,3},{1,0},{2,1},{3,2},{64,65},{65,66},{66,67},{67,64},{4,7},{5,4... | collective-permute-start | bytes 1966088 | tf_op jit(solution)/shard_map/ppermute | solution.py:39
  101.5 13.9 %collective-permute-start.8 = (bf16[4,8,16,640]{3,2,1,0:T(8,128)(2,1)}, bf16[4,8,16,640]{3,2,1,0:T(8,128)(2,1)S(1)}, u32[]{:S(2)}, u32[]{:S(2)}) collective-permute-start(bf16[4,8,16,640]{3,2,1,0:T(8,128)(2,1)} %collective-permute-done.6.refs_7_), channel_id=1, source_target_pairs={{0,128},{128,256},{256,384},{384,0},{64,448},{192,64},{320,192},{4... | collective-permute-start | bytes 1966088 | tf_op jit(solution)/shard_map/ppermute | solution.py:40
  105.4 13.7 %collective-permute-start.2 = (bf16[4,8,16,640]{3,2,1,0:T(8,128)(2,1)S(1)}, bf16[4,8,16,640]{3,2,1,0:T(8,128)(2,1)S(1)}, u32[]{:S(2)}, u32[]{:S(2)}) collective-permute-start(bf16[4,8,16,640]{3,2,1,0:T(8,128)(2,1)S(1)} %collective-permute-done.refs_3_), channel_id=1, source_target_pairs={{0,1},{1,2},{2,3},{3,0},{64,67},{65,64},{66,65},{67,66},{4,5},{5,6... | collective-permute-start | bytes 1966088 | tf_op jit(solution)/shard_map/ppermute | solution.py:40
  107.4 3.4 %copy-start.1 = (bf16[4,8,16,640]{3,2,1,0:T(8,128)(2,1)}, bf16[4,8,16,640]{3,2,1,0:T(8,128)(2,1)S(1)}, u32[]{:S(2)}) copy-start(bf16[4,8,16,640]{3,2,1,0:T(8,128)(2,1)S(1)} %collective-permute-done.7.refs_8_) | copy-start | bytes 1966084
  115.4 0.9 copy-start.2
  127.2 4.4 %collective-permute-start.9 = (f32[320,640]{1,0:T(8,128)}, f32[320,640]{1,0:T(8,128)S(1)}, u32[]{:S(2)}, u32[]{:S(2)}) collective-permute-start(f32[320,640]{1,0:T(8,128)} %get-tuple-element.14), channel_id=1, source_target_pairs={{0,64},{64,0},{1,65},{65,1},{2,66},{66,2},{3,67},{67,3},{4,68},{68... | collective-permute-start | bytes 2457608 | tf_op jit(solution)/shard_map/ppermute | solution.py:275
  131.6 1.1 copy-start
  133.9 14.3 %collective-permute-start.10 = (bf16[320,640]{1,0:T(8,128)(2,1)S(1)}, bf16[320,640]{1,0:T(8,128)(2,1)S(1)}, u32[]{:S(2)}, u32[]{:S(2)}) collective-permute-start(bf16[320,640]{1,0:T(8,128)(2,1)S(1)} %finish.1.own_ref), channel_id=1, source_target_pairs={{0,1},{1,2},{2,3},{3,0},{64,67},{65,64},{66,65},{67,66},{4,5},{5,6... | collective-permute-start | bytes 1228808 | tf_op jit(solution)/shard_map/ppermute | solution.py:38
  135.8 14.3 %collective-permute-start.11 = (bf16[320,640]{1,0:T(8,128)(2,1)S(1)}, bf16[320,640]{1,0:T(8,128)(2,1)S(1)}, u32[]{:S(2)}, u32[]{:S(2)}) collective-permute-start(bf16[320,640]{1,0:T(8,128)(2,1)S(1)} %finish.1.own_ref), channel_id=1, source_target_pairs={{0,3},{1,0},{2,1},{3,2},{64,65},{65,66},{66,67},{67,64},{4,7},{5,4... | collective-permute-start | bytes 1228808 | tf_op jit(solution)/shard_map/ppermute | solution.py:39
  148.3 11.0 %collective-permute-start.12 = (bf16[320,640]{1,0:T(8,128)(2,1)S(1)}, bf16[320,640]{1,0:T(8,128)(2,1)S(1)}, u32[]{:S(2)}, u32[]{:S(2)}) collective-permute-start(bf16[320,640]{1,0:T(8,128)(2,1)S(1)} %collective-permute-done.10.ahead_ref), channel_id=1, source_target_pairs={{0,1},{1,2},{2,3},{3,0},{64,67},{65,64},{66,65},{67,66},{4,5},{5,6... | collective-permute-start | bytes 1228808 | tf_op jit(solution)/shard_map/ppermute | solution.py:40
Sparse Core Ops, SparseCore 0:
  25.2 90.5 all-gather.1
